TPU v7x, 32 devices: a whole 2x2x4 slice. The times are simulated.
32 devices in a mesh: grp: 4 (over y, x), tile: 8 (over z, core).
Axes of the slice: x: 2, y: 2, z: 4, core: 2. Of those that a mesh axis runs over, the one named last changes fastest.
Arguments:
- pool_input: float32 [32, 512, 256], P('grp', 'tile'), may hold values from 0 to 20
- weight_first: bfloat16 [3, 3, 256, 512], replicated, may hold values from -0.125 to 0.125
- weight_second: bfloat16 [3, 3, 512, 512], replicated, may hold values from -0.09375 to 0.09375
- targets: float32 [2, 512, 512], replicated, may hold values from -0.3 to 0.3
Outputs:
- image_grad: float32 [32, 512, 256], P('grp', 'tile')
All inputs are finite; a program needn't handle non-finite values.
Results may differ from a plain program's by a relative error of at most 0.0028.
Values may be sent and summed in bfloat16 or wider, within the bound.
No kernel may reach another device: no remote copies, remote signals or barrier semaphores. Data moves between devices by JAX's collectives and lax.ppermute only.
A program may use at most 64 MiB of HBM per device.

v0:
```python
import jax
import jax.numpy as jnp
from jax import lax
from jax.sharding import PartitionSpec as P

GELU_SCALE = 0.7978845608
GELU_CUBIC = 0.044715


def with_halo(array, sides, width):
    for axis, dim in sides:
        size, length = (lax.axis_size(axis), array.shape[dim])
        up = [(i, (i + 1) % size) for i in range(size - 1)]
        down = [(j, i) for i, j in up]
        last = lax.slice_in_dim(array, length - width, length, axis=dim)
        leading = lax.slice_in_dim(array, 0, width, axis=dim)
        before = lax.ppermute(last, axis, up)
        after = lax.ppermute(leading, axis, down)
        array = jnp.concatenate([before, array, after], axis=dim)
    return array


def gelu_value(values):
    return 0.5 * values * (1.0 + jnp.tanh(GELU_SCALE * (values + GELU_CUBIC * values**3)))


def gelu_slope(values):
    hyper = jnp.tanh(GELU_SCALE * (values + GELU_CUBIC * values**3))
    return 0.5 * (1.0 + hyper) + 0.5 * values * (1.0 - hyper * hyper) * GELU_SCALE * (
        1.0 + 3.0 * GELU_CUBIC * values * values
    )


def conv_fwd(padded, weight, height, breadth):
    summed = None
    for row_shift in range(3):
        for col_shift in range(3):
            window = padded[
                row_shift : row_shift + height, col_shift : col_shift + breadth, :
            ].reshape(height * breadth, -1)
            product = jnp.dot(
                window, weight[row_shift, col_shift], preferred_element_type=jnp.float32
            )
            summed = product if summed is None else summed + product
    return summed.reshape(height, breadth, -1)


def conv_back(padded, weight, height, breadth):
    summed = None
    for row_shift in range(3):
        for col_shift in range(3):
            window = padded[
                2 - row_shift : 2 - row_shift + height, 2 - col_shift : 2 - col_shift + breadth, :
            ].reshape(height * breadth, -1)
            product = lax.dot_general(
                window,
                weight[row_shift, col_shift],
                (((1,), (1,)), ((), ())),
                preferred_element_type=jnp.float32,
            )
            summed = product if summed is None else summed + product
    return summed.reshape(height, breadth, -1)


def inner_dot(left, right):
    return lax.dot_general(
        left,
        right,
        (((0,), (0,)), ((), ())),
        precision=lax.Precision.HIGHEST,
        preferred_element_type=jnp.float32,
    )


def local(pool_input, weight_first, weight_second, targets):
    tile_rows = pool_input.shape[0]
    tile_cols = pool_input.shape[1]
    width_out = weight_first.shape[3]
    pool_bf = pool_input.astype(jnp.bfloat16)
    reach = 1
    padded_pool = with_halo(pool_bf, (("grp", 0), ("tile", 1)), reach)
    pre_first = conv_fwd(padded_pool, weight_first, tile_rows, tile_cols)
    act_first = gelu_value(pre_first)
    padded_first = with_halo(act_first.astype(jnp.bfloat16), (("grp", 0), ("tile", 1)), 1)
    pre_second = conv_fwd(padded_first, weight_second, tile_rows, tile_cols)
    act_second = gelu_value(pre_second)
    flat_first = act_first.reshape(-1, width_out)
    flat_second = act_second.reshape(-1, width_out)
    positions = tile_rows * tile_cols * lax.axis_size("grp") * lax.axis_size("tile")
    column_sums = lax.psum(
        (jnp.sum(flat_first, axis=0), jnp.sum(flat_second, axis=0)), ("grp", "tile")
    )
    mean_first = column_sums[0] / positions
    mean_second = column_sums[1] / positions
    centred_first = flat_first - mean_first
    centred_second = flat_second - mean_second
    left_first, left_second = (centred_first, centred_second)
    share_rows = width_out // lax.axis_size("tile")
    gram_share = lax.psum_scatter(
        jnp.concatenate(
            [inner_dot(left_first, left_first), inner_dot(left_second, left_second)], axis=1
        ).astype(jnp.bfloat16),
        "tile",
        scatter_dimension=0,
        tiled=True,
    ).astype(jnp.float32)
    gram_share = lax.psum(gram_share, "grp")
    offset = lax.axis_index("tile") * share_rows
    gram_first = gram_share[:, :width_out] / positions
    gram_second = gram_share[:, width_out:] / positions
    miss_first = gram_first - lax.dynamic_slice_in_dim(targets[0], offset, share_rows, 0)
    miss_second = gram_second - lax.dynamic_slice_in_dim(targets[1], offset, share_rows, 0)
    diff_share = jnp.concatenate([miss_first, miss_second], axis=1)
    mismatch = lax.all_gather(diff_share, "tile", axis=0, tiled=True)
    miss_first = mismatch[:, :width_out]
    miss_second = mismatch[:, width_out:]
    symmetric_first = (miss_first + miss_first.T) * 0.5
    symmetric_second = (miss_second + miss_second.T) * 0.5
    push_first = jnp.dot(
        centred_first,
        symmetric_first,
        precision=lax.Precision.HIGHEST,
        preferred_element_type=jnp.float32,
    ).reshape(tile_rows, tile_cols, width_out)
    push_second = jnp.dot(
        centred_second,
        symmetric_second,
        precision=lax.Precision.HIGHEST,
        preferred_element_type=jnp.float32,
    ).reshape(tile_rows, tile_cols, width_out)
    grad_second = (push_second * gelu_slope(pre_second)).astype(jnp.bfloat16)
    padded_second = with_halo(grad_second, (("grp", 0), ("tile", 1)), 1)
    flow_first = push_first + conv_back(padded_second, weight_second, tile_rows, tile_cols)
    grad_first = (flow_first * gelu_slope(pre_first)).astype(jnp.bfloat16)
    padded_grad = with_halo(grad_first, (("grp", 0), ("tile", 1)), 1)
    return conv_back(padded_grad, weight_first, tile_rows, tile_cols)


def solution(mesh):
    return jax.shard_map(
        local,
        mesh=mesh,
        in_specs=(P("grp", "tile", None), P(), P(), P()),
        out_specs=P("grp", "tile", None),
        check_vma=False,
    )
```

profile of v0, /device:TPU:1, one launch (start us, length us, event | category | flops | bytes accessed | tf_op | source)
XLA Modules:
  0.0 250.3 jit_solution(12958362300728123917)
XLA Ops:
  6.5 1.1 convert_element_type.19
  7.6 3.9 %collective-permute-start = (bf16[1,64,256]{2,1,0:T(8,128)(2,1)S(1)}, bf16[1,64,256]{2,1,0:T(8,128)(2,1)S(1)}, u32[]{:S(2)}, u32[]{:S(2)}) collective-permute-start(bf16[1,64,256]{2,1,0:T(8,128)(2,1)S(1)} %get-tuple-element.67), channel_id=1, source_target_pairs={{0,8},{8,16},{16,24},{1,9},{9,17},{17,25},{2,10},{10,18},{18,26},{... | collective-permute-start | bytes 98312 | tf_op jit(solution)/shard_map/ppermute | solution.py:17
  11.6 1.3 collective-permute-start.1
  12.9 3.3 %collective-permute-done.1 = bf16[1,64,256]{2,1,0:T(8,128)(2,1)S(1)} collective-permute-done((bf16[1,64,256]{2,1,0:T(8,128)(2,1)S(1)}, bf16[1,64,256]{2,1,0:T(8,128)(2,1)S(1)}, u32[]{:S(2)}, u32[]{:S(2)}) %collective-permute-start.1) | collective-permute-done | bytes 32800 | tf_op jit(solution)/shard_map/ppermute | solution.py:18
  16.3 5.2 %collective-permute-start.2 = (bf16[10,1,256]{2,1,0:T(2,128)(2,1)S(1)}, bf16[10,1,256]{2,1,0:T(2,128)(2,1)S(1)}, u32[]{:S(2)}, u32[]{:S(2)}) collective-permute-start(bf16[10,1,256]{2,1,0:T(2,128)(2,1)S(1)} %get-tuple-element.63), channel_id=1, source_target_pairs={{0,1},{1,2},{2,3},{3,4},{4,5},{5,6},{6,7},{8,9},{9,10},{10,11},{11... | collective-permute-start | bytes 15368 | tf_op jit(solution)/shard_map/ppermute | solution.py:17
  21.5 1.9 collective-permute-start.3
  23.4 1.2 fusion.104
  24.7 1.8 collective-permute-done.3
  28.9 0.6 fusion.131
  29.8 4.1 %collective-permute-start.4 = (bf16[1,64,512]{2,1,0:T(8,128)(2,1)S(1)}, bf16[1,64,512]{2,1,0:T(8,128)(2,1)S(1)}, u32[]{:S(2)}, u32[]{:S(2)}) collective-permute-start(bf16[1,64,512]{2,1,0:T(8,128)(2,1)S(1)} %get-tuple-element.53), channel_id=1, source_target_pairs={{0,8},{8,16},{16,24},{1,9},{9,17},{17,25},{2,10},{10,18},{18,26},{... | collective-permute-start | bytes 196616 | tf_op jit(solution)/shard_map/ppermute | solution.py:17
  34.0 1.3 collective-permute-start.5
  35.3 3.7 %collective-permute-done.5 = bf16[1,64,512]{2,1,0:T(8,128)(2,1)S(1)} collective-permute-done((bf16[1,64,512]{2,1,0:T(8,128)(2,1)S(1)}, bf16[1,64,512]{2,1,0:T(8,128)(2,1)S(1)}, u32[]{:S(2)}, u32[]{:S(2)}) %collective-permute-start.5) | collective-permute-done | bytes 65568 | tf_op jit(solution)/shard_map/ppermute | solution.py:18
  39.0 4.6 %collective-permute-start.6 = (bf16[10,1,512]{2,1,0:T(2,128)(2,1)S(1)}, bf16[10,1,512]{2,1,0:T(2,128)(2,1)S(1)}, u32[]{:S(2)}, u32[]{:S(2)}) collective-permute-start(bf16[10,1,512]{2,1,0:T(2,128)(2,1)S(1)} %get-tuple-element.39), channel_id=1, source_target_pairs={{0,1},{1,2},{2,3},{3,4},{4,5},{5,6},{6,7},{8,9},{9,10},{10,11},{11... | collective-permute-start | bytes 30728 | tf_op jit(solution)/shard_map/ppermute | solution.py:17
  43.7 1.9 collective-permute-start.7
  46.2 2.6 %collective-permute-done.7 = bf16[10,1,512]{2,1,0:T(2,128)(2,1)S(1)} collective-permute-done((bf16[10,1,512]{2,1,0:T(2,128)(2,1)S(1)}, bf16[10,1,512]{2,1,0:T(2,128)(2,1)S(1)}, u32[]{:S(2)}, u32[]{:S(2)}) %collective-permute-start.7) | collective-permute-done | bytes 10272 | tf_op jit(solution)/shard_map/ppermute | solution.py:18
  50.8 0.5 convolution_add_fusion.10
  52.7 1.7 fusion.65
  54.3 38.1 %all-reduce = (f32[512]{0:T(512)S(1)}, f32[512]{0:T(512)S(1)}) all-reduce(f32[512]{0:T(512)S(1)} %get-tuple-element.69, f32[512]{0:T(512)S(1)} %get-tuple-element.71), channel_id=1, replica_groups=mesh['grp'=4,'tile'=8] {'grp','tile'}, use_global_device_ids=true, to_apply=%region_3.0 | all-reduce | flops 1024 | bytes 8192 | tf_op jit(solution)/shard_map/psum | solution.py:90
  92.8 1.9 convolution_convert_fusion.1
  95.0 1.9 convolution_convert_fusion
  96.9 1.1 pad_maximum_fusion
  98.0 2.3 copy.18
  100.3 1.7 fusion.133
  102.4 27.8 %reduce-scatter.4.cloned.1.call-done = bf16[64,1024]{1,0:T(8,128)(2,1)} async-done(((bf16[512,1024]{1,0:T(8,128)(2,1)}), bf16[64,1024]{1,0:T(8,128)(2,1)}) %reduce-scatter.4.cloned.1.call-update) | async-done | bytes 131088
  130.2 1.1 copy.19
  131.3 22.6 %all-reduce.2 = f32[64,1024]{0,1:T(8,128)S(1)} all-reduce(bf16[64,1024]{0,1:T(8,128)(2,1)S(1)} %copy.19), channel_id=1, replica_groups=mesh['grp'=4,'tile'=8] {'grp'}, use_global_device_ids=true, to_apply=%region_5.0 | all-reduce | flops 65536 | bytes 393216 | tf_op jit(solution)/shard_map/psum | solution.py:107
  154.0 0.9 copy.13
  154.9 35.3 %all-gather.2.cloned.1.call-done = f32[512,1024]{1,0:T(8,128)} async-done(((f32[64,1024]{1,0:T(8,128)}), f32[512,1024]{1,0:T(8,128)}) %all-gather.2.cloned.1.call-update) | async-done | bytes 2097168 | tf_op jit(solution)/shard_map/all_gather | solution.py:114
  190.2 2.7 %fusion.132 = (f32[512,512]{1,0:T(8,128)S(1)}, f32[512,512]{1,0:T(8,128)}) fusion(f32[512,1024]{1,0:T(8,128)} %all-gather.2.cloned.1.call-done), kind=kLoop, calls=%fused_computation.207 | loop fusion | bytes 4194304 | tf_op jit(solution)/shard_map/slice | solution.py:116
  192.9 1.3 copy.21
  194.2 4.6 %fusion.3 = bf16[8,64,512]{2,1,0:T(8,128)(2,1)S(1)} fusion(f32[8,64,512]{2,1,0:T(8,128)} %bitcast.210, f32[8,64,512]{2,1,0:T(8,128)} %bitcast.241, f32[512,512]{0,1:T(8,128)} %copy.21, f32[512,1024]{1,0:T(8,128)} %all-gather.2.cloned.1.call-done), kind=kOutput, calls=%fused_computation.31 | convolution fusion | flops 1616117760 | bytes 4718592 | tf_op jit(solution)/shard_map/dot_general | solution.py:125
  198.8 3.1 %collective-permute-start.8 = (bf16[1,64,512]{2,1,0:T(8,128)(2,1)S(1)}, bf16[1,64,512]{2,1,0:T(8,128)(2,1)S(1)}, u32[]{:S(2)}, u32[]{:S(2)}) collective-permute-start(bf16[1,64,512]{2,1,0:T(8,128)(2,1)S(1)} %get-tuple-element.47), channel_id=1, source_target_pairs={{0,8},{8,16},{16,24},{1,9},{9,17},{17,25},{2,10},{10,18},{18,26},{... | collective-permute-start | bytes 196616 | tf_op jit(solution)/shard_map/ppermute | solution.py:17
  201.9 1.3 collective-permute-start.9
  203.2 2.5 %copy.20 = f32[512,512]{0,1:T(8,128)} copy(f32[512,512]{1,0:T(8,128)} %get-tuple-element.8) | data formatting | bytes 2097152
  205.7 3.6 %fusion.36 = f32[8,64,512]{2,1,0:T(8,128)S(1)} fusion(f32[8,64,512]{2,1,0:T(8,128)S(1)} %bitcast.203, f32[512,512]{0,1:T(8,128)} %copy.20, f32[512,1024]{1,0:T(8,128)} %all-gather.2.cloned.1.call-done), kind=kOutput, calls=%fused_computation.74 | convolution fusion | flops 1611137024 | bytes 4194304 | tf_op jit(solution)/shard_map/dot_general | solution.py:119
  209.4 2.5 collective-permute-start.10
  211.9 3.3 %collective-permute-start.11 = (bf16[10,1,512]{2,1,0:T(2,128)(2,1)S(1)}, bf16[10,1,512]{2,1,0:T(2,128)(2,1)S(1)}, u32[]{:S(2)}, u32[]{:S(2)}) collective-permute-start(bf16[10,1,512]{2,1,0:T(2,128)(2,1)S(1)} %get-tuple-element.36), channel_id=1, source_target_pairs={{0,1},{1,2},{2,3},{3,4},{4,5},{5,6},{6,7},{8,9},{9,10},{10,11},{11... | collective-permute-start | bytes 30728 | tf_op jit(solution)/shard_map/ppermute | solution.py:17
  215.3 1.6 fusion.56
  220.0 0.5 convolution_add_fusion.2
  220.9 0.5 fusion
  221.4 0.7 fusion.32
  222.2 4.2 %collective-permute-start.12 = (bf16[1,64,512]{2,1,0:T(8,128)(2,1)S(1)}, bf16[1,64,512]{2,1,0:T(8,128)(2,1)S(1)}, u32[]{:S(2)}, u32[]{:S(2)}) collective-permute-start(bf16[1,64,512]{2,1,0:T(8,128)(2,1)S(1)} %get-tuple-element.43), channel_id=1, source_target_pairs={{0,8},{8,16},{16,24},{1,9},{9,17},{17,25},{2,10},{10,18},{18,26},{... | collective-permute-start | bytes 196616 | tf_op jit(solution)/shard_map/ppermute | solution.py:17
  226.3 1.3 collective-permute-start.13
  227.6 0.6 collective-permute-done.12
  228.2 4.5 %collective-permute-done.13 = bf16[1,64,512]{2,1,0:T(8,128)(2,1)S(1)} collective-permute-done((bf16[1,64,512]{2,1,0:T(8,128)(2,1)S(1)}, bf16[1,64,512]{2,1,0:T(8,128)(2,1)S(1)}, u32[]{:S(2)}, u32[]{:S(2)}) %collective-permute-start.13) | collective-permute-done | bytes 65568 | tf_op jit(solution)/shard_map/ppermute | solution.py:18
  232.8 2.3 collective-permute-start.14
  235.1 3.3 %collective-permute-start.15 = (bf16[10,1,512]{2,1,0:T(2,128)(2,1)S(1)}, bf16[10,1,512]{2,1,0:T(2,128)(2,1)S(1)}, u32[]{:S(2)}, u32[]{:S(2)}) collective-permute-start(bf16[10,1,512]{2,1,0:T(2,128)(2,1)S(1)} %get-tuple-element.32), channel_id=1, source_target_pairs={{0,1},{1,2},{2,3},{3,4},{4,5},{5,6},{6,7},{8,9},{9,10},{10,11},{11... | collective-permute-start | bytes 30728 | tf_op jit(solution)/shard_map/ppermute | solution.py:17
  242.3 1.2 fusion.4
  (93 shorter events, 15.3 us)
Async XLA Ops:
  6.5 123.6 %reduce-scatter.4.cloned.1.call-start = ((), (), s32[]{:S(2)}) async-start(), calls=%async_computation.2 | async-start | bytes 1179648
  7.6 5.2 %collective-permute-start = (bf16[1,64,256]{2,1,0:T(8,128)(2,1)S(1)}, bf16[1,64,256]{2,1,0:T(8,128)(2,1)S(1)}, u32[]{:S(2)}, u32[]{:S(2)}) collective-permute-start(bf16[1,64,256]{2,1,0:T(8,128)(2,1)S(1)} %get-tuple-element.67), channel_id=1, source_target_pairs={{0,8},{8,16},{16,24},{1,9},{9,17},{17,25},{2,10},{10,18},{18,26},{... | collective-permute-start | bytes 98312 | tf_op jit(solution)/shard_map/ppermute | solution.py:17
  11.6 4.7 %collective-permute-start.1 = (bf16[1,64,256]{2,1,0:T(8,128)(2,1)S(1)}, bf16[1,64,256]{2,1,0:T(8,128)(2,1)S(1)}, u32[]{:S(2)}, u32[]{:S(2)}) collective-permute-start(bf16[1,64,256]{2,1,0:T(8,128)(2,1)S(1)} %get-tuple-element.68), channel_id=1, source_target_pairs={{8,0},{16,8},{24,16},{9,1},{17,9},{25,17},{10,2},{18,10},{26,18},{... | collective-permute-start | bytes 98312 | tf_op jit(solution)/shard_map/ppermute | solution.py:18
  16.3 8.4 %collective-permute-start.2 = (bf16[10,1,256]{2,1,0:T(2,128)(2,1)S(1)}, bf16[10,1,256]{2,1,0:T(2,128)(2,1)S(1)}, u32[]{:S(2)}, u32[]{:S(2)}) collective-permute-start(bf16[10,1,256]{2,1,0:T(2,128)(2,1)S(1)} %get-tuple-element.63), channel_id=1, source_target_pairs={{0,1},{1,2},{2,3},{3,4},{4,5},{5,6},{6,7},{8,9},{9,10},{10,11},{11... | collective-permute-start | bytes 15368 | tf_op jit(solution)/shard_map/ppermute | solution.py:17
  21.5 5.0 %collective-permute-start.3 = (bf16[10,1,256]{2,1,0:T(2,128)(2,1)S(1)}, bf16[10,1,256]{2,1,0:T(2,128)(2,1)S(1)}, u32[]{:S(2)}, u32[]{:S(2)}) collective-permute-start(bf16[10,1,256]{2,1,0:T(2,128)(2,1)S(1)} %get-tuple-element.64), channel_id=1, source_target_pairs={{1,0},{2,1},{3,2},{4,3},{5,4},{6,5},{7,6},{9,8},{10,9},{11,10},{12... | collective-permute-start | bytes 15368 | tf_op jit(solution)/shard_map/ppermute | solution.py:18
  24.7 2.1 copy-start
  28.6 17.1 %slice-start = ((s8[4718592]{0:T(1024)(128)(4,1)}), s8[4194304]{0:T(1024)(128)(4,1)S(1)}, s32[]{:S(2)}) async-start(s8[4718592]{0:T(1024)(128)(4,1)} %bitcast.204), calls=%async_computation.3 | async-start | bytes 8388608
  28.9 16.8 %slice-start.1 = ((s8[4718592]{0:T(1024)(128)(4,1)}), s8[524288]{0:T(1024)(128)(4,1)S(1)}, s32[]{:S(2)}) async-start(s8[4718592]{0:T(1024)(128)(4,1)} %bitcast.204), calls=%async_computation.4 | async-start | bytes 1048576
  29.8 5.5 %collective-permute-start.4 = (bf16[1,64,512]{2,1,0:T(8,128)(2,1)S(1)}, bf16[1,64,512]{2,1,0:T(8,128)(2,1)S(1)}, u32[]{:S(2)}, u32[]{:S(2)}) collective-permute-start(bf16[1,64,512]{2,1,0:T(8,128)(2,1)S(1)} %get-tuple-element.53), channel_id=1, source_target_pairs={{0,8},{8,16},{16,24},{1,9},{9,17},{17,25},{2,10},{10,18},{18,26},{... | collective-permute-start | bytes 196616 | tf_op jit(solution)/shard_map/ppermute | solution.py:17
  34.0 5.0 %collective-permute-start.5 = (bf16[1,64,512]{2,1,0:T(8,128)(2,1)S(1)}, bf16[1,64,512]{2,1,0:T(8,128)(2,1)S(1)}, u32[]{:S(2)}, u32[]{:S(2)}) collective-permute-start(bf16[1,64,512]{2,1,0:T(8,128)(2,1)S(1)} %get-tuple-element.54), channel_id=1, source_target_pairs={{8,0},{16,8},{24,16},{9,1},{17,9},{25,17},{10,2},{18,10},{26,18},{... | collective-permute-start | bytes 196616 | tf_op jit(solution)/shard_map/ppermute | solution.py:18
  39.0 7.1 %collective-permute-start.6 = (bf16[10,1,512]{2,1,0:T(2,128)(2,1)S(1)}, bf16[10,1,512]{2,1,0:T(2,128)(2,1)S(1)}, u32[]{:S(2)}, u32[]{:S(2)}) collective-permute-start(bf16[10,1,512]{2,1,0:T(2,128)(2,1)S(1)} %get-tuple-element.39), channel_id=1, source_target_pairs={{0,1},{1,2},{2,3},{3,4},{4,5},{5,6},{6,7},{8,9},{9,10},{10,11},{11... | collective-permute-start | bytes 30728 | tf_op jit(solution)/shard_map/ppermute | solution.py:17
  43.7 5.1 %collective-permute-start.7 = (bf16[10,1,512]{2,1,0:T(2,128)(2,1)S(1)}, bf16[10,1,512]{2,1,0:T(2,128)(2,1)S(1)}, u32[]{:S(2)}, u32[]{:S(2)}) collective-permute-start(bf16[10,1,512]{2,1,0:T(2,128)(2,1)S(1)} %get-tuple-element.40), channel_id=1, source_target_pairs={{1,0},{2,1},{3,2},{4,3},{5,4},{6,5},{7,6},{9,8},{10,9},{11,10},{12... | collective-permute-start | bytes 30728 | tf_op jit(solution)/shard_map/ppermute | solution.py:18
  92.4 2.2 copy-start.3
  95.0 3.0 %copy-start.2 = (f32[512,512]{1,0:T(8,128)}, f32[512,512]{1,0:T(8,128)S(1)}, u32[]{:S(2)}) copy-start(f32[512,512]{1,0:T(8,128)S(1)} %broadcast_subtract_fusion) | copy-start | bytes 3145732
  100.3 89.9 %all-gather.2.cloned.1.call-start = ((), (), s32[]{:S(2)}) async-start(), calls=%async_computation.1 | async-start | bytes 2359296 | tf_op jit(solution)/shard_map/all_gather | solution.py:114
  198.8 10.5 %collective-permute-start.8 = (bf16[1,64,512]{2,1,0:T(8,128)(2,1)S(1)}, bf16[1,64,512]{2,1,0:T(8,128)(2,1)S(1)}, u32[]{:S(2)}, u32[]{:S(2)}) collective-permute-start(bf16[1,64,512]{2,1,0:T(8,128)(2,1)S(1)} %get-tuple-element.47), channel_id=1, source_target_pairs={{0,8},{8,16},{16,24},{1,9},{9,17},{17,25},{2,10},{10,18},{18,26},{... | collective-permute-start | bytes 196616 | tf_op jit(solution)/shard_map/ppermute | solution.py:17
  201.9 7.4 %collective-permute-start.9 = (bf16[1,64,512]{2,1,0:T(8,128)(2,1)S(1)}, bf16[1,64,512]{2,1,0:T(8,128)(2,1)S(1)}, u32[]{:S(2)}, u32[]{:S(2)}) collective-permute-start(bf16[1,64,512]{2,1,0:T(8,128)(2,1)S(1)} %get-tuple-element.48), channel_id=1, source_target_pairs={{8,0},{16,8},{24,16},{9,1},{17,9},{25,17},{10,2},{18,10},{26,18},{... | collective-permute-start | bytes 196616 | tf_op jit(solution)/shard_map/ppermute | solution.py:18
  205.7 11.8 %slice-start.2 = ((s8[4718592]{0:T(1024)(128)(4,1)}), s8[4194304]{0:T(1024)(128)(4,1)S(1)}, s32[]{:S(2)}) async-start(s8[4718592]{0:T(1024)(128)(4,1)} %bitcast.206), calls=%async_computation.5 | async-start | bytes 8388608
  209.4 7.5 %collective-permute-start.10 = (bf16[10,1,512]{2,1,0:T(2,128)(2,1)S(1)}, bf16[10,1,512]{2,1,0:T(2,128)(2,1)S(1)}, u32[]{:S(2)}, u32[]{:S(2)}) collective-permute-start(bf16[10,1,512]{2,1,0:T(2,128)(2,1)S(1)} %get-tuple-element.35), channel_id=1, source_target_pairs={{1,0},{2,1},{3,2},{4,3},{5,4},{6,5},{7,6},{9,8},{10,9},{11,10},{12... | collective-permute-start | bytes 30728 | tf_op jit(solution)/shard_map/ppermute | solution.py:18
  211.9 5.0 %collective-permute-start.11 = (bf16[10,1,512]{2,1,0:T(2,128)(2,1)S(1)}, bf16[10,1,512]{2,1,0:T(2,128)(2,1)S(1)}, u32[]{:S(2)}, u32[]{:S(2)}) collective-permute-start(bf16[10,1,512]{2,1,0:T(2,128)(2,1)S(1)} %get-tuple-element.36), channel_id=1, source_target_pairs={{0,1},{1,2},{2,3},{3,4},{4,5},{5,6},{6,7},{8,9},{9,10},{10,11},{11... | collective-permute-start | bytes 30728 | tf_op jit(solution)/shard_map/ppermute | solution.py:17
  215.3 2.3 slice-start.3
  221.4 17.0 %copy-start.1 = (bf16[3,3,256,512]{3,2,1,0:T(8,128)(2,1)S(1)}, bf16[3,3,256,512]{3,2,1,0:T(8,128)(2,1)}, u32[]{:S(2)}) copy-start(bf16[3,3,256,512]{3,2,1,0:T(8,128)(2,1)} %param.5) | copy-start | bytes 7077892
  222.2 6.0 %collective-permute-start.12 = (bf16[1,64,512]{2,1,0:T(8,128)(2,1)S(1)}, bf16[1,64,512]{2,1,0:T(8,128)(2,1)S(1)}, u32[]{:S(2)}, u32[]{:S(2)}) collective-permute-start(bf16[1,64,512]{2,1,0:T(8,128)(2,1)S(1)} %get-tuple-element.43), channel_id=1, source_target_pairs={{0,8},{8,16},{16,24},{1,9},{9,17},{17,25},{2,10},{10,18},{18,26},{... | collective-permute-start | bytes 196616 | tf_op jit(solution)/shard_map/ppermute | solution.py:17
  226.3 6.4 %collective-permute-start.13 = (bf16[1,64,512]{2,1,0:T(8,128)(2,1)S(1)}, bf16[1,64,512]{2,1,0:T(8,128)(2,1)S(1)}, u32[]{:S(2)}, u32[]{:S(2)}) collective-permute-start(bf16[1,64,512]{2,1,0:T(8,128)(2,1)S(1)} %get-tuple-element.44), channel_id=1, source_target_pairs={{8,0},{16,8},{24,16},{9,1},{17,9},{25,17},{10,2},{18,10},{26,18},{... | collective-permute-start | bytes 196616 | tf_op jit(solution)/shard_map/ppermute | solution.py:18
  232.8 6.0 %collective-permute-start.14 = (bf16[10,1,512]{2,1,0:T(2,128)(2,1)S(1)}, bf16[10,1,512]{2,1,0:T(2,128)(2,1)S(1)}, u32[]{:S(2)}, u32[]{:S(2)}) collective-permute-start(bf16[10,1,512]{2,1,0:T(2,128)(2,1)S(1)} %get-tuple-element.31), channel_id=1, source_target_pairs={{1,0},{2,1},{3,2},{4,3},{5,4},{6,5},{7,6},{9,8},{10,9},{11,10},{12... | collective-permute-start | bytes 30728 | tf_op jit(solution)/shard_map/ppermute | solution.py:18
  235.1 4.2 %collective-permute-start.15 = (bf16[10,1,512]{2,1,0:T(2,128)(2,1)S(1)}, bf16[10,1,512]{2,1,0:T(2,128)(2,1)S(1)}, u32[]{:S(2)}, u32[]{:S(2)}) collective-permute-start(bf16[10,1,512]{2,1,0:T(2,128)(2,1)S(1)} %get-tuple-element.32), channel_id=1, source_target_pairs={{0,1},{1,2},{2,3},{3,4},{4,5},{5,6},{6,7},{8,9},{9,10},{10,11},{11... | collective-permute-start | bytes 30728 | tf_op jit(solution)/shard_map/ppermute | solution.py:17
Sparse Core Ops, SparseCore 0:
  100.4 29.7 reduce-scatter.3
  155.0 35.1 all-gather.1
where the time goes:
time: 252 us; the launch traced here: 250 us
  waiting for transfers between devices  80.1 us (32%)
  blocking collectives  60.6 us (24%)
  starting transfers between devices  45.6 us (18%)
  matrix products  30.2 us (12%)
  local copies, waits for them, and re-layouts  14.2 us (6%)
  between operations  14.2 us (6%)
  other arithmetic  5.27 us (2%)
    psum x1, blocking collectives, local(): lax.psum((jnp.sum(flat_first, axis=0), jnp.sum(flat_second, axis=0)), ('g...  38.1 us
    all_gather x1, waiting for transfers between devices, local(): mismatch = lax.all_gather(diff_share, 'tile', axis=0, tiled=True)  35.3 us
    ppermute x8, starting transfers between devices, with_halo(): before = lax.ppermute(last, axis, up)  31.7 us
    unnamed x3, waiting for transfers between devices  27.9 us
    psum x1, blocking collectives, local(): gram_share = lax.psum(gram_share, 'grp')  22.6 us
    ppermute x8, waiting for transfers between devices, with_halo(): after = lax.ppermute(leading, axis, down)  16 us
    ppermute x8, starting transfers between devices, with_halo(): after = lax.ppermute(leading, axis, down)  13.8 us
    dot_general x18, matrix products, conv_fwd(): jnp.dot(window, weight[row_shift, col_shift], preferred_element_type=jnp....  9.16 us
  transfers between devices with their start and end apart: 18, of which 9 were waited for; matrix products, arithmetic and copies ran while one was open for 5% of the time, Pallas kernels for 0%

commit v1 on v0

v1 whole, which is shorter than its diff:
```python
import jax
import jax.numpy as jnp
from jax import lax
from jax.sharding import PartitionSpec as P

GELU_SCALE = 0.7978845608
GELU_CUBIC = 0.044715
REACH = 4
BLOCK = 128
BF = jnp.bfloat16
F32 = jnp.float32


def gelu_pair(values):
    hyper = jnp.tanh(GELU_SCALE * (values + GELU_CUBIC * values * values * values))
    act = 0.5 * values * (1.0 + hyper)
    slope = 0.5 * (1.0 + hyper) + 0.5 * values * (1.0 - hyper * hyper) * GELU_SCALE * (
        1.0 + 3.0 * GELU_CUBIC * values * values
    )
    return act, slope


def taps(padded, weight, back):
    height, breadth = padded.shape[0] - 2, padded.shape[1] - 2
    summed = None
    for a in range(3):
        for b in range(3):
            window = padded[a : a + height, b : b + breadth, :].reshape(height * breadth, -1)
            kernel = weight[2 - a, 2 - b] if back else weight[a, b]
            dims = (((1,), (1 if back else 0,)), ((), ()))
            product = lax.dot_general(window, kernel, dims, preferred_element_type=F32)
            summed = product if summed is None else summed + product
    return summed.reshape(height, breadth, -1)


def halo(pool, tiles, groups, core):
    right, left = pool[:, -REACH:], pool[:, :REACH]
    swap = [(i, i ^ 1) for i in range(tiles)]
    cross = [(i, i + 1) for i in range(1, tiles - 1, 2)]
    cross = cross + [(j, i) for i, j in cross]
    far = lax.ppermute(jnp.where(core == 0, left, right), "tile", cross)
    near = lax.ppermute(jnp.where(core == 0, right, left), "tile", swap)
    pool = jnp.concatenate(
        [jnp.where(core == 0, far, near), pool, jnp.where(core == 0, near, far)], axis=1
    )
    up = [(i, i + 1) for i in range(groups - 1)]
    down = [(j, i) for i, j in up]
    above = lax.ppermute(pool[-REACH:], "grp", up)
    below = lax.ppermute(pool[:REACH], "grp", down)
    return jnp.concatenate([above, pool, below], axis=0)


def pairs(width):
    blocks = width // BLOCK
    return [(i, j) for i in range(blocks) for j in range(i, blocks)]


def pack(matrix):
    width = matrix.shape[0]
    return jnp.concatenate(
        [
            matrix[i * BLOCK : (i + 1) * BLOCK, j * BLOCK : (j + 1) * BLOCK]
            for i, j in pairs(width)
        ],
        axis=0,
    )


def unpack(packed, width):
    blocks = width // BLOCK
    table = {}
    for n, (i, j) in enumerate(pairs(width)):
        table[i, j] = packed[n * BLOCK : (n + 1) * BLOCK]
        if i != j:
            table[j, i] = table[i, j].T
    return jnp.concatenate(
        [jnp.concatenate([table[i, j] for j in range(blocks)], axis=1) for i in range(blocks)],
        axis=0,
    )


def split(mean):
    high = mean.astype(BF)
    low = (mean - high.astype(F32)).astype(BF)
    rows = jnp.concatenate([high.reshape(-1, BLOCK), low.reshape(-1, BLOCK)], axis=0)
    return jnp.pad(rows, ((0, -rows.shape[0] % 16), (0, 0)))


def join(rows, width):
    half = width // BLOCK
    rows = rows.astype(F32)
    return (rows[:half] + rows[half : 2 * half]).reshape(-1)


def spread(means, count):
    centre = sum(means) / len(means)
    away = jnp.stack(means) - centre
    scatter = lax.dot_general(
        away, away, (((0,), (0,)), ((), ())), precision=lax.Precision.HIGHEST
    )
    return centre, pack(scatter * count)


def local(pool_input, weight_first, weight_second, targets):
    height, breadth = pool_input.shape[0], pool_input.shape[1]
    width = weight_first.shape[3]
    groups, tiles = lax.axis_size("grp"), lax.axis_size("tile")
    row, tile = lax.axis_index("grp"), lax.axis_index("tile")
    core = tile % 2
    cells = height * breadth
    positions = cells * groups * tiles

    def inside(rim):
        i = row * height - rim + jnp.arange(height + 2 * rim)
        j = tile * breadth - rim + jnp.arange(breadth + 2 * rim)
        i = (i >= 0) & (i < height * groups)
        j = (j >= 0) & (j < breadth * tiles)
        return (i[:, None] & j[None, :])[:, :, None]

    padded = halo(pool_input.astype(BF), tiles, groups, core)
    act_first, slope_first = gelu_pair(taps(padded, weight_first, False))
    first_bf = jnp.where(inside(3), act_first, 0.0).astype(BF)
    act_second, slope_second = gelu_pair(taps(first_bf, weight_second, False))

    def stats(act, rim):
        own = act[rim:-rim, rim:-rim].reshape(cells, width)
        mean = jnp.sum(own, axis=0) / cells
        own = (own - mean).astype(BF)
        return mean, pack(
            lax.dot_general(own, own, (((0,), (0,)), ((), ())), preferred_element_type=F32)
        )

    mean_first, gram_first = stats(act_first, 3)
    mean_second, gram_second = stats(act_second, 2)
    first_core = core == 0
    mean = jnp.where(first_core, mean_first, mean_second)
    gram = jnp.where(first_core, gram_first, gram_second)

    def message(part, vector):
        return jnp.concatenate([part.astype(BF), split(vector)], axis=0)

    swap = [(i, i ^ 1) for i in range(tiles)]
    sent = message(
        jnp.where(first_core, gram_second, gram_first),
        jnp.where(first_core, mean_second, mean_first),
    )
    got = lax.ppermute(sent, "tile", swap)
    rows = gram.shape[0]
    centre, extra = spread([mean, join(got[rows:], width)], cells)
    gram = gram + got[:rows].astype(F32) + extra
    chunk = rows // groups
    share = lax.dynamic_slice_in_dim(gram, row * chunk, chunk, 0)
    means, parts = [centre], [share]
    for k in range(1, groups):
        part = lax.dynamic_slice_in_dim(gram, (row ^ k) * chunk, chunk, 0)
        got = lax.ppermute(message(part, centre), "grp", [(i, i ^ k) for i in range(groups)])
        parts.append(got[:chunk].astype(F32))
        means.append(join(got[chunk:], width))
    centre, extra = spread(means, cells * 2)
    share = sum(parts) + lax.dynamic_slice_in_dim(extra, row * chunk, chunk, 0)
    sent = message(share, centre)
    means, parts = [centre], [share]
    for k in range(1, tiles // 2):
        got = lax.ppermute(sent, "tile", [(i, i ^ (2 * k)) for i in range(tiles)])
        parts.append(got[:chunk].astype(F32))
        means.append(join(got[chunk:], width))
    centre, extra = spread(means, cells * 2 * groups)
    share = sum(parts) + lax.dynamic_slice_in_dim(extra, row * chunk, chunk, 0)
    goal = [pack((t + t.T) * 0.5) for t in targets]
    goal = lax.dynamic_slice_in_dim(jnp.where(first_core, goal[0], goal[1]), row * chunk, chunk, 0)
    share = (share / positions - goal).astype(BF)
    whole = jnp.zeros((rows, BLOCK), BF)
    whole = lax.dynamic_update_slice_in_dim(whole, share, row * chunk, 0)
    for k in range(1, groups):
        got = lax.ppermute(share, "grp", [(i, i ^ k) for i in range(groups)])
        whole = lax.dynamic_update_slice_in_dim(whole, got, (row ^ k) * chunk, 0)
    mine = jnp.concatenate([whole, split(centre)], axis=0)
    other = lax.ppermute(mine, "tile", swap)

    def recentre(act, table):
        cen = act - join(table[rows:], width)
        flat = cen.reshape(-1, width).astype(BF)
        push = jnp.dot(flat, unpack(table[:rows], width), preferred_element_type=F32)
        return push.reshape(act.shape)

    push_second = recentre(act_second, jnp.where(first_core, other, mine))
    push_first = recentre(act_first[2:-2, 2:-2], jnp.where(first_core, mine, other))
    grad_second = jnp.where(inside(2), push_second * slope_second, 0.0).astype(BF)
    flow_first = push_first + taps(grad_second, weight_second, True)
    slope_first = slope_first[2:-2, 2:-2]
    grad_first = jnp.where(inside(1), flow_first * slope_first, 0.0).astype(BF)
    return taps(grad_first, weight_first, True)


def solution(mesh):
    return jax.shard_map(
        local,
        mesh=mesh,
        in_specs=(P("grp", "tile", None), P(), P(), P()),
        out_specs=P("grp", "tile", None),
        check_vma=False,
    )
```

time: 252 us -> 238 us (0.944)
  local copies, waits for them, and re-layouts: 14.2 us -> 92.2 us
  blocking collectives: 60.6 us -> 0 us
  waiting for transfers between devices: 80.1 us -> 19.8 us
  matrix products: 30.2 us -> 81.1 us
  starting transfers between devices: 45.6 us -> 22.4 us
  between operations: 14.2 us -> 1.36 us
  other arithmetic: 5.27 us -> 17.7 us
    psum x2 -> x0, blocking collectives: 60.6 us -> none  [the longest x1 38.1 us: local(): lax.psum((jnp.sum(flat_first, axis=0), jnp.sum(flat_second, axis=0)), ('g...]
    dot_general x40 -> x43, matrix products: 30.2 us -> 81.1 us  [the longest x36 70.5 us: taps(): product = lax.dot_general(window, kernel, dims, preferred_element_type=F32)]
    reshape x0 -> x30, local copies, waits for them, and re-layouts: none -> 49.6 us  [the longest x27 46.6 us: taps(): padded[a:a + height, b:b + breadth, :].reshape(height * breadth, -1)]
    all_gather x1 -> x0, waiting for transfers between devices: 35.3 us -> none  [local(): mismatch = lax.all_gather(diff_share, 'tile', axis=0, tiled=True)]
    unnamed x3 -> x0, waiting for transfers between devices: 27.9 us -> none
    ppermute x16 -> x15, starting transfers between devices: 45.5 us -> 22.4 us  [the longest x1 4.58 us: halo(): far = lax.ppermute(jnp.where(core == 0, left, right), 'tile', cross)]
    unnamed x20 -> x136, local copies, waits for them, and re-layouts: 7.25 us -> 21.7 us
    mul x0 -> x3, other arithmetic: none -> 6.11 us  [the longest x2 4.39 us: gelu_pair(): act = 0.5 * values * (1.0 + hyper)]
  transfers between devices with their start and end apart: 18 -> 15, of which waited for: 9 -> 10; matrix products, arithmetic and copies ran while one was open for 5% -> 6% of each run, Pallas kernels for 0% -> 0%
where the time goes in v1:
time: 238 us; the launch traced here: 235 us
  local copies, waits for them, and re-layouts  92.2 us (39%)
  matrix products  81.1 us (34%)
  starting transfers between devices  22.4 us (9%)
  waiting for transfers between devices  19.8 us (8%)
  other arithmetic  17.7 us (7%)
    dot_general x36, matrix products, taps(): product = lax.dot_general(window, kernel, dims, preferred_element_type=F32)  70.5 us
    reshape x27, local copies, waits for them, and re-layouts, taps(): padded[a:a + height, b:b + breadth, :].reshape(height * breadth, -1)  46.6 us
    unnamed x136, local copies, waits for them, and re-layouts  21.7 us
    slice x4, local copies, waits for them, and re-layouts, taps(): padded[a:a + height, b:b + breadth, :].reshape(height * breadth, -1)  8.02 us
    ppermute x3, waiting for transfers between devices, local(): got = lax.ppermute(sent, 'tile', [(i, i ^ 2 * k) for i in range(tiles)])  6.67 us
    dot_general x2, matrix products, recentre(): jnp.dot(flat, unpack(table[:rows], width), preferred_element_type=F32)  6.27 us
    ppermute x1, waiting for transfers between devices, halo(): below = lax.ppermute(pool[:REACH], 'grp', down)  5.1 us
  transfers between devices with their start and end apart: 15, of which 10 were waited for; matrix products, arithmetic and copies ran while one was open for 6% of the time, Pallas kernels for 0%

profile of v1, /device:TPU:1, one launch (start us, length us, event | category | flops | bytes accessed | tf_op | source)
XLA Modules:
  0.0 234.6 jit_solution(1779036907533551162)
XLA Ops:
  1.1 4.6 %collective-permute-start = (bf16[8,4,256]{2,1,0:T(4,128)(2,1)S(1)}, bf16[8,4,256]{2,1,0:T(4,128)(2,1)S(1)}, u32[]{:S(2)}, u32[]{:S(2)}) collective-permute-start(bf16[8,4,256]{2,1,0:T(4,128)(2,1)S(1)} %get-tuple-element.109), channel_id=1, source_target_pairs={{1,2},{3,4},{5,6},{2,1},{4,3},{6,5},{9,10},{11,12},{13,14},{10,9},... | collective-permute-start | bytes 49160 | tf_op jit(solution)/shard_map/ppermute | solution.py:41
  5.8 3.0 %fusion.218 = (f32[1,512,512]{2,1,0:T(8,128)}, f32[1,512,512]{2,1,0:T(8,128)}) fusion(f32[2,512,512]{2,1,0:T(8,128)} %param.7), kind=kLoop, calls=%fused_computation.410 | loop fusion | bytes 4194304 | tf_op jit(solution)/shard_map/unstack | solution.py:169
  10.6 2.6 %copy.24 = f32[1,512,512]{1,2,0:T(8,128)} copy(f32[1,512,512]{2,1,0:T(8,128)} %get-tuple-element.30) | data formatting | bytes 2097152
  17.2 3.1 %collective-permute-start.2 = (bf16[4,72,256]{2,1,0:T(8,128)(2,1)S(1)}, bf16[4,72,256]{2,1,0:T(8,128)(2,1)S(1)}, u32[]{:S(2)}, u32[]{:S(2)}) collective-permute-start(bf16[4,72,256]{2,1,0:T(8,128)(2,1)S(1)} %get-tuple-element.107), channel_id=1, source_target_pairs={{0,8},{8,16},{16,24},{1,9},{9,17},{17,25},{2,10},{10,18},{18,26},{... | collective-permute-start | bytes 442376 | tf_op jit(solution)/shard_map/ppermute | solution.py:48
  23.0 5.1 %collective-permute-done.3 = bf16[4,72,256]{2,1,0:T(8,128)(2,1)S(1)} collective-permute-done((bf16[4,72,256]{2,1,0:T(8,128)(2,1)S(1)}, bf16[4,72,256]{2,1,0:T(8,128)(2,1)S(1)}, u32[]{:S(2)}, u32[]{:S(2)}) %collective-permute-start.3) | collective-permute-done | bytes 147488 | tf_op jit(solution)/shard_map/ppermute | solution.py:49
  28.2 2.0 fusion.222
  30.2 2.0 reshape.457
  32.2 1.9 reshape.456
  34.1 2.8 %fusion.130 = f32[980,512]{1,0:T(8,128)} fusion(bf16[980,256]{1,0:T(8,128)(2,1)} %reshape.457, bf16[3,3,256,512]{3,2,1,0:T(8,128)(2,1)S(1)} %copy-done), kind=kOutput, calls=%fused_computation.181 | convolution fusion | flops 256901120 | bytes 2770944 | tf_op jit(solution)/shard_map/dot_general | solution.py:31
  38.7 1.9 reshape.455
  40.7 2.8 %fusion.136 = f32[980,512]{1,0:T(8,128)} fusion(bf16[980,256]{1,0:T(8,128)(2,1)} %reshape.455, bf16[3,3,256,512]{3,2,1,0:T(8,128)(2,1)S(1)} %copy-done), kind=kOutput, calls=%fused_computation.187 | convolution fusion | flops 256901120 | bytes 2770944 | tf_op jit(solution)/shard_map/dot_general | solution.py:31
  43.4 1.9 reshape.454
  45.4 2.8 %fusion.139 = f32[980,512]{1,0:T(8,128)} fusion(bf16[980,256]{1,0:T(8,128)(2,1)} %reshape.454, bf16[3,3,256,512]{3,2,1,0:T(8,128)(2,1)S(1)} %copy-done), kind=kOutput, calls=%fused_computation.190 | convolution fusion | flops 256901120 | bytes 2770944 | tf_op jit(solution)/shard_map/dot_general | solution.py:31
  50.2 2.7 %fusion.142 = f32[980,512]{1,0:T(8,128)} fusion(bf16[980,256]{1,0:T(8,128)(2,1)} %reshape.453, bf16[3,3,256,512]{3,2,1,0:T(8,128)(2,1)S(1)} %copy-done), kind=kOutput, calls=%fused_computation.193 | convolution fusion | flops 256901120 | bytes 2770944 | tf_op jit(solution)/shard_map/dot_general | solution.py:31
  54.8 2.8 %fusion.145 = f32[980,512]{1,0:T(8,128)} fusion(bf16[980,256]{1,0:T(8,128)(2,1)} %reshape.452, bf16[3,3,256,512]{3,2,1,0:T(8,128)(2,1)S(1)} %copy-done), kind=kOutput, calls=%fused_computation.196 | convolution fusion | flops 256901120 | bytes 2770944 | tf_op jit(solution)/shard_map/dot_general | solution.py:31
  59.6 2.7 %fusion.148 = f32[980,512]{1,0:T(8,128)} fusion(bf16[980,256]{1,0:T(8,128)(2,1)} %reshape.451, bf16[3,3,256,512]{3,2,1,0:T(8,128)(2,1)S(1)} %copy-done), kind=kOutput, calls=%fused_computation.199 | convolution fusion | flops 256901120 | bytes 2770944 | tf_op jit(solution)/shard_map/dot_general | solution.py:31
  63.2 2.7 %fusion.151 = f32[980,512]{1,0:T(8,128)} fusion(bf16[980,256]{1,0:T(8,128)(2,1)} %reshape.450, bf16[3,3,256,512]{3,2,1,0:T(8,128)(2,1)S(1)} %copy-done), kind=kOutput, calls=%fused_computation.202 | convolution fusion | flops 256901120 | bytes 2770944 | tf_op jit(solution)/shard_map/dot_general | solution.py:31
  66.1 7.8 %add_add_fusion = f32[980,512]{1,0:T(8,128)} fusion(f32[980,512]{1,0:T(8,128)} %fusion.130, f32[980,512]{1,0:T(8,128)} %fusion.133, f32[980,512]{1,0:T(8,128)} %fusion.136, f32[980,512]{1,0:T(8,128)} %fusion.139, f32[980,512]{1,0:T(8,128)} %fusion.142, f32[980,512]{1,0:T(8,128)} %fusion.145, f32[980,512]{1,0:T(8,128)} %fusion.151, f32[980,512]{1,0:T(8,128)} %fusion.148, ...), kind=kOutput, calls=%fused_computation.8 | convolution fusion | flops 260915200 | bytes 18829312 | tf_op jit(solution)/shard_map/dot_general | solution.py:31
  75.6 3.9 %fusion.215 = (f32[14,70,512]{2,1,0:T(8,128)}, bf16[14,70,512]{2,1,0:T(8,128)(2,1)S(1)}, f32[14,70,512]{2,1,0:T(8,128)}, f32[14,70,512]{2,1,0:T(8,128)}, f32[14,70,512]{2,1,0:T(8,128)}) fusion(f32[14,70,512]{2,1,0:T(8,128)S(1)} %reshape.459, pred[14,70]{1,0:T(8,128)(4,1)S(1)} %broadcast_and_fusion.1), kind=kLoop, calls=%fused_computation.408 | loop fusion | flops 5017600 | bytes 11039700 | tf_op jit(solution)/shard_map/mul | solution.py:16
  79.5 2.8 %fusion.219 = (bf16[12,68,512]{2,1,0:T(8,128)(2,1)S(1)}, bf16[12,68,512]{2,1,0:T(8,128)(2,1)}, bf16[12,68,512]{2,1,0:T(8,128)(2,1)}, bf16[12,68,512]{2,1,0:T(8,1...) fusion(bf16[14,70,512]{2,1,0:T(8,128)(2,1)S(1)} %get-tuple-elem, ...), kind=kLoop, calls=%fused_computation.411 | loop fusion | bytes 15040512 | tf_op jit(solution)/shard_map/slice | solution.py:28
  84.5 2.0 fusion.100
  86.4 2.9 %fusion.103 = f32[816,512]{1,0:T(8,128)} fusion(bf16[816,512]{1,0:T(8,128)(2,1)S(1)} %copy-done.6, bf16[3,3,512,512]{3,2,1,0:T(8,128)(2,1)} %param.6), kind=kOutput, calls=%fused_computation.149 | convolution fusion | flops 427819008 | bytes 3031040 | tf_op jit(solution)/shard_map/dot_general | solution.py:31
  89.3 2.2 reshape.467
  91.5 3.1 %fusion.82 = f32[816,512]{1,0:T(8,128)} fusion(bf16[816,512]{1,0:T(8,128)(2,1)} %reshape.467, bf16[3,3,512,512]{3,2,1,0:T(8,128)(2,1)} %param.6), kind=kOutput, calls=%fused_computation.128 | convolution fusion | flops 427819008 | bytes 3031040 | tf_op jit(solution)/shard_map/dot_general | solution.py:31
  94.6 2.2 reshape.466
  96.7 3.1 %fusion.85 = f32[816,512]{1,0:T(8,128)} fusion(bf16[816,512]{1,0:T(8,128)(2,1)} %reshape.466, bf16[3,3,512,512]{3,2,1,0:T(8,128)(2,1)} %param.6), kind=kOutput, calls=%fused_computation.131 | convolution fusion | flops 427819008 | bytes 3031040 | tf_op jit(solution)/shard_map/dot_general | solution.py:31
  99.8 2.2 reshape.465
  102.0 3.1 %fusion.88 = f32[816,512]{1,0:T(8,128)} fusion(bf16[816,512]{1,0:T(8,128)(2,1)} %reshape.465, bf16[3,3,512,512]{3,2,1,0:T(8,128)(2,1)} %param.6), kind=kOutput, calls=%fused_computation.134 | convolution fusion | flops 427819008 | bytes 3031040 | tf_op jit(solution)/shard_map/dot_general | solution.py:31
  105.0 2.2 reshape.464
  107.2 3.1 %fusion.91 = f32[816,512]{1,0:T(8,128)} fusion(bf16[816,512]{1,0:T(8,128)(2,1)} %reshape.464, bf16[3,3,512,512]{3,2,1,0:T(8,128)(2,1)} %param.6), kind=kOutput, calls=%fused_computation.137 | convolution fusion | flops 427819008 | bytes 3031040 | tf_op jit(solution)/shard_map/dot_general | solution.py:31
  110.3 2.2 reshape.463
  112.4 3.1 %fusion.94 = f32[816,512]{1,0:T(8,128)} fusion(bf16[816,512]{1,0:T(8,128)(2,1)} %reshape.463, bf16[3,3,512,512]{3,2,1,0:T(8,128)(2,1)} %param.6), kind=kOutput, calls=%fused_computation.140 | convolution fusion | flops 427819008 | bytes 3031040 | tf_op jit(solution)/shard_map/dot_general | solution.py:31
  115.5 2.2 reshape.462
  117.7 3.1 %fusion.97 = f32[816,512]{1,0:T(8,128)} fusion(bf16[816,512]{1,0:T(8,128)(2,1)} %reshape.462, bf16[3,3,512,512]{3,2,1,0:T(8,128)(2,1)} %param.6), kind=kOutput, calls=%fused_computation.143 | convolution fusion | flops 427819008 | bytes 3031040 | tf_op jit(solution)/shard_map/dot_general | solution.py:31
  121.9 5.7 %add_add_fusion.1 = f32[816,512]{1,0:T(8,128)S(1)} fusion(f32[816,512]{1,0:T(8,128)} %fusion.82, f32[816,512]{1,0:T(8,128)} %fusion.85, f32[816,512]{1,0:T(8,128)} %fusion.88, f32[816,512]{1,0:T(8,128)} %fusion.91, f32[816,512]{1,0:T(8,128)} %fusion.94, f32[816,512]{1,0:T(8,128)} %fusion.97, f32[816,512]{1,0:T(8,128)} %fusion.103, ...), kind=kOutput, calls=%fused_computation.23 | convolution fusion | flops 431161344 | bytes 16400384 | tf_op jit(solution)/shard_map/dot_general | solution.py:31
  138.3 2.4 %collective-permute-start.6 = (bf16[336,128]{1,0:T(8,128)(2,1)}, bf16[336,128]{1,0:T(8,128)(2,1)S(1)}, u32[]{:S(2)}, u32[]{:S(2)}) collective-permute-start(bf16[336,128]{1,0:T(8,128)(2,1)} %get-tuple-element.114), channel_id=1, source_target_pairs={{0,16},{8,24},{16,0},{24,8},{1,17},{9,25},{17,1},{25,9},{2,18},{10... | collective-permute-start | bytes 258056 | tf_op jit(solution)/shard_map/ppermute | solution.py:156
  141.0 2.0 collective-permute-done.7
  147.5 2.2 collective-permute-start.10
  152.8 5.0 %collective-permute-done.9 = bf16[336,128]{1,0:T(8,128)(2,1)S(1)} collective-permute-done((bf16[336,128]{1,0:T(8,128)(2,1)S(1)}, bf16[336,128]{1,0:T(8,128)(2,1)S(1)}, u32[]{:S(2)}, u32[]{:S(2)}) %collective-permute-start.9) | collective-permute-done | bytes 86048 | tf_op jit(solution)/shard_map/ppermute | solution.py:164
  165.7 2.9 %collective-permute-start.14 = (bf16[1296,128]{1,0:T(8,128)(2,1)S(1)}, bf16[1296,128]{1,0:T(8,128)(2,1)S(1)}, u32[]{:S(2)}, u32[]{:S(2)}) collective-permute-start(bf16[1296,128]{1,0:T(8,128)(2,1)S(1)} %pad_maximum_fusion.2), channel_id=1, source_target_pairs={{0,1},{1,0},{2,3},{3,2},{4,5},{5,4},{6,7},{7,6},{8,9},{9,8},{10,11... | collective-permute-start | bytes 995336 | tf_op jit(solution)/shard_map/ppermute | solution.py:178
  192.6 2.5 %fusion.220 = (bf16[10,66,512]{2,1,0:T(8,128)(2,1)S(1)}, bf16[10,66,512]{2,1,0:T(8,128)(2,1)S(1)}, bf16[10,66,512]{2,1,0:T(8,128)(2,1)}, bf16[10,66,512]{2,1,0:T...) fusion(bf16[12,68,512]{2,1,0:T(8,128)(2,1)S(1)} %fusion.9), kind=kLoop, calls=%fused_computation.412 | loop fusion | bytes 12165120 | tf_op jit(solution)/shard_map/slice | solution.py:28
  197.9 2.1 reshape.471
  200.0 2.1 reshape.472
  202.1 2.1 reshape.473
  204.2 2.1 reshape.474
  206.3 2.1 reshape.475
  208.4 2.1 reshape.476
  224.5 4.7 %fusion.21 = bf16[10,66,512]{2,1,0:T(8,128)(2,1)S(1)} fusion(f32[14,70,512]{2,1,0:T(8,128)} %get-tuple-element.33, f32[14,70,512]{2,1,0:T(8,128)} %get-tuple-element.35, f32[14,70,512]{2,1,0:T(8,128)S(1)} %copy-done.4, f32[14,70,512]{2,1,0:T(8,128)} %get-tuple-element.34, f32[10,66,512]{2,1,0:T(8,128)} %reshape.479, f32[14,70,512]{2,1,0:T(8,128)} %get-tuple-element.31, ...), kind=kOutput, calls=%fused_computation.29 | convolution fusion | flops 358252544 | bytes 9927316 | tf_op jit(solution)/shard_map/dot_general | solution.py:183
  (274 shorter events, 94.9 us)
Async XLA Ops:
  1.1 15.1 %collective-permute-start = (bf16[8,4,256]{2,1,0:T(4,128)(2,1)S(1)}, bf16[8,4,256]{2,1,0:T(4,128)(2,1)S(1)}, u32[]{:S(2)}, u32[]{:S(2)}) collective-permute-start(bf16[8,4,256]{2,1,0:T(4,128)(2,1)S(1)} %get-tuple-element.109), channel_id=1, source_target_pairs={{1,2},{3,4},{5,6},{2,1},{4,3},{6,5},{9,10},{11,12},{13,14},{10,9},... | collective-permute-start | bytes 49160 | tf_op jit(solution)/shard_map/ppermute | solution.py:41
  5.7 10.6 %collective-permute-start.1 = (bf16[8,4,256]{2,1,0:T(4,128)(2,1)S(1)}, bf16[8,4,256]{2,1,0:T(4,128)(2,1)S(1)}, u32[]{:S(2)}, u32[]{:S(2)}) collective-permute-start(bf16[8,4,256]{2,1,0:T(4,128)(2,1)S(1)} %get-tuple-element.110), channel_id=1, source_target_pairs={{0,1},{1,0},{2,3},{3,2},{4,5},{5,4},{6,7},{7,6},{8,9},{9,8},{10,11... | collective-permute-start | bytes 49160 | tf_op jit(solution)/shard_map/ppermute | solution.py:42
  8.8 4.3 %copy-start.2 = (f32[2,512,512]{2,1,0:T(8,128)S(1)}, f32[2,512,512]{2,1,0:T(8,128)}, u32[]{:S(2)}) copy-start(f32[2,512,512]{2,1,0:T(8,128)} %param.7) | copy-start | bytes 6291460
  14.8 1.0 copy-start.7
  14.8 1.4 copy-start.8
  17.2 5.8 %collective-permute-start.2 = (bf16[4,72,256]{2,1,0:T(8,128)(2,1)S(1)}, bf16[4,72,256]{2,1,0:T(8,128)(2,1)S(1)}, u32[]{:S(2)}, u32[]{:S(2)}) collective-permute-start(bf16[4,72,256]{2,1,0:T(8,128)(2,1)S(1)} %get-tuple-element.107), channel_id=1, source_target_pairs={{0,8},{8,16},{16,24},{1,9},{9,17},{17,25},{2,10},{10,18},{18,26},{... | collective-permute-start | bytes 442376 | tf_op jit(solution)/shard_map/ppermute | solution.py:48
  20.3 7.8 %collective-permute-start.3 = (bf16[4,72,256]{2,1,0:T(8,128)(2,1)S(1)}, bf16[4,72,256]{2,1,0:T(8,128)(2,1)S(1)}, u32[]{:S(2)}, u32[]{:S(2)}) collective-permute-start(bf16[4,72,256]{2,1,0:T(8,128)(2,1)S(1)} %get-tuple-element.108), channel_id=1, source_target_pairs={{8,0},{16,8},{24,16},{9,1},{17,9},{25,17},{10,2},{18,10},{26,18},{... | collective-permute-start | bytes 442376 | tf_op jit(solution)/shard_map/ppermute | solution.py:49
  28.2 5.9 %copy-start = (bf16[3,3,256,512]{3,2,1,0:T(8,128)(2,1)S(1)}, bf16[3,3,256,512]{3,2,1,0:T(8,128)(2,1)}, u32[]{:S(2)}) copy-start(bf16[3,3,256,512]{3,2,1,0:T(8,128)(2,1)} %param.5) | copy-start | bytes 7077892
  34.1 2.8 %copy-start.16 = (bf16[980,256]{1,0:T(8,128)(2,1)S(1)}, bf16[980,256]{1,0:T(8,128)(2,1)}, u32[]{:S(2)}) copy-start(bf16[980,256]{1,0:T(8,128)(2,1)} %reshape.456) | copy-start | bytes 1505284
  75.6 3.9 %copy-start.3 = (f32[14,70,512]{2,1,0:T(8,128)}, f32[14,70,512]{2,1,0:T(8,128)S(1)}, u32[]{:S(2)}) copy-start(f32[14,70,512]{2,1,0:T(8,128)S(1)} %reshape.459) | copy-start | bytes 6021124
  84.5 2.0 copy-start.6
  127.8 1.6 copy-start.5
  131.6 3.1 %collective-permute-start.4 = (bf16[1296,128]{1,0:T(8,128)(2,1)S(1)}, bf16[1296,128]{1,0:T(8,128)(2,1)S(1)}, u32[]{:S(2)}, u32[]{:S(2)}) collective-permute-start(bf16[1296,128]{1,0:T(8,128)(2,1)S(1)} %pad_maximum_fusion.1), channel_id=1, source_target_pairs={{0,1},{1,0},{2,3},{3,2},{4,5},{5,4},{6,7},{7,6},{8,9},{9,8},{10,11... | collective-permute-start | bytes 995336 | tf_op jit(solution)/shard_map/ppermute | solution.py:147
  137.6 5.3 %collective-permute-start.7 = (bf16[336,128]{1,0:T(8,128)(2,1)}, bf16[336,128]{1,0:T(8,128)(2,1)}, u32[]{:S(2)}, u32[]{:S(2)}) collective-permute-start(bf16[336,128]{1,0:T(8,128)(2,1)} %get-tuple-element.113), channel_id=1, source_target_pairs={{0,24},{8,16},{16,8},{24,0},{1,25},{9,17},{17,9},{25,1},{2,26},{10... | collective-permute-start | bytes 258056 | tf_op jit(solution)/shard_map/ppermute | solution.py:156
  138.3 6.8 %collective-permute-start.6 = (bf16[336,128]{1,0:T(8,128)(2,1)}, bf16[336,128]{1,0:T(8,128)(2,1)S(1)}, u32[]{:S(2)}, u32[]{:S(2)}) collective-permute-start(bf16[336,128]{1,0:T(8,128)(2,1)} %get-tuple-element.114), channel_id=1, source_target_pairs={{0,16},{8,24},{16,0},{24,8},{1,17},{9,25},{17,1},{25,9},{2,18},{10... | collective-permute-start | bytes 258056 | tf_op jit(solution)/shard_map/ppermute | solution.py:156
  140.7 4.4 %collective-permute-start.5 = (bf16[336,128]{1,0:T(8,128)(2,1)S(1)}, bf16[336,128]{1,0:T(8,128)(2,1)S(1)}, u32[]{:S(2)}, u32[]{:S(2)}) collective-permute-start(bf16[336,128]{1,0:T(8,128)(2,1)S(1)} %get-tuple-element.115), channel_id=1, source_target_pairs={{0,8},{8,0},{16,24},{24,16},{1,9},{9,1},{17,25},{25,17},{2,10},{10... | collective-permute-start | bytes 258056 | tf_op jit(solution)/shard_map/ppermute | solution.py:156
  147.5 5.3 %collective-permute-start.10 = (bf16[336,128]{1,0:T(8,128)(2,1)S(1)}, bf16[336,128]{1,0:T(8,128)(2,1)S(1)}, u32[]{:S(2)}, u32[]{:S(2)}) collective-permute-start(bf16[336,128]{1,0:T(8,128)(2,1)S(1)} %pad_maximum_fusion.9), channel_id=1, source_target_pairs={{0,6},{1,7},{2,4},{3,5},{4,2},{5,3},{6,0},{7,1},{8,14},{9,15},{10,... | collective-permute-start | bytes 258056 | tf_op jit(solution)/shard_map/ppermute | solution.py:164
  149.7 8.1 %collective-permute-start.9 = (bf16[336,128]{1,0:T(8,128)(2,1)S(1)}, bf16[336,128]{1,0:T(8,128)(2,1)S(1)}, u32[]{:S(2)}, u32[]{:S(2)}) collective-permute-start(bf16[336,128]{1,0:T(8,128)(2,1)S(1)} %pad_maximum_fusion.9), channel_id=1, source_target_pairs={{0,4},{1,5},{2,6},{3,7},{4,0},{5,1},{6,2},{7,3},{8,12},{9,13},{10,... | collective-permute-start | bytes 258056 | tf_op jit(solution)/shard_map/ppermute | solution.py:164
  150.0 7.7 %collective-permute-start.8 = (bf16[336,128]{1,0:T(8,128)(2,1)S(1)}, bf16[336,128]{1,0:T(8,128)(2,1)S(1)}, u32[]{:S(2)}, u32[]{:S(2)}) collective-permute-start(bf16[336,128]{1,0:T(8,128)(2,1)S(1)} %pad_maximum_fusion.9), channel_id=1, source_target_pairs={{0,2},{1,3},{2,0},{3,1},{4,6},{5,7},{6,4},{7,5},{8,10},{9,11},{10,... | collective-permute-start | bytes 258056 | tf_op jit(solution)/shard_map/ppermute | solution.py:164
  160.2 3.4 %collective-permute-start.11 = (bf16[320,128]{1,0:T(8,128)(2,1)S(1)}, bf16[320,128]{1,0:T(8,128)(2,1)S(1)}, u32[]{:S(2)}, u32[]{:S(2)}) collective-permute-start(bf16[320,128]{1,0:T(8,128)(2,1)S(1)} %get-tuple-element.6), channel_id=1, source_target_pairs={{0,8},{8,0},{16,24},{24,16},{1,9},{9,1},{17,25},{25,17},{2,10},{10... | collective-permute-start | bytes 245768 | tf_op jit(solution)/shard_map/ppermute | solution.py:175
  161.4 3.6 %collective-permute-start.12 = (bf16[320,128]{1,0:T(8,128)(2,1)S(1)}, bf16[320,128]{1,0:T(8,128)(2,1)S(1)}, u32[]{:S(2)}, u32[]{:S(2)}) collective-permute-start(bf16[320,128]{1,0:T(8,128)(2,1)S(1)} %get-tuple-element.6), channel_id=1, source_target_pairs={{0,16},{8,24},{16,0},{24,8},{1,17},{9,25},{17,1},{25,9},{2,18},{10... | collective-permute-start | bytes 245768 | tf_op jit(solution)/shard_map/ppermute | solution.py:175
  161.4 4.2 %collective-permute-start.13 = (bf16[320,128]{1,0:T(8,128)(2,1)S(1)}, bf16[320,128]{1,0:T(8,128)(2,1)S(1)}, u32[]{:S(2)}, u32[]{:S(2)}) collective-permute-start(bf16[320,128]{1,0:T(8,128)(2,1)S(1)} %get-tuple-element.6), channel_id=1, source_target_pairs={{0,24},{8,16},{16,8},{24,0},{1,25},{9,17},{17,9},{25,1},{2,26},{10... | collective-permute-start | bytes 245768 | tf_op jit(solution)/shard_map/ppermute | solution.py:175
  165.7 4.2 %collective-permute-start.14 = (bf16[1296,128]{1,0:T(8,128)(2,1)S(1)}, bf16[1296,128]{1,0:T(8,128)(2,1)S(1)}, u32[]{:S(2)}, u32[]{:S(2)}) collective-permute-start(bf16[1296,128]{1,0:T(8,128)(2,1)S(1)} %pad_maximum_fusion.2), channel_id=1, source_target_pairs={{0,1},{1,0},{2,3},{3,2},{4,5},{5,4},{6,7},{7,6},{8,9},{9,8},{10,11... | collective-permute-start | bytes 995336 | tf_op jit(solution)/shard_map/ppermute | solution.py:178
  186.6 4.3 %copy-start.32 = (pred[12,68]{1,0:T(8,128)(4,1)S(1)}, pred[12,68]{1,0:T(8,128)(4,1)}, u32[]{:S(2)}) copy-start(pred[12,68]{1,0:T(8,128)(4,1)} %broadcast_and_fusion) | copy-start | bytes 2452
  188.0 2.6 %copy-start.19 = (bf16[128,128]{0,1:T(8,128)(2,1)S(1)}, bf16[128,128]{0,1:T(8,128)(2,1)}, u32[]{:S(2)}) copy-start(bf16[128,128]{0,1:T(8,128)(2,1)} %get-tuple-element.96) | copy-start | bytes 98308
  188.0 2.7 %copy-start.18 = (bf16[128,128]{0,1:T(8,128)(2,1)S(1)}, bf16[128,128]{0,1:T(8,128)(2,1)}, u32[]{:S(2)}) copy-start(bf16[128,128]{0,1:T(8,128)(2,1)} %get-tuple-element.97) | copy-start | bytes 98308
  188.0 2.8 %copy-start.20 = (bf16[128,512]{1,0:T(8,128)(2,1)S(1)}, bf16[128,512]{1,0:T(8,128)(2,1)}, u32[]{:S(2)}) copy-start(bf16[128,512]{1,0:T(8,128)(2,1)} %copy.22) | copy-start | bytes 393220
  188.0 2.9 %copy-start.21 = (bf16[128,128]{0,1:T(8,128)(2,1)S(1)}, bf16[128,128]{0,1:T(8,128)(2,1)}, u32[]{:S(2)}) copy-start(bf16[128,128]{0,1:T(8,128)(2,1)} %copy.29) | copy-start | bytes 98308
  188.1 2.9 %copy-start.22 = (bf16[128,128]{0,1:T(8,128)(2,1)S(1)}, bf16[128,128]{0,1:T(8,128)(2,1)}, u32[]{:S(2)}) copy-start(bf16[128,128]{0,1:T(8,128)(2,1)} %copy.30) | copy-start | bytes 98308
  188.1 2.9 %copy-start.25 = (bf16[128,128]{1,0:T(8,128)(2,1)S(1)}, bf16[128,128]{1,0:T(8,128)(2,1)}, u32[]{:S(2)}) copy-start(bf16[128,128]{1,0:T(8,128)(2,1)} %get-tuple-element.93) | copy-start | bytes 98308
  188.1 2.9 %copy-start.26 = (bf16[128,128]{1,0:T(8,128)(2,1)S(1)}, bf16[128,128]{1,0:T(8,128)(2,1)}, u32[]{:S(2)}) copy-start(bf16[128,128]{1,0:T(8,128)(2,1)} %get-tuple-element.100) | copy-start | bytes 98308
  188.1 2.9 %copy-start.27 = (bf16[128,128]{1,0:T(8,128)(2,1)S(1)}, bf16[128,128]{1,0:T(8,128)(2,1)}, u32[]{:S(2)}) copy-start(bf16[128,128]{1,0:T(8,128)(2,1)} %get-tuple-element.101) | copy-start | bytes 98308
  188.1 2.9 %copy-start.28 = (bf16[128,128]{1,0:T(8,128)(2,1)S(1)}, bf16[128,128]{1,0:T(8,128)(2,1)}, u32[]{:S(2)}) copy-start(bf16[128,128]{1,0:T(8,128)(2,1)} %get-tuple-element.102) | copy-start | bytes 98308
  188.1 2.9 %copy-start.29 = (bf16[128,128]{1,0:T(8,128)(2,1)S(1)}, bf16[128,128]{1,0:T(8,128)(2,1)}, u32[]{:S(2)}) copy-start(bf16[128,128]{1,0:T(8,128)(2,1)} %get-tuple-element.104) | copy-start | bytes 98308
  188.1 2.9 %copy-start.30 = (bf16[128,128]{1,0:T(8,128)(2,1)S(1)}, bf16[128,128]{1,0:T(8,128)(2,1)}, u32[]{:S(2)}) copy-start(bf16[128,128]{1,0:T(8,128)(2,1)} %get-tuple-element.105) | copy-start | bytes 98308
  188.1 2.9 %copy-start.31 = (bf16[128,128]{1,0:T(8,128)(2,1)S(1)}, bf16[128,128]{1,0:T(8,128)(2,1)}, u32[]{:S(2)}) copy-start(bf16[128,128]{1,0:T(8,128)(2,1)} %get-tuple-element.106) | copy-start | bytes 98308
  210.5 5.8 %slice-start = ((s8[4718592]{0:T(1024)(128)(4,1)}), s8[524288]{0:T(1024)(128)(4,1)S(1)}, s32[]{:S(2)}) async-start(s8[4718592]{0:T(1024)(128)(4,1)} %bitcast.247), calls=%async_computation | async-start | bytes 1048576
  211.5 1.1 copy-start.15
  212.6 3.6 %slice-start.1 = ((s8[4718592]{0:T(1024)(128)(4,1)}), s8[4194304]{0:T(1024)(128)(4,1)S(1)}, s32[]{:S(2)}) async-start(s8[4718592]{0:T(1024)(128)(4,1)} %bitcast.247), calls=%async_computation.1 | async-start | bytes 8388608
  214.4 1.9 copy-start.14
  216.3 1.1 copy-start.13
  217.4 1.1 copy-start.12
  218.5 1.1 copy-start.11
  219.6 1.1 copy-start.9
  220.7 1.1 copy-start.10
  222.3 2.1 copy-start.4
  222.3 2.1 copy-start.33
  229.2 1.7 copy-start.1
  (3 other events, 2.5 us)

commit v2 on v0

v2 whole, which is shorter than its diff:
```python
import functools

import jax
import jax.numpy as jnp
from jax import lax
from jax.experimental import pallas as pl
from jax.experimental.pallas import tpu as pltpu
from jax.sharding import PartitionSpec as P

GELU_SCALE = 0.7978845608
GELU_CUBIC = 0.044715
REACH = 4
BLOCK = 128
EXTRA = 16
BF = jnp.bfloat16
F32 = jnp.float32
VMEM = pl.BlockSpec(memory_space=pltpu.VMEM)
SMEM = pl.BlockSpec(memory_space=pltpu.SMEM)
MIB = 2**20


def gelu_pair(values):
    square = values * values
    hyper = jnp.tanh(GELU_SCALE * (values + GELU_CUBIC * values * square))
    half = 0.5 * (1.0 + hyper)
    slope = half + 0.5 * values * (1.0 - hyper * hyper) * (
        GELU_SCALE + 3.0 * GELU_SCALE * GELU_CUBIC * square
    )
    return values * half, slope


def pairs(width):
    blocks = width // BLOCK
    return [(i, j) for i in range(blocks) for j in range(i, blocks)]


def wide(mask, width):
    return jnp.concatenate([mask] * (width // BLOCK), axis=1)


def fill_mask(mask_ref, place_ref, rim, pitch, limits):
    rows = mask_ref.shape[0] // pitch
    col = lax.broadcasted_iota(jnp.int32, (pitch, BLOCK), 0) + (place_ref[2] - rim)
    inside = jnp.where((col >= 0) & (col < limits[1]), 1.0, 0.0).astype(F32)
    for r in range(rows):
        row = place_ref[1] - rim + r
        ok = jnp.where((row >= 0) & (row < limits[0]), 1.0, 0.0).astype(F32)
        mask_ref[r * pitch : (r + 1) * pitch, :] = inside * ok


def shifted(ref, base, step, offset):
    return ref[pl.ds(base, step + 8), :][offset : offset + step]


def spread_taps(flat_ref, base, out_ref, at, step):
    depth = flat_ref.shape[1]
    whole = flat_ref[pl.ds(base, step + 8), :]
    for b in range(3):
        out_ref[pl.ds(at, step), b * depth : (b + 1) * depth] = whole[b : b + step].astype(BF)


def conv(taps_ref, base, weight_ref, pitch, step):
    lhs = jnp.concatenate(
        [taps_ref[pl.ds(base + a * pitch, step), :] for a in range(3)], axis=1
    )
    return jnp.dot(lhs, weight_ref[...], preferred_element_type=F32)


def tiles_of(start, stop, step, body):
    def one(t, carry):
        body(pl.multiple_of(start + t * step, 16))
        return carry

    lax.fori_loop(0, (stop - start) // step, one, 0)


def put_mean(rows_ref, mean, parts):
    blocks = mean.shape[1] // BLOCK
    high = mean.astype(BF).astype(F32)
    for p, row in enumerate((high, mean - high) if parts == 2 else (mean,)):
        for j in range(blocks):
            at = p * blocks + j
            rows_ref[at : at + 1, :] = row[:, j * BLOCK : (j + 1) * BLOCK]


def get_mean(rows, blocks, parts):
    rows = rows.astype(F32)
    found = rows[:blocks] + rows[blocks : 2 * blocks] if parts == 2 else rows[:blocks]
    return jnp.concatenate([found[j : j + 1] for j in range(blocks)], axis=1)


def spread(means, count, left_ref, right_ref, emit):
    centre = means[0]
    for mean in means[1:]:
        centre = centre + mean
    centre = centre * (1.0 / len(means))
    left_ref[...] = jnp.zeros(left_ref.shape, F32)
    right_ref[...] = jnp.zeros(right_ref.shape, F32)
    for n, mean in enumerate(means):
        away = mean - centre
        high = away.astype(BF).astype(F32)
        low = away - high
        for q, (lhs, rhs) in enumerate(((high, high), (high, low), (low, high))):
            at = 3 * n + q
            left_ref[at : at + 1, :] = lhs
            right_ref[at : at + 1, :] = rhs
    lhs, rhs = left_ref[...].astype(BF), right_ref[...].astype(BF)
    for n, (i, j) in enumerate(pairs(lhs.shape[1])):
        product = lax.dot_general(
            lhs[:, i * BLOCK : (i + 1) * BLOCK],
            rhs[:, j * BLOCK : (j + 1) * BLOCK],
            (((0,), (0,)), ((), ())),
            preferred_element_type=F32,
        )
        emit(n, product * float(count))
    return centre


def front(dims, place, pool, far, near, above, below, w1, w2, *rest):
    (act1, slope1, act2, slope2, keep, mine, sent) = rest[:7]
    (flat, taps1, taps2, own, gram, stat, mask) = rest[7:]
    height, breadth, pitch, limits = dims
    step = 2 * pitch
    width = w1.shape[1]
    blocks = width // BLOCK
    flat[...] = jnp.zeros(flat.shape, F32)
    left_core = place[0] == 0
    for r in range(height):
        at = (r + REACH) * pitch
        one, two = far[r].astype(F32), near[r].astype(F32)
        flat[at : at + REACH, :] = jnp.where(left_core, one, two)
        flat[at + REACH : at + REACH + breadth, :] = pool[r]
        flat[at + REACH + breadth : at + 2 * REACH + breadth, :] = jnp.where(left_core, two, one)
    for r in range(REACH):
        at = r * pitch
        flat[at : at + breadth + 2 * REACH, :] = above[r].astype(F32)
        at = (r + REACH + height) * pitch
        flat[at : at + breadth + 2 * REACH, :] = below[r].astype(F32)
    fill_mask(mask, place, 3, pitch, limits)
    tiles_of(
        0, (height + 8) * pitch, step, lambda at: spread_taps(flat, at, taps1, at, step)
    )

    def first(at):
        act, slope = gelu_pair(conv(taps1, at, w1, pitch, step))
        act1[pl.ds(at, step), :] = act * wide(mask[pl.ds(at, step), :], width)
        slope1[pl.ds(at, step), :] = slope

    rows1 = (height + 6) * pitch
    act1[rows1:, :] = jnp.zeros((act1.shape[0] - rows1, width), F32)
    tiles_of(0, rows1, step, first)
    tiles_of(step, rows1 - step, step, lambda at: spread_taps(act1, at, taps2, at, step))

    def second(at):
        act, slope = gelu_pair(conv(taps2, at, w2, pitch, step))
        act2[pl.ds(at - step, step), :] = act
        slope2[pl.ds(at - step, step), :] = slope

    tiles_of(step, step + height * pitch, step, second)
    cells = height * breadth
    for layer, (act, offset) in enumerate(((act1, 3 * pitch + 3), (act2, 2))):
        total = jnp.zeros((8, width), F32)
        for r in range(height):
            cut = act[offset + r * pitch : offset + r * pitch + breadth, :]
            own[r * breadth : (r + 1) * breadth, :] = cut
            total = total + jnp.sum(cut.reshape(breadth // 8, 8, width), axis=0)
        mean = jnp.sum(total, axis=0, keepdims=True) * (1.0 / cells)
        centred = (own[...] - mean).astype(BF)
        n = 0
        for i in range(blocks):
            panel = lax.dot_general(
                centred[:, i * BLOCK : (i + 1) * BLOCK],
                centred[:, i * BLOCK :],
                (((0,), (0,)), ((), ())),
                preferred_element_type=F32,
            )
            for j in range(i, blocks):
                gram[layer, n * BLOCK : (n + 1) * BLOCK, :] = panel[
                    :, (j - i) * BLOCK : (j - i + 1) * BLOCK
                ]
                n += 1
        stat[layer] = jnp.zeros(stat.shape[1:], F32)
        put_mean(stat.at[layer, 0:EXTRA], mean, 2)
        put_mean(stat.at[layer, EXTRA : 2 * EXTRA], mean, 1)
    rows = keep.shape[0]
    keep[...] = gram[place[0]]
    mine[...] = stat[place[0], EXTRA : EXTRA + 8, :]
    sent[0:rows, :] = gram[1 - place[0]].astype(BF)
    sent[rows:, :] = stat[1 - place[0], 0:EXTRA, :].astype(BF)


def ring(dims, act1, w2, act2, slope2, taps2):
    height, _, pitch, _ = dims
    step = 2 * pitch
    for n, start in enumerate((0, (height + 2) * pitch)):
        for q in range(2):
            spread_taps(act1, start + q * step, taps2, q * step, step)
        act, slope = gelu_pair(conv(taps2, 0, w2, pitch, step))
        act2[n * step : (n + 1) * step, :] = act
        slope2[n * step : (n + 1) * step, :] = slope


def write_message(ref, part, rows_ref, centre):
    count = part.shape[0]
    rows_ref[...] = jnp.zeros(rows_ref.shape, F32)
    put_mean(rows_ref, centre, 2)
    ref[0:count, :] = part.astype(BF)
    ref[count:, :] = rows_ref[...].astype(BF)


def merge_pair(dims, place, keep, mine, got, share, centre_out, *rest):
    count, groups, blocks = dims
    messages, (full, left, right, rows_ref) = rest[: groups - 1], rest[groups - 1 :]
    rows = keep.shape[0]
    chunk = rows // groups

    def emit(n, product):
        at = slice(n * BLOCK, (n + 1) * BLOCK)
        full[at, :] = keep[at, :] + got[at, :].astype(F32) + product

    means = [get_mean(mine[...], blocks, 1), get_mean(got[rows:, :], blocks, 2)]
    centre = spread(means, count, left, right, emit)
    centre_out[...] = jnp.zeros(centre_out.shape, F32)
    put_mean(centre_out, centre, 1)
    for k, ref in enumerate(messages, 1):
        at = pl.multiple_of((place[3] ^ k) * chunk, 16)
        write_message(ref, full[pl.ds(at, chunk), :], rows_ref, centre)
    share[...] = full[pl.ds(pl.multiple_of(place[3] * chunk, 16), chunk), :]


def merge_many(dims, final, place, share, mine, *rest):
    count, members, blocks = dims
    gots, rest = rest[: members - 1], rest[members - 1 :]
    chunk = share.shape[0]
    full, left, right, rows_ref = rest[-4:]

    def emit(n, product):
        full[n * BLOCK : (n + 1) * BLOCK, :] = product

    means = [get_mean(mine[...], blocks, 1)]
    means += [get_mean(got[chunk:, :], blocks, 2) for got in gots]
    centre = spread(means, count, left, right, emit)
    total = share[...] + full[pl.ds(pl.multiple_of(place[3] * chunk, 16), chunk), :]
    for got in gots:
        total = total + got[0:chunk, :].astype(F32)
    if final is None:
        out, centre_out, sent = rest[:3]
        out[...] = total
        centre_out[...] = jnp.zeros(centre_out.shape, F32)
        put_mean(centre_out, centre, 1)
        write_message(sent, total, rows_ref, centre)
    else:
        goal, sent, centre_out = rest[:3]
        rows_ref[...] = jnp.zeros(rows_ref.shape, F32)
        put_mean(rows_ref, centre, 2)
        centre_out[...] = rows_ref[...].astype(BF)
        sent[...] = (total * (1.0 / final) - goal[...]).astype(BF)


def assemble(place, share, centre, *rest):
    gots, out = rest[:-1], rest[-1]
    chunk = share.shape[0]
    for k, ref in enumerate((share,) + tuple(gots)):
        out[pl.ds(pl.multiple_of((place[3] ^ k) * chunk, 16), chunk), :] = ref[...]
    rows = chunk * (len(gots) + 1)
    out[rows:, :] = centre[...]


def back(dims, place, act1, slope1, act2, slope2, act2r, slope2r, mine, other, w2, w1, out, *scratch):
    (flat2, taps2, flat1, taps1, first_m, second_m, table, mask) = scratch
    height, breadth, pitch, limits = dims
    step = 2 * pitch
    width = act1.shape[1]
    blocks = width // BLOCK
    packed = table.shape[1] - EXTRA
    table[place[0]] = mine[...]
    table[1 - place[0]] = other[...]
    means = []
    for layer, ref in enumerate((first_m, second_m)):
        for n, (i, j) in enumerate(pairs(width)):
            block = table[layer, n * BLOCK : (n + 1) * BLOCK, :]
            ref[i * BLOCK : (i + 1) * BLOCK, j * BLOCK : (j + 1) * BLOCK] = block
            if i != j:
                ref[j * BLOCK : (j + 1) * BLOCK, i * BLOCK : (i + 1) * BLOCK] = (
                    block.astype(F32).T.astype(BF)
                )
        means.append(get_mean(table[layer, packed:, :], blocks, 2))
    fill_mask(mask, place, 3, pitch, limits)

    def second(act, slope, at, to):
        centred = (act[pl.ds(at, step), :] - means[1]).astype(BF)
        push = jnp.dot(centred, second_m[...], preferred_element_type=F32)
        allow = wide(shifted(mask, to + pitch, step, 1), width)
        flat2[pl.ds(to, step), :] = push * slope[pl.ds(at, step), :] * allow

    rows2 = (height + 4) * pitch
    flat2[rows2:, :] = jnp.zeros((flat2.shape[0] - rows2, width), F32)
    second(act2r, slope2r, 0, 0)
    second(act2r, slope2r, step, rows2 - step)
    tiles_of(
        0, height * pitch, step, lambda at: second(act2, slope2, at, pl.multiple_of(at + step, 16))
    )
    tiles_of(0, rows2, step, lambda at: spread_taps(flat2, at, taps2, at, step))
    rows1 = (height + 2) * pitch
    flat1[rows1:, :] = jnp.zeros((flat1.shape[0] - rows1, width), F32)

    def first(at):
        near = pl.multiple_of(at + 2 * pitch, 16)
        centred = (shifted(act1, near, step, 2) - means[0]).astype(BF)
        flow = conv(taps2, at, w2, pitch, step) + jnp.dot(
            centred, first_m[...], preferred_element_type=F32
        )
        allow = wide(shifted(mask, near, step, 2), width)
        flat1[pl.ds(at, step), :] = flow * shifted(slope1, near, step, 2) * allow

    tiles_of(0, rows1, step, first)
    tiles_of(0, rows1, step, lambda at: spread_taps(flat1, at, taps1, at, step))

    def last(t, carry):
        got = conv(taps1, pl.multiple_of(t * step, 16), w1, pitch, step)
        out[2 * t] = got[0:breadth]
        out[2 * t + 1] = got[pitch : pitch + breadth]
        return carry

    lax.fori_loop(0, height // 2, last, 0)


def call(body, ins, outs, scratch, flops=0, limit=None, name=None):
    moved = sum(x.size * x.dtype.itemsize for x in ins) + sum(
        x.size * x.dtype.itemsize for x in outs
    )
    return pl.pallas_call(
        body,
        out_shape=tuple(outs),
        in_specs=[SMEM if x.dtype == jnp.int32 else VMEM for x in ins],
        out_specs=tuple(VMEM for _ in outs),
        scratch_shapes=scratch,
        compiler_params=pltpu.CompilerParams(vmem_limit_bytes=(limit or 8) * MIB),
        cost_estimate=pl.CostEstimate(flops=flops, bytes_accessed=moved, transcendentals=0),
        name=name,
    )(*ins)


def shape(dims, dtype):
    return jax.ShapeDtypeStruct(dims, dtype)


def transposed(weight):
    flipped = weight[::-1, ::-1].transpose(0, 1, 3, 2)
    return flipped.reshape(-1, weight.shape[2])


def local(pool_input, weight_first, weight_second, targets):
    height, breadth, depth = pool_input.shape
    width = weight_first.shape[3]
    groups, tiles = lax.axis_size("grp"), lax.axis_size("tile")
    chips = tiles // 2
    row, tile = lax.axis_index("grp"), lax.axis_index("tile")
    core = tile % 2
    cells = height * breadth
    positions = cells * groups * tiles
    pitch = -(-(breadth + 2 * REACH) // 16) * 16
    step = 2 * pitch
    blocks = width // BLOCK
    place = jnp.stack([core, row * height, tile * breadth, row]).astype(jnp.int32)
    dims = (height, breadth, pitch, (height * groups, breadth * tiles))
    swap = [(i, i ^ 1) for i in range(tiles)]
    cross = [(i, i + 1) for i in range(1, tiles - 1, 2)]
    cross = cross + [(j, i) for i, j in cross]

    first_core = core == 0
    right = pool_input[:, -REACH:].astype(BF)
    left = pool_input[:, :REACH].astype(BF)
    far = lax.ppermute(jnp.where(first_core, left, right), "tile", cross)
    near = lax.ppermute(jnp.where(first_core, right, left), "tile", swap)

    def band(part):
        rows = slice(0, REACH) if part == 0 else slice(height - REACH, height)
        one, two = far[rows], near[rows]
        middle = pool_input[rows].astype(BF)
        return jnp.concatenate(
            [jnp.where(first_core, one, two), middle, jnp.where(first_core, two, one)], axis=1
        )

    up = [(i, i + 1) for i in range(groups - 1)]
    down = [(j, i) for i, j in up]
    above = lax.ppermute(band(1), "grp", up)
    below = lax.ppermute(band(0), "grp", down)

    rows0, rows1, rows2 = ((height + n) * pitch for n in (8, 6, 0))
    packed = len(pairs(width)) * BLOCK
    w1 = weight_first.reshape(-1, width)
    w2 = weight_second.reshape(-1, width)
    act1, slope1, act2, slope2, keep, mine, sent = call(
        functools.partial(front, dims),
        [place, pool_input, far, near, above, below, w1, w2],
        [
            shape((rows1 + 16, width), F32),
            shape((rows1, width), F32),
            shape((rows2, width), F32),
            shape((rows2, width), F32),
            shape((packed, BLOCK), F32),
            shape((8, BLOCK), F32),
            shape((packed + EXTRA, BLOCK), BF),
        ],
        [
            pltpu.VMEM((rows0 + 16, depth), F32),
            pltpu.VMEM((rows0, 3 * depth), BF),
            pltpu.VMEM((rows1, 3 * width), BF),
            pltpu.VMEM((cells, width), F32),
            pltpu.VMEM((2, packed, BLOCK), F32),
            pltpu.VMEM((2, 2 * EXTRA, BLOCK), F32),
            pltpu.VMEM((rows1, BLOCK), F32),
        ],
        flops=2 * 9 * width * (rows1 * depth + rows2 * width),
        limit=30,
        name="front",
    )
    act2r, slope2r = call(
        functools.partial(ring, dims),
        [act1, w2],
        [shape((2 * step, width), F32)] * 2,
        [pltpu.VMEM((2 * step, 3 * width), BF)],
        flops=2 * 9 * width * width * 2 * step,
        limit=16,
        name="ring",
    )
    goal = jnp.where(first_core, targets[0], targets[1])
    goal = (goal + goal.T) * 0.5
    goal = jnp.concatenate(
        [
            goal[i * BLOCK : (i + 1) * BLOCK, j * BLOCK : (j + 1) * BLOCK]
            for i, j in pairs(width)
        ],
        axis=0,
    )
    chunk = packed // groups
    goal = lax.dynamic_slice_in_dim(goal, row * chunk, chunk, 0)

    def helpers(members):
        deep = -(-3 * members // 16) * 16
        return [
            pltpu.VMEM((packed, BLOCK), F32),
            pltpu.VMEM((deep, width), F32),
            pltpu.VMEM((deep, width), F32),
            pltpu.VMEM((EXTRA, BLOCK), F32),
        ]

    message = shape((chunk + EXTRA, BLOCK), BF)
    part, centre = shape((chunk, BLOCK), F32), shape((8, BLOCK), F32)
    got = lax.ppermute(sent, "tile", swap)
    share, mean, *sents = call(
        functools.partial(merge_pair, (cells, groups, blocks)),
        [place, keep, mine, got],
        [part, centre] + [message] * (groups - 1),
        helpers(2),
        name="merge_cores",
    )
    gots = [
        lax.ppermute(sents[k - 1], "grp", [(i, i ^ k) for i in range(groups)])
        for k in range(1, groups)
    ]
    share, mean, sent = call(
        functools.partial(merge_many, (2 * cells, groups, blocks), None),
        [place, share, mean] + gots,
        [part, centre, message],
        helpers(groups),
        name="merge_groups",
    )
    gots = [
        lax.ppermute(sent, "tile", [(i, i ^ (2 * k)) for i in range(tiles)])
        for k in range(1, chips)
    ]
    share, mean = call(
        functools.partial(merge_many, (2 * groups * cells, chips, blocks), positions),
        [place, share, mean] + gots + [goal],
        [shape((chunk, BLOCK), BF), shape((EXTRA, BLOCK), BF)],
        helpers(chips),
        name="merge_chips",
    )
    gots = [
        lax.ppermute(share, "grp", [(i, i ^ k) for i in range(groups)])
        for k in range(1, groups)
    ]
    table = shape((packed + EXTRA, BLOCK), BF)
    (mine,) = call(assemble, [place, share, mean] + gots, [table], [], name="assemble")
    other = lax.ppermute(mine, "tile", swap)
    rows_b, rows_d = (height + 4) * pitch, (height + 2) * pitch
    (out,) = call(
        functools.partial(back, dims),
        [place, act1, slope1, act2, slope2, act2r, slope2r, mine, other]
        + [transposed(weight_second), transposed(weight_first)],
        [shape(pool_input.shape, F32)],
        [
            pltpu.VMEM((rows_b + 16, width), F32),
            pltpu.VMEM((rows_b, 3 * width), BF),
            pltpu.VMEM((rows_d + 16, width), F32),
            pltpu.VMEM((rows_d, 3 * width), BF),
            pltpu.VMEM((width, width), BF),
            pltpu.VMEM((width, width), BF),
            pltpu.VMEM((2, packed + EXTRA, BLOCK), BF),
            pltpu.VMEM((rows1, BLOCK), F32),
        ],
        flops=2 * 9 * width * (rows_d * width + rows2 * depth),
        limit=32,
        name="back",
    )
    return out


def solution(mesh):
    return jax.shard_map(
        local,
        mesh=mesh,
        in_specs=(P("grp", "tile", None), P(), P(), P()),
        out_specs=P("grp", "tile", None),
        check_vma=False,
    )
```

time: 252 us -> 115 us (0.46)
  waiting for transfers between devices: 80.1 us -> 12.7 us
  blocking collectives: 60.6 us -> 0 us
  local copies, waits for them, and re-layouts: 14.2 us -> 47 us
  matrix products: 30.2 us -> 0 us
  Pallas kernels: 0 us -> 27.8 us
  starting transfers between devices: 45.6 us -> 22.4 us
  between operations: 14.2 us -> 0.27 us
    psum x2 -> x0, blocking collectives: 60.6 us -> none  [the longest x1 38.1 us: local(): lax.psum((jnp.sum(flat_first, axis=0), jnp.sum(flat_second, axis=0)), ('g...]
    all_gather x1 -> x0, waiting for transfers between devices: 35.3 us -> none  [local(): mismatch = lax.all_gather(diff_share, 'tile', axis=0, tiled=True)]
    dot_general x40 -> x0, matrix products: 30.2 us -> none  [the longest x18 9.16 us: conv_fwd(): jnp.dot(window, weight[row_shift, col_shift], preferred_element_type=jnp....]
    unnamed x3 -> x0, waiting for transfers between devices: 27.9 us -> none
    pallas_call x0 -> x7, Pallas kernels: none -> 27.8 us  [call(): pl.pallas_call(body, out_shape=tuple(outs), in_specs=[SMEM if x.dtype ==...]
    ppermute x16 -> x15, starting transfers between devices: 45.5 us -> 22.4 us  [the longest x3 6.22 us: local(): lax.ppermute(sent, 'tile', [(i, i ^ 2 * k) for i in range(tiles)])]
    unnamed x20 -> x48, local copies, waits for them, and re-layouts: 7.25 us -> 24.8 us
    transpose x0 -> x4, local copies, waits for them, and re-layouts: none -> 15.9 us  [transposed(): flipped = weight[::-1, ::-1].transpose(0, 1, 3, 2)]
  transfers between devices with their start and end apart: 18 -> 15, of which waited for: 9 -> 5; matrix products, arithmetic and copies ran while one was open for 5% -> 28% of each run, Pallas kernels for 0% -> 2%
where the time goes in v2:
time: 115 us; the launch traced here: 114 us
  local copies, waits for them, and re-layouts  47 us (41%)
  Pallas kernels  27.8 us (24%)
  starting transfers between devices  22.4 us (19%)
  waiting for transfers between devices  12.7 us (11%)
  other arithmetic  3.55 us (3%)
    pallas_call x7, Pallas kernels, call(): pl.pallas_call(body, out_shape=tuple(outs), in_specs=[SMEM if x.dtype ==...  27.8 us
    unnamed x48, local copies, waits for them, and re-layouts  24.8 us
    transpose x4, local copies, waits for them, and re-layouts, transposed(): flipped = weight[::-1, ::-1].transpose(0, 1, 3, 2)  15.9 us
    ppermute x3, waiting for transfers between devices, local(): lax.ppermute(sent, 'tile', [(i, i ^ 2 * k) for i in range(tiles)])  6.54 us
    ppermute x3, starting transfers between devices, local(): lax.ppermute(sent, 'tile', [(i, i ^ 2 * k) for i in range(tiles)])  6.22 us
    ppermute x1, waiting for transfers between devices, local(): below = lax.ppermute(band(0), 'grp', down)  4.78 us
    ppermute x1, starting transfers between devices, local(): far = lax.ppermute(jnp.where(first_core, left, right), 'tile', cross)  4.58 us
    ppermute x1, starting transfers between devices, local(): above = lax.ppermute(band(1), 'grp', up)  3.12 us
  transfers between devices with their start and end apart: 15, of which 5 were waited for; matrix products, arithmetic and copies ran while one was open for 28% of the time, Pallas kernels for 2%

profile of v2, /device:TPU:1, one launch (start us, length us, event | category | flops | bytes accessed | tf_op | source)
XLA Modules:
  0.0 113.7 jit_solution(15346497678479972866)
XLA Ops:
  0.0 1.1 convert.6
  1.2 4.6 %collective-permute-start = (bf16[8,4,256]{2,1,0:T(4,128)(2,1)S(1)}, bf16[8,4,256]{2,1,0:T(4,128)(2,1)S(1)}, u32[]{:S(2)}, u32[]{:S(2)}) collective-permute-start(bf16[8,4,256]{2,1,0:T(4,128)(2,1)S(1)} %get-tuple-element.48), channel_id=1, source_target_pairs={{1,2},{3,4},{5,6},{2,1},{4,3},{6,5},{9,10},{11,12},{13,14},{10,9},... | collective-permute-start | bytes 49160 | tf_op jit(solution)/shard_map/ppermute | solution.py:374
  5.8 0.7 fusion.3
  6.5 1.7 %fusion.2 = (f32[1,512,512]{2,1,0:T(8,128)S(1)}, f32[1,512,512]{2,1,0:T(8,128)S(1)}) fusion(f32[2,512,512]{2,1,0:T(8,128)} %param.7), kind=kLoop, calls=%fused_computation.25 | loop fusion | bytes 4194304 | tf_op jit(solution)/shard_map/slice | solution.py:428
  9.9 1.3 %copy.7 = f32[512,512]{1,0:T(8,128)} copy(f32[512,512]{0,1:T(8,128)S(1)} %fusion.1) | data formatting | bytes 2097152 | tf_op jit(solution)/shard_map/jit(_where)/select_n | solution.py:428
  11.2 2.1 %fusion = f32[512,512]{1,0:T(8,128)S(1)} fusion(f32[512,512]{1,0:T(8,128)} %copy.7, f32[1,512,512]{1,2,0:T(8,128)} %copy-done.15, f32[1,512,512]{1,2,0:T(8,128)} %copy-done.14, pred[]{:T(512)S(6)} %eq.5), kind=kLoop, calls=%fused_computation.3 | loop fusion | flops 786432 | bytes 4194305 | tf_op jit(solution)/shard_map/mul | solution.py:429
  13.3 0.7 slice_dynamic-update-slice_fusion.8
  14.0 0.6 slice_dynamic-update-slice_fusion.7
  15.2 0.6 slice_dynamic-update-slice_fusion.5
  15.9 0.6 slice_dynamic-update-slice_fusion.4
  16.6 3.1 %collective-permute-start.2 = (bf16[4,72,256]{2,1,0:T(8,128)(2,1)S(1)}, bf16[4,72,256]{2,1,0:T(8,128)(2,1)S(1)}, u32[]{:S(2)}, u32[]{:S(2)}) collective-permute-start(bf16[4,72,256]{2,1,0:T(8,128)(2,1)S(1)} %pad_maximum_fusion), channel_id=1, source_target_pairs={{0,8},{8,16},{16,24},{1,9},{9,17},{17,25},{2,10},{10,18},{18,26},{... | collective-permute-start | bytes 442376 | tf_op jit(solution)/shard_map/ppermute | solution.py:387
  19.8 1.3 %collective-permute-start.3 = (bf16[4,72,256]{2,1,0:T(8,128)(2,1)S(1)}, bf16[4,72,256]{2,1,0:T(8,128)(2,1)S(1)}, u32[]{:S(2)}, u32[]{:S(2)}) collective-permute-start(bf16[4,72,256]{2,1,0:T(8,128)(2,1)S(1)} %pad_maximum_fusion.1), channel_id=1, source_target_pairs={{8,0},{16,8},{24,16},{9,1},{17,9},{25,17},{10,2},{18,10},{26,18},{... | collective-permute-start | bytes 442376 | tf_op jit(solution)/shard_map/ppermute | solution.py:388
  21.1 0.6 slice_dynamic-update-slice_fusion.3
  21.8 4.8 %collective-permute-done.3.below = bf16[4,72,256]{2,1,0:T(8,128)(2,1)S(1)} collective-permute-done((bf16[4,72,256]{2,1,0:T(8,128)(2,1)S(1)}, bf16[4,72,256]{2,1,0:T(8,128)(2,1)S(1)}, u32[]{:S(2)}, u32[]{:S(2)}) %collective-permute-start.3) | collective-permute-done | bytes 147488 | tf_op jit(solution)/shard_map/ppermute | solution.py:388
  26.6 2.3 %copy-done = bf16[3,3,512,512]{3,2,1,0:T(8,128)(2,1)S(1)} copy-done((bf16[3,3,512,512]{3,2,1,0:T(8,128)(2,1)S(1)}, bf16[3,3,512,512]{3,2,1,0:T(8,128)(2,1)}, u32[]{:S(2)}) %copy-start) | copy-done | bytes 4718616
  29.0 11.5 %front.1 = (f32[1136,512]{1,0:T(8,128)S(1)}, f32[1120,512]{1,0:T(8,128)S(1)}, f32[640,512]{1,0:T(8,128)S(1)}, f32[640,512]{1,0:T(8,128)S(1)}, f32[1280,128]{1,0:...) custom-call(s32[4]{0:T(128)S(1)} %pad_add_fusion.place, f32[8,64,256]{2,1,0:T(8,128)S(1)} %copy-done.7, ...), custom_call_target="tpu_custom_call" | custom-call | flops 5662310400 | bytes 16162832 | tf_op jit(solution)/shard_map/front/pallas_call | solution.py:332
  40.5 1.4 %copy-done.4 = f32[1136,512]{1,0:T(8,128)} copy-done((f32[1136,512]{1,0:T(8,128)}, f32[1136,512]{1,0:T(8,128)S(1)}, u32[]{:S(2)}) %copy-start.4) | copy-done | bytes 2326552
  41.9 1.4 %copy-done.8 = f32[1120,512]{1,0:T(8,128)} copy-done((f32[1120,512]{1,0:T(8,128)}, f32[1120,512]{1,0:T(8,128)S(1)}, u32[]{:S(2)}) %copy-start.8) | copy-done | bytes 2293784
  43.3 1.1 copy-done.10
  44.4 1.1 copy-done.12
  45.4 1.5 %slice_dynamic-update-slice_fusion.2 = f32[1280,128]{1,0:T(8,128)} fusion(f32[1280,128]{1,0:T(8,128)} %slice_dynamic-update-slice_fusion.3, f32[512,512]{1,0:T(8,128)} %copy-done.16), kind=kLoop, calls=%fused_computation.10 | loop fusion | bytes 131072
  46.9 1.5 %slice_dynamic-update-slice_fusion.1 = f32[1280,128]{1,0:T(8,128)} fusion(f32[1280,128]{1,0:T(8,128)} %slice_dynamic-update-slice_fusion.2, f32[512,512]{1,0:T(8,128)} %copy-done.16), kind=kLoop, calls=%fused_computation.9 | loop fusion | bytes 131072
  48.4 0.9 merge_cores.1
  49.3 1.3 %collective-permute-start.5 = (bf16[336,128]{1,0:T(8,128)(2,1)S(1)}, bf16[336,128]{1,0:T(8,128)(2,1)S(1)}, u32[]{:S(2)}, u32[]{:S(2)}) collective-permute-start(bf16[336,128]{1,0:T(8,128)(2,1)S(1)} %get-tuple-element.35), channel_id=1, source_target_pairs={{0,8},{8,0},{16,24},{24,16},{1,9},{9,1},{17,25},{25,17},{2,10},{10... | collective-permute-start | bytes 258056 | tf_op jit(solution)/shard_map/ppermute | solution.py:460
  50.5 1.4 %collective-permute-start.7 = (bf16[336,128]{1,0:T(8,128)(2,1)S(1)}, bf16[336,128]{1,0:T(8,128)(2,1)S(1)}, u32[]{:S(2)}, u32[]{:S(2)}) collective-permute-start(bf16[336,128]{1,0:T(8,128)(2,1)S(1)} %get-tuple-element.37), channel_id=1, source_target_pairs={{0,24},{8,16},{16,8},{24,0},{1,25},{9,17},{17,9},{25,1},{2,26},{10... | collective-permute-start | bytes 258056 | tf_op jit(solution)/shard_map/ppermute | solution.py:460
  52.0 1.6 %slice_dynamic-update-slice_fusion = f32[1280,128]{1,0:T(8,128)} fusion(f32[1280,128]{1,0:T(8,128)} %slice_dynamic-update-slice_fusion.1, f32[512,512]{1,0:T(8,128)} %copy-done.16), kind=kLoop, calls=%fused_computation.8 | loop fusion | bytes 262144 | tf_op jit(solution)/shard_map/concatenate | solution.py:430
  53.9 0.9 collective-permute-done.7.rest_2_
  54.9 0.9 merge_groups.1
  55.8 5.5 %collective-permute-start.10 = (bf16[336,128]{1,0:T(8,128)(2,1)S(1)}, bf16[336,128]{1,0:T(8,128)(2,1)S(1)}, u32[]{:S(2)}, u32[]{:S(2)}) collective-permute-start(bf16[336,128]{1,0:T(8,128)(2,1)S(1)} %get-tuple-element.40), channel_id=1, source_target_pairs={{0,6},{1,7},{2,4},{3,5},{4,2},{5,3},{6,0},{7,1},{8,14},{9,15},{10,... | collective-permute-start | bytes 258056 | tf_op jit(solution)/shard_map/ppermute | solution.py:471
  61.2 0.6 collective-permute-start.9
  62.0 0.9 constant_dynamic-slice_fusion.rest_3_
  63.2 6.3 %collective-permute-done.9.rest_1_ = bf16[336,128]{1,0:T(8,128)(2,1)S(1)} collective-permute-done((bf16[336,128]{1,0:T(8,128)(2,1)S(1)}, bf16[336,128]{1,0:T(8,128)(2,1)S(1)}, u32[]{:S(2)}, u32[]{:S(2)}) %collective-permute-start.9) | collective-permute-done | bytes 86048 | tf_op jit(solution)/shard_map/ppermute | solution.py:471
  69.5 0.9 merge_chips.1
  70.4 1.5 %collective-permute-start.13 = (bf16[320,128]{1,0:T(8,128)(2,1)S(1)}, bf16[320,128]{1,0:T(8,128)(2,1)S(1)}, u32[]{:S(2)}, u32[]{:S(2)}) collective-permute-start(bf16[320,128]{1,0:T(8,128)(2,1)S(1)} %get-tuple-element.41.share), channel_id=1, source_target_pairs={{0,24},{8,16},{16,8},{24,0},{1,25},{9,17},{17,9},{25,1},{2,26},{10... | collective-permute-start | bytes 245768 | tf_op jit(solution)/shard_map/ppermute | solution.py:482
  71.9 1.2 %collective-permute-start.11 = (bf16[320,128]{1,0:T(8,128)(2,1)S(1)}, bf16[320,128]{1,0:T(8,128)(2,1)S(1)}, u32[]{:S(2)}, u32[]{:S(2)}) collective-permute-start(bf16[320,128]{1,0:T(8,128)(2,1)S(1)} %get-tuple-element.41.share), channel_id=1, source_target_pairs={{0,8},{8,0},{16,24},{24,16},{1,9},{9,1},{17,25},{25,17},{2,10},{10... | collective-permute-start | bytes 245768 | tf_op jit(solution)/shard_map/ppermute | solution.py:482
  73.1 1.7 %reverse_bitcast_fusion.1 = bf16[3,3,512,256]{2,3,1,0:T(8,128)(2,1)} fusion(bf16[3,3,256,512]{3,2,1,0:T(8,128)(2,1)S(1)} %copy-done.3), kind=kLoop, calls=%fused_computation.1 | loop fusion | bytes 4718592 | tf_op jit(solution)/shard_map/transpose | solution.py:349
  74.8 2.8 %copy.9 = bf16[3,3,512,256]{3,2,1,0:T(8,128)(2,1)S(1)} copy(bf16[3,3,512,256]{2,3,1,0:T(8,128)(2,1)} %reverse_bitcast_fusion.1) | data formatting | bytes 4718592 | tf_op jit(solution)/shard_map/transpose | solution.py:349
  78.2 1.7 %collective-permute-start.14 = (bf16[1296,128]{1,0:T(8,128)(2,1)S(1)}, bf16[1296,128]{1,0:T(8,128)(2,1)S(1)}, u32[]{:S(2)}, u32[]{:S(2)}) collective-permute-start(bf16[1296,128]{1,0:T(8,128)(2,1)S(1)} %assemble.1.mine), channel_id=1, source_target_pairs={{0,1},{1,0},{2,3},{3,2},{4,5},{5,4},{6,7},{7,6},{8,9},{9,8},{10,11... | collective-permute-start | bytes 995336 | tf_op jit(solution)/shard_map/ppermute | solution.py:487
  79.9 4.8 %reverse_bitcast_fusion = bf16[3,3,512,512]{2,3,1,0:T(8,128)(2,1)} fusion(bf16[3,3,512,512]{3,2,1,0:T(8,128)(2,1)} %param.6), kind=kLoop, calls=%fused_computation | loop fusion | bytes 9437184 | tf_op jit(solution)/shard_map/transpose | solution.py:349
  84.7 6.7 %copy.8 = bf16[3,3,512,512]{3,2,1,0:T(8,128)(2,1)} copy(bf16[3,3,512,512]{2,3,1,0:T(8,128)(2,1)} %reverse_bitcast_fusion) | data formatting | bytes 9437184 | tf_op jit(solution)/shard_map/transpose | solution.py:349
  91.4 2.3 %copy-done.1 = bf16[3,3,512,512]{3,2,1,0:T(8,128)(2,1)S(1)} copy-done((bf16[3,3,512,512]{3,2,1,0:T(8,128)(2,1)S(1)}, bf16[3,3,512,512]{3,2,1,0:T(8,128)(2,1)}, u32[]{:S(2)}) %copy-start.1) | copy-done | bytes 4718616
  93.7 1.7 %copy-done.5 = f32[1136,512]{1,0:T(8,128)S(1)} copy-done((f32[1136,512]{1,0:T(8,128)S(1)}, f32[1136,512]{1,0:T(8,128)}, u32[]{:S(2)}) %copy-start.5) | copy-done | bytes 2326552
  95.4 2.0 %ring.1 = (f32[320,512]{1,0:T(8,128)S(1)}, f32[320,512]{1,0:T(8,128)S(1)}) custom-call(f32[1136,512]{1,0:T(8,128)S(1)} %copy-done.5, bf16[4608,512]{1,0:T(8,128)(2,1)S(1)} %bitcast.20), custom_call_target="tpu_custom_call" | custom-call | flops 1509949440 | bytes 8355840 | tf_op jit(solution)/shard_map/ring/pallas_call | solution.py:332
  97.7 0.8 copy-done.6
  98.4 1.6 %copy-done.9 = f32[1120,512]{1,0:T(8,128)S(1)} copy-done((f32[1120,512]{1,0:T(8,128)S(1)}, f32[1120,512]{1,0:T(8,128)}, u32[]{:S(2)}) %copy-start.9) | copy-done | bytes 2293784
  100.1 1.3 %copy-done.11 = f32[640,512]{1,0:T(8,128)S(1)} copy-done((f32[640,512]{1,0:T(8,128)S(1)}, f32[640,512]{1,0:T(8,128)}, u32[]{:S(2)}) %copy-start.11) | copy-done | bytes 1310744
  101.4 1.3 %copy-done.13 = f32[640,512]{1,0:T(8,128)S(1)} copy-done((f32[640,512]{1,0:T(8,128)S(1)}, f32[640,512]{1,0:T(8,128)}, u32[]{:S(2)}) %copy-start.13) | copy-done | bytes 1310744
  102.7 11.0 %back.1 = f32[8,64,256]{2,1,0:T(8,128)} custom-call(s32[4]{0:T(128)S(1)} %pad_add_fusion.place, f32[1136,512]{1,0:T(8,128)S(1)} %copy-done.6, f32[1120,512]{1,0:T(8,128)S(1)} %copy-done.9, f32[640,512]{1,0:T(8,128)S(1)} %copy-done.11, f32[640,512]{1,0:T(8,128)S(1)} %copy-done.13, f32[320,512]{1,0:T(8,128)S(1)} %get-tuple-element.28.act2r, ...), custom_call_target="tpu_custom_call" | custom-call | flops 5284823040 | bytes 16818192 | tf_op jit(solution)/shard_map/back/pallas_call | solution.py:332
  (54 shorter events, 4.2 us)
Async XLA Ops:
  1.1 15.4 %collective-permute-start.1 = (bf16[8,4,256]{2,1,0:T(4,128)(2,1)S(1)}, bf16[8,4,256]{2,1,0:T(4,128)(2,1)S(1)}, u32[]{:S(2)}, u32[]{:S(2)}) collective-permute-start(bf16[8,4,256]{2,1,0:T(4,128)(2,1)S(1)} %get-tuple-element.47), channel_id=1, source_target_pairs={{0,1},{1,0},{2,3},{3,2},{4,5},{5,4},{6,7},{7,6},{8,9},{9,8},{10,11... | collective-permute-start | bytes 49160 | tf_op jit(solution)/shard_map/ppermute | solution.py:375
  1.2 15.3 %collective-permute-start = (bf16[8,4,256]{2,1,0:T(4,128)(2,1)S(1)}, bf16[8,4,256]{2,1,0:T(4,128)(2,1)S(1)}, u32[]{:S(2)}, u32[]{:S(2)}) collective-permute-start(bf16[8,4,256]{2,1,0:T(4,128)(2,1)S(1)} %get-tuple-element.48), channel_id=1, source_target_pairs={{1,2},{3,4},{5,6},{2,1},{4,3},{6,5},{9,10},{11,12},{13,14},{10,9},... | collective-permute-start | bytes 49160 | tf_op jit(solution)/shard_map/ppermute | solution.py:374
  8.5 1.0 copy-start.14
  8.9 1.0 copy-start.15
  11.2 5.4 %copy-start.18 = (bf16[4,64,256]{2,1,0:T(8,128)(2,1)S(1)}, bf16[4,64,256]{2,1,0:T(8,128)(2,1)}, u32[]{:S(2)}) copy-start(bf16[4,64,256]{2,1,0:T(8,128)(2,1)} %get-tuple-element.46) | copy-start | bytes 393220
  11.2 8.6 %copy-start.17 = (bf16[4,64,256]{2,1,0:T(8,128)(2,1)S(1)}, bf16[4,64,256]{2,1,0:T(8,128)(2,1)}, u32[]{:S(2)}) copy-start(bf16[4,64,256]{2,1,0:T(8,128)(2,1)} %get-tuple-element.45) | copy-start | bytes 393220
  11.2 15.4 %copy-start.3 = (bf16[3,3,256,512]{3,2,1,0:T(8,128)(2,1)S(1)}, bf16[3,3,256,512]{3,2,1,0:T(8,128)(2,1)}, u32[]{:S(2)}) copy-start(bf16[3,3,256,512]{3,2,1,0:T(8,128)(2,1)} %param.5) | copy-start | bytes 7077892
  11.2 15.4 %copy-start.7 = (f32[8,64,256]{2,1,0:T(8,128)S(1)}, f32[8,64,256]{2,1,0:T(8,128)}, u32[]{:S(2)}) copy-start(f32[8,64,256]{2,1,0:T(8,128)} %pool.1) | copy-start | bytes 1572868
  13.3 7.8 %copy-start.16 = (f32[512,512]{1,0:T(8,128)}, f32[512,512]{1,0:T(8,128)S(1)}, u32[]{:S(2)}) copy-start(f32[512,512]{1,0:T(8,128)S(1)} %fusion) | copy-start | bytes 3145732
  16.6 5.2 %collective-permute-start.2 = (bf16[4,72,256]{2,1,0:T(8,128)(2,1)S(1)}, bf16[4,72,256]{2,1,0:T(8,128)(2,1)S(1)}, u32[]{:S(2)}, u32[]{:S(2)}) collective-permute-start(bf16[4,72,256]{2,1,0:T(8,128)(2,1)S(1)} %pad_maximum_fusion), channel_id=1, source_target_pairs={{0,8},{8,16},{16,24},{1,9},{9,17},{17,25},{2,10},{10,18},{18,26},{... | collective-permute-start | bytes 442376 | tf_op jit(solution)/shard_map/ppermute | solution.py:387
  19.8 6.8 %collective-permute-start.3 = (bf16[4,72,256]{2,1,0:T(8,128)(2,1)S(1)}, bf16[4,72,256]{2,1,0:T(8,128)(2,1)S(1)}, u32[]{:S(2)}, u32[]{:S(2)}) collective-permute-start(bf16[4,72,256]{2,1,0:T(8,128)(2,1)S(1)} %pad_maximum_fusion.1), channel_id=1, source_target_pairs={{8,0},{16,8},{24,16},{9,1},{17,9},{25,17},{10,2},{18,10},{26,18},{... | collective-permute-start | bytes 442376 | tf_op jit(solution)/shard_map/ppermute | solution.py:388
  26.6 2.3 %copy-start = (bf16[3,3,512,512]{3,2,1,0:T(8,128)(2,1)S(1)}, bf16[3,3,512,512]{3,2,1,0:T(8,128)(2,1)}, u32[]{:S(2)}) copy-start(bf16[3,3,512,512]{3,2,1,0:T(8,128)(2,1)} %param.6) | copy-start | bytes 14155780
  40.5 1.4 %copy-start.4 = (f32[1136,512]{1,0:T(8,128)}, f32[1136,512]{1,0:T(8,128)S(1)}, u32[]{:S(2)}) copy-start(f32[1136,512]{1,0:T(8,128)S(1)} %get-tuple-element.24.act1) | copy-start | bytes 6979588
  41.9 1.4 %copy-start.8 = (f32[1120,512]{1,0:T(8,128)}, f32[1120,512]{1,0:T(8,128)S(1)}, u32[]{:S(2)}) copy-start(f32[1120,512]{1,0:T(8,128)S(1)} %get-tuple-element.25.slope1) | copy-start | bytes 6881284
  43.3 1.1 copy-start.10
  44.4 1.1 copy-start.12
  45.4 2.9 %collective-permute-start.4 = (bf16[1296,128]{1,0:T(8,128)(2,1)S(1)}, bf16[1296,128]{1,0:T(8,128)(2,1)S(1)}, u32[]{:S(2)}, u32[]{:S(2)}) collective-permute-start(bf16[1296,128]{1,0:T(8,128)(2,1)S(1)} %get-tuple-element.32), channel_id=1, source_target_pairs={{0,1},{1,0},{2,3},{3,2},{4,5},{5,4},{6,7},{7,6},{8,9},{9,8},{10,11... | collective-permute-start | bytes 995336 | tf_op jit(solution)/shard_map/ppermute | solution.py:451
  49.3 4.3 %collective-permute-start.5 = (bf16[336,128]{1,0:T(8,128)(2,1)S(1)}, bf16[336,128]{1,0:T(8,128)(2,1)S(1)}, u32[]{:S(2)}, u32[]{:S(2)}) collective-permute-start(bf16[336,128]{1,0:T(8,128)(2,1)S(1)} %get-tuple-element.35), channel_id=1, source_target_pairs={{0,8},{8,0},{16,24},{24,16},{1,9},{9,1},{17,25},{25,17},{2,10},{10... | collective-permute-start | bytes 258056 | tf_op jit(solution)/shard_map/ppermute | solution.py:460
  50.5 3.4 %collective-permute-start.6 = (bf16[336,128]{1,0:T(8,128)(2,1)S(1)}, bf16[336,128]{1,0:T(8,128)(2,1)S(1)}, u32[]{:S(2)}, u32[]{:S(2)}) collective-permute-start(bf16[336,128]{1,0:T(8,128)(2,1)S(1)} %get-tuple-element.36), channel_id=1, source_target_pairs={{0,16},{8,24},{16,0},{24,8},{1,17},{9,25},{17,1},{25,9},{2,18},{10... | collective-permute-start | bytes 258056 | tf_op jit(solution)/shard_map/ppermute | solution.py:460
  50.5 4.3 %collective-permute-start.7 = (bf16[336,128]{1,0:T(8,128)(2,1)S(1)}, bf16[336,128]{1,0:T(8,128)(2,1)S(1)}, u32[]{:S(2)}, u32[]{:S(2)}) collective-permute-start(bf16[336,128]{1,0:T(8,128)(2,1)S(1)} %get-tuple-element.37), channel_id=1, source_target_pairs={{0,24},{8,16},{16,8},{24,0},{1,25},{9,17},{17,9},{25,1},{2,26},{10... | collective-permute-start | bytes 258056 | tf_op jit(solution)/shard_map/ppermute | solution.py:460
  55.8 7.4 %collective-permute-start.10 = (bf16[336,128]{1,0:T(8,128)(2,1)S(1)}, bf16[336,128]{1,0:T(8,128)(2,1)S(1)}, u32[]{:S(2)}, u32[]{:S(2)}) collective-permute-start(bf16[336,128]{1,0:T(8,128)(2,1)S(1)} %get-tuple-element.40), channel_id=1, source_target_pairs={{0,6},{1,7},{2,4},{3,5},{4,2},{5,3},{6,0},{7,1},{8,14},{9,15},{10,... | collective-permute-start | bytes 258056 | tf_op jit(solution)/shard_map/ppermute | solution.py:471
  61.2 8.2 %collective-permute-start.9 = (bf16[336,128]{1,0:T(8,128)(2,1)S(1)}, bf16[336,128]{1,0:T(8,128)(2,1)S(1)}, u32[]{:S(2)}, u32[]{:S(2)}) collective-permute-start(bf16[336,128]{1,0:T(8,128)(2,1)S(1)} %get-tuple-element.40), channel_id=1, source_target_pairs={{0,4},{1,5},{2,6},{3,7},{4,0},{5,1},{6,2},{7,3},{8,12},{9,13},{10,... | collective-permute-start | bytes 258056 | tf_op jit(solution)/shard_map/ppermute | solution.py:471
  61.9 7.6 %collective-permute-start.8 = (bf16[336,128]{1,0:T(8,128)(2,1)S(1)}, bf16[336,128]{1,0:T(8,128)(2,1)S(1)}, u32[]{:S(2)}, u32[]{:S(2)}) collective-permute-start(bf16[336,128]{1,0:T(8,128)(2,1)S(1)} %get-tuple-element.40), channel_id=1, source_target_pairs={{0,2},{1,3},{2,0},{3,1},{4,6},{5,7},{6,4},{7,5},{8,10},{9,11},{10,... | collective-permute-start | bytes 258056 | tf_op jit(solution)/shard_map/ppermute | solution.py:471
  70.4 7.2 %collective-permute-start.13 = (bf16[320,128]{1,0:T(8,128)(2,1)S(1)}, bf16[320,128]{1,0:T(8,128)(2,1)S(1)}, u32[]{:S(2)}, u32[]{:S(2)}) collective-permute-start(bf16[320,128]{1,0:T(8,128)(2,1)S(1)} %get-tuple-element.41.share), channel_id=1, source_target_pairs={{0,24},{8,16},{16,8},{24,0},{1,25},{9,17},{17,9},{25,1},{2,26},{10... | collective-permute-start | bytes 245768 | tf_op jit(solution)/shard_map/ppermute | solution.py:482
  71.9 5.7 %collective-permute-start.12 = (bf16[320,128]{1,0:T(8,128)(2,1)S(1)}, bf16[320,128]{1,0:T(8,128)(2,1)S(1)}, u32[]{:S(2)}, u32[]{:S(2)}) collective-permute-start(bf16[320,128]{1,0:T(8,128)(2,1)S(1)} %get-tuple-element.41.share), channel_id=1, source_target_pairs={{0,16},{8,24},{16,0},{24,8},{1,17},{9,25},{17,1},{25,9},{2,18},{10... | collective-permute-start | bytes 245768 | tf_op jit(solution)/shard_map/ppermute | solution.py:482
  71.9 5.7 %collective-permute-start.11 = (bf16[320,128]{1,0:T(8,128)(2,1)S(1)}, bf16[320,128]{1,0:T(8,128)(2,1)S(1)}, u32[]{:S(2)}, u32[]{:S(2)}) collective-permute-start(bf16[320,128]{1,0:T(8,128)(2,1)S(1)} %get-tuple-element.41.share), channel_id=1, source_target_pairs={{0,8},{8,0},{16,24},{24,16},{1,9},{9,1},{17,25},{25,17},{2,10},{10... | collective-permute-start | bytes 245768 | tf_op jit(solution)/shard_map/ppermute | solution.py:482
  78.2 19.2 %collective-permute-start.14 = (bf16[1296,128]{1,0:T(8,128)(2,1)S(1)}, bf16[1296,128]{1,0:T(8,128)(2,1)S(1)}, u32[]{:S(2)}, u32[]{:S(2)}) collective-permute-start(bf16[1296,128]{1,0:T(8,128)(2,1)S(1)} %assemble.1.mine), channel_id=1, source_target_pairs={{0,1},{1,0},{2,3},{3,2},{4,5},{5,4},{6,7},{7,6},{8,9},{9,8},{10,11... | collective-permute-start | bytes 995336 | tf_op jit(solution)/shard_map/ppermute | solution.py:487
  91.4 2.3 %copy-start.1 = (bf16[3,3,512,512]{3,2,1,0:T(8,128)(2,1)S(1)}, bf16[3,3,512,512]{3,2,1,0:T(8,128)(2,1)}, u32[]{:S(2)}) copy-start(bf16[3,3,512,512]{3,2,1,0:T(8,128)(2,1)} %param.6) | copy-start | bytes 14155780
  93.7 1.7 %copy-start.5 = (f32[1136,512]{1,0:T(8,128)S(1)}, f32[1136,512]{1,0:T(8,128)}, u32[]{:S(2)}) copy-start(f32[1136,512]{1,0:T(8,128)} %copy-done.4) | copy-start | bytes 6979588
  95.3 2.3 %copy-start.2 = (bf16[3,3,512,512]{3,2,1,0:T(8,128)(2,1)S(1)}, bf16[3,3,512,512]{3,2,1,0:T(8,128)(2,1)}, u32[]{:S(2)}) copy-start(bf16[3,3,512,512]{3,2,1,0:T(8,128)(2,1)} %copy.8) | copy-start | bytes 14155780
  95.3 3.1 %copy-start.6 = (f32[1136,512]{1,0:T(8,128)S(1)}, f32[1136,512]{1,0:T(8,128)}, u32[]{:S(2)}) copy-start(f32[1136,512]{1,0:T(8,128)} %copy-done.4) | copy-start | bytes 6979588
  98.4 1.6 %copy-start.9 = (f32[1120,512]{1,0:T(8,128)S(1)}, f32[1120,512]{1,0:T(8,128)}, u32[]{:S(2)}) copy-start(f32[1120,512]{1,0:T(8,128)} %copy-done.8) | copy-start | bytes 6881284
  100.1 1.3 %copy-start.11 = (f32[640,512]{1,0:T(8,128)S(1)}, f32[640,512]{1,0:T(8,128)}, u32[]{:S(2)}) copy-start(f32[640,512]{1,0:T(8,128)} %copy-done.10) | copy-start | bytes 3932164
  101.4 1.3 %copy-start.13 = (f32[640,512]{1,0:T(8,128)S(1)}, f32[640,512]{1,0:T(8,128)}, u32[]{:S(2)}) copy-start(f32[640,512]{1,0:T(8,128)} %copy-done.12) | copy-start | bytes 3932164

commit v3 on v2

--- a/solution.py
+++ b/solution.py
@@ -325,6 +325,48 @@
     lax.fori_loop(0, height // 2, last, 0)
 
 
+def edges(place, pool, far, near):
+    breadth = pool.shape[1]
+    left_core = place[0] == 0
+    left = pool[:, 0:REACH, :]
+    right = pool[:, breadth - REACH : breadth, :]
+    far[...] = jnp.where(left_core, left, right).astype(BF)
+    near[...] = jnp.where(left_core, right, left).astype(BF)
+
+
+def bands(place, pool, far, near, above, below, row):
+    height, breadth, _ = pool.shape
+    left_core = place[0] == 0
+    for start, ref in ((height - REACH, above), (0, below)):
+        for r in range(REACH):
+            one, two = far[start + r].astype(F32), near[start + r].astype(F32)
+            row[0:REACH, :] = jnp.where(left_core, one, two)
+            row[REACH : REACH + breadth, :] = pool[start + r]
+            row[REACH + breadth :, :] = jnp.where(left_core, two, one)
+            ref[r] = row[...].astype(BF)
+
+
+def flip(weight, out):
+    taps, _, width = weight.shape
+
+    def one(t, carry):
+        at = pl.multiple_of(t * width, 16)
+        out[pl.ds(at, width), :] = weight[taps - 1 - t].T
+        return carry
+
+    lax.fori_loop(0, taps, one, 0)
+
+
+def aim(place, targets, goal, full):
+    core = place[0]
+    chunk = goal.shape[0]
+    for n, (i, j) in enumerate(pairs(targets.shape[1])):
+        rows, cols = slice(i * BLOCK, (i + 1) * BLOCK), slice(j * BLOCK, (j + 1) * BLOCK)
+        block = (targets[core, rows, cols] + targets[core, cols, rows].T) * 0.5
+        full[n * BLOCK : (n + 1) * BLOCK, :] = block
+    goal[...] = full[pl.ds(pl.multiple_of(place[3] * chunk, 16), chunk), :]
+
+
 def call(body, ins, outs, scratch, flops=0, limit=None, name=None):
     moved = sum(x.size * x.dtype.itemsize for x in ins) + sum(
         x.size * x.dtype.itemsize for x in outs
@@ -343,11 +385,6 @@
 
 def shape(dims, dtype):
     return jax.ShapeDtypeStruct(dims, dtype)
-
-
-def transposed(weight):
-    flipped = weight[::-1, ::-1].transpose(0, 1, 3, 2)
-    return flipped.reshape(-1, weight.shape[2])
 
 
 def local(pool_input, weight_first, weight_second, targets):
@@ -368,24 +405,22 @@
     cross = [(i, i + 1) for i in range(1, tiles - 1, 2)]
     cross = cross + [(j, i) for i, j in cross]
 
-    first_core = core == 0
-    right = pool_input[:, -REACH:].astype(BF)
-    left = pool_input[:, :REACH].astype(BF)
-    far = lax.ppermute(jnp.where(first_core, left, right), "tile", cross)
-    near = lax.ppermute(jnp.where(first_core, right, left), "tile", swap)
-
-    def band(part):
-        rows = slice(0, REACH) if part == 0 else slice(height - REACH, height)
-        one, two = far[rows], near[rows]
-        middle = pool_input[rows].astype(BF)
-        return jnp.concatenate(
-            [jnp.where(first_core, one, two), middle, jnp.where(first_core, two, one)], axis=1
-        )
-
+    rim = shape((height, REACH, depth), BF)
+    far, near = call(edges, [place, pool_input], [rim] * 2, [], name="edges")
+    far = lax.ppermute(far, "tile", cross)
+    near = lax.ppermute(near, "tile", swap)
+    band = shape((REACH, breadth + 2 * REACH, depth), BF)
+    above, below = call(
+        bands,
+        [place, pool_input, far, near],
+        [band] * 2,
+        [pltpu.VMEM((breadth + 2 * REACH, depth), F32)],
+        name="bands",
+    )
     up = [(i, i + 1) for i in range(groups - 1)]
     down = [(j, i) for i, j in up]
-    above = lax.ppermute(band(1), "grp", up)
-    below = lax.ppermute(band(0), "grp", down)
+    above = lax.ppermute(above, "grp", up)
+    below = lax.ppermute(below, "grp", down)
 
     rows0, rows1, rows2 = ((height + n) * pitch for n in (8, 6, 0))
     packed = len(pairs(width)) * BLOCK
@@ -425,17 +460,28 @@
         limit=16,
         name="ring",
     )
-    goal = jnp.where(first_core, targets[0], targets[1])
-    goal = (goal + goal.T) * 0.5
-    goal = jnp.concatenate(
-        [
-            goal[i * BLOCK : (i + 1) * BLOCK, j * BLOCK : (j + 1) * BLOCK]
-            for i, j in pairs(width)
-        ],
-        axis=0,
-    )
     chunk = packed // groups
-    goal = lax.dynamic_slice_in_dim(goal, row * chunk, chunk, 0)
+    (goal,) = call(
+        aim,
+        [place, targets],
+        [shape((chunk, BLOCK), F32)],
+        [pltpu.VMEM((packed, BLOCK), F32)],
+        flops=2 * 10**8,
+        name="aim",
+    )
+    backs = []
+    for weight in (weight_second, weight_first):
+        taps, inner = 9, weight.shape[2]
+        (turned,) = call(
+            flip,
+            [weight.reshape(taps, inner, width)],
+            [shape((taps * width, inner), BF)],
+            [],
+            flops=2 * 10**9,
+            limit=16,
+            name="flip",
+        )
+        backs.append(turned)
 
     def helpers(members):
         deep = -(-3 * members // 16) * 16
@@ -489,7 +535,7 @@
     (out,) = call(
         functools.partial(back, dims),
         [place, act1, slope1, act2, slope2, act2r, slope2r, mine, other]
-        + [transposed(weight_second), transposed(weight_first)],
+        + backs,
         [shape(pool_input.shape, F32)],
         [
             pltpu.VMEM((rows_b + 16, width), F32),

time: 115 us -> 82.6 us (0.72)
  local copies, waits for them, and re-layouts: 47 us -> 6.09 us
  waiting for transfers between devices: 12.7 us -> 21.5 us
  Pallas kernels: 27.8 us -> 32.7 us
  other arithmetic: 3.55 us -> 0.08 us
    unnamed x48 -> x12, local copies, waits for them, and re-layouts: 24.8 us -> 6.09 us
    transpose x4 -> x0, local copies, waits for them, and re-layouts: 15.9 us -> none  [transposed(): flipped = weight[::-1, ::-1].transpose(0, 1, 3, 2)]
    pallas_call x7 -> x12, Pallas kernels: 27.8 us -> 32.7 us  [call(): pl.pallas_call(body, out_shape=tuple(outs), in_specs=[SMEM if x.dtype ==...]
    ppermute x4, waiting for transfers between devices: 4.79 us -> 8.31 us  [the longest x1 5.1 us: local(): below = lax.ppermute(below, 'grp', down)]
    ppermute x3, waiting for transfers between devices: 0.01 us -> 2.99 us  [local(): lax.ppermute(share, 'grp', [(i, i ^ k) for i in range(groups)])]
    ppermute x3, starting transfers between devices: 6.22 us -> 3.61 us  [local(): lax.ppermute(sent, 'tile', [(i, i ^ 2 * k) for i in range(tiles)])]
    slice x2 -> x0, local copies, waits for them, and re-layouts: 2.43 us -> none  [the longest x1 1.71 us: local(): goal = jnp.where(first_core, targets[0], targets[1])]
    mul x1 -> x0, other arithmetic: 2.06 us -> none  [local(): goal = (goal + goal.T) * 0.5]
  transfers between devices with their start and end apart: 15 -> 15, of which waited for: 5 -> 12; matrix products, arithmetic and copies ran while one was open for 28% -> 0% of each run, Pallas kernels for 2% -> 7%
where the time goes in v3:
time: 82.6 us; the launch traced here: 82.3 us
  Pallas kernels  32.7 us (40%)
  starting transfers between devices  21.8 us (26%)
  waiting for transfers between devices  21.5 us (26%)
  local copies, waits for them, and re-layouts  6.09 us (7%)
    pallas_call x12, Pallas kernels, call(): pl.pallas_call(body, out_shape=tuple(outs), in_specs=[SMEM if x.dtype ==...  32.7 us
    unnamed x12, local copies, waits for them, and re-layouts  6.09 us
    ppermute x3, waiting for transfers between devices, local(): lax.ppermute(sent, 'tile', [(i, i ^ 2 * k) for i in range(tiles)])  6.02 us
    ppermute x1, waiting for transfers between devices, local(): below = lax.ppermute(below, 'grp', down)  5.1 us
    ppermute x1, starting transfers between devices, local(): far = lax.ppermute(far, 'tile', cross)  4.58 us
    ppermute x3, starting transfers between devices, local(): lax.ppermute(sent, 'tile', [(i, i ^ 2 * k) for i in range(tiles)])  3.61 us
    ppermute x1, starting transfers between devices, local(): above = lax.ppermute(above, 'grp', up)  3.12 us
    ppermute x3, waiting for transfers between devices, local(): lax.ppermute(share, 'grp', [(i, i ^ k) for i in range(groups)])  2.99 us
  transfers between devices with their start and end apart: 15, of which 12 were waited for; matrix products, arithmetic and copies ran while one was open for 0% of the time, Pallas kernels for 7%

profile of v3, /device:TPU:1, one launch (start us, length us, event | category | flops | bytes accessed | tf_op | source)
XLA Modules:
  0.0 82.3 jit_solution(18237877564988145987)
XLA Ops:
  0.0 0.1 pad_add_fusion.place
  0.1 1.0 %copy-done.1 = f32[8,64,256]{2,1,0:T(8,128)S(1)} copy-done((f32[8,64,256]{2,1,0:T(8,128)S(1)}, f32[8,64,256]{2,1,0:T(8,128)}, u32[]{:S(2)}) %copy-start.1) | copy-done | bytes 524312
  1.1 0.6 edges.1
  1.7 4.6 %collective-permute-start = (bf16[8,4,256]{2,1,0:T(4,128)(2,1)S(1)}, bf16[8,4,256]{2,1,0:T(4,128)(2,1)S(1)}, u32[]{:S(2)}, u32[]{:S(2)}) collective-permute-start(bf16[8,4,256]{2,1,0:T(4,128)(2,1)S(1)} %get-tuple-element.28), channel_id=1, source_target_pairs={{1,2},{3,4},{5,6},{2,1},{4,3},{6,5},{9,10},{11,12},{13,14},{10,9},... | collective-permute-start | bytes 49160 | tf_op jit(solution)/shard_map/ppermute | solution.py:410
  6.3 0.1 collective-permute-start.1
  6.4 1.3 %collective-permute-done.far = bf16[8,4,256]{2,1,0:T(4,128)(2,1)S(1)} collective-permute-done((bf16[8,4,256]{2,1,0:T(4,128)(2,1)S(1)}, bf16[8,4,256]{2,1,0:T(4,128)(2,1)S(1)}, u32[]{:S(2)}, u32[]{:S(2)}) %collective-permute-start) | collective-permute-done | bytes 16416 | tf_op jit(solution)/shard_map/ppermute | solution.py:410
  7.7 0.0 collective-permute-done.1.near
  7.7 0.6 bands.1
  8.3 3.1 %collective-permute-start.2 = (bf16[4,72,256]{2,1,0:T(8,128)(2,1)S(1)}, bf16[4,72,256]{2,1,0:T(8,128)(2,1)S(1)}, u32[]{:S(2)}, u32[]{:S(2)}) collective-permute-start(bf16[4,72,256]{2,1,0:T(8,128)(2,1)S(1)} %get-tuple-element.30), channel_id=1, source_target_pairs={{0,8},{8,16},{16,24},{1,9},{9,17},{17,25},{2,10},{10,18},{18,26},{... | collective-permute-start | bytes 442376 | tf_op jit(solution)/shard_map/ppermute | solution.py:422
  11.4 1.3 %collective-permute-start.3 = (bf16[4,72,256]{2,1,0:T(8,128)(2,1)S(1)}, bf16[4,72,256]{2,1,0:T(8,128)(2,1)S(1)}, u32[]{:S(2)}, u32[]{:S(2)}) collective-permute-start(bf16[4,72,256]{2,1,0:T(8,128)(2,1)S(1)} %get-tuple-element.31), channel_id=1, source_target_pairs={{8,0},{16,8},{24,16},{9,1},{17,9},{25,17},{10,2},{18,10},{26,18},{... | collective-permute-start | bytes 442376 | tf_op jit(solution)/shard_map/ppermute | solution.py:423
  12.7 1.9 %collective-permute-done.2.above = bf16[4,72,256]{2,1,0:T(8,128)(2,1)S(1)} collective-permute-done((bf16[4,72,256]{2,1,0:T(8,128)(2,1)S(1)}, bf16[4,72,256]{2,1,0:T(8,128)(2,1)S(1)}, u32[]{:S(2)}, u32[]{:S(2)}) %collective-permute-start.2) | collective-permute-done | bytes 147488 | tf_op jit(solution)/shard_map/ppermute | solution.py:422
  14.6 5.1 %collective-permute-done.3.below = bf16[4,72,256]{2,1,0:T(8,128)(2,1)S(1)} collective-permute-done((bf16[4,72,256]{2,1,0:T(8,128)(2,1)S(1)}, bf16[4,72,256]{2,1,0:T(8,128)(2,1)S(1)}, u32[]{:S(2)}, u32[]{:S(2)}) %collective-permute-start.3) | collective-permute-done | bytes 147488 | tf_op jit(solution)/shard_map/ppermute | solution.py:423
  19.7 2.3 %copy-done = bf16[3,3,512,512]{3,2,1,0:T(8,128)(2,1)S(1)} copy-done((bf16[3,3,512,512]{3,2,1,0:T(8,128)(2,1)S(1)}, bf16[3,3,512,512]{3,2,1,0:T(8,128)(2,1)}, u32[]{:S(2)}) %copy-start) | copy-done | bytes 4718616
  22.1 1.0 %copy-done.2 = f32[8,64,256]{2,1,0:T(8,128)S(1)} copy-done((f32[8,64,256]{2,1,0:T(8,128)S(1)}, f32[8,64,256]{2,1,0:T(8,128)}, u32[]{:S(2)}) %copy-start.2) | copy-done | bytes 524312
  23.1 1.7 %copy-done.4 = bf16[3,3,256,512]{3,2,1,0:T(8,128)(2,1)S(1)} copy-done((bf16[3,3,256,512]{3,2,1,0:T(8,128)(2,1)S(1)}, bf16[3,3,256,512]{3,2,1,0:T(8,128)(2,1)}, u32[]{:S(2)}) %copy-start.4) | copy-done | bytes 2359320
  24.8 11.5 %front.1 = (f32[1136,512]{1,0:T(8,128)S(1)}, f32[1120,512]{1,0:T(8,128)S(1)}, f32[640,512]{1,0:T(8,128)S(1)}, f32[640,512]{1,0:T(8,128)S(1)}, f32[1280,128]{1,0:...) custom-call(s32[4]{0:T(128)S(1)} %pad_add_fusion.place, f32[8,64,256]{2,1,0:T(8,128)S(1)} %copy-done.2, ...), custom_call_target="tpu_custom_call" | custom-call | flops 5662310400 | bytes 16162832 | tf_op jit(solution)/shard_map/front/pallas_call | solution.py:374
  36.3 0.9 %collective-permute-start.4 = (bf16[1296,128]{1,0:T(8,128)(2,1)S(1)}, bf16[1296,128]{1,0:T(8,128)(2,1)S(1)}, u32[]{:S(2)}, u32[]{:S(2)}) collective-permute-start(bf16[1296,128]{1,0:T(8,128)(2,1)S(1)} %get-tuple-element.40), channel_id=1, source_target_pairs={{0,1},{1,0},{2,3},{3,2},{4,5},{5,4},{6,7},{7,6},{8,9},{9,8},{10,11... | collective-permute-start | bytes 995336 | tf_op jit(solution)/shard_map/ppermute | solution.py:497
  37.2 1.3 %collective-permute-done.4.got = bf16[1296,128]{1,0:T(8,128)(2,1)S(1)} collective-permute-done((bf16[1296,128]{1,0:T(8,128)(2,1)S(1)}, bf16[1296,128]{1,0:T(8,128)(2,1)S(1)}, u32[]{:S(2)}, u32[]{:S(2)}) %collective-permute-start.4) | collective-permute-done | bytes 331808 | tf_op jit(solution)/shard_map/ppermute | solution.py:497
  38.5 0.9 %merge_cores.1 = (f32[320,128]{1,0:T(8,128)S(1)}, f32[8,128]{1,0:T(8,128)S(1)}, bf16[336,128]{1,0:T(8,128)(2,1)S(1)}, bf16[336,128]{1,0:T(8,128)(2,1)S(1)}, bf16[336,128]{1,0:T(8,128)(2,1)S(1)}) custom-call(s32[4]{0:T(128)S(1)} %pad_add_fusion.place, f32[1280,128]{1,0:T(8,128)S(1)} %get-tuple-element.38.keep, f32[8,128]{1,0:T(8,128)S(1)} %get-tuple-element.39.mine, ...), custom_call_target="tpu_custom_call" | custom-call | bytes 1417232 | tf_op jit(solution)/shard_map/merge_cores/pallas_call | solution.py:374
  39.4 1.3 %collective-permute-start.5 = (bf16[336,128]{1,0:T(8,128)(2,1)S(1)}, bf16[336,128]{1,0:T(8,128)(2,1)S(1)}, u32[]{:S(2)}, u32[]{:S(2)}) collective-permute-start(bf16[336,128]{1,0:T(8,128)(2,1)S(1)} %get-tuple-element.43), channel_id=1, source_target_pairs={{0,8},{8,0},{16,24},{24,16},{1,9},{9,1},{17,25},{25,17},{2,10},{10... | collective-permute-start | bytes 258056 | tf_op jit(solution)/shard_map/ppermute | solution.py:506
  40.7 0.0 collective-permute-start.6
  40.7 1.4 %collective-permute-start.7 = (bf16[336,128]{1,0:T(8,128)(2,1)S(1)}, bf16[336,128]{1,0:T(8,128)(2,1)S(1)}, u32[]{:S(2)}, u32[]{:S(2)}) collective-permute-start(bf16[336,128]{1,0:T(8,128)(2,1)S(1)} %get-tuple-element.45), channel_id=1, source_target_pairs={{0,24},{8,16},{16,8},{24,0},{1,25},{9,17},{17,9},{25,1},{2,26},{10... | collective-permute-start | bytes 258056 | tf_op jit(solution)/shard_map/ppermute | solution.py:506
  42.1 1.1 %collective-permute-done.5.rest_0_ = bf16[336,128]{1,0:T(8,128)(2,1)S(1)} collective-permute-done((bf16[336,128]{1,0:T(8,128)(2,1)S(1)}, bf16[336,128]{1,0:T(8,128)(2,1)S(1)}, u32[]{:S(2)}, u32[]{:S(2)}) %collective-permute-start.5) | collective-permute-done | bytes 86048 | tf_op jit(solution)/shard_map/ppermute | solution.py:506
  43.2 0.8 %collective-permute-done.6.rest_1_ = bf16[336,128]{1,0:T(8,128)(2,1)S(1)} collective-permute-done((bf16[336,128]{1,0:T(8,128)(2,1)S(1)}, bf16[336,128]{1,0:T(8,128)(2,1)S(1)}, u32[]{:S(2)}, u32[]{:S(2)}) %collective-permute-start.6) | collective-permute-done | bytes 86048 | tf_op jit(solution)/shard_map/ppermute | solution.py:506
  44.0 1.0 %collective-permute-done.7.rest_2_ = bf16[336,128]{1,0:T(8,128)(2,1)S(1)} collective-permute-done((bf16[336,128]{1,0:T(8,128)(2,1)S(1)}, bf16[336,128]{1,0:T(8,128)(2,1)S(1)}, u32[]{:S(2)}, u32[]{:S(2)}) %collective-permute-start.7) | collective-permute-done | bytes 86048 | tf_op jit(solution)/shard_map/ppermute | solution.py:506
  45.0 0.9 %merge_groups.1 = (f32[320,128]{1,0:T(8,128)S(1)}, f32[8,128]{1,0:T(8,128)S(1)}, bf16[336,128]{1,0:T(8,128)(2,1)S(1)}) custom-call(s32[4]{0:T(128)S(1)} %pad_add_fusion.place, f32[320,128]{1,0:T(8,128)S(1)} %get-tuple-element.41.share, f32[8,128]{1,0:T(8,128)S(1)} %get-tuple-element.42.mine, bf16[336,128]{1,0:T(8,128)(2,1)S(1)} %collective-permute-done.5.rest_0_, ...), custom_call_target="tpu_custom_call" | custom-call | bytes 679952 | tf_op jit(solution)/shard_map/merge_groups/pallas_call | solution.py:374
  45.9 3.0 %collective-permute-start.10 = (bf16[336,128]{1,0:T(8,128)(2,1)S(1)}, bf16[336,128]{1,0:T(8,128)(2,1)S(1)}, u32[]{:S(2)}, u32[]{:S(2)}) collective-permute-start(bf16[336,128]{1,0:T(8,128)(2,1)S(1)} %get-tuple-element.48), channel_id=1, source_target_pairs={{0,6},{1,7},{2,4},{3,5},{4,2},{5,3},{6,0},{7,1},{8,14},{9,15},{10,... | collective-permute-start | bytes 258056 | tf_op jit(solution)/shard_map/ppermute | solution.py:517
  48.9 0.0 collective-permute-start.9
  48.9 0.6 collective-permute-start.8
  49.5 0.0 copy-done.3
  49.5 0.8 aim.1.rest_3_
  50.3 0.9 %collective-permute-done.10.rest_2_ = bf16[336,128]{1,0:T(8,128)(2,1)S(1)} collective-permute-done((bf16[336,128]{1,0:T(8,128)(2,1)S(1)}, bf16[336,128]{1,0:T(8,128)(2,1)S(1)}, u32[]{:S(2)}, u32[]{:S(2)}) %collective-permute-start.10) | collective-permute-done | bytes 86048 | tf_op jit(solution)/shard_map/ppermute | solution.py:517
  51.2 5.1 %collective-permute-done.9.rest_1_ = bf16[336,128]{1,0:T(8,128)(2,1)S(1)} collective-permute-done((bf16[336,128]{1,0:T(8,128)(2,1)S(1)}, bf16[336,128]{1,0:T(8,128)(2,1)S(1)}, u32[]{:S(2)}, u32[]{:S(2)}) %collective-permute-start.9) | collective-permute-done | bytes 86048 | tf_op jit(solution)/shard_map/ppermute | solution.py:517
  56.3 0.0 collective-permute-done.8.rest_0_
  56.3 0.9 %merge_chips.1 = (bf16[320,128]{1,0:T(8,128)(2,1)S(1)}, bf16[16,128]{1,0:T(8,128)(2,1)S(1)}) custom-call(s32[4]{0:T(128)S(1)} %pad_add_fusion.place, f32[320,128]{1,0:T(8,128)S(1)} %get-tuple-element.46.share, f32[8,128]{1,0:T(8,128)S(1)} %get-tuple-element.47.mine, bf16[336,128]{1,0:T(8,128)(2,1)S(1)} %collective-permute-done.8.rest_0_, ...), custom_call_target="tpu_custom_call" | custom-call | bytes 675856 | tf_op jit(solution)/shard_map/merge_chips/pallas_call | solution.py:374
  57.2 2.2 %collective-permute-start.13 = (bf16[320,128]{1,0:T(8,128)(2,1)S(1)}, bf16[320,128]{1,0:T(8,128)(2,1)S(1)}, u32[]{:S(2)}, u32[]{:S(2)}) collective-permute-start(bf16[320,128]{1,0:T(8,128)(2,1)S(1)} %get-tuple-element.49.share), channel_id=1, source_target_pairs={{0,24},{8,16},{16,8},{24,0},{1,25},{9,17},{17,9},{25,1},{2,26},{10... | collective-permute-start | bytes 245768 | tf_op jit(solution)/shard_map/ppermute | solution.py:528
  59.5 0.0 collective-permute-start.12
  59.5 0.7 collective-permute-start.11
  60.2 1.3 %collective-permute-done.13.rest_2_ = bf16[320,128]{1,0:T(8,128)(2,1)S(1)} collective-permute-done((bf16[320,128]{1,0:T(8,128)(2,1)S(1)}, bf16[320,128]{1,0:T(8,128)(2,1)S(1)}, u32[]{:S(2)}, u32[]{:S(2)}) %collective-permute-start.13) | collective-permute-done | bytes 81952 | tf_op jit(solution)/shard_map/ppermute | solution.py:528
  61.5 1.6 %collective-permute-done.12.rest_1_ = bf16[320,128]{1,0:T(8,128)(2,1)S(1)} collective-permute-done((bf16[320,128]{1,0:T(8,128)(2,1)S(1)}, bf16[320,128]{1,0:T(8,128)(2,1)S(1)}, u32[]{:S(2)}, u32[]{:S(2)}) %collective-permute-start.12) | collective-permute-done | bytes 81952 | tf_op jit(solution)/shard_map/ppermute | solution.py:528
  63.1 0.1 collective-permute-done.11.rest_0_
  63.2 0.6 assemble.1.mine
  63.7 2.5 %collective-permute-start.14 = (bf16[1296,128]{1,0:T(8,128)(2,1)S(1)}, bf16[1296,128]{1,0:T(8,128)(2,1)S(1)}, u32[]{:S(2)}, u32[]{:S(2)}) collective-permute-start(bf16[1296,128]{1,0:T(8,128)(2,1)S(1)} %assemble.1.mine), channel_id=1, source_target_pairs={{0,1},{1,0},{2,3},{3,2},{4,5},{5,4},{6,7},{7,6},{8,9},{9,8},{10,11... | collective-permute-start | bytes 995336 | tf_op jit(solution)/shard_map/ppermute | solution.py:533
  66.3 1.1 %flip.3.w1 = bf16[4608,256]{1,0:T(8,128)(2,1)S(1)} custom-call(bf16[9,256,512]{2,1,0:T(8,128)(2,1)S(1)} %bitcast.12), custom_call_target="tpu_custom_call" | custom-call | flops 2000000000 | bytes 4718592 | tf_op jit(solution)/shard_map/flip/pallas_call | solution.py:374
  67.4 1.7 %flip.2.w2 = bf16[4608,512]{1,0:T(8,128)(2,1)S(1)} custom-call(bf16[9,512,512]{2,1,0:T(8,128)(2,1)S(1)} %bitcast.9), custom_call_target="tpu_custom_call" | custom-call | flops 2000000000 | bytes 9437184 | tf_op jit(solution)/shard_map/flip/pallas_call | solution.py:374
  69.1 2.1 %ring.1 = (f32[320,512]{1,0:T(8,128)S(1)}, f32[320,512]{1,0:T(8,128)S(1)}) custom-call(f32[1136,512]{1,0:T(8,128)S(1)} %get-tuple-element.32.act1, bf16[4608,512]{1,0:T(8,128)(2,1)S(1)} %bitcast.10), custom_call_target="tpu_custom_call" | custom-call | flops 1509949440 | bytes 8355840 | tf_op jit(solution)/shard_map/ring/pallas_call | solution.py:374
  71.2 0.0 collective-permute-done.14.other
  71.2 11.1 %back.1 = f32[8,64,256]{2,1,0:T(8,128)} custom-call(s32[4]{0:T(128)S(1)} %pad_add_fusion.place, f32[1136,512]{1,0:T(8,128)S(1)} %get-tuple-element.32.act1, f32[1120,512]{1,0:T(8,128)S(1)} %get-tuple-element.33.slope1, f32[640,512]{1,0:T(8,128)S(1)} %get-tuple-element.34.act2, f32[640,512]{1,0:T(8,128)S(1)} %get-tuple-element.35.slope2, ...), custom_call_target="tpu_custom_call" | custom-call | flops 5284823040 | bytes 16818192 | tf_op jit(solution)/shard_map/back/pallas_call | solution.py:374
  (7 shorter events, 0.0 us)
Async XLA Ops:
  0.1 1.0 %copy-start.1 = (f32[8,64,256]{2,1,0:T(8,128)S(1)}, f32[8,64,256]{2,1,0:T(8,128)}, u32[]{:S(2)}) copy-start(f32[8,64,256]{2,1,0:T(8,128)} %pool.5) | copy-start | bytes 1572868
  1.7 6.0 %collective-permute-start = (bf16[8,4,256]{2,1,0:T(4,128)(2,1)S(1)}, bf16[8,4,256]{2,1,0:T(4,128)(2,1)S(1)}, u32[]{:S(2)}, u32[]{:S(2)}) collective-permute-start(bf16[8,4,256]{2,1,0:T(4,128)(2,1)S(1)} %get-tuple-element.28), channel_id=1, source_target_pairs={{1,2},{3,4},{5,6},{2,1},{4,3},{6,5},{9,10},{11,12},{13,14},{10,9},... | collective-permute-start | bytes 49160 | tf_op jit(solution)/shard_map/ppermute | solution.py:410
  6.3 1.4 %collective-permute-start.1 = (bf16[8,4,256]{2,1,0:T(4,128)(2,1)S(1)}, bf16[8,4,256]{2,1,0:T(4,128)(2,1)S(1)}, u32[]{:S(2)}, u32[]{:S(2)}) collective-permute-start(bf16[8,4,256]{2,1,0:T(4,128)(2,1)S(1)} %get-tuple-element.29), channel_id=1, source_target_pairs={{0,1},{1,0},{2,3},{3,2},{4,5},{5,4},{6,7},{7,6},{8,9},{9,8},{10,11... | collective-permute-start | bytes 49160 | tf_op jit(solution)/shard_map/ppermute | solution.py:411
  8.3 6.3 %collective-permute-start.2 = (bf16[4,72,256]{2,1,0:T(8,128)(2,1)S(1)}, bf16[4,72,256]{2,1,0:T(8,128)(2,1)S(1)}, u32[]{:S(2)}, u32[]{:S(2)}) collective-permute-start(bf16[4,72,256]{2,1,0:T(8,128)(2,1)S(1)} %get-tuple-element.30), channel_id=1, source_target_pairs={{0,8},{8,16},{16,24},{1,9},{9,17},{17,25},{2,10},{10,18},{18,26},{... | collective-permute-start | bytes 442376 | tf_op jit(solution)/shard_map/ppermute | solution.py:422
  11.4 8.3 %collective-permute-start.3 = (bf16[4,72,256]{2,1,0:T(8,128)(2,1)S(1)}, bf16[4,72,256]{2,1,0:T(8,128)(2,1)S(1)}, u32[]{:S(2)}, u32[]{:S(2)}) collective-permute-start(bf16[4,72,256]{2,1,0:T(8,128)(2,1)S(1)} %get-tuple-element.31), channel_id=1, source_target_pairs={{8,0},{16,8},{24,16},{9,1},{17,9},{25,17},{10,2},{18,10},{26,18},{... | collective-permute-start | bytes 442376 | tf_op jit(solution)/shard_map/ppermute | solution.py:423
  19.7 2.3 %copy-start = (bf16[3,3,512,512]{3,2,1,0:T(8,128)(2,1)S(1)}, bf16[3,3,512,512]{3,2,1,0:T(8,128)(2,1)}, u32[]{:S(2)}) copy-start(bf16[3,3,512,512]{3,2,1,0:T(8,128)(2,1)} %param.6) | copy-start | bytes 14155780
  22.1 1.0 %copy-start.2 = (f32[8,64,256]{2,1,0:T(8,128)S(1)}, f32[8,64,256]{2,1,0:T(8,128)}, u32[]{:S(2)}) copy-start(f32[8,64,256]{2,1,0:T(8,128)} %pool.5) | copy-start | bytes 1572868
  23.1 1.7 %copy-start.4 = (bf16[3,3,256,512]{3,2,1,0:T(8,128)(2,1)S(1)}, bf16[3,3,256,512]{3,2,1,0:T(8,128)(2,1)}, u32[]{:S(2)}) copy-start(bf16[3,3,256,512]{3,2,1,0:T(8,128)(2,1)} %param.5) | copy-start | bytes 7077892
  24.8 24.7 %copy-start.3 = (f32[2,512,512]{2,1,0:T(8,128)S(1)}, f32[2,512,512]{2,1,0:T(8,128)}, u32[]{:S(2)}) copy-start(f32[2,512,512]{2,1,0:T(8,128)} %targets.1) | copy-start | bytes 6291460
  36.3 2.2 %collective-permute-start.4 = (bf16[1296,128]{1,0:T(8,128)(2,1)S(1)}, bf16[1296,128]{1,0:T(8,128)(2,1)S(1)}, u32[]{:S(2)}, u32[]{:S(2)}) collective-permute-start(bf16[1296,128]{1,0:T(8,128)(2,1)S(1)} %get-tuple-element.40), channel_id=1, source_target_pairs={{0,1},{1,0},{2,3},{3,2},{4,5},{5,4},{6,7},{7,6},{8,9},{9,8},{10,11... | collective-permute-start | bytes 995336 | tf_op jit(solution)/shard_map/ppermute | solution.py:497
  38.5 27.8 %copy-start.5 = (bf16[3,3,256,512]{3,2,1,0:T(8,128)(2,1)S(1)}, bf16[3,3,256,512]{3,2,1,0:T(8,128)(2,1)}, u32[]{:S(2)}) copy-start(bf16[3,3,256,512]{3,2,1,0:T(8,128)(2,1)} %param.5) | copy-start | bytes 7077892
  39.4 3.8 %collective-permute-start.5 = (bf16[336,128]{1,0:T(8,128)(2,1)S(1)}, bf16[336,128]{1,0:T(8,128)(2,1)S(1)}, u32[]{:S(2)}, u32[]{:S(2)}) collective-permute-start(bf16[336,128]{1,0:T(8,128)(2,1)S(1)} %get-tuple-element.43), channel_id=1, source_target_pairs={{0,8},{8,0},{16,24},{24,16},{1,9},{9,1},{17,25},{25,17},{2,10},{10... | collective-permute-start | bytes 258056 | tf_op jit(solution)/shard_map/ppermute | solution.py:506
  40.7 3.3 %collective-permute-start.6 = (bf16[336,128]{1,0:T(8,128)(2,1)S(1)}, bf16[336,128]{1,0:T(8,128)(2,1)S(1)}, u32[]{:S(2)}, u32[]{:S(2)}) collective-permute-start(bf16[336,128]{1,0:T(8,128)(2,1)S(1)} %get-tuple-element.44), channel_id=1, source_target_pairs={{0,16},{8,24},{16,0},{24,8},{1,17},{9,25},{17,1},{25,9},{2,18},{10... | collective-permute-start | bytes 258056 | tf_op jit(solution)/shard_map/ppermute | solution.py:506
  40.7 4.3 %collective-permute-start.7 = (bf16[336,128]{1,0:T(8,128)(2,1)S(1)}, bf16[336,128]{1,0:T(8,128)(2,1)S(1)}, u32[]{:S(2)}, u32[]{:S(2)}) collective-permute-start(bf16[336,128]{1,0:T(8,128)(2,1)S(1)} %get-tuple-element.45), channel_id=1, source_target_pairs={{0,24},{8,16},{16,8},{24,0},{1,25},{9,17},{17,9},{25,1},{2,26},{10... | collective-permute-start | bytes 258056 | tf_op jit(solution)/shard_map/ppermute | solution.py:506
  45.9 5.3 %collective-permute-start.10 = (bf16[336,128]{1,0:T(8,128)(2,1)S(1)}, bf16[336,128]{1,0:T(8,128)(2,1)S(1)}, u32[]{:S(2)}, u32[]{:S(2)}) collective-permute-start(bf16[336,128]{1,0:T(8,128)(2,1)S(1)} %get-tuple-element.48), channel_id=1, source_target_pairs={{0,6},{1,7},{2,4},{3,5},{4,2},{5,3},{6,0},{7,1},{8,14},{9,15},{10,... | collective-permute-start | bytes 258056 | tf_op jit(solution)/shard_map/ppermute | solution.py:517
  48.9 7.4 %collective-permute-start.9 = (bf16[336,128]{1,0:T(8,128)(2,1)S(1)}, bf16[336,128]{1,0:T(8,128)(2,1)S(1)}, u32[]{:S(2)}, u32[]{:S(2)}) collective-permute-start(bf16[336,128]{1,0:T(8,128)(2,1)S(1)} %get-tuple-element.48), channel_id=1, source_target_pairs={{0,4},{1,5},{2,6},{3,7},{4,0},{5,1},{6,2},{7,3},{8,12},{9,13},{10,... | collective-permute-start | bytes 258056 | tf_op jit(solution)/shard_map/ppermute | solution.py:517
  48.9 7.4 %collective-permute-start.8 = (bf16[336,128]{1,0:T(8,128)(2,1)S(1)}, bf16[336,128]{1,0:T(8,128)(2,1)S(1)}, u32[]{:S(2)}, u32[]{:S(2)}) collective-permute-start(bf16[336,128]{1,0:T(8,128)(2,1)S(1)} %get-tuple-element.48), channel_id=1, source_target_pairs={{0,2},{1,3},{2,0},{3,1},{4,6},{5,7},{6,4},{7,5},{8,10},{9,11},{10,... | collective-permute-start | bytes 258056 | tf_op jit(solution)/shard_map/ppermute | solution.py:517
  57.2 4.3 %collective-permute-start.13 = (bf16[320,128]{1,0:T(8,128)(2,1)S(1)}, bf16[320,128]{1,0:T(8,128)(2,1)S(1)}, u32[]{:S(2)}, u32[]{:S(2)}) collective-permute-start(bf16[320,128]{1,0:T(8,128)(2,1)S(1)} %get-tuple-element.49.share), channel_id=1, source_target_pairs={{0,24},{8,16},{16,8},{24,0},{1,25},{9,17},{17,9},{25,1},{2,26},{10... | collective-permute-start | bytes 245768 | tf_op jit(solution)/shard_map/ppermute | solution.py:528
  59.5 3.6 %collective-permute-start.12 = (bf16[320,128]{1,0:T(8,128)(2,1)S(1)}, bf16[320,128]{1,0:T(8,128)(2,1)S(1)}, u32[]{:S(2)}, u32[]{:S(2)}) collective-permute-start(bf16[320,128]{1,0:T(8,128)(2,1)S(1)} %get-tuple-element.49.share), channel_id=1, source_target_pairs={{0,16},{8,24},{16,0},{24,8},{1,17},{9,25},{17,1},{25,9},{2,18},{10... | collective-permute-start | bytes 245768 | tf_op jit(solution)/shard_map/ppermute | solution.py:528
  59.5 3.7 %collective-permute-start.11 = (bf16[320,128]{1,0:T(8,128)(2,1)S(1)}, bf16[320,128]{1,0:T(8,128)(2,1)S(1)}, u32[]{:S(2)}, u32[]{:S(2)}) collective-permute-start(bf16[320,128]{1,0:T(8,128)(2,1)S(1)} %get-tuple-element.49.share), channel_id=1, source_target_pairs={{0,8},{8,0},{16,24},{24,16},{1,9},{9,1},{17,25},{25,17},{2,10},{10... | collective-permute-start | bytes 245768 | tf_op jit(solution)/shard_map/ppermute | solution.py:528
  63.7 7.4 %collective-permute-start.14 = (bf16[1296,128]{1,0:T(8,128)(2,1)S(1)}, bf16[1296,128]{1,0:T(8,128)(2,1)S(1)}, u32[]{:S(2)}, u32[]{:S(2)}) collective-permute-start(bf16[1296,128]{1,0:T(8,128)(2,1)S(1)} %assemble.1.mine), channel_id=1, source_target_pairs={{0,1},{1,0},{2,3},{3,2},{4,5},{5,4},{6,7},{7,6},{8,9},{9,8},{10,11... | collective-permute-start | bytes 995336 | tf_op jit(solution)/shard_map/ppermute | solution.py:533

commit v4 on v3

--- a/solution.py
+++ b/solution.py
@@ -6,6 +6,7 @@
 from jax.experimental import pallas as pl
 from jax.experimental.pallas import tpu as pltpu
 from jax.sharding import PartitionSpec as P
+
 
 GELU_SCALE = 0.7978845608
 GELU_CUBIC = 0.044715
@@ -367,7 +368,7 @@
     goal[...] = full[pl.ds(pl.multiple_of(place[3] * chunk, 16), chunk), :]
 
 
-def call(body, ins, outs, scratch, flops=0, limit=None, name=None):
+def call(body, ins, outs, scratch, flops=0, limit=None):
     moved = sum(x.size * x.dtype.itemsize for x in ins) + sum(
         x.size * x.dtype.itemsize for x in outs
     )
@@ -379,7 +380,6 @@
         scratch_shapes=scratch,
         compiler_params=pltpu.CompilerParams(vmem_limit_bytes=(limit or 8) * MIB),
         cost_estimate=pl.CostEstimate(flops=flops, bytes_accessed=moved, transcendentals=0),
-        name=name,
     )(*ins)
 
 
@@ -406,7 +406,7 @@
     cross = cross + [(j, i) for i, j in cross]
 
     rim = shape((height, REACH, depth), BF)
-    far, near = call(edges, [place, pool_input], [rim] * 2, [], name="edges")
+    far, near = call(edges, [place, pool_input], [rim] * 2, [])
     far = lax.ppermute(far, "tile", cross)
     near = lax.ppermute(near, "tile", swap)
     band = shape((REACH, breadth + 2 * REACH, depth), BF)
@@ -415,7 +415,6 @@
         [place, pool_input, far, near],
         [band] * 2,
         [pltpu.VMEM((breadth + 2 * REACH, depth), F32)],
-        name="bands",
     )
     up = [(i, i + 1) for i in range(groups - 1)]
     down = [(j, i) for i, j in up]
@@ -449,7 +448,6 @@
         ],
         flops=2 * 9 * width * (rows1 * depth + rows2 * width),
         limit=30,
-        name="front",
     )
     act2r, slope2r = call(
         functools.partial(ring, dims),
@@ -458,7 +456,6 @@
         [pltpu.VMEM((2 * step, 3 * width), BF)],
         flops=2 * 9 * width * width * 2 * step,
         limit=16,
-        name="ring",
     )
     chunk = packed // groups
     (goal,) = call(
@@ -467,7 +464,6 @@
         [shape((chunk, BLOCK), F32)],
         [pltpu.VMEM((packed, BLOCK), F32)],
         flops=2 * 10**8,
-        name="aim",
     )
     backs = []
     for weight in (weight_second, weight_first):
@@ -479,7 +475,6 @@
             [],
             flops=2 * 10**9,
             limit=16,
-            name="flip",
         )
         backs.append(turned)
 
@@ -500,7 +495,6 @@
         [place, keep, mine, got],
         [part, centre] + [message] * (groups - 1),
         helpers(2),
-        name="merge_cores",
     )
     gots = [
         lax.ppermute(sents[k - 1], "grp", [(i, i ^ k) for i in range(groups)])
@@ -511,7 +505,6 @@
         [place, share, mean] + gots,
         [part, centre, message],
         helpers(groups),
-        name="merge_groups",
     )
     gots = [
         lax.ppermute(sent, "tile", [(i, i ^ (2 * k)) for i in range(tiles)])
@@ -522,14 +515,13 @@
         [place, share, mean] + gots + [goal],
         [shape((chunk, BLOCK), BF), shape((EXTRA, BLOCK), BF)],
         helpers(chips),
-        name="merge_chips",
     )
     gots = [
         lax.ppermute(share, "grp", [(i, i ^ k) for i in range(groups)])
         for k in range(1, groups)
     ]
     table = shape((packed + EXTRA, BLOCK), BF)
-    (mine,) = call(assemble, [place, share, mean] + gots, [table], [], name="assemble")
+    (mine,) = call(assemble, [place, share, mean] + gots, [table], [])
     other = lax.ppermute(mine, "tile", swap)
     rows_b, rows_d = (height + 4) * pitch, (height + 2) * pitch
     (out,) = call(
@@ -549,7 +541,6 @@
         ],
         flops=2 * 9 * width * (rows_d * width + rows2 * depth),
         limit=32,
-        name="back",
     )
     return out
 

time: 82.6 us -> 82.6 us (level)
  no operation moved by 1% of the time
where the time goes in v4:
time: 82.6 us; the launch traced here: 82.3 us
  Pallas kernels  32.7 us (40%)
  starting transfers between devices  21.8 us (26%)
  waiting for transfers between devices  21.5 us (26%)
  local copies, waits for them, and re-layouts  6.09 us (7%)
    pallas_call x12, Pallas kernels, call(): pl.pallas_call(body, out_shape=tuple(outs), in_specs=[SMEM if x.dtype ==...  32.7 us
    unnamed x12, local copies, waits for them, and re-layouts  6.09 us
    ppermute x3, waiting for transfers between devices, local(): lax.ppermute(sent, 'tile', [(i, i ^ 2 * k) for i in range(tiles)])  6.02 us
    ppermute x1, waiting for transfers between devices, local(): below = lax.ppermute(below, 'grp', down)  5.1 us
    ppermute x1, starting transfers between devices, local(): far = lax.ppermute(far, 'tile', cross)  4.58 us
    ppermute x3, starting transfers between devices, local(): lax.ppermute(sent, 'tile', [(i, i ^ 2 * k) for i in range(tiles)])  3.61 us
    ppermute x1, starting transfers between devices, local(): above = lax.ppermute(above, 'grp', up)  3.12 us
    ppermute x3, waiting for transfers between devices, local(): lax.ppermute(share, 'grp', [(i, i ^ k) for i in range(groups)])  2.99 us
  transfers between devices with their start and end apart: 15, of which 12 were waited for; matrix products, arithmetic and copies ran while one was open for 0% of the time, Pallas kernels for 7%

profile of v4, /device:TPU:1, one launch (start us, length us, event | category | flops | bytes accessed | tf_op | source)
XLA Modules:
  0.0 82.3 jit_solution(18237877564988145987)
XLA Ops:
  0.0 0.1 pad_add_fusion.place
  0.1 1.0 %copy-done.1 = f32[8,64,256]{2,1,0:T(8,128)S(1)} copy-done((f32[8,64,256]{2,1,0:T(8,128)S(1)}, f32[8,64,256]{2,1,0:T(8,128)}, u32[]{:S(2)}) %copy-start.1) | copy-done | bytes 524312
  1.1 0.6 shard_map.46
  1.7 4.6 %collective-permute-start = (bf16[8,4,256]{2,1,0:T(4,128)(2,1)S(1)}, bf16[8,4,256]{2,1,0:T(4,128)(2,1)S(1)}, u32[]{:S(2)}, u32[]{:S(2)}) collective-permute-start(bf16[8,4,256]{2,1,0:T(4,128)(2,1)S(1)} %get-tuple-element.28), channel_id=1, source_target_pairs={{1,2},{3,4},{5,6},{2,1},{4,3},{6,5},{9,10},{11,12},{13,14},{10,9},... | collective-permute-start | bytes 49160 | tf_op jit(solution)/shard_map/ppermute | solution.py:410
  6.3 0.1 collective-permute-start.1
  6.4 1.3 %collective-permute-done.far = bf16[8,4,256]{2,1,0:T(4,128)(2,1)S(1)} collective-permute-done((bf16[8,4,256]{2,1,0:T(4,128)(2,1)S(1)}, bf16[8,4,256]{2,1,0:T(4,128)(2,1)S(1)}, u32[]{:S(2)}, u32[]{:S(2)}) %collective-permute-start) | collective-permute-done | bytes 16416 | tf_op jit(solution)/shard_map/ppermute | solution.py:410
  7.7 0.0 collective-permute-done.1.near
  7.7 0.6 shard_map.47
  8.3 3.1 %collective-permute-start.2 = (bf16[4,72,256]{2,1,0:T(8,128)(2,1)S(1)}, bf16[4,72,256]{2,1,0:T(8,128)(2,1)S(1)}, u32[]{:S(2)}, u32[]{:S(2)}) collective-permute-start(bf16[4,72,256]{2,1,0:T(8,128)(2,1)S(1)} %get-tuple-element.30), channel_id=1, source_target_pairs={{0,8},{8,16},{16,24},{1,9},{9,17},{17,25},{2,10},{10,18},{18,26},{... | collective-permute-start | bytes 442376 | tf_op jit(solution)/shard_map/ppermute | solution.py:421
  11.4 1.3 %collective-permute-start.3 = (bf16[4,72,256]{2,1,0:T(8,128)(2,1)S(1)}, bf16[4,72,256]{2,1,0:T(8,128)(2,1)S(1)}, u32[]{:S(2)}, u32[]{:S(2)}) collective-permute-start(bf16[4,72,256]{2,1,0:T(8,128)(2,1)S(1)} %get-tuple-element.31), channel_id=1, source_target_pairs={{8,0},{16,8},{24,16},{9,1},{17,9},{25,17},{10,2},{18,10},{26,18},{... | collective-permute-start | bytes 442376 | tf_op jit(solution)/shard_map/ppermute | solution.py:422
  12.7 1.9 %collective-permute-done.2.above = bf16[4,72,256]{2,1,0:T(8,128)(2,1)S(1)} collective-permute-done((bf16[4,72,256]{2,1,0:T(8,128)(2,1)S(1)}, bf16[4,72,256]{2,1,0:T(8,128)(2,1)S(1)}, u32[]{:S(2)}, u32[]{:S(2)}) %collective-permute-start.2) | collective-permute-done | bytes 147488 | tf_op jit(solution)/shard_map/ppermute | solution.py:421
  14.6 5.1 %collective-permute-done.3.below = bf16[4,72,256]{2,1,0:T(8,128)(2,1)S(1)} collective-permute-done((bf16[4,72,256]{2,1,0:T(8,128)(2,1)S(1)}, bf16[4,72,256]{2,1,0:T(8,128)(2,1)S(1)}, u32[]{:S(2)}, u32[]{:S(2)}) %collective-permute-start.3) | collective-permute-done | bytes 147488 | tf_op jit(solution)/shard_map/ppermute | solution.py:422
  19.7 2.3 %copy-done = bf16[3,3,512,512]{3,2,1,0:T(8,128)(2,1)S(1)} copy-done((bf16[3,3,512,512]{3,2,1,0:T(8,128)(2,1)S(1)}, bf16[3,3,512,512]{3,2,1,0:T(8,128)(2,1)}, u32[]{:S(2)}) %copy-start) | copy-done | bytes 4718616
  22.1 1.0 %copy-done.2 = f32[8,64,256]{2,1,0:T(8,128)S(1)} copy-done((f32[8,64,256]{2,1,0:T(8,128)S(1)}, f32[8,64,256]{2,1,0:T(8,128)}, u32[]{:S(2)}) %copy-start.2) | copy-done | bytes 524312
  23.1 1.7 %copy-done.4 = bf16[3,3,256,512]{3,2,1,0:T(8,128)(2,1)S(1)} copy-done((bf16[3,3,256,512]{3,2,1,0:T(8,128)(2,1)S(1)}, bf16[3,3,256,512]{3,2,1,0:T(8,128)(2,1)}, u32[]{:S(2)}) %copy-start.4) | copy-done | bytes 2359320
  24.8 11.5 %shard_map.48 = (f32[1136,512]{1,0:T(8,128)S(1)}, f32[1120,512]{1,0:T(8,128)S(1)}, f32[640,512]{1,0:T(8,128)S(1)}, f32[640,512]{1,0:T(8,128)S(1)}, f32[1280,128]...) custom-call(s32[4]{0:T(128)S(1)} %pad_add_fusion.place, f32[8,64,256]{2,1,0:T(8,128)S(1)} %copy-done.2, ...), custom_call_target="tpu_custom_call" | custom-call | flops 5662310400 | bytes 16162832 | tf_op jit(solution)/shard_map/pallas_call | solution.py:375
  36.3 0.9 %collective-permute-start.4 = (bf16[1296,128]{1,0:T(8,128)(2,1)S(1)}, bf16[1296,128]{1,0:T(8,128)(2,1)S(1)}, u32[]{:S(2)}, u32[]{:S(2)}) collective-permute-start(bf16[1296,128]{1,0:T(8,128)(2,1)S(1)} %get-tuple-element.40), channel_id=1, source_target_pairs={{0,1},{1,0},{2,3},{3,2},{4,5},{5,4},{6,7},{7,6},{8,9},{9,8},{10,11... | collective-permute-start | bytes 995336 | tf_op jit(solution)/shard_map/ppermute | solution.py:492
  37.2 1.3 %collective-permute-done.4.got = bf16[1296,128]{1,0:T(8,128)(2,1)S(1)} collective-permute-done((bf16[1296,128]{1,0:T(8,128)(2,1)S(1)}, bf16[1296,128]{1,0:T(8,128)(2,1)S(1)}, u32[]{:S(2)}, u32[]{:S(2)}) %collective-permute-start.4) | collective-permute-done | bytes 331808 | tf_op jit(solution)/shard_map/ppermute | solution.py:492
  38.5 0.9 %shard_map.50 = (f32[320,128]{1,0:T(8,128)S(1)}, f32[8,128]{1,0:T(8,128)S(1)}, bf16[336,128]{1,0:T(8,128)(2,1)S(1)}, bf16[336,128]{1,0:T(8,128)(2,1)S(1)}, bf16[336,128]{1,0:T(8,128)(2,1)S(1)}) custom-call(s32[4]{0:T(128)S(1)} %pad_add_fusion.place, f32[1280,128]{1,0:T(8,128)S(1)} %get-tuple-element.38.keep, f32[8,128]{1,0:T(8,128)S(1)} %get-tuple-element.39.mine, ...), custom_call_target="tpu_custom_call" | custom-call | bytes 1417232 | tf_op jit(solution)/shard_map/pallas_call | solution.py:375
  39.4 1.3 %collective-permute-start.5 = (bf16[336,128]{1,0:T(8,128)(2,1)S(1)}, bf16[336,128]{1,0:T(8,128)(2,1)S(1)}, u32[]{:S(2)}, u32[]{:S(2)}) collective-permute-start(bf16[336,128]{1,0:T(8,128)(2,1)S(1)} %get-tuple-element.43), channel_id=1, source_target_pairs={{0,8},{8,0},{16,24},{24,16},{1,9},{9,1},{17,25},{25,17},{2,10},{10... | collective-permute-start | bytes 258056 | tf_op jit(solution)/shard_map/ppermute | solution.py:500
  40.7 0.0 collective-permute-start.6
  40.7 1.4 %collective-permute-start.7 = (bf16[336,128]{1,0:T(8,128)(2,1)S(1)}, bf16[336,128]{1,0:T(8,128)(2,1)S(1)}, u32[]{:S(2)}, u32[]{:S(2)}) collective-permute-start(bf16[336,128]{1,0:T(8,128)(2,1)S(1)} %get-tuple-element.45), channel_id=1, source_target_pairs={{0,24},{8,16},{16,8},{24,0},{1,25},{9,17},{17,9},{25,1},{2,26},{10... | collective-permute-start | bytes 258056 | tf_op jit(solution)/shard_map/ppermute | solution.py:500
  42.1 1.1 %collective-permute-done.5.rest_0_ = bf16[336,128]{1,0:T(8,128)(2,1)S(1)} collective-permute-done((bf16[336,128]{1,0:T(8,128)(2,1)S(1)}, bf16[336,128]{1,0:T(8,128)(2,1)S(1)}, u32[]{:S(2)}, u32[]{:S(2)}) %collective-permute-start.5) | collective-permute-done | bytes 86048 | tf_op jit(solution)/shard_map/ppermute | solution.py:500
  43.2 0.8 %collective-permute-done.6.rest_1_ = bf16[336,128]{1,0:T(8,128)(2,1)S(1)} collective-permute-done((bf16[336,128]{1,0:T(8,128)(2,1)S(1)}, bf16[336,128]{1,0:T(8,128)(2,1)S(1)}, u32[]{:S(2)}, u32[]{:S(2)}) %collective-permute-start.6) | collective-permute-done | bytes 86048 | tf_op jit(solution)/shard_map/ppermute | solution.py:500
  44.0 1.0 %collective-permute-done.7.rest_2_ = bf16[336,128]{1,0:T(8,128)(2,1)S(1)} collective-permute-done((bf16[336,128]{1,0:T(8,128)(2,1)S(1)}, bf16[336,128]{1,0:T(8,128)(2,1)S(1)}, u32[]{:S(2)}, u32[]{:S(2)}) %collective-permute-start.7) | collective-permute-done | bytes 86048 | tf_op jit(solution)/shard_map/ppermute | solution.py:500
  45.0 0.9 %shard_map.51 = (f32[320,128]{1,0:T(8,128)S(1)}, f32[8,128]{1,0:T(8,128)S(1)}, bf16[336,128]{1,0:T(8,128)(2,1)S(1)}) custom-call(s32[4]{0:T(128)S(1)} %pad_add_fusion.place, f32[320,128]{1,0:T(8,128)S(1)} %get-tuple-element.41.share, f32[8,128]{1,0:T(8,128)S(1)} %get-tuple-element.42.mine, bf16[336,128]{1,0:T(8,128)(2,1)S(1)} %collective-permute-done.5.rest_0_, ...), custom_call_target="tpu_custom_call" | custom-call | bytes 679952 | tf_op jit(solution)/shard_map/pallas_call | solution.py:375
  45.9 3.0 %collective-permute-start.10 = (bf16[336,128]{1,0:T(8,128)(2,1)S(1)}, bf16[336,128]{1,0:T(8,128)(2,1)S(1)}, u32[]{:S(2)}, u32[]{:S(2)}) collective-permute-start(bf16[336,128]{1,0:T(8,128)(2,1)S(1)} %get-tuple-element.48), channel_id=1, source_target_pairs={{0,6},{1,7},{2,4},{3,5},{4,2},{5,3},{6,0},{7,1},{8,14},{9,15},{10,... | collective-permute-start | bytes 258056 | tf_op jit(solution)/shard_map/ppermute | solution.py:510
  48.9 0.0 collective-permute-start.9
  48.9 0.6 collective-permute-start.8
  49.5 0.0 copy-done.3
  49.5 0.8 shard_map.52.rest_3_
  50.3 0.9 %collective-permute-done.10.rest_2_ = bf16[336,128]{1,0:T(8,128)(2,1)S(1)} collective-permute-done((bf16[336,128]{1,0:T(8,128)(2,1)S(1)}, bf16[336,128]{1,0:T(8,128)(2,1)S(1)}, u32[]{:S(2)}, u32[]{:S(2)}) %collective-permute-start.10) | collective-permute-done | bytes 86048 | tf_op jit(solution)/shard_map/ppermute | solution.py:510
  51.2 5.1 %collective-permute-done.9.rest_1_ = bf16[336,128]{1,0:T(8,128)(2,1)S(1)} collective-permute-done((bf16[336,128]{1,0:T(8,128)(2,1)S(1)}, bf16[336,128]{1,0:T(8,128)(2,1)S(1)}, u32[]{:S(2)}, u32[]{:S(2)}) %collective-permute-start.9) | collective-permute-done | bytes 86048 | tf_op jit(solution)/shard_map/ppermute | solution.py:510
  56.3 0.0 collective-permute-done.8.rest_0_
  56.3 0.9 %shard_map.53 = (bf16[320,128]{1,0:T(8,128)(2,1)S(1)}, bf16[16,128]{1,0:T(8,128)(2,1)S(1)}) custom-call(s32[4]{0:T(128)S(1)} %pad_add_fusion.place, f32[320,128]{1,0:T(8,128)S(1)} %get-tuple-element.46.share, f32[8,128]{1,0:T(8,128)S(1)} %get-tuple-element.47.mine, bf16[336,128]{1,0:T(8,128)(2,1)S(1)} %collective-permute-done.8.rest_0_, ...), custom_call_target="tpu_custom_call" | custom-call | bytes 675856 | tf_op jit(solution)/shard_map/pallas_call | solution.py:375
  57.2 2.2 %collective-permute-start.13 = (bf16[320,128]{1,0:T(8,128)(2,1)S(1)}, bf16[320,128]{1,0:T(8,128)(2,1)S(1)}, u32[]{:S(2)}, u32[]{:S(2)}) collective-permute-start(bf16[320,128]{1,0:T(8,128)(2,1)S(1)} %get-tuple-element.49.share), channel_id=1, source_target_pairs={{0,24},{8,16},{16,8},{24,0},{1,25},{9,17},{17,9},{25,1},{2,26},{10... | collective-permute-start | bytes 245768 | tf_op jit(solution)/shard_map/ppermute | solution.py:520
  59.5 0.0 collective-permute-start.12
  59.5 0.7 collective-permute-start.11
  60.2 1.3 %collective-permute-done.13.rest_2_ = bf16[320,128]{1,0:T(8,128)(2,1)S(1)} collective-permute-done((bf16[320,128]{1,0:T(8,128)(2,1)S(1)}, bf16[320,128]{1,0:T(8,128)(2,1)S(1)}, u32[]{:S(2)}, u32[]{:S(2)}) %collective-permute-start.13) | collective-permute-done | bytes 81952 | tf_op jit(solution)/shard_map/ppermute | solution.py:520
  61.5 1.6 %collective-permute-done.12.rest_1_ = bf16[320,128]{1,0:T(8,128)(2,1)S(1)} collective-permute-done((bf16[320,128]{1,0:T(8,128)(2,1)S(1)}, bf16[320,128]{1,0:T(8,128)(2,1)S(1)}, u32[]{:S(2)}, u32[]{:S(2)}) %collective-permute-start.12) | collective-permute-done | bytes 81952 | tf_op jit(solution)/shard_map/ppermute | solution.py:520
  63.1 0.1 collective-permute-done.11.rest_0_
  63.2 0.6 shard_map.54.mine
  63.7 2.5 %collective-permute-start.14 = (bf16[1296,128]{1,0:T(8,128)(2,1)S(1)}, bf16[1296,128]{1,0:T(8,128)(2,1)S(1)}, u32[]{:S(2)}, u32[]{:S(2)}) collective-permute-start(bf16[1296,128]{1,0:T(8,128)(2,1)S(1)} %shard_map.54.mine), channel_id=1, source_target_pairs={{0,1},{1,0},{2,3},{3,2},{4,5},{5,4},{6,7},{7,6},{8,9},{9,8},{10,11... | collective-permute-start | bytes 995336 | tf_op jit(solution)/shard_map/ppermute | solution.py:525
  66.3 1.1 %shard_map.56.w1 = bf16[4608,256]{1,0:T(8,128)(2,1)S(1)} custom-call(bf16[9,256,512]{2,1,0:T(8,128)(2,1)S(1)} %bitcast.12), custom_call_target="tpu_custom_call" | custom-call | flops 2000000000 | bytes 4718592 | tf_op jit(solution)/shard_map/pallas_call | solution.py:375
  67.4 1.7 %shard_map.55.w2 = bf16[4608,512]{1,0:T(8,128)(2,1)S(1)} custom-call(bf16[9,512,512]{2,1,0:T(8,128)(2,1)S(1)} %bitcast.9), custom_call_target="tpu_custom_call" | custom-call | flops 2000000000 | bytes 9437184 | tf_op jit(solution)/shard_map/pallas_call | solution.py:375
  69.1 2.1 %shard_map.49 = (f32[320,512]{1,0:T(8,128)S(1)}, f32[320,512]{1,0:T(8,128)S(1)}) custom-call(f32[1136,512]{1,0:T(8,128)S(1)} %get-tuple-element.32.act1, bf16[4608,512]{1,0:T(8,128)(2,1)S(1)} %bitcast.10), custom_call_target="tpu_custom_call" | custom-call | flops 1509949440 | bytes 8355840 | tf_op jit(solution)/shard_map/pallas_call | solution.py:375
  71.2 0.0 collective-permute-done.14.other
  71.2 11.1 %shard_map.57 = f32[8,64,256]{2,1,0:T(8,128)} custom-call(s32[4]{0:T(128)S(1)} %pad_add_fusion.place, f32[1136,512]{1,0:T(8,128)S(1)} %get-tuple-element.32.act1, f32[1120,512]{1,0:T(8,128)S(1)} %get-tuple-element.33.slope1, f32[640,512]{1,0:T(8,128)S(1)} %get-tuple-element.34.act2, f32[640,512]{1,0:T(8,128)S(1)} %get-tuple-element.35.slope2, ...), custom_call_target="tpu_custom_call" | custom-call | flops 5284823040 | bytes 16818192 | tf_op jit(solution)/shard_map/pallas_call | solution.py:375
  (7 shorter events, 0.0 us)
Async XLA Ops:
  0.1 1.0 %copy-start.1 = (f32[8,64,256]{2,1,0:T(8,128)S(1)}, f32[8,64,256]{2,1,0:T(8,128)}, u32[]{:S(2)}) copy-start(f32[8,64,256]{2,1,0:T(8,128)} %pool.5) | copy-start | bytes 1572868
  1.7 6.0 %collective-permute-start = (bf16[8,4,256]{2,1,0:T(4,128)(2,1)S(1)}, bf16[8,4,256]{2,1,0:T(4,128)(2,1)S(1)}, u32[]{:S(2)}, u32[]{:S(2)}) collective-permute-start(bf16[8,4,256]{2,1,0:T(4,128)(2,1)S(1)} %get-tuple-element.28), channel_id=1, source_target_pairs={{1,2},{3,4},{5,6},{2,1},{4,3},{6,5},{9,10},{11,12},{13,14},{10,9},... | collective-permute-start | bytes 49160 | tf_op jit(solution)/shard_map/ppermute | solution.py:410
  6.3 1.4 %collective-permute-start.1 = (bf16[8,4,256]{2,1,0:T(4,128)(2,1)S(1)}, bf16[8,4,256]{2,1,0:T(4,128)(2,1)S(1)}, u32[]{:S(2)}, u32[]{:S(2)}) collective-permute-start(bf16[8,4,256]{2,1,0:T(4,128)(2,1)S(1)} %get-tuple-element.29), channel_id=1, source_target_pairs={{0,1},{1,0},{2,3},{3,2},{4,5},{5,4},{6,7},{7,6},{8,9},{9,8},{10,11... | collective-permute-start | bytes 49160 | tf_op jit(solution)/shard_map/ppermute | solution.py:411
  8.3 6.3 %collective-permute-start.2 = (bf16[4,72,256]{2,1,0:T(8,128)(2,1)S(1)}, bf16[4,72,256]{2,1,0:T(8,128)(2,1)S(1)}, u32[]{:S(2)}, u32[]{:S(2)}) collective-permute-start(bf16[4,72,256]{2,1,0:T(8,128)(2,1)S(1)} %get-tuple-element.30), channel_id=1, source_target_pairs={{0,8},{8,16},{16,24},{1,9},{9,17},{17,25},{2,10},{10,18},{18,26},{... | collective-permute-start | bytes 442376 | tf_op jit(solution)/shard_map/ppermute | solution.py:421
  11.4 8.3 %collective-permute-start.3 = (bf16[4,72,256]{2,1,0:T(8,128)(2,1)S(1)}, bf16[4,72,256]{2,1,0:T(8,128)(2,1)S(1)}, u32[]{:S(2)}, u32[]{:S(2)}) collective-permute-start(bf16[4,72,256]{2,1,0:T(8,128)(2,1)S(1)} %get-tuple-element.31), channel_id=1, source_target_pairs={{8,0},{16,8},{24,16},{9,1},{17,9},{25,17},{10,2},{18,10},{26,18},{... | collective-permute-start | bytes 442376 | tf_op jit(solution)/shard_map/ppermute | solution.py:422
  19.7 2.3 %copy-start = (bf16[3,3,512,512]{3,2,1,0:T(8,128)(2,1)S(1)}, bf16[3,3,512,512]{3,2,1,0:T(8,128)(2,1)}, u32[]{:S(2)}) copy-start(bf16[3,3,512,512]{3,2,1,0:T(8,128)(2,1)} %param.6) | copy-start | bytes 14155780
  22.1 1.0 %copy-start.2 = (f32[8,64,256]{2,1,0:T(8,128)S(1)}, f32[8,64,256]{2,1,0:T(8,128)}, u32[]{:S(2)}) copy-start(f32[8,64,256]{2,1,0:T(8,128)} %pool.5) | copy-start | bytes 1572868
  23.1 1.7 %copy-start.4 = (bf16[3,3,256,512]{3,2,1,0:T(8,128)(2,1)S(1)}, bf16[3,3,256,512]{3,2,1,0:T(8,128)(2,1)}, u32[]{:S(2)}) copy-start(bf16[3,3,256,512]{3,2,1,0:T(8,128)(2,1)} %param.5) | copy-start | bytes 7077892
  24.8 24.7 %copy-start.3 = (f32[2,512,512]{2,1,0:T(8,128)S(1)}, f32[2,512,512]{2,1,0:T(8,128)}, u32[]{:S(2)}) copy-start(f32[2,512,512]{2,1,0:T(8,128)} %targets.1) | copy-start | bytes 6291460
  36.3 2.2 %collective-permute-start.4 = (bf16[1296,128]{1,0:T(8,128)(2,1)S(1)}, bf16[1296,128]{1,0:T(8,128)(2,1)S(1)}, u32[]{:S(2)}, u32[]{:S(2)}) collective-permute-start(bf16[1296,128]{1,0:T(8,128)(2,1)S(1)} %get-tuple-element.40), channel_id=1, source_target_pairs={{0,1},{1,0},{2,3},{3,2},{4,5},{5,4},{6,7},{7,6},{8,9},{9,8},{10,11... | collective-permute-start | bytes 995336 | tf_op jit(solution)/shard_map/ppermute | solution.py:492
  38.5 27.8 %copy-start.5 = (bf16[3,3,256,512]{3,2,1,0:T(8,128)(2,1)S(1)}, bf16[3,3,256,512]{3,2,1,0:T(8,128)(2,1)}, u32[]{:S(2)}) copy-start(bf16[3,3,256,512]{3,2,1,0:T(8,128)(2,1)} %param.5) | copy-start | bytes 7077892
  39.4 3.8 %collective-permute-start.5 = (bf16[336,128]{1,0:T(8,128)(2,1)S(1)}, bf16[336,128]{1,0:T(8,128)(2,1)S(1)}, u32[]{:S(2)}, u32[]{:S(2)}) collective-permute-start(bf16[336,128]{1,0:T(8,128)(2,1)S(1)} %get-tuple-element.43), channel_id=1, source_target_pairs={{0,8},{8,0},{16,24},{24,16},{1,9},{9,1},{17,25},{25,17},{2,10},{10... | collective-permute-start | bytes 258056 | tf_op jit(solution)/shard_map/ppermute | solution.py:500
  40.7 3.3 %collective-permute-start.6 = (bf16[336,128]{1,0:T(8,128)(2,1)S(1)}, bf16[336,128]{1,0:T(8,128)(2,1)S(1)}, u32[]{:S(2)}, u32[]{:S(2)}) collective-permute-start(bf16[336,128]{1,0:T(8,128)(2,1)S(1)} %get-tuple-element.44), channel_id=1, source_target_pairs={{0,16},{8,24},{16,0},{24,8},{1,17},{9,25},{17,1},{25,9},{2,18},{10... | collective-permute-start | bytes 258056 | tf_op jit(solution)/shard_map/ppermute | solution.py:500
  40.7 4.3 %collective-permute-start.7 = (bf16[336,128]{1,0:T(8,128)(2,1)S(1)}, bf16[336,128]{1,0:T(8,128)(2,1)S(1)}, u32[]{:S(2)}, u32[]{:S(2)}) collective-permute-start(bf16[336,128]{1,0:T(8,128)(2,1)S(1)} %get-tuple-element.45), channel_id=1, source_target_pairs={{0,24},{8,16},{16,8},{24,0},{1,25},{9,17},{17,9},{25,1},{2,26},{10... | collective-permute-start | bytes 258056 | tf_op jit(solution)/shard_map/ppermute | solution.py:500
  45.9 5.3 %collective-permute-start.10 = (bf16[336,128]{1,0:T(8,128)(2,1)S(1)}, bf16[336,128]{1,0:T(8,128)(2,1)S(1)}, u32[]{:S(2)}, u32[]{:S(2)}) collective-permute-start(bf16[336,128]{1,0:T(8,128)(2,1)S(1)} %get-tuple-element.48), channel_id=1, source_target_pairs={{0,6},{1,7},{2,4},{3,5},{4,2},{5,3},{6,0},{7,1},{8,14},{9,15},{10,... | collective-permute-start | bytes 258056 | tf_op jit(solution)/shard_map/ppermute | solution.py:510
  48.9 7.4 %collective-permute-start.9 = (bf16[336,128]{1,0:T(8,128)(2,1)S(1)}, bf16[336,128]{1,0:T(8,128)(2,1)S(1)}, u32[]{:S(2)}, u32[]{:S(2)}) collective-permute-start(bf16[336,128]{1,0:T(8,128)(2,1)S(1)} %get-tuple-element.48), channel_id=1, source_target_pairs={{0,4},{1,5},{2,6},{3,7},{4,0},{5,1},{6,2},{7,3},{8,12},{9,13},{10,... | collective-permute-start | bytes 258056 | tf_op jit(solution)/shard_map/ppermute | solution.py:510
  48.9 7.4 %collective-permute-start.8 = (bf16[336,128]{1,0:T(8,128)(2,1)S(1)}, bf16[336,128]{1,0:T(8,128)(2,1)S(1)}, u32[]{:S(2)}, u32[]{:S(2)}) collective-permute-start(bf16[336,128]{1,0:T(8,128)(2,1)S(1)} %get-tuple-element.48), channel_id=1, source_target_pairs={{0,2},{1,3},{2,0},{3,1},{4,6},{5,7},{6,4},{7,5},{8,10},{9,11},{10,... | collective-permute-start | bytes 258056 | tf_op jit(solution)/shard_map/ppermute | solution.py:510
  57.2 4.3 %collective-permute-start.13 = (bf16[320,128]{1,0:T(8,128)(2,1)S(1)}, bf16[320,128]{1,0:T(8,128)(2,1)S(1)}, u32[]{:S(2)}, u32[]{:S(2)}) collective-permute-start(bf16[320,128]{1,0:T(8,128)(2,1)S(1)} %get-tuple-element.49.share), channel_id=1, source_target_pairs={{0,24},{8,16},{16,8},{24,0},{1,25},{9,17},{17,9},{25,1},{2,26},{10... | collective-permute-start | bytes 245768 | tf_op jit(solution)/shard_map/ppermute | solution.py:520
  59.5 3.6 %collective-permute-start.12 = (bf16[320,128]{1,0:T(8,128)(2,1)S(1)}, bf16[320,128]{1,0:T(8,128)(2,1)S(1)}, u32[]{:S(2)}, u32[]{:S(2)}) collective-permute-start(bf16[320,128]{1,0:T(8,128)(2,1)S(1)} %get-tuple-element.49.share), channel_id=1, source_target_pairs={{0,16},{8,24},{16,0},{24,8},{1,17},{9,25},{17,1},{25,9},{2,18},{10... | collective-permute-start | bytes 245768 | tf_op jit(solution)/shard_map/ppermute | solution.py:520
  59.5 3.7 %collective-permute-start.11 = (bf16[320,128]{1,0:T(8,128)(2,1)S(1)}, bf16[320,128]{1,0:T(8,128)(2,1)S(1)}, u32[]{:S(2)}, u32[]{:S(2)}) collective-permute-start(bf16[320,128]{1,0:T(8,128)(2,1)S(1)} %get-tuple-element.49.share), channel_id=1, source_target_pairs={{0,8},{8,0},{16,24},{24,16},{1,9},{9,1},{17,25},{25,17},{2,10},{10... | collective-permute-start | bytes 245768 | tf_op jit(solution)/shard_map/ppermute | solution.py:520
  63.7 7.4 %collective-permute-start.14 = (bf16[1296,128]{1,0:T(8,128)(2,1)S(1)}, bf16[1296,128]{1,0:T(8,128)(2,1)S(1)}, u32[]{:S(2)}, u32[]{:S(2)}) collective-permute-start(bf16[1296,128]{1,0:T(8,128)(2,1)S(1)} %shard_map.54.mine), channel_id=1, source_target_pairs={{0,1},{1,0},{2,3},{3,2},{4,5},{5,4},{6,7},{7,6},{8,9},{9,8},{10,11... | collective-permute-start | bytes 995336 | tf_op jit(solution)/shard_map/ppermute | solution.py:525

commit v5 on v4

--- a/solution.py
+++ b/solution.py
@@ -39,40 +39,98 @@
     return jnp.concatenate([mask] * (width // BLOCK), axis=1)
 
 
-def fill_mask(mask_ref, place_ref, rim, pitch, limits):
-    rows = mask_ref.shape[0] // pitch
-    col = lax.broadcasted_iota(jnp.int32, (pitch, BLOCK), 0) + (place_ref[2] - rim)
-    inside = jnp.where((col >= 0) & (col < limits[1]), 1.0, 0.0).astype(F32)
-    for r in range(rows):
-        row = place_ref[1] - rim + r
-        ok = jnp.where((row >= 0) & (row < limits[0]), 1.0, 0.0).astype(F32)
-        mask_ref[r * pitch : (r + 1) * pitch, :] = inside * ok
-
-
-def shifted(ref, base, step, offset):
-    return ref[pl.ds(base, step + 8), :][offset : offset + step]
-
-
-def spread_taps(flat_ref, base, out_ref, at, step):
-    depth = flat_ref.shape[1]
-    whole = flat_ref[pl.ds(base, step + 8), :]
-    for b in range(3):
-        out_ref[pl.ds(at, step), b * depth : (b + 1) * depth] = whole[b : b + step].astype(BF)
-
-
-def conv(taps_ref, base, weight_ref, pitch, step):
-    lhs = jnp.concatenate(
-        [taps_ref[pl.ds(base + a * pitch, step), :] for a in range(3)], axis=1
-    )
-    return jnp.dot(lhs, weight_ref[...], preferred_element_type=F32)
-
-
-def tiles_of(start, stop, step, body):
-    def one(t, carry):
-        body(pl.multiple_of(start + t * step, 16))
-        return carry
-
-    lax.fori_loop(0, (stop - start) // step, one, 0)
+def columns(groups):
+    n = lax.broadcasted_iota(jnp.int32, (groups * 16, BLOCK), 0)
+    return (n & 15) * groups + (n >> 4)
+
+
+def span(groups, low, high):
+    col = columns(groups)
+    return jnp.where((col >= low) & (col < high), 1.0, 0.0).astype(F32)
+
+
+def pair_mask(inside, place, limits, row):
+    parts = []
+    for r in range(2):
+        at = place[1] + row + r
+        parts.append(inside * jnp.where((at >= 0) & (at < limits[0]), 1.0, 0.0).astype(F32))
+    return jnp.concatenate(parts, axis=0)
+
+
+def roll_group(value):
+    return [pltpu.roll(value[n * 16 : (n + 1) * 16], 15, 0) for n in range(2)]
+
+
+def write_taps(ref, row, value, groups, lanes=slice(None)):
+    at, pitch = row * (groups + 2) * 16, groups * 16
+    ref[at : at + pitch, lanes] = value.astype(BF)
+    for n, block in enumerate(roll_group(value)):
+        ref[at + pitch + n * 16 : at + pitch + (n + 1) * 16, lanes] = block.astype(BF)
+
+
+def fold_row(ref, row, buf_ref, at, groups):
+    base = row * (groups + 2) * 16
+    for n in range(groups + 2):
+        for p in range(buf_ref.shape[0]):
+            ref[base + n * 16 : base + (n + 1) * 16, p * BLOCK : (p + 1) * BLOCK] = buf_ref[
+                p, pl.ds(at + n, 16, stride=groups), :
+            ].astype(BF)
+
+
+def put_row(buf_ref, at, value):
+    for p in range(buf_ref.shape[0]):
+        buf_ref[p, at : at + value.shape[0], :] = value[:, p * BLOCK : (p + 1) * BLOCK]
+
+
+def clear_rows(buf_ref, start, stop):
+    for p in range(buf_ref.shape[0]):
+        buf_ref[p, start:stop, :] = jnp.zeros((stop - start, BLOCK), F32)
+
+
+def conv(find, weight_ref, groups, lanes):
+    pitch, pieces = groups * 16, []
+    for a in range(3):
+        for b in range(3):
+            both = []
+            for r in range(2):
+                ref, row = find(r + a)
+                at = (row * (groups + 2) + b) * 16
+                both.append(ref[at : at + pitch, :])
+            pieces.append(jnp.concatenate(both, axis=0))
+    lhs = jnp.concatenate(pieces, axis=1)
+    return jnp.dot(lhs, weight_ref[:, lanes], preferred_element_type=F32)
+
+
+def halves(width):
+    half = 2 * BLOCK
+    return [slice(n, n + half) for n in range(0, width, half)]
+
+
+def first_rows(find, w1, taps_ref, row, act, slope, at, groups, mask):
+    width, pitch = w1.shape[1], groups * 16
+    for lanes in halves(width):
+        value, tilt = gelu_pair(conv(find, w1, groups, lanes))
+        value = value * wide(mask, 2 * BLOCK)
+        for r in range(2):
+            one = value[r * pitch : (r + 1) * pitch]
+            write_taps(taps_ref, row + r, one, groups, lanes)
+            if act is None:
+                continue
+            two = tilt[r * pitch : (r + 1) * pitch]
+            base = at + r * pitch
+            for ref, part in ((act, one), (slope, two)):
+                ref[base : base + pitch - 32, lanes] = part[32:]
+                for n, block in enumerate(roll_group(part)):
+                    to = base + pitch - 32 + n * 16
+                    ref[to : to + 16, lanes] = block
+
+
+def second_rows(find, w2, act, slope, at, groups):
+    step = groups * 32
+    for lanes in halves(w2.shape[1]):
+        value, tilt = gelu_pair(conv(find, w2, groups, lanes))
+        act[at : at + step, lanes] = value
+        slope[at : at + step, lanes] = tilt
 
 
 def put_mean(rows_ref, mean, parts):
@@ -117,56 +175,85 @@
     return centre
 
 
-def front(dims, place, pool, far, near, above, below, w1, w2, *rest):
-    (act1, slope1, act2, slope2, keep, mine, sent) = rest[:7]
-    (flat, taps1, taps2, own, gram, stat, mask) = rest[7:]
-    height, breadth, pitch, limits = dims
-    step = 2 * pitch
+def middle(dims, place, pool, far, near, w1, w2, taps1, taps2, act1, slope1, act2, slope2, buf):
+    height, breadth, groups, limits = dims
+    pitch = groups * 16
+    left_core = place[0] == 0
+    space = buf.shape[1] // height
+    for r in range(height):
+        at = r * space
+        one, two = far[r].astype(F32), near[r].astype(F32)
+        put_row(buf, at, jnp.where(left_core, one, two))
+        put_row(buf, at + REACH, pool[r])
+        put_row(buf, at + REACH + breadth, jnp.where(left_core, two, one))
+        clear_rows(buf, at + 2 * REACH + breadth, at + space)
+        fold_row(taps1, r, buf, at, groups)
+    low = 3 - place[2]
+    inside = span(groups, low, low + limits[1])
+    for t in range(0, height - 2, 2):
+        mask = pair_mask(inside, place, limits, t + 1)
+        first_rows(
+            lambda r: (taps1, t + r), w1, taps2, t, act1, slope1, t * pitch, groups, mask
+        )
+    for t in range(0, height - 4, 2):
+        second_rows(lambda r: (taps2, t + r), w2, act2, slope2, t * pitch, groups)
+
+
+def rim_taps(ref, rows, buf, groups):
+    space = buf.shape[1] // len(rows)
+    for n, (source, r) in enumerate(rows):
+        breadth = source.shape[1]
+        at = n * space
+        put_row(buf, at, source[r].astype(F32))
+        clear_rows(buf, at + breadth, at + space)
+        fold_row(ref, n, buf, at, groups)
+
+
+def front(dims, place, above, below, taps1, taps2, act1, act2, w1, w2, *rest):
+    (taps2b, act1b, slope1b, act2b, slope2b, keep, mine, sent) = rest[:8]
+    (rim, buf, gram, stat) = rest[8:]
+    height, breadth, groups, limits = dims
+    pitch = groups * 16
     width = w1.shape[1]
     blocks = width // BLOCK
-    flat[...] = jnp.zeros(flat.shape, F32)
-    left_core = place[0] == 0
-    for r in range(height):
-        at = (r + REACH) * pitch
-        one, two = far[r].astype(F32), near[r].astype(F32)
-        flat[at : at + REACH, :] = jnp.where(left_core, one, two)
-        flat[at + REACH : at + REACH + breadth, :] = pool[r]
-        flat[at + REACH + breadth : at + 2 * REACH + breadth, :] = jnp.where(left_core, two, one)
-    for r in range(REACH):
-        at = r * pitch
-        flat[at : at + breadth + 2 * REACH, :] = above[r].astype(F32)
-        at = (r + REACH + height) * pitch
-        flat[at : at + breadth + 2 * REACH, :] = below[r].astype(F32)
-    fill_mask(mask, place, 3, pitch, limits)
-    tiles_of(
-        0, (height + 8) * pitch, step, lambda at: spread_taps(flat, at, taps1, at, step)
-    )
-
-    def first(at):
-        act, slope = gelu_pair(conv(taps1, at, w1, pitch, step))
-        act1[pl.ds(at, step), :] = act * wide(mask[pl.ds(at, step), :], width)
-        slope1[pl.ds(at, step), :] = slope
-
-    rows1 = (height + 6) * pitch
-    act1[rows1:, :] = jnp.zeros((act1.shape[0] - rows1, width), F32)
-    tiles_of(0, rows1, step, first)
-    tiles_of(step, rows1 - step, step, lambda at: spread_taps(act1, at, taps2, at, step))
-
-    def second(at):
-        act, slope = gelu_pair(conv(taps2, at, w2, pitch, step))
-        act2[pl.ds(at - step, step), :] = act
-        slope2[pl.ds(at - step, step), :] = slope
-
-    tiles_of(step, step + height * pitch, step, second)
+    rim_taps(rim, [(above, 2), (above, 3), (below, 0), (below, 1)], buf, groups)
+    low = 3 - place[2]
+    inside = span(groups, low, low + limits[1])
+    last = height - 2
+    finds = (
+        lambda r: (rim, r) if r < 2 else (taps1, r - 2),
+        lambda r: (taps1, last + r) if r < 2 else (rim, r),
+    )
+    for n, row in enumerate((-1, height - 1)):
+        mask = pair_mask(inside, place, limits, row)
+        first_rows(
+            finds[n], w1, taps2b, 2 * n, act1b, slope1b, 2 * n * pitch, groups, mask
+        )
+    last = height - 4
+    finds = (
+        lambda r: (taps2b, r) if r < 2 else (taps2, r - 2),
+        lambda r: (taps2, last + r) if r < 2 else (taps2b, r),
+    )
+    for n in range(2):
+        second_rows(finds[n], w2, act2b, slope2b, 2 * n * pitch, groups)
     cells = height * breadth
-    for layer, (act, offset) in enumerate(((act1, 3 * pitch + 3), (act2, 2))):
-        total = jnp.zeros((8, width), F32)
-        for r in range(height):
-            cut = act[offset + r * pitch : offset + r * pitch + breadth, :]
-            own[r * breadth : (r + 1) * breadth, :] = cut
-            total = total + jnp.sum(cut.reshape(breadth // 8, 8, width), axis=0)
-        mean = jnp.sum(total, axis=0, keepdims=True) * (1.0 / cells)
-        centred = (own[...] - mean).astype(BF)
+    first_parts = [(act1b, pitch, 2 * pitch), (act1, 0, (height - 2) * pitch)]
+    second_parts = [(act2b, 0, 4 * pitch), (act2, 0, (height - 4) * pitch)]
+    for layer, (parts, offset) in enumerate(((first_parts, 1), (second_parts, 2))):
+        own = wide(span(groups, offset, offset + breadth), width)
+        total = jnp.zeros((pitch, width), F32)
+        for ref, start, count in parts:
+            for at in range(start, start + count, pitch):
+                total = total + ref[at : at + pitch, :]
+        mean = jnp.sum(total * own, axis=0, keepdims=True) * (1.0 / cells)
+        centred = jnp.concatenate(
+            [
+                ((ref[at : at + pitch, :] - mean) * own).astype(BF)
+                for ref, start, count in parts
+                for at in range(start, start + count, pitch)
+            ],
+            axis=0,
+        )
         n = 0
         for i in range(blocks):
             panel = lax.dot_general(
@@ -190,15 +277,19 @@
     sent[rows:, :] = stat[1 - place[0], 0:EXTRA, :].astype(BF)
 
 
-def ring(dims, act1, w2, act2, slope2, taps2):
-    height, _, pitch, _ = dims
-    step = 2 * pitch
-    for n, start in enumerate((0, (height + 2) * pitch)):
-        for q in range(2):
-            spread_taps(act1, start + q * step, taps2, q * step, step)
-        act, slope = gelu_pair(conv(taps2, 0, w2, pitch, step))
-        act2[n * step : (n + 1) * step, :] = act
-        slope2[n * step : (n + 1) * step, :] = slope
+def ring(dims, place, above, below, taps2b, w1, w2, act2, slope2, rim, outer, buf):
+    height, _, groups, limits = dims
+    low = 3 - place[2]
+    inside = span(groups, low, low + limits[1])
+    finds = (
+        lambda r: (outer, r) if r < 2 else (taps2b, r - 2),
+        lambda r: (taps2b, 2 + r) if r < 2 else (outer, r),
+    )
+    for n, (source, row) in enumerate(((above, -3), (below, height + 1))):
+        rim_taps(rim, [(source, r) for r in range(REACH)], buf, groups)
+        mask = pair_mask(inside, place, limits, row)
+        first_rows(lambda r: (rim, r), w1, outer, 2 * n, None, None, 0, groups, mask)
+        second_rows(finds[n], w2, act2, slope2, 2 * n * groups * 16, groups)
 
 
 def write_message(ref, part, rows_ref, centre):
@@ -267,9 +358,11 @@
     out[rows:, :] = centre[...]
 
 
-def back(dims, place, act1, slope1, act2, slope2, act2r, slope2r, mine, other, w2, w1, out, *scratch):
-    (flat2, taps2, flat1, taps1, first_m, second_m, table, mask) = scratch
-    height, breadth, pitch, limits = dims
+def back(dims, place, *rest):
+    (act1, slope1, act1b, slope1b, act2, slope2, act2b, slope2b, act2r, slope2r) = rest[:10]
+    (mine, other, w2, w1, out, taps2, taps1, first_m, second_m, table, buf) = rest[10:]
+    height, breadth, groups, limits = dims
+    pitch = groups * 16
     step = 2 * pitch
     width = act1.shape[1]
     blocks = width // BLOCK
@@ -282,48 +375,48 @@
             block = table[layer, n * BLOCK : (n + 1) * BLOCK, :]
             ref[i * BLOCK : (i + 1) * BLOCK, j * BLOCK : (j + 1) * BLOCK] = block
             if i != j:
-                ref[j * BLOCK : (j + 1) * BLOCK, i * BLOCK : (i + 1) * BLOCK] = (
-                    block.astype(F32).T.astype(BF)
-                )
+                ref[j * BLOCK : (j + 1) * BLOCK, i * BLOCK : (i + 1) * BLOCK] = block.T
         means.append(get_mean(table[layer, packed:, :], blocks, 2))
-    fill_mask(mask, place, 3, pitch, limits)
-
-    def second(act, slope, at, to):
-        centred = (act[pl.ds(at, step), :] - means[1]).astype(BF)
-        push = jnp.dot(centred, second_m[...], preferred_element_type=F32)
-        allow = wide(shifted(mask, to + pitch, step, 1), width)
-        flat2[pl.ds(to, step), :] = push * slope[pl.ds(at, step), :] * allow
-
-    rows2 = (height + 4) * pitch
-    flat2[rows2:, :] = jnp.zeros((flat2.shape[0] - rows2, width), F32)
-    second(act2r, slope2r, 0, 0)
-    second(act2r, slope2r, step, rows2 - step)
-    tiles_of(
-        0, height * pitch, step, lambda at: second(act2, slope2, at, pl.multiple_of(at + step, 16))
-    )
-    tiles_of(0, rows2, step, lambda at: spread_taps(flat2, at, taps2, at, step))
-    rows1 = (height + 2) * pitch
-    flat1[rows1:, :] = jnp.zeros((flat1.shape[0] - rows1, width), F32)
-
-    def first(at):
-        near = pl.multiple_of(at + 2 * pitch, 16)
-        centred = (shifted(act1, near, step, 2) - means[0]).astype(BF)
-        flow = conv(taps2, at, w2, pitch, step) + jnp.dot(
-            centred, first_m[...], preferred_element_type=F32
-        )
-        allow = wide(shifted(mask, near, step, 2), width)
-        flat1[pl.ds(at, step), :] = flow * shifted(slope1, near, step, 2) * allow
-
-    tiles_of(0, rows1, step, first)
-    tiles_of(0, rows1, step, lambda at: spread_taps(flat1, at, taps1, at, step))
-
-    def last(t, carry):
-        got = conv(taps1, pl.multiple_of(t * step, 16), w1, pitch, step)
-        out[2 * t] = got[0:breadth]
-        out[2 * t + 1] = got[pitch : pitch + breadth]
-        return carry
-
-    lax.fori_loop(0, height // 2, last, 0)
+    low = 2 - place[2]
+    inside = span(groups, low, low + limits[1])
+    tiles = [(act2r, slope2r, 0), (act2b, slope2b, 0)]
+    tiles += [(act2, slope2, t * pitch) for t in range(0, height - 4, 2)]
+    tiles += [(act2b, slope2b, step), (act2r, slope2r, step)]
+    for t, (act, slope, at) in enumerate(tiles):
+        centred = (act[at : at + step, :] - means[1]).astype(BF)
+        mask = wide(pair_mask(inside, place, limits, 2 * t - 2), 2 * BLOCK)
+        for lanes in halves(width):
+            push = jnp.dot(centred, second_m[:, lanes], preferred_element_type=F32)
+            grad = push * slope[at : at + step, lanes] * mask
+            for r in range(2):
+                write_taps(taps2, 2 * t + r, grad[r * pitch : (r + 1) * pitch], groups, lanes)
+    low = 1 - place[2]
+    inside = span(groups, low, low + limits[1])
+    tiles = [(act1b, slope1b, 0)]
+    tiles += [(act1, slope1, t * pitch) for t in range(0, height - 2, 2)]
+    tiles += [(act1b, slope1b, step)]
+    for t, (act, slope, at) in enumerate(tiles):
+        centred = (act[at : at + step, :] - means[0]).astype(BF)
+        mask = wide(pair_mask(inside, place, limits, 2 * t - 1), 2 * BLOCK)
+        for lanes in halves(width):
+            flow = conv(lambda r: (taps2, 2 * t + r), w2, groups, lanes) + jnp.dot(
+                centred, first_m[:, lanes], preferred_element_type=F32
+            )
+            grad = flow * slope[at : at + step, lanes] * mask
+            for r in range(2):
+                write_taps(taps1, 2 * t + r, grad[r * pitch : (r + 1) * pitch], groups, lanes)
+    for t in range(0, height, 2):
+        got = conv(lambda r: (taps1, t + r), w1, groups, slice(None))
+        for r in range(2):
+            at = (t + r) * pitch
+            for n in range(groups):
+                part = got[r * pitch + n * 16 : r * pitch + (n + 1) * 16]
+                for p in range(buf.shape[0]):
+                    lanes = slice(p * BLOCK, (p + 1) * BLOCK)
+                    buf[p, pl.ds(at + n, 16, stride=groups), :] = part[:, lanes]
+            for p in range(buf.shape[0]):
+                lanes = slice(p * BLOCK, (p + 1) * BLOCK)
+                out[t + r, :, lanes] = buf[p, at : at + breadth, :]
 
 
 def edges(place, pool, far, near):
@@ -396,11 +489,11 @@
     core = tile % 2
     cells = height * breadth
     positions = cells * groups * tiles
-    pitch = -(-(breadth + 2 * REACH) // 16) * 16
-    step = 2 * pitch
+    fold = -(-(breadth + 2 * REACH) // 16)
+    pitch, wider = fold * 16, (fold + 2) * 16
     blocks = width // BLOCK
     place = jnp.stack([core, row * height, tile * breadth, row]).astype(jnp.int32)
-    dims = (height, breadth, pitch, (height * groups, breadth * tiles))
+    dims = (height, breadth, fold, (height * groups, breadth * tiles))
     swap = [(i, i ^ 1) for i in range(tiles)]
     cross = [(i, i + 1) for i in range(1, tiles - 1, 2)]
     cross = cross + [(j, i) for i, j in cross]
@@ -421,40 +514,57 @@
     above = lax.ppermute(above, "grp", up)
     below = lax.ppermute(below, "grp", down)
 
-    rows0, rows1, rows2 = ((height + n) * pitch for n in (8, 6, 0))
     packed = len(pairs(width)) * BLOCK
     w1 = weight_first.reshape(-1, width)
     w2 = weight_second.reshape(-1, width)
-    act1, slope1, act2, slope2, keep, mine, sent = call(
+    space = (fold * 15 + fold + 2 + 7) // 8 * 8
+
+    def maps(rows):
+        return [shape((rows * pitch, width), F32)] * 2
+
+    def cost(rows_first, rows_second):
+        return 2 * 9 * width * pitch * (rows_first * depth + rows_second * width)
+
+    taps1, taps2, act1, slope1, act2, slope2 = call(
+        functools.partial(middle, dims),
+        [place, pool_input, far, near, w1, w2],
+        [shape((height * wider, depth), BF), shape(((height - 2) * wider, width), BF)]
+        + maps(height - 2)
+        + maps(height - 4),
+        [pltpu.VMEM((depth // BLOCK, height * space, BLOCK), F32)],
+        flops=cost(height - 2, height - 4),
+        limit=24,
+    )
+    taps2b, act1b, slope1b, act2b, slope2b, keep, mine, sent = call(
         functools.partial(front, dims),
-        [place, pool_input, far, near, above, below, w1, w2],
-        [
-            shape((rows1 + 16, width), F32),
-            shape((rows1, width), F32),
-            shape((rows2, width), F32),
-            shape((rows2, width), F32),
+        [place, above, below, taps1, taps2, act1, act2, w1, w2],
+        [shape((4 * wider, width), BF)]
+        + maps(4)
+        + maps(4)
+        + [
             shape((packed, BLOCK), F32),
             shape((8, BLOCK), F32),
             shape((packed + EXTRA, BLOCK), BF),
         ],
         [
-            pltpu.VMEM((rows0 + 16, depth), F32),
-            pltpu.VMEM((rows0, 3 * depth), BF),
-            pltpu.VMEM((rows1, 3 * width), BF),
-            pltpu.VMEM((cells, width), F32),
+            pltpu.VMEM((4 * wider, depth), BF),
+            pltpu.VMEM((depth // BLOCK, 4 * space, BLOCK), F32),
             pltpu.VMEM((2, packed, BLOCK), F32),
             pltpu.VMEM((2, 2 * EXTRA, BLOCK), F32),
-            pltpu.VMEM((rows1, BLOCK), F32),
         ],
-        flops=2 * 9 * width * (rows1 * depth + rows2 * width),
-        limit=30,
+        flops=cost(4, 4),
+        limit=24,
     )
     act2r, slope2r = call(
         functools.partial(ring, dims),
-        [act1, w2],
-        [shape((2 * step, width), F32)] * 2,
-        [pltpu.VMEM((2 * step, 3 * width), BF)],
-        flops=2 * 9 * width * width * 2 * step,
+        [place, above, below, taps2b, w1, w2],
+        maps(4),
+        [
+            pltpu.VMEM((4 * wider, depth), BF),
+            pltpu.VMEM((4 * wider, width), BF),
+            pltpu.VMEM((depth // BLOCK, 4 * space, BLOCK), F32),
+        ],
+        flops=cost(4, 4),
         limit=16,
     )
     chunk = packed // groups
@@ -465,18 +575,21 @@
         [pltpu.VMEM((packed, BLOCK), F32)],
         flops=2 * 10**8,
     )
-    backs = []
-    for weight in (weight_second, weight_first):
-        taps, inner = 9, weight.shape[2]
-        (turned,) = call(
+
+    def turned(weight):
+        inner = weight.shape[2]
+        (out,) = call(
             flip,
-            [weight.reshape(taps, inner, width)],
-            [shape((taps * width, inner), BF)],
+            [weight.reshape(9, inner, width)],
+            [shape((9 * width, inner), BF)],
             [],
             flops=2 * 10**9,
             limit=16,
         )
-        backs.append(turned)
+        return out
+
+    back2 = turned(weight_second)
+    back1 = turned(weight_first)
 
     def helpers(members):
         deep = -(-3 * members // 16) * 16
@@ -523,23 +636,20 @@
     table = shape((packed + EXTRA, BLOCK), BF)
     (mine,) = call(assemble, [place, share, mean] + gots, [table], [])
     other = lax.ppermute(mine, "tile", swap)
-    rows_b, rows_d = (height + 4) * pitch, (height + 2) * pitch
+    maps_in = [act1, slope1, act1b, slope1b, act2, slope2, act2b, slope2b, act2r, slope2r]
     (out,) = call(
         functools.partial(back, dims),
-        [place, act1, slope1, act2, slope2, act2r, slope2r, mine, other]
-        + backs,
+        [place] + maps_in + [mine, other, back2, back1],
         [shape(pool_input.shape, F32)],
         [
-            pltpu.VMEM((rows_b + 16, width), F32),
-            pltpu.VMEM((rows_b, 3 * width), BF),
-            pltpu.VMEM((rows_d + 16, width), F32),
-            pltpu.VMEM((rows_d, 3 * width), BF),
+            pltpu.VMEM(((height + 4) * wider, width), BF),
+            pltpu.VMEM(((height + 2) * wider, width), BF),
             pltpu.VMEM((width, width), BF),
             pltpu.VMEM((width, width), BF),
             pltpu.VMEM((2, packed + EXTRA, BLOCK), BF),
-            pltpu.VMEM((rows1, BLOCK), F32),
+            pltpu.VMEM((depth // BLOCK, height * pitch, BLOCK), F32),
         ],
-        flops=2 * 9 * width * (rows_d * width + rows2 * depth),
+        flops=2 * 9 * width * pitch * ((height + 2) * width + height * depth),
         limit=32,
     )
     return out

time: 82.6 us -> 73.3 us (0.89)
  waiting for transfers between devices: 21.5 us -> 14.6 us
  Pallas kernels: 32.7 us -> 28.6 us
  starting transfers between devices: 21.8 us -> 23.3 us
    ppermute x1, waiting for transfers between devices: 5.1 us -> 0.01 us  [local(): below = lax.ppermute(below, 'grp', down)]
    pallas_call x12 -> x13, Pallas kernels: 32.7 us -> 28.6 us  [call(): pl.pallas_call(body, out_shape=tuple(outs), in_specs=[SMEM if x.dtype ==...]
    ppermute x1, waiting for transfers between devices: 1.88 us -> 0.01 us  [local(): above = lax.ppermute(above, 'grp', up)]
    ppermute x3, starting transfers between devices: 2.71 us -> 4.45 us  [local(): lax.ppermute(sents[k - 1], 'grp', [(i, i ^ k) for i in range(groups)])]
    ppermute x3, waiting for transfers between devices: 2.99 us -> 2.17 us  [local(): lax.ppermute(share, 'grp', [(i, i ^ k) for i in range(groups)])]
    unnamed x12 -> x14, local copies, waits for them, and re-layouts: 6.09 us -> 6.09 us
  transfers between devices with their start and end apart: 15 -> 15, of which waited for: 12 -> 10; matrix products, arithmetic and copies ran while one was open for 0% -> 0% of each run, Pallas kernels for 7% -> 16%
where the time goes in v5:
time: 73.3 us; the launch traced here: 72.9 us
  Pallas kernels  28.6 us (39%)
  starting transfers between devices  23.3 us (32%)
  waiting for transfers between devices  14.6 us (20%)
  local copies, waits for them, and re-layouts  6.09 us (8%)
    pallas_call x13, Pallas kernels, call(): pl.pallas_call(body, out_shape=tuple(outs), in_specs=[SMEM if x.dtype ==...  28.6 us
    unnamed x14, local copies, waits for them, and re-layouts  6.09 us
    ppermute x3, waiting for transfers between devices, local(): lax.ppermute(sent, 'tile', [(i, i ^ 2 * k) for i in range(tiles)])  6.07 us
    ppermute x1, starting transfers between devices, local(): far = lax.ppermute(far, 'tile', cross)  4.58 us
    ppermute x3, starting transfers between devices, local(): lax.ppermute(sents[k - 1], 'grp', [(i, i ^ k) for i in range(groups)])  4.45 us
    ppermute x3, starting transfers between devices, local(): lax.ppermute(sent, 'tile', [(i, i ^ 2 * k) for i in range(tiles)])  4.3 us
    ppermute x3, waiting for transfers between devices, local(): lax.ppermute(sents[k - 1], 'grp', [(i, i ^ k) for i in range(groups)])  3.71 us
    ppermute x1, starting transfers between devices, local(): above = lax.ppermute(above, 'grp', up)  3.12 us
  transfers between devices with their start and end apart: 15, of which 10 were waited for; matrix products, arithmetic and copies ran while one was open for 0% of the time, Pallas kernels for 16%

profile of v5, /device:TPU:1, one launch (start us, length us, event | category | flops | bytes accessed | tf_op | source)
XLA Modules:
  0.0 72.9 jit_solution(6266294029772064344)
XLA Ops:
  0.0 0.1 pad_add_fusion.place
  0.1 1.0 %copy-done.4 = f32[8,64,256]{2,1,0:T(8,128)S(1)} copy-done((f32[8,64,256]{2,1,0:T(8,128)S(1)}, f32[8,64,256]{2,1,0:T(8,128)}, u32[]{:S(2)}) %copy-start.4) | copy-done | bytes 524312
  1.1 0.6 shard_map.46
  1.7 4.6 %collective-permute-start = (bf16[8,4,256]{2,1,0:T(4,128)(2,1)S(1)}, bf16[8,4,256]{2,1,0:T(4,128)(2,1)S(1)}, u32[]{:S(2)}, u32[]{:S(2)}) collective-permute-start(bf16[8,4,256]{2,1,0:T(4,128)(2,1)S(1)} %get-tuple-element.35), channel_id=1, source_target_pairs={{1,2},{3,4},{5,6},{2,1},{4,3},{6,5},{9,10},{11,12},{13,14},{10,9},... | collective-permute-start | bytes 49160 | tf_op jit(solution)/shard_map/ppermute | solution.py:503
  6.3 0.1 collective-permute-start.1
  6.4 1.3 %collective-permute-done.far = bf16[8,4,256]{2,1,0:T(4,128)(2,1)S(1)} collective-permute-done((bf16[8,4,256]{2,1,0:T(4,128)(2,1)S(1)}, bf16[8,4,256]{2,1,0:T(4,128)(2,1)S(1)}, u32[]{:S(2)}, u32[]{:S(2)}) %collective-permute-start) | collective-permute-done | bytes 16416 | tf_op jit(solution)/shard_map/ppermute | solution.py:503
  7.7 0.0 collective-permute-done.1.near
  7.7 0.6 shard_map.48
  8.3 3.1 %collective-permute-start.2 = (bf16[4,72,256]{2,1,0:T(8,128)(2,1)S(1)}, bf16[4,72,256]{2,1,0:T(8,128)(2,1)S(1)}, u32[]{:S(2)}, u32[]{:S(2)}) collective-permute-start(bf16[4,72,256]{2,1,0:T(8,128)(2,1)S(1)} %get-tuple-element.39), channel_id=1, source_target_pairs={{0,8},{8,16},{16,24},{1,9},{9,17},{17,25},{2,10},{10,18},{18,26},{... | collective-permute-start | bytes 442376 | tf_op jit(solution)/shard_map/ppermute | solution.py:514
  11.4 1.3 %collective-permute-start.3 = (bf16[4,72,256]{2,1,0:T(8,128)(2,1)S(1)}, bf16[4,72,256]{2,1,0:T(8,128)(2,1)S(1)}, u32[]{:S(2)}, u32[]{:S(2)}) collective-permute-start(bf16[4,72,256]{2,1,0:T(8,128)(2,1)S(1)} %get-tuple-element.40), channel_id=1, source_target_pairs={{8,0},{16,8},{24,16},{9,1},{17,9},{25,17},{10,2},{18,10},{26,18},{... | collective-permute-start | bytes 442376 | tf_op jit(solution)/shard_map/ppermute | solution.py:515
  12.7 0.0 copy-start
  12.7 2.3 %copy-done = bf16[3,3,512,512]{3,2,1,0:T(8,128)(2,1)S(1)} copy-done((bf16[3,3,512,512]{3,2,1,0:T(8,128)(2,1)S(1)}, bf16[3,3,512,512]{3,2,1,0:T(8,128)(2,1)}, u32[]{:S(2)}) %copy-start) | copy-done | bytes 4718616
  15.1 1.7 %copy-done.2 = bf16[3,3,256,512]{3,2,1,0:T(8,128)(2,1)S(1)} copy-done((bf16[3,3,256,512]{3,2,1,0:T(8,128)(2,1)S(1)}, bf16[3,3,256,512]{3,2,1,0:T(8,128)(2,1)}, u32[]{:S(2)}) %copy-start.2) | copy-done | bytes 2359320
  16.7 1.0 %copy-done.5 = f32[8,64,256]{2,1,0:T(8,128)S(1)} copy-done((f32[8,64,256]{2,1,0:T(8,128)S(1)}, f32[8,64,256]{2,1,0:T(8,128)}, u32[]{:S(2)}) %copy-start.5) | copy-done | bytes 524312
  17.8 4.2 %shard_map.47 = (bf16[896,256]{1,0:T(8,128)(2,1)S(1)}, bf16[672,512]{1,0:T(8,128)(2,1)S(1)}, f32[480,512]{1,0:T(8,128)S(1)}, f32[480,512]{1,0:T(8,128)S(1)}, f32...) custom-call(s32[4]{0:T(128)S(1)} %pad_add_fusion.place, f32[8,64,256]{2,1,0:T(8,128)S(1)} %copy-done.5, ...), custom_call_target="tpu_custom_call" | custom-call | flops 2642411520 | bytes 12058640 | tf_op jit(solution)/shard_map/pallas_call | solution.py:468
  22.0 0.0 collective-permute-done.2.above
  22.0 0.0 collective-permute-done.3.below
  22.0 0.0 copy-start.6
  22.1 4.7 %shard_map.49 = (bf16[448,512]{1,0:T(8,128)(2,1)S(1)}, f32[320,512]{1,0:T(8,128)S(1)}, f32[320,512]{1,0:T(8,128)S(1)}, f32[320,512]{1,0:T(8,128)S(1)}, f32[320,5...) custom-call(s32[4]{0:T(128)S(1)} %pad_add_fusion.place, ...), custom_call_target="tpu_custom_call" | custom-call | flops 2264924160 | bytes 14229520 | tf_op jit(solution)/shard_map/pallas_call | solution.py:468
  26.7 0.4 collective-permute-start.4
  27.1 1.3 %collective-permute-done.4.got = bf16[1296,128]{1,0:T(8,128)(2,1)S(1)} collective-permute-done((bf16[1296,128]{1,0:T(8,128)(2,1)S(1)}, bf16[1296,128]{1,0:T(8,128)(2,1)S(1)}, u32[]{:S(2)}, u32[]{:S(2)}) %collective-permute-start.4) | collective-permute-done | bytes 331808 | tf_op jit(solution)/shard_map/ppermute | solution.py:605
  28.4 0.9 %shard_map.51 = (f32[320,128]{1,0:T(8,128)S(1)}, f32[8,128]{1,0:T(8,128)S(1)}, bf16[336,128]{1,0:T(8,128)(2,1)S(1)}, bf16[336,128]{1,0:T(8,128)(2,1)S(1)}, bf16[336,128]{1,0:T(8,128)(2,1)S(1)}) custom-call(s32[4]{0:T(128)S(1)} %pad_add_fusion.place, f32[1280,128]{1,0:T(8,128)S(1)} %get-tuple-element.52.keep, f32[8,128]{1,0:T(8,128)S(1)} %get-tuple-element.53.mine, ...), custom_call_target="tpu_custom_call" | custom-call | bytes 1417232 | tf_op jit(solution)/shard_map/pallas_call | solution.py:468
  29.3 2.3 %collective-permute-start.5 = (bf16[336,128]{1,0:T(8,128)(2,1)S(1)}, bf16[336,128]{1,0:T(8,128)(2,1)S(1)}, u32[]{:S(2)}, u32[]{:S(2)}) collective-permute-start(bf16[336,128]{1,0:T(8,128)(2,1)S(1)} %get-tuple-element.57), channel_id=1, source_target_pairs={{0,8},{8,0},{16,24},{24,16},{1,9},{9,1},{17,25},{25,17},{2,10},{10... | collective-permute-start | bytes 258056 | tf_op jit(solution)/shard_map/ppermute | solution.py:613
  31.6 1.2 %collective-permute-start.6 = (bf16[336,128]{1,0:T(8,128)(2,1)S(1)}, bf16[336,128]{1,0:T(8,128)(2,1)S(1)}, u32[]{:S(2)}, u32[]{:S(2)}) collective-permute-start(bf16[336,128]{1,0:T(8,128)(2,1)S(1)} %get-tuple-element.58), channel_id=1, source_target_pairs={{0,16},{8,24},{16,0},{24,8},{1,17},{9,25},{17,1},{25,9},{2,18},{10... | collective-permute-start | bytes 258056 | tf_op jit(solution)/shard_map/ppermute | solution.py:613
  32.9 0.9 %collective-permute-start.7 = (bf16[336,128]{1,0:T(8,128)(2,1)S(1)}, bf16[336,128]{1,0:T(8,128)(2,1)S(1)}, u32[]{:S(2)}, u32[]{:S(2)}) collective-permute-start(bf16[336,128]{1,0:T(8,128)(2,1)S(1)} %get-tuple-element.59), channel_id=1, source_target_pairs={{0,24},{8,16},{16,8},{24,0},{1,25},{9,17},{17,9},{25,1},{2,26},{10... | collective-permute-start | bytes 258056 | tf_op jit(solution)/shard_map/ppermute | solution.py:613
  33.7 0.4 collective-permute-done.5.rest_0_
  34.2 0.8 %collective-permute-done.6.rest_1_ = bf16[336,128]{1,0:T(8,128)(2,1)S(1)} collective-permute-done((bf16[336,128]{1,0:T(8,128)(2,1)S(1)}, bf16[336,128]{1,0:T(8,128)(2,1)S(1)}, u32[]{:S(2)}, u32[]{:S(2)}) %collective-permute-start.6) | collective-permute-done | bytes 86048 | tf_op jit(solution)/shard_map/ppermute | solution.py:613
  35.0 2.5 %collective-permute-done.7.rest_2_ = bf16[336,128]{1,0:T(8,128)(2,1)S(1)} collective-permute-done((bf16[336,128]{1,0:T(8,128)(2,1)S(1)}, bf16[336,128]{1,0:T(8,128)(2,1)S(1)}, u32[]{:S(2)}, u32[]{:S(2)}) %collective-permute-start.7) | collective-permute-done | bytes 86048 | tf_op jit(solution)/shard_map/ppermute | solution.py:613
  37.5 0.9 %shard_map.52 = (f32[320,128]{1,0:T(8,128)S(1)}, f32[8,128]{1,0:T(8,128)S(1)}, bf16[336,128]{1,0:T(8,128)(2,1)S(1)}) custom-call(s32[4]{0:T(128)S(1)} %pad_add_fusion.place, f32[320,128]{1,0:T(8,128)S(1)} %get-tuple-element.55.share, f32[8,128]{1,0:T(8,128)S(1)} %get-tuple-element.56.mine, bf16[336,128]{1,0:T(8,128)(2,1)S(1)} %collective-permute-done.5.rest_0_, ...), custom_call_target="tpu_custom_call" | custom-call | bytes 679952 | tf_op jit(solution)/shard_map/pallas_call | solution.py:468
  38.4 3.9 %collective-permute-start.10 = (bf16[336,128]{1,0:T(8,128)(2,1)S(1)}, bf16[336,128]{1,0:T(8,128)(2,1)S(1)}, u32[]{:S(2)}, u32[]{:S(2)}) collective-permute-start(bf16[336,128]{1,0:T(8,128)(2,1)S(1)} %get-tuple-element.62), channel_id=1, source_target_pairs={{0,6},{1,7},{2,4},{3,5},{4,2},{5,3},{6,0},{7,1},{8,14},{9,15},{10,... | collective-permute-start | bytes 258056 | tf_op jit(solution)/shard_map/ppermute | solution.py:623
  42.3 0.4 collective-permute-start.8
  42.7 0.8 %shard_map.53.rest_3_ = f32[320,128]{1,0:T(8,128)S(1)} custom-call(s32[4]{0:T(128)S(1)} %pad_add_fusion.place, f32[2,512,512]{2,1,0:T(8,128)S(1)} %copy-done.6), custom_call_target="tpu_custom_call" | custom-call | flops 200000000 | bytes 2261008 | tf_op jit(solution)/shard_map/pallas_call | solution.py:468
  43.5 0.8 %collective-permute-done.10.rest_2_ = bf16[336,128]{1,0:T(8,128)(2,1)S(1)} collective-permute-done((bf16[336,128]{1,0:T(8,128)(2,1)S(1)}, bf16[336,128]{1,0:T(8,128)(2,1)S(1)}, u32[]{:S(2)}, u32[]{:S(2)}) %collective-permute-start.10) | collective-permute-done | bytes 86048 | tf_op jit(solution)/shard_map/ppermute | solution.py:623
  44.2 5.3 %collective-permute-done.9.rest_1_ = bf16[336,128]{1,0:T(8,128)(2,1)S(1)} collective-permute-done((bf16[336,128]{1,0:T(8,128)(2,1)S(1)}, bf16[336,128]{1,0:T(8,128)(2,1)S(1)}, u32[]{:S(2)}, u32[]{:S(2)}) %collective-permute-start.9) | collective-permute-done | bytes 86048 | tf_op jit(solution)/shard_map/ppermute | solution.py:623
  49.5 0.9 %shard_map.54 = (bf16[320,128]{1,0:T(8,128)(2,1)S(1)}, bf16[16,128]{1,0:T(8,128)(2,1)S(1)}) custom-call(s32[4]{0:T(128)S(1)} %pad_add_fusion.place, f32[320,128]{1,0:T(8,128)S(1)} %get-tuple-element.60.share, f32[8,128]{1,0:T(8,128)S(1)} %get-tuple-element.61.mine, bf16[336,128]{1,0:T(8,128)(2,1)S(1)} %collective-permute-done.8.rest_0_, ...), custom_call_target="tpu_custom_call" | custom-call | bytes 675856 | tf_op jit(solution)/shard_map/pallas_call | solution.py:468
  50.4 0.8 %collective-permute-start.13 = (bf16[320,128]{1,0:T(8,128)(2,1)S(1)}, bf16[320,128]{1,0:T(8,128)(2,1)S(1)}, u32[]{:S(2)}, u32[]{:S(2)}) collective-permute-start(bf16[320,128]{1,0:T(8,128)(2,1)S(1)} %get-tuple-element.63.share), channel_id=1, source_target_pairs={{0,24},{8,16},{16,8},{24,0},{1,25},{9,17},{17,9},{25,1},{2,26},{10... | collective-permute-start | bytes 245768 | tf_op jit(solution)/shard_map/ppermute | solution.py:633
  51.2 1.3 %collective-permute-start.12 = (bf16[320,128]{1,0:T(8,128)(2,1)S(1)}, bf16[320,128]{1,0:T(8,128)(2,1)S(1)}, u32[]{:S(2)}, u32[]{:S(2)}) collective-permute-start(bf16[320,128]{1,0:T(8,128)(2,1)S(1)} %get-tuple-element.63.share), channel_id=1, source_target_pairs={{0,16},{8,24},{16,0},{24,8},{1,17},{9,25},{17,1},{25,9},{2,18},{10... | collective-permute-start | bytes 245768 | tf_op jit(solution)/shard_map/ppermute | solution.py:633
  52.5 0.6 collective-permute-start.11
  53.2 1.1 %shard_map.57.rest_13_ = bf16[4608,256]{1,0:T(8,128)(2,1)S(1)} custom-call(bf16[9,256,512]{2,1,0:T(8,128)(2,1)S(1)} %bitcast.14), custom_call_target="tpu_custom_call" | custom-call | flops 2000000000 | bytes 4718592 | tf_op jit(solution)/shard_map/pallas_call | solution.py:468
  54.3 0.5 collective-permute-done.13.rest_2_
  54.8 0.6 collective-permute-done.12.rest_1_
  55.4 1.1 %collective-permute-done.11.rest_0_ = bf16[320,128]{1,0:T(8,128)(2,1)S(1)} collective-permute-done((bf16[320,128]{1,0:T(8,128)(2,1)S(1)}, bf16[320,128]{1,0:T(8,128)(2,1)S(1)}, u32[]{:S(2)}, u32[]{:S(2)}) %collective-permute-start.11) | collective-permute-done | bytes 81952 | tf_op jit(solution)/shard_map/ppermute | solution.py:633
  56.4 0.6 shard_map.55.rest_10_
  57.0 2.4 %collective-permute-start.14 = (bf16[1296,128]{1,0:T(8,128)(2,1)S(1)}, bf16[1296,128]{1,0:T(8,128)(2,1)S(1)}, u32[]{:S(2)}, u32[]{:S(2)}) collective-permute-start(bf16[1296,128]{1,0:T(8,128)(2,1)S(1)} %shard_map.55.rest_10_), channel_id=1, source_target_pairs={{0,1},{1,0},{2,3},{3,2},{4,5},{5,4},{6,7},{7,6},{8,9},{9,8},{10,11... | collective-permute-start | bytes 995336 | tf_op jit(solution)/shard_map/ppermute | solution.py:638
  59.4 1.7 %shard_map.56.rest_12_ = bf16[4608,512]{1,0:T(8,128)(2,1)S(1)} custom-call(bf16[9,512,512]{2,1,0:T(8,128)(2,1)S(1)} %bitcast.10), custom_call_target="tpu_custom_call" | custom-call | flops 2000000000 | bytes 9437184 | tf_op jit(solution)/shard_map/pallas_call | solution.py:468
  61.2 3.5 %shard_map.50 = (f32[320,512]{1,0:T(8,128)S(1)}, f32[320,512]{1,0:T(8,128)S(1)}) custom-call(s32[4]{0:T(128)S(1)} %pad_add_fusion.place, bf16[4,72,256]{2,1,0:T(8,128)(2,1)S(1)} %collective-permute-done.2.above, bf16[4,72,256]{2,1,0:T(8,128)(2,1)S(1)} %collective-permute-done.3.below, bf16[448,512]{1,0:T(8,128)(2,1)S(1)} %get-tuple-element.49.taps2b, ...), custom_call_target="tpu_custom_call" | custom-call | flops 2264924160 | bytes 9142288 | tf_op jit(solution)/shard_map/pallas_call | solution.py:468
  64.7 0.0 collective-permute-done.14.rest_11_
  64.7 8.2 %shard_map.58 = f32[8,64,256]{2,1,0:T(8,128)} custom-call(s32[4]{0:T(128)S(1)} %pad_add_fusion.place, f32[480,512]{1,0:T(8,128)S(1)} %get-tuple-element.37.act1.rest_0_, f32[480,512]{1,0:T(8,128)S(1)} %get-tuple-element.38.rest_1_, f32[320,512]{1,0:T(8,128)S(1)} %get-tuple-element.44.rest_2_, f32[320,512]{1,0:T(8,128)S(1)} %get-tuple-element.45.rest_3_, ...), custom_call_target="tpu_custom_call" | custom-call | flops 5284823040 | bytes 15474704 | tf_op jit(solution)/shard_map/pallas_call | solution.py:468
  (10 shorter events, 0.0 us)
Async XLA Ops:
  0.1 1.0 %copy-start.4 = (f32[8,64,256]{2,1,0:T(8,128)S(1)}, f32[8,64,256]{2,1,0:T(8,128)}, u32[]{:S(2)}) copy-start(f32[8,64,256]{2,1,0:T(8,128)} %pool.5) | copy-start | bytes 1572868
  1.7 6.0 %collective-permute-start = (bf16[8,4,256]{2,1,0:T(4,128)(2,1)S(1)}, bf16[8,4,256]{2,1,0:T(4,128)(2,1)S(1)}, u32[]{:S(2)}, u32[]{:S(2)}) collective-permute-start(bf16[8,4,256]{2,1,0:T(4,128)(2,1)S(1)} %get-tuple-element.35), channel_id=1, source_target_pairs={{1,2},{3,4},{5,6},{2,1},{4,3},{6,5},{9,10},{11,12},{13,14},{10,9},... | collective-permute-start | bytes 49160 | tf_op jit(solution)/shard_map/ppermute | solution.py:503
  6.3 1.4 %collective-permute-start.1 = (bf16[8,4,256]{2,1,0:T(4,128)(2,1)S(1)}, bf16[8,4,256]{2,1,0:T(4,128)(2,1)S(1)}, u32[]{:S(2)}, u32[]{:S(2)}) collective-permute-start(bf16[8,4,256]{2,1,0:T(4,128)(2,1)S(1)} %get-tuple-element.36), channel_id=1, source_target_pairs={{0,1},{1,0},{2,3},{3,2},{4,5},{5,4},{6,7},{7,6},{8,9},{9,8},{10,11... | collective-permute-start | bytes 49160 | tf_op jit(solution)/shard_map/ppermute | solution.py:504
  8.3 13.7 %collective-permute-start.2 = (bf16[4,72,256]{2,1,0:T(8,128)(2,1)S(1)}, bf16[4,72,256]{2,1,0:T(8,128)(2,1)S(1)}, u32[]{:S(2)}, u32[]{:S(2)}) collective-permute-start(bf16[4,72,256]{2,1,0:T(8,128)(2,1)S(1)} %get-tuple-element.39), channel_id=1, source_target_pairs={{0,8},{8,16},{16,24},{1,9},{9,17},{17,25},{2,10},{10,18},{18,26},{... | collective-permute-start | bytes 442376 | tf_op jit(solution)/shard_map/ppermute | solution.py:514
  11.4 10.6 %collective-permute-start.3 = (bf16[4,72,256]{2,1,0:T(8,128)(2,1)S(1)}, bf16[4,72,256]{2,1,0:T(8,128)(2,1)S(1)}, u32[]{:S(2)}, u32[]{:S(2)}) collective-permute-start(bf16[4,72,256]{2,1,0:T(8,128)(2,1)S(1)} %get-tuple-element.40), channel_id=1, source_target_pairs={{8,0},{16,8},{24,16},{9,1},{17,9},{25,17},{10,2},{18,10},{26,18},{... | collective-permute-start | bytes 442376 | tf_op jit(solution)/shard_map/ppermute | solution.py:515
  12.7 2.3 %copy-start = (bf16[3,3,512,512]{3,2,1,0:T(8,128)(2,1)S(1)}, bf16[3,3,512,512]{3,2,1,0:T(8,128)(2,1)}, u32[]{:S(2)}) copy-start(bf16[3,3,512,512]{3,2,1,0:T(8,128)(2,1)} %param.6) | copy-start | bytes 14155780
  15.1 1.7 %copy-start.2 = (bf16[3,3,256,512]{3,2,1,0:T(8,128)(2,1)S(1)}, bf16[3,3,256,512]{3,2,1,0:T(8,128)(2,1)}, u32[]{:S(2)}) copy-start(bf16[3,3,256,512]{3,2,1,0:T(8,128)(2,1)} %param.5) | copy-start | bytes 7077892
  16.7 1.0 %copy-start.5 = (f32[8,64,256]{2,1,0:T(8,128)S(1)}, f32[8,64,256]{2,1,0:T(8,128)}, u32[]{:S(2)}) copy-start(f32[8,64,256]{2,1,0:T(8,128)} %pool.5) | copy-start | bytes 1572868
  17.8 4.3 %copy-start.1 = (bf16[3,3,512,512]{3,2,1,0:T(8,128)(2,1)S(1)}, bf16[3,3,512,512]{3,2,1,0:T(8,128)(2,1)}, u32[]{:S(2)}) copy-start(bf16[3,3,512,512]{3,2,1,0:T(8,128)(2,1)} %param.6) | copy-start | bytes 14155780
  22.0 20.6 %copy-start.6 = (f32[2,512,512]{2,1,0:T(8,128)S(1)}, f32[2,512,512]{2,1,0:T(8,128)}, u32[]{:S(2)}) copy-start(f32[2,512,512]{2,1,0:T(8,128)} %targets.1) | copy-start | bytes 6291460
  26.7 1.7 %collective-permute-start.4 = (bf16[1296,128]{1,0:T(8,128)(2,1)S(1)}, bf16[1296,128]{1,0:T(8,128)(2,1)S(1)}, u32[]{:S(2)}, u32[]{:S(2)}) collective-permute-start(bf16[1296,128]{1,0:T(8,128)(2,1)S(1)} %get-tuple-element.54), channel_id=1, source_target_pairs={{0,1},{1,0},{2,3},{3,2},{4,5},{5,4},{6,7},{7,6},{8,9},{9,8},{10,11... | collective-permute-start | bytes 995336 | tf_op jit(solution)/shard_map/ppermute | solution.py:605
  29.3 4.9 %collective-permute-start.5 = (bf16[336,128]{1,0:T(8,128)(2,1)S(1)}, bf16[336,128]{1,0:T(8,128)(2,1)S(1)}, u32[]{:S(2)}, u32[]{:S(2)}) collective-permute-start(bf16[336,128]{1,0:T(8,128)(2,1)S(1)} %get-tuple-element.57), channel_id=1, source_target_pairs={{0,8},{8,0},{16,24},{24,16},{1,9},{9,1},{17,25},{25,17},{2,10},{10... | collective-permute-start | bytes 258056 | tf_op jit(solution)/shard_map/ppermute | solution.py:613
  31.6 3.3 %collective-permute-start.6 = (bf16[336,128]{1,0:T(8,128)(2,1)S(1)}, bf16[336,128]{1,0:T(8,128)(2,1)S(1)}, u32[]{:S(2)}, u32[]{:S(2)}) collective-permute-start(bf16[336,128]{1,0:T(8,128)(2,1)S(1)} %get-tuple-element.58), channel_id=1, source_target_pairs={{0,16},{8,24},{16,0},{24,8},{1,17},{9,25},{17,1},{25,9},{2,18},{10... | collective-permute-start | bytes 258056 | tf_op jit(solution)/shard_map/ppermute | solution.py:613
  32.9 4.6 %collective-permute-start.7 = (bf16[336,128]{1,0:T(8,128)(2,1)S(1)}, bf16[336,128]{1,0:T(8,128)(2,1)S(1)}, u32[]{:S(2)}, u32[]{:S(2)}) collective-permute-start(bf16[336,128]{1,0:T(8,128)(2,1)S(1)} %get-tuple-element.59), channel_id=1, source_target_pairs={{0,24},{8,16},{16,8},{24,0},{1,25},{9,17},{17,9},{25,1},{2,26},{10... | collective-permute-start | bytes 258056 | tf_op jit(solution)/shard_map/ppermute | solution.py:613
  38.4 5.9 %collective-permute-start.10 = (bf16[336,128]{1,0:T(8,128)(2,1)S(1)}, bf16[336,128]{1,0:T(8,128)(2,1)S(1)}, u32[]{:S(2)}, u32[]{:S(2)}) collective-permute-start(bf16[336,128]{1,0:T(8,128)(2,1)S(1)} %get-tuple-element.62), channel_id=1, source_target_pairs={{0,6},{1,7},{2,4},{3,5},{4,2},{5,3},{6,0},{7,1},{8,14},{9,15},{10,... | collective-permute-start | bytes 258056 | tf_op jit(solution)/shard_map/ppermute | solution.py:623
  42.3 7.2 %collective-permute-start.9 = (bf16[336,128]{1,0:T(8,128)(2,1)S(1)}, bf16[336,128]{1,0:T(8,128)(2,1)S(1)}, u32[]{:S(2)}, u32[]{:S(2)}) collective-permute-start(bf16[336,128]{1,0:T(8,128)(2,1)S(1)} %get-tuple-element.62), channel_id=1, source_target_pairs={{0,4},{1,5},{2,6},{3,7},{4,0},{5,1},{6,2},{7,3},{8,12},{9,13},{10,... | collective-permute-start | bytes 258056 | tf_op jit(solution)/shard_map/ppermute | solution.py:623
  42.3 7.2 %collective-permute-start.8 = (bf16[336,128]{1,0:T(8,128)(2,1)S(1)}, bf16[336,128]{1,0:T(8,128)(2,1)S(1)}, u32[]{:S(2)}, u32[]{:S(2)}) collective-permute-start(bf16[336,128]{1,0:T(8,128)(2,1)S(1)} %get-tuple-element.62), channel_id=1, source_target_pairs={{0,2},{1,3},{2,0},{3,1},{4,6},{5,7},{6,4},{7,5},{8,10},{9,11},{10,... | collective-permute-start | bytes 258056 | tf_op jit(solution)/shard_map/ppermute | solution.py:623
  50.4 4.4 %collective-permute-start.13 = (bf16[320,128]{1,0:T(8,128)(2,1)S(1)}, bf16[320,128]{1,0:T(8,128)(2,1)S(1)}, u32[]{:S(2)}, u32[]{:S(2)}) collective-permute-start(bf16[320,128]{1,0:T(8,128)(2,1)S(1)} %get-tuple-element.63.share), channel_id=1, source_target_pairs={{0,24},{8,16},{16,8},{24,0},{1,25},{9,17},{17,9},{25,1},{2,26},{10... | collective-permute-start | bytes 245768 | tf_op jit(solution)/shard_map/ppermute | solution.py:633
  51.2 4.2 %collective-permute-start.12 = (bf16[320,128]{1,0:T(8,128)(2,1)S(1)}, bf16[320,128]{1,0:T(8,128)(2,1)S(1)}, u32[]{:S(2)}, u32[]{:S(2)}) collective-permute-start(bf16[320,128]{1,0:T(8,128)(2,1)S(1)} %get-tuple-element.63.share), channel_id=1, source_target_pairs={{0,16},{8,24},{16,0},{24,8},{1,17},{9,25},{17,1},{25,9},{2,18},{10... | collective-permute-start | bytes 245768 | tf_op jit(solution)/shard_map/ppermute | solution.py:633
  52.5 3.9 %collective-permute-start.11 = (bf16[320,128]{1,0:T(8,128)(2,1)S(1)}, bf16[320,128]{1,0:T(8,128)(2,1)S(1)}, u32[]{:S(2)}, u32[]{:S(2)}) collective-permute-start(bf16[320,128]{1,0:T(8,128)(2,1)S(1)} %get-tuple-element.63.share), channel_id=1, source_target_pairs={{0,8},{8,0},{16,24},{24,16},{1,9},{9,1},{17,25},{25,17},{2,10},{10... | collective-permute-start | bytes 245768 | tf_op jit(solution)/shard_map/ppermute | solution.py:633
  57.0 7.7 %collective-permute-start.14 = (bf16[1296,128]{1,0:T(8,128)(2,1)S(1)}, bf16[1296,128]{1,0:T(8,128)(2,1)S(1)}, u32[]{:S(2)}, u32[]{:S(2)}) collective-permute-start(bf16[1296,128]{1,0:T(8,128)(2,1)S(1)} %shard_map.55.rest_10_), channel_id=1, source_target_pairs={{0,1},{1,0},{2,3},{3,2},{4,5},{5,4},{6,7},{7,6},{8,9},{9,8},{10,11... | collective-permute-start | bytes 995336 | tf_op jit(solution)/shard_map/ppermute | solution.py:638
  59.4 1.7 %copy-start.3 = (bf16[3,3,256,512]{3,2,1,0:T(8,128)(2,1)S(1)}, bf16[3,3,256,512]{3,2,1,0:T(8,128)(2,1)}, u32[]{:S(2)}) copy-start(bf16[3,3,256,512]{3,2,1,0:T(8,128)(2,1)} %param.5) | copy-start | bytes 7077892

commit v6 on v5

--- a/solution.py
+++ b/solution.py
@@ -17,6 +17,7 @@
 F32 = jnp.float32
 VMEM = pl.BlockSpec(memory_space=pltpu.VMEM)
 SMEM = pl.BlockSpec(memory_space=pltpu.SMEM)
+HBM = pl.BlockSpec(memory_space=pltpu.HBM)
 MIB = 2**20
 
 
@@ -175,8 +176,15 @@
     return centre
 
 
-def middle(dims, place, pool, far, near, w1, w2, taps1, taps2, act1, slope1, act2, slope2, buf):
+def middle(dims, place, pool, far, near, w1_hbm, w2_hbm, *rest):
+    taps1, taps2, act1, slope1, act2, slope2, w1, w2, buf, sems = rest
     height, breadth, groups, limits = dims
+    loads = [
+        pltpu.make_async_copy(w1_hbm, w1, sems.at[0]),
+        pltpu.make_async_copy(w2_hbm, w2, sems.at[1]),
+    ]
+    for load in loads:
+        load.start()
     pitch = groups * 16
     left_core = place[0] == 0
     space = buf.shape[1] // height
@@ -190,33 +198,37 @@
         fold_row(taps1, r, buf, at, groups)
     low = 3 - place[2]
     inside = span(groups, low, low + limits[1])
+    loads[0].wait()
     for t in range(0, height - 2, 2):
         mask = pair_mask(inside, place, limits, t + 1)
         first_rows(
             lambda r: (taps1, t + r), w1, taps2, t, act1, slope1, t * pitch, groups, mask
         )
+    loads[1].wait()
     for t in range(0, height - 4, 2):
         second_rows(lambda r: (taps2, t + r), w2, act2, slope2, t * pitch, groups)
 
 
-def rim_taps(ref, rows, buf, groups):
+def rim_taps(ref, rows, place, buf, groups):
     space = buf.shape[1] // len(rows)
-    for n, (source, r) in enumerate(rows):
-        breadth = source.shape[1]
+    even = (place[3] & 1) == 0
+    for n, (one, two, r) in enumerate(rows):
+        breadth = one.shape[1]
         at = n * space
-        put_row(buf, at, source[r].astype(F32))
+        put_row(buf, at, jnp.where(even, one[r].astype(F32), two[r].astype(F32)))
         clear_rows(buf, at + breadth, at + space)
         fold_row(ref, n, buf, at, groups)
 
 
-def front(dims, place, above, below, taps1, taps2, act1, act2, w1, w2, *rest):
+def front(dims, place, even, odd, taps1, taps2, act1, act2, w1, w2, *rest):
     (taps2b, act1b, slope1b, act2b, slope2b, keep, mine, sent) = rest[:8]
     (rim, buf, gram, stat) = rest[8:]
     height, breadth, groups, limits = dims
     pitch = groups * 16
     width = w1.shape[1]
     blocks = width // BLOCK
-    rim_taps(rim, [(above, 2), (above, 3), (below, 0), (below, 1)], buf, groups)
+    rows = [(odd, even, REACH - 2), (odd, even, REACH - 1), (even, odd, 0), (even, odd, 1)]
+    rim_taps(rim, rows, place, buf, groups)
     low = 3 - place[2]
     inside = span(groups, low, low + limits[1])
     last = height - 2
@@ -277,7 +289,7 @@
     sent[rows:, :] = stat[1 - place[0], 0:EXTRA, :].astype(BF)
 
 
-def ring(dims, place, above, below, taps2b, w1, w2, act2, slope2, rim, outer, buf):
+def ring(dims, place, even, odd, taps2b, w1, w2, act2, slope2, rim, outer, buf):
     height, _, groups, limits = dims
     low = 3 - place[2]
     inside = span(groups, low, low + limits[1])
@@ -285,8 +297,8 @@
         lambda r: (outer, r) if r < 2 else (taps2b, r - 2),
         lambda r: (taps2b, 2 + r) if r < 2 else (outer, r),
     )
-    for n, (source, row) in enumerate(((above, -3), (below, height + 1))):
-        rim_taps(rim, [(source, r) for r in range(REACH)], buf, groups)
+    for n, (one, two, row) in enumerate(((odd, even, -3), (even, odd, height + 1))):
+        rim_taps(rim, [(one, two, r) for r in range(REACH)], place, buf, groups)
         mask = pair_mask(inside, place, limits, row)
         first_rows(lambda r: (rim, r), w1, outer, 2 * n, None, None, 0, groups, mask)
         second_rows(finds[n], w2, act2, slope2, 2 * n * groups * 16, groups)
@@ -419,7 +431,10 @@
                 out[t + r, :, lanes] = buf[p, at : at + breadth, :]
 
 
-def edges(place, pool, far, near):
+def edges(place, pool_hbm, pool, far, near, sem):
+    load = pltpu.make_async_copy(pool_hbm, pool, sem)
+    load.start()
+    load.wait()
     breadth = pool.shape[1]
     left_core = place[0] == 0
     left = pool[:, 0:REACH, :]
@@ -428,14 +443,16 @@
     near[...] = jnp.where(left_core, right, left).astype(BF)
 
 
-def bands(place, pool, far, near, above, below, row):
+def bands(place, pool, far, near, even, odd, row):
     height, breadth, _ = pool.shape
     left_core = place[0] == 0
-    for start, ref in ((height - REACH, above), (0, below)):
+    odd_row = place[3] & 1
+    for start, ref in ((1 - odd_row, even), (odd_row, odd)):
         for r in range(REACH):
-            one, two = far[start + r].astype(F32), near[start + r].astype(F32)
+            at = start * (height - REACH) + r
+            one, two = far[at].astype(F32), near[at].astype(F32)
             row[0:REACH, :] = jnp.where(left_core, one, two)
-            row[REACH : REACH + breadth, :] = pool[start + r]
+            row[REACH : REACH + breadth, :] = pool[at]
             row[REACH + breadth :, :] = jnp.where(left_core, two, one)
             ref[r] = row[...].astype(BF)
 
@@ -461,14 +478,20 @@
     goal[...] = full[pl.ds(pl.multiple_of(place[3] * chunk, 16), chunk), :]
 
 
-def call(body, ins, outs, scratch, flops=0, limit=None):
+def call(body, ins, outs, scratch, flops=0, limit=None, far=()):
+    ins = [
+        pltpu.with_memory_space_constraint(x, pltpu.HBM) if n in far else x
+        for n, x in enumerate(ins)
+    ]
     moved = sum(x.size * x.dtype.itemsize for x in ins) + sum(
         x.size * x.dtype.itemsize for x in outs
     )
     return pl.pallas_call(
         body,
         out_shape=tuple(outs),
-        in_specs=[SMEM if x.dtype == jnp.int32 else VMEM for x in ins],
+        in_specs=[
+            HBM if n in far else SMEM if x.dtype == jnp.int32 else VMEM for n, x in enumerate(ins)
+        ],
         out_specs=tuple(VMEM for _ in outs),
         scratch_shapes=scratch,
         compiler_params=pltpu.CompilerParams(vmem_limit_bytes=(limit or 8) * MIB),
@@ -499,24 +522,28 @@
     cross = cross + [(j, i) for i, j in cross]
 
     rim = shape((height, REACH, depth), BF)
-    far, near = call(edges, [place, pool_input], [rim] * 2, [])
+    pool, far, near = call(
+        edges,
+        [place, pool_input],
+        [shape(pool_input.shape, F32)] + [rim] * 2,
+        [pltpu.SemaphoreType.DMA],
+        far=(1,),
+    )
     far = lax.ppermute(far, "tile", cross)
     near = lax.ppermute(near, "tile", swap)
     band = shape((REACH, breadth + 2 * REACH, depth), BF)
-    above, below = call(
-        bands,
-        [place, pool_input, far, near],
-        [band] * 2,
-        [pltpu.VMEM((breadth + 2 * REACH, depth), F32)],
-    )
-    up = [(i, i + 1) for i in range(groups - 1)]
-    down = [(j, i) for i, j in up]
-    above = lax.ppermute(above, "grp", up)
-    below = lax.ppermute(below, "grp", down)
+    even, odd = call(
+        bands, [place, pool, far, near], [band] * 2, [pltpu.VMEM((breadth + 2 * REACH, depth), F32)]
+    )
+
+    def couples(start):
+        ways = [(i, i + 1) for i in range(start, groups - 1, 2)]
+        return ways + [(j, i) for i, j in ways]
+
+    even = lax.ppermute(even, "grp", couples(0))
+    odd = lax.ppermute(odd, "grp", couples(1))
 
     packed = len(pairs(width)) * BLOCK
-    w1 = weight_first.reshape(-1, width)
-    w2 = weight_second.reshape(-1, width)
     space = (fold * 15 + fold + 2 + 7) // 8 * 8
 
     def maps(rows):
@@ -525,19 +552,22 @@
     def cost(rows_first, rows_second):
         return 2 * 9 * width * pitch * (rows_first * depth + rows_second * width)
 
-    taps1, taps2, act1, slope1, act2, slope2 = call(
+    taps1, taps2, act1, slope1, act2, slope2, w1, w2 = call(
         functools.partial(middle, dims),
-        [place, pool_input, far, near, w1, w2],
+        [place, pool, far, near]
+        + [weight_first.reshape(-1, width), weight_second.reshape(-1, width)],
         [shape((height * wider, depth), BF), shape(((height - 2) * wider, width), BF)]
         + maps(height - 2)
-        + maps(height - 4),
-        [pltpu.VMEM((depth // BLOCK, height * space, BLOCK), F32)],
+        + maps(height - 4)
+        + [shape((9 * depth, width), BF), shape((9 * width, width), BF)],
+        [pltpu.VMEM((depth // BLOCK, height * space, BLOCK), F32), pltpu.SemaphoreType.DMA((2,))],
         flops=cost(height - 2, height - 4),
         limit=24,
+        far=(4, 5),
     )
     taps2b, act1b, slope1b, act2b, slope2b, keep, mine, sent = call(
         functools.partial(front, dims),
-        [place, above, below, taps1, taps2, act1, act2, w1, w2],
+        [place, even, odd, taps1, taps2, act1, act2, w1, w2],
         [shape((4 * wider, width), BF)]
         + maps(4)
         + maps(4)
@@ -557,7 +587,7 @@
     )
     act2r, slope2r = call(
         functools.partial(ring, dims),
-        [place, above, below, taps2b, w1, w2],
+        [place, even, odd, taps2b, w1, w2],
         maps(4),
         [
             pltpu.VMEM((4 * wider, depth), BF),
@@ -576,8 +606,7 @@
         flops=2 * 10**8,
     )
 
-    def turned(weight):
-        inner = weight.shape[2]
+    def turned(weight, inner):
         (out,) = call(
             flip,
             [weight.reshape(9, inner, width)],
@@ -588,8 +617,8 @@
         )
         return out
 
-    back2 = turned(weight_second)
-    back1 = turned(weight_first)
+    back2 = turned(w2, width)
+    back1 = turned(w1, depth)
 
     def helpers(members):
         deep = -(-3 * members // 16) * 16

time: 73.3 us -> 67.2 us (0.917)
  local copies, waits for them, and re-layouts: 6.09 us -> 0.01 us
  Pallas kernels: 28.6 us -> 31.5 us
  starting transfers between devices: 23.3 us -> 20.8 us
    unnamed x14 -> x2, local copies, waits for them, and re-layouts: 6.09 us -> 0.01 us
    pallas_call x13, Pallas kernels: 28.6 us -> 31.5 us  [call(): pl.pallas_call(body, out_shape=tuple(outs), in_specs=[HBM if n in far els...]
    ppermute x2, starting transfers between devices: 4.41 us -> 1.93 us  [the longest x1 1.28 us: local(): even = lax.ppermute(even, 'grp', couples(0))]
    ppermute x1, starting transfers between devices: 2.45 us -> 1.69 us  [local(): other = lax.ppermute(mine, 'tile', swap)]
  transfers between devices with their start and end apart: 15 -> 15, of which waited for: 10 -> 9; matrix products, arithmetic and copies ran while one was open for 0% -> 0% of each run, Pallas kernels for 16% -> 20%
where the time goes in v6:
time: 67.2 us; the launch traced here: 67 us
  Pallas kernels  31.5 us (47%)
  starting transfers between devices  20.8 us (31%)
  waiting for transfers between devices  14.5 us (22%)
    pallas_call x13, Pallas kernels, call(): pl.pallas_call(body, out_shape=tuple(outs), in_specs=[HBM if n in far els...  31.5 us
    ppermute x3, waiting for transfers between devices, local(): lax.ppermute(sent, 'tile', [(i, i ^ 2 * k) for i in range(tiles)])  6.13 us
    ppermute x3, starting transfers between devices, local(): lax.ppermute(sents[k - 1], 'grp', [(i, i ^ k) for i in range(groups)])  5.18 us
    ppermute x1, starting transfers between devices, local(): far = lax.ppermute(far, 'tile', cross)  4.58 us
    ppermute x3, starting transfers between devices, local(): lax.ppermute(sent, 'tile', [(i, i ^ 2 * k) for i in range(tiles)])  4.3 us
    ppermute x3, waiting for transfers between devices, local(): lax.ppermute(sents[k - 1], 'grp', [(i, i ^ k) for i in range(groups)])  3.07 us
    ppermute x3, starting transfers between devices, local(): lax.ppermute(share, 'grp', [(i, i ^ k) for i in range(groups)])  2.71 us
    ppermute x3, waiting for transfers between devices, local(): lax.ppermute(share, 'grp', [(i, i ^ k) for i in range(groups)])  2.61 us
  transfers between devices with their start and end apart: 15, of which 9 were waited for; matrix products, arithmetic and copies ran while one was open for 0% of the time, Pallas kernels for 20%

profile of v6, /device:TPU:1, one launch (start us, length us, event | category | flops | bytes accessed | tf_op | source)
XLA Modules:
  0.0 67.0 jit_solution(10806125581046274526)
XLA Ops:
  0.0 0.1 pad_add_fusion.place
  0.1 1.6 %shard_map.46 = (f32[8,64,256]{2,1,0:T(8,128)S(1)}, bf16[8,4,256]{2,1,0:T(4,128)(2,1)S(1)}, bf16[8,4,256]{2,1,0:T(4,128)(2,1)S(1)}) custom-call(s32[4]{0:T(128)S(1)} %pad_add_fusion.place, f32[8,64,256]{2,1,0:T(8,128)} %pool_hbm.1), custom_call_target="tpu_custom_call" | custom-call | bytes 1081360 | tf_op jit(solution)/shard_map/pallas_call | solution.py:489
  1.7 4.6 %collective-permute-start = (bf16[8,4,256]{2,1,0:T(4,128)(2,1)S(1)}, bf16[8,4,256]{2,1,0:T(4,128)(2,1)S(1)}, u32[]{:S(2)}, u32[]{:S(2)}) collective-permute-start(bf16[8,4,256]{2,1,0:T(4,128)(2,1)S(1)} %get-tuple-element.39), channel_id=1, source_target_pairs={{1,2},{3,4},{5,6},{2,1},{4,3},{6,5},{9,10},{11,12},{13,14},{10,9},... | collective-permute-start | bytes 49160 | tf_op jit(solution)/shard_map/ppermute | solution.py:532
  6.3 0.1 collective-permute-start.1
  6.4 1.3 %collective-permute-done.far = bf16[8,4,256]{2,1,0:T(4,128)(2,1)S(1)} collective-permute-done((bf16[8,4,256]{2,1,0:T(4,128)(2,1)S(1)}, bf16[8,4,256]{2,1,0:T(4,128)(2,1)S(1)}, u32[]{:S(2)}, u32[]{:S(2)}) %collective-permute-start) | collective-permute-done | bytes 16416 | tf_op jit(solution)/shard_map/ppermute | solution.py:532
  7.7 0.0 collective-permute-done.1.near
  7.7 0.6 shard_map.48
  8.3 1.3 %collective-permute-start.2 = (bf16[4,72,256]{2,1,0:T(8,128)(2,1)S(1)}, bf16[4,72,256]{2,1,0:T(8,128)(2,1)S(1)}, u32[]{:S(2)}, u32[]{:S(2)}) collective-permute-start(bf16[4,72,256]{2,1,0:T(8,128)(2,1)S(1)} %get-tuple-element.43), channel_id=1, source_target_pairs={{0,8},{16,24},{8,0},{24,16},{1,9},{17,25},{9,1},{25,17},{2,10},{18... | collective-permute-start | bytes 442376 | tf_op jit(solution)/shard_map/ppermute | solution.py:543
  9.6 0.7 collective-permute-start.3
  10.3 6.0 %shard_map.47 = (bf16[896,256]{1,0:T(8,128)(2,1)S(1)}, bf16[672,512]{1,0:T(8,128)(2,1)S(1)}, f32[480,512]{1,0:T(8,128)S(1)}, f32[480,512]{1,0:T(8,128)S(1)}, f32...) custom-call(s32[4]{0:T(128)S(1)} %pad_add_fusion.place, ...), custom_call_target="tpu_custom_call" | custom-call | flops 2642411520 | bytes 19136528 | tf_op jit(solution)/shard_map/pallas_call | solution.py:489
  16.3 0.0 collective-permute-done.2.even
  16.3 0.0 collective-permute-done.3.odd
  16.3 0.0 copy-start
  16.3 4.7 %shard_map.49 = (bf16[448,512]{1,0:T(8,128)(2,1)S(1)}, f32[320,512]{1,0:T(8,128)S(1)}, f32[320,512]{1,0:T(8,128)S(1)}, f32[320,512]{1,0:T(8,128)S(1)}, f32[320,5...) custom-call(s32[4]{0:T(128)S(1)} %pad_add_fusion.place, ...), custom_call_target="tpu_custom_call" | custom-call | flops 2264924160 | bytes 14229520 | tf_op jit(solution)/shard_map/pallas_call | solution.py:489
  21.0 0.4 collective-permute-start.4
  21.3 1.3 %collective-permute-done.4.got = bf16[1296,128]{1,0:T(8,128)(2,1)S(1)} collective-permute-done((bf16[1296,128]{1,0:T(8,128)(2,1)S(1)}, bf16[1296,128]{1,0:T(8,128)(2,1)S(1)}, u32[]{:S(2)}, u32[]{:S(2)}) %collective-permute-start.4) | collective-permute-done | bytes 331808 | tf_op jit(solution)/shard_map/ppermute | solution.py:634
  22.7 0.9 %shard_map.51 = (f32[320,128]{1,0:T(8,128)S(1)}, f32[8,128]{1,0:T(8,128)S(1)}, bf16[336,128]{1,0:T(8,128)(2,1)S(1)}, bf16[336,128]{1,0:T(8,128)(2,1)S(1)}, bf16[336,128]{1,0:T(8,128)(2,1)S(1)}) custom-call(s32[4]{0:T(128)S(1)} %pad_add_fusion.place, f32[1280,128]{1,0:T(8,128)S(1)} %get-tuple-element.58.keep, f32[8,128]{1,0:T(8,128)S(1)} %get-tuple-element.59.mine, ...), custom_call_target="tpu_custom_call" | custom-call | bytes 1417232 | tf_op jit(solution)/shard_map/pallas_call | solution.py:489
  23.5 3.9 %collective-permute-start.5 = (bf16[336,128]{1,0:T(8,128)(2,1)S(1)}, bf16[336,128]{1,0:T(8,128)(2,1)S(1)}, u32[]{:S(2)}, u32[]{:S(2)}) collective-permute-start(bf16[336,128]{1,0:T(8,128)(2,1)S(1)} %get-tuple-element.63), channel_id=1, source_target_pairs={{0,8},{8,0},{16,24},{24,16},{1,9},{9,1},{17,25},{25,17},{2,10},{10... | collective-permute-start | bytes 258056 | tf_op jit(solution)/shard_map/ppermute | solution.py:642
  27.5 0.0 collective-permute-start.6
  27.5 1.3 %collective-permute-start.7 = (bf16[336,128]{1,0:T(8,128)(2,1)S(1)}, bf16[336,128]{1,0:T(8,128)(2,1)S(1)}, u32[]{:S(2)}, u32[]{:S(2)}) collective-permute-start(bf16[336,128]{1,0:T(8,128)(2,1)S(1)} %get-tuple-element.65), channel_id=1, source_target_pairs={{0,24},{8,16},{16,8},{24,0},{1,25},{9,17},{17,9},{25,1},{2,26},{10... | collective-permute-start | bytes 258056 | tf_op jit(solution)/shard_map/ppermute | solution.py:642
  28.7 1.3 %collective-permute-done.5.rest_0_ = bf16[336,128]{1,0:T(8,128)(2,1)S(1)} collective-permute-done((bf16[336,128]{1,0:T(8,128)(2,1)S(1)}, bf16[336,128]{1,0:T(8,128)(2,1)S(1)}, u32[]{:S(2)}, u32[]{:S(2)}) %collective-permute-start.5) | collective-permute-done | bytes 86048 | tf_op jit(solution)/shard_map/ppermute | solution.py:642
  30.0 0.8 %collective-permute-done.6.rest_1_ = bf16[336,128]{1,0:T(8,128)(2,1)S(1)} collective-permute-done((bf16[336,128]{1,0:T(8,128)(2,1)S(1)}, bf16[336,128]{1,0:T(8,128)(2,1)S(1)}, u32[]{:S(2)}, u32[]{:S(2)}) %collective-permute-start.6) | collective-permute-done | bytes 86048 | tf_op jit(solution)/shard_map/ppermute | solution.py:642
  30.8 1.0 %collective-permute-done.7.rest_2_ = bf16[336,128]{1,0:T(8,128)(2,1)S(1)} collective-permute-done((bf16[336,128]{1,0:T(8,128)(2,1)S(1)}, bf16[336,128]{1,0:T(8,128)(2,1)S(1)}, u32[]{:S(2)}, u32[]{:S(2)}) %collective-permute-start.7) | collective-permute-done | bytes 86048 | tf_op jit(solution)/shard_map/ppermute | solution.py:642
  31.8 0.9 %shard_map.52 = (f32[320,128]{1,0:T(8,128)S(1)}, f32[8,128]{1,0:T(8,128)S(1)}, bf16[336,128]{1,0:T(8,128)(2,1)S(1)}) custom-call(s32[4]{0:T(128)S(1)} %pad_add_fusion.place, f32[320,128]{1,0:T(8,128)S(1)} %get-tuple-element.61.share, f32[8,128]{1,0:T(8,128)S(1)} %get-tuple-element.62.mine, bf16[336,128]{1,0:T(8,128)(2,1)S(1)} %collective-permute-done.5.rest_0_, ...), custom_call_target="tpu_custom_call" | custom-call | bytes 679952 | tf_op jit(solution)/shard_map/pallas_call | solution.py:489
  32.7 3.9 %collective-permute-start.10 = (bf16[336,128]{1,0:T(8,128)(2,1)S(1)}, bf16[336,128]{1,0:T(8,128)(2,1)S(1)}, u32[]{:S(2)}, u32[]{:S(2)}) collective-permute-start(bf16[336,128]{1,0:T(8,128)(2,1)S(1)} %get-tuple-element.68), channel_id=1, source_target_pairs={{0,6},{1,7},{2,4},{3,5},{4,2},{5,3},{6,0},{7,1},{8,14},{9,15},{10,... | collective-permute-start | bytes 258056 | tf_op jit(solution)/shard_map/ppermute | solution.py:652
  36.6 0.0 collective-permute-start.9
  36.6 0.4 collective-permute-start.8
  37.0 0.0 copy-done
  37.0 0.8 %shard_map.53.rest_3_ = f32[320,128]{1,0:T(8,128)S(1)} custom-call(s32[4]{0:T(128)S(1)} %pad_add_fusion.place, f32[2,512,512]{2,1,0:T(8,128)S(1)} %copy-done), custom_call_target="tpu_custom_call" | custom-call | flops 200000000 | bytes 2261008 | tf_op jit(solution)/shard_map/pallas_call | solution.py:489
  37.8 0.8 %collective-permute-done.10.rest_2_ = bf16[336,128]{1,0:T(8,128)(2,1)S(1)} collective-permute-done((bf16[336,128]{1,0:T(8,128)(2,1)S(1)}, bf16[336,128]{1,0:T(8,128)(2,1)S(1)}, u32[]{:S(2)}, u32[]{:S(2)}) %collective-permute-start.10) | collective-permute-done | bytes 86048 | tf_op jit(solution)/shard_map/ppermute | solution.py:652
  38.6 5.3 %collective-permute-done.9.rest_1_ = bf16[336,128]{1,0:T(8,128)(2,1)S(1)} collective-permute-done((bf16[336,128]{1,0:T(8,128)(2,1)S(1)}, bf16[336,128]{1,0:T(8,128)(2,1)S(1)}, u32[]{:S(2)}, u32[]{:S(2)}) %collective-permute-start.9) | collective-permute-done | bytes 86048 | tf_op jit(solution)/shard_map/ppermute | solution.py:652
  43.9 0.0 collective-permute-done.8.rest_0_
  43.9 0.9 %shard_map.54 = (bf16[320,128]{1,0:T(8,128)(2,1)S(1)}, bf16[16,128]{1,0:T(8,128)(2,1)S(1)}) custom-call(s32[4]{0:T(128)S(1)} %pad_add_fusion.place, f32[320,128]{1,0:T(8,128)S(1)} %get-tuple-element.66.share, f32[8,128]{1,0:T(8,128)S(1)} %get-tuple-element.67.mine, bf16[336,128]{1,0:T(8,128)(2,1)S(1)} %collective-permute-done.8.rest_0_, ...), custom_call_target="tpu_custom_call" | custom-call | bytes 675856 | tf_op jit(solution)/shard_map/pallas_call | solution.py:489
  44.8 2.2 %collective-permute-start.13 = (bf16[320,128]{1,0:T(8,128)(2,1)S(1)}, bf16[320,128]{1,0:T(8,128)(2,1)S(1)}, u32[]{:S(2)}, u32[]{:S(2)}) collective-permute-start(bf16[320,128]{1,0:T(8,128)(2,1)S(1)} %get-tuple-element.69.share), channel_id=1, source_target_pairs={{0,24},{8,16},{16,8},{24,0},{1,25},{9,17},{17,9},{25,1},{2,26},{10... | collective-permute-start | bytes 245768 | tf_op jit(solution)/shard_map/ppermute | solution.py:662
  47.0 0.0 collective-permute-start.12
  47.0 0.5 collective-permute-start.11
  47.6 1.1 %shard_map.57.rest_13_ = bf16[4608,256]{1,0:T(8,128)(2,1)S(1)} custom-call(bf16[9,256,512]{2,1,0:T(8,128)(2,1)S(1)} %bitcast.9), custom_call_target="tpu_custom_call" | custom-call | flops 2000000000 | bytes 4718592 | tf_op jit(solution)/shard_map/pallas_call | solution.py:489
  48.7 0.4 collective-permute-done.13.rest_2_
  49.1 2.2 %collective-permute-done.12.rest_1_ = bf16[320,128]{1,0:T(8,128)(2,1)S(1)} collective-permute-done((bf16[320,128]{1,0:T(8,128)(2,1)S(1)}, bf16[320,128]{1,0:T(8,128)(2,1)S(1)}, u32[]{:S(2)}, u32[]{:S(2)}) %collective-permute-start.12) | collective-permute-done | bytes 81952 | tf_op jit(solution)/shard_map/ppermute | solution.py:662
  51.3 0.0 collective-permute-done.11.rest_0_
  51.3 0.6 shard_map.55.rest_10_
  51.8 1.7 %collective-permute-start.14 = (bf16[1296,128]{1,0:T(8,128)(2,1)S(1)}, bf16[1296,128]{1,0:T(8,128)(2,1)S(1)}, u32[]{:S(2)}, u32[]{:S(2)}) collective-permute-start(bf16[1296,128]{1,0:T(8,128)(2,1)S(1)} %shard_map.55.rest_10_), channel_id=1, source_target_pairs={{0,1},{1,0},{2,3},{3,2},{4,5},{5,4},{6,7},{7,6},{8,9},{9,8},{10,11... | collective-permute-start | bytes 995336 | tf_op jit(solution)/shard_map/ppermute | solution.py:667
  53.5 1.7 %shard_map.56.rest_12_ = bf16[4608,512]{1,0:T(8,128)(2,1)S(1)} custom-call(bf16[9,512,512]{2,1,0:T(8,128)(2,1)S(1)} %bitcast.8), custom_call_target="tpu_custom_call" | custom-call | flops 2000000000 | bytes 9437184 | tf_op jit(solution)/shard_map/pallas_call | solution.py:489
  55.2 3.5 %shard_map.50 = (f32[320,512]{1,0:T(8,128)S(1)}, f32[320,512]{1,0:T(8,128)S(1)}) custom-call(s32[4]{0:T(128)S(1)} %pad_add_fusion.place, bf16[4,72,256]{2,1,0:T(8,128)(2,1)S(1)} %collective-permute-done.2.even, bf16[4,72,256]{2,1,0:T(8,128)(2,1)S(1)} %collective-permute-done.3.odd, bf16[448,512]{1,0:T(8,128)(2,1)S(1)} %get-tuple-element.55.taps2b, ...), custom_call_target="tpu_custom_call" | custom-call | flops 2264924160 | bytes 9142288 | tf_op jit(solution)/shard_map/pallas_call | solution.py:489
  58.8 0.0 collective-permute-done.14.rest_11_
  58.8 8.2 %shard_map.58 = f32[8,64,256]{2,1,0:T(8,128)} custom-call(s32[4]{0:T(128)S(1)} %pad_add_fusion.place, f32[480,512]{1,0:T(8,128)S(1)} %get-tuple-element.41.act1.rest_0_, f32[480,512]{1,0:T(8,128)S(1)} %get-tuple-element.42.rest_1_, f32[320,512]{1,0:T(8,128)S(1)} %get-tuple-element.50.rest_2_, f32[320,512]{1,0:T(8,128)S(1)} %get-tuple-element.51.rest_3_, ...), custom_call_target="tpu_custom_call" | custom-call | flops 5284823040 | bytes 15474704 | tf_op jit(solution)/shard_map/pallas_call | solution.py:489
Async XLA Ops:
  1.7 6.0 %collective-permute-start = (bf16[8,4,256]{2,1,0:T(4,128)(2,1)S(1)}, bf16[8,4,256]{2,1,0:T(4,128)(2,1)S(1)}, u32[]{:S(2)}, u32[]{:S(2)}) collective-permute-start(bf16[8,4,256]{2,1,0:T(4,128)(2,1)S(1)} %get-tuple-element.39), channel_id=1, source_target_pairs={{1,2},{3,4},{5,6},{2,1},{4,3},{6,5},{9,10},{11,12},{13,14},{10,9},... | collective-permute-start | bytes 49160 | tf_op jit(solution)/shard_map/ppermute | solution.py:532
  6.3 1.4 %collective-permute-start.1 = (bf16[8,4,256]{2,1,0:T(4,128)(2,1)S(1)}, bf16[8,4,256]{2,1,0:T(4,128)(2,1)S(1)}, u32[]{:S(2)}, u32[]{:S(2)}) collective-permute-start(bf16[8,4,256]{2,1,0:T(4,128)(2,1)S(1)} %get-tuple-element.40), channel_id=1, source_target_pairs={{0,1},{1,0},{2,3},{3,2},{4,5},{5,4},{6,7},{7,6},{8,9},{9,8},{10,11... | collective-permute-start | bytes 49160 | tf_op jit(solution)/shard_map/ppermute | solution.py:533
  8.3 7.9 %collective-permute-start.2 = (bf16[4,72,256]{2,1,0:T(8,128)(2,1)S(1)}, bf16[4,72,256]{2,1,0:T(8,128)(2,1)S(1)}, u32[]{:S(2)}, u32[]{:S(2)}) collective-permute-start(bf16[4,72,256]{2,1,0:T(8,128)(2,1)S(1)} %get-tuple-element.43), channel_id=1, source_target_pairs={{0,8},{16,24},{8,0},{24,16},{1,9},{17,25},{9,1},{25,17},{2,10},{18... | collective-permute-start | bytes 442376 | tf_op jit(solution)/shard_map/ppermute | solution.py:543
  9.6 6.7 %collective-permute-start.3 = (bf16[4,72,256]{2,1,0:T(8,128)(2,1)S(1)}, bf16[4,72,256]{2,1,0:T(8,128)(2,1)S(1)}, u32[]{:S(2)}, u32[]{:S(2)}) collective-permute-start(bf16[4,72,256]{2,1,0:T(8,128)(2,1)S(1)} %get-tuple-element.44), channel_id=1, source_target_pairs={{8,16},{16,8},{9,17},{17,9},{10,18},{18,10},{11,19},{19,11},{12,20... | collective-permute-start | bytes 442376 | tf_op jit(solution)/shard_map/ppermute | solution.py:544
  16.3 20.7 %copy-start = (f32[2,512,512]{2,1,0:T(8,128)S(1)}, f32[2,512,512]{2,1,0:T(8,128)}, u32[]{:S(2)}) copy-start(f32[2,512,512]{2,1,0:T(8,128)} %targets.1) | copy-start | bytes 6291460
  21.0 1.7 %collective-permute-start.4 = (bf16[1296,128]{1,0:T(8,128)(2,1)S(1)}, bf16[1296,128]{1,0:T(8,128)(2,1)S(1)}, u32[]{:S(2)}, u32[]{:S(2)}) collective-permute-start(bf16[1296,128]{1,0:T(8,128)(2,1)S(1)} %get-tuple-element.60), channel_id=1, source_target_pairs={{0,1},{1,0},{2,3},{3,2},{4,5},{5,4},{6,7},{7,6},{8,9},{9,8},{10,11... | collective-permute-start | bytes 995336 | tf_op jit(solution)/shard_map/ppermute | solution.py:634
  23.5 6.4 %collective-permute-start.5 = (bf16[336,128]{1,0:T(8,128)(2,1)S(1)}, bf16[336,128]{1,0:T(8,128)(2,1)S(1)}, u32[]{:S(2)}, u32[]{:S(2)}) collective-permute-start(bf16[336,128]{1,0:T(8,128)(2,1)S(1)} %get-tuple-element.63), channel_id=1, source_target_pairs={{0,8},{8,0},{16,24},{24,16},{1,9},{9,1},{17,25},{25,17},{2,10},{10... | collective-permute-start | bytes 258056 | tf_op jit(solution)/shard_map/ppermute | solution.py:642
  27.5 3.3 %collective-permute-start.6 = (bf16[336,128]{1,0:T(8,128)(2,1)S(1)}, bf16[336,128]{1,0:T(8,128)(2,1)S(1)}, u32[]{:S(2)}, u32[]{:S(2)}) collective-permute-start(bf16[336,128]{1,0:T(8,128)(2,1)S(1)} %get-tuple-element.64), channel_id=1, source_target_pairs={{0,16},{8,24},{16,0},{24,8},{1,17},{9,25},{17,1},{25,9},{2,18},{10... | collective-permute-start | bytes 258056 | tf_op jit(solution)/shard_map/ppermute | solution.py:642
  27.5 4.3 %collective-permute-start.7 = (bf16[336,128]{1,0:T(8,128)(2,1)S(1)}, bf16[336,128]{1,0:T(8,128)(2,1)S(1)}, u32[]{:S(2)}, u32[]{:S(2)}) collective-permute-start(bf16[336,128]{1,0:T(8,128)(2,1)S(1)} %get-tuple-element.65), channel_id=1, source_target_pairs={{0,24},{8,16},{16,8},{24,0},{1,25},{9,17},{17,9},{25,1},{2,26},{10... | collective-permute-start | bytes 258056 | tf_op jit(solution)/shard_map/ppermute | solution.py:642
  32.7 5.9 %collective-permute-start.10 = (bf16[336,128]{1,0:T(8,128)(2,1)S(1)}, bf16[336,128]{1,0:T(8,128)(2,1)S(1)}, u32[]{:S(2)}, u32[]{:S(2)}) collective-permute-start(bf16[336,128]{1,0:T(8,128)(2,1)S(1)} %get-tuple-element.68), channel_id=1, source_target_pairs={{0,6},{1,7},{2,4},{3,5},{4,2},{5,3},{6,0},{7,1},{8,14},{9,15},{10,... | collective-permute-start | bytes 258056 | tf_op jit(solution)/shard_map/ppermute | solution.py:652
  36.6 7.3 %collective-permute-start.9 = (bf16[336,128]{1,0:T(8,128)(2,1)S(1)}, bf16[336,128]{1,0:T(8,128)(2,1)S(1)}, u32[]{:S(2)}, u32[]{:S(2)}) collective-permute-start(bf16[336,128]{1,0:T(8,128)(2,1)S(1)} %get-tuple-element.68), channel_id=1, source_target_pairs={{0,4},{1,5},{2,6},{3,7},{4,0},{5,1},{6,2},{7,3},{8,12},{9,13},{10,... | collective-permute-start | bytes 258056 | tf_op jit(solution)/shard_map/ppermute | solution.py:652
  36.6 7.3 %collective-permute-start.8 = (bf16[336,128]{1,0:T(8,128)(2,1)S(1)}, bf16[336,128]{1,0:T(8,128)(2,1)S(1)}, u32[]{:S(2)}, u32[]{:S(2)}) collective-permute-start(bf16[336,128]{1,0:T(8,128)(2,1)S(1)} %get-tuple-element.68), channel_id=1, source_target_pairs={{0,2},{1,3},{2,0},{3,1},{4,6},{5,7},{6,4},{7,5},{8,10},{9,11},{10,... | collective-permute-start | bytes 258056 | tf_op jit(solution)/shard_map/ppermute | solution.py:652
  44.8 4.3 %collective-permute-start.13 = (bf16[320,128]{1,0:T(8,128)(2,1)S(1)}, bf16[320,128]{1,0:T(8,128)(2,1)S(1)}, u32[]{:S(2)}, u32[]{:S(2)}) collective-permute-start(bf16[320,128]{1,0:T(8,128)(2,1)S(1)} %get-tuple-element.69.share), channel_id=1, source_target_pairs={{0,24},{8,16},{16,8},{24,0},{1,25},{9,17},{17,9},{25,1},{2,26},{10... | collective-permute-start | bytes 245768 | tf_op jit(solution)/shard_map/ppermute | solution.py:662
  47.0 4.2 %collective-permute-start.12 = (bf16[320,128]{1,0:T(8,128)(2,1)S(1)}, bf16[320,128]{1,0:T(8,128)(2,1)S(1)}, u32[]{:S(2)}, u32[]{:S(2)}) collective-permute-start(bf16[320,128]{1,0:T(8,128)(2,1)S(1)} %get-tuple-element.69.share), channel_id=1, source_target_pairs={{0,16},{8,24},{16,0},{24,8},{1,17},{9,25},{17,1},{25,9},{2,18},{10... | collective-permute-start | bytes 245768 | tf_op jit(solution)/shard_map/ppermute | solution.py:662
  47.0 4.2 %collective-permute-start.11 = (bf16[320,128]{1,0:T(8,128)(2,1)S(1)}, bf16[320,128]{1,0:T(8,128)(2,1)S(1)}, u32[]{:S(2)}, u32[]{:S(2)}) collective-permute-start(bf16[320,128]{1,0:T(8,128)(2,1)S(1)} %get-tuple-element.69.share), channel_id=1, source_target_pairs={{0,8},{8,0},{16,24},{24,16},{1,9},{9,1},{17,25},{25,17},{2,10},{10... | collective-permute-start | bytes 245768 | tf_op jit(solution)/shard_map/ppermute | solution.py:662
  51.8 6.9 %collective-permute-start.14 = (bf16[1296,128]{1,0:T(8,128)(2,1)S(1)}, bf16[1296,128]{1,0:T(8,128)(2,1)S(1)}, u32[]{:S(2)}, u32[]{:S(2)}) collective-permute-start(bf16[1296,128]{1,0:T(8,128)(2,1)S(1)} %shard_map.55.rest_10_), channel_id=1, source_target_pairs={{0,1},{1,0},{2,3},{3,2},{4,5},{5,4},{6,7},{7,6},{8,9},{9,8},{10,11... | collective-permute-start | bytes 995336 | tf_op jit(solution)/shard_map/ppermute | solution.py:667

commit v7 on v6

--- a/solution.py
+++ b/solution.py
@@ -149,6 +149,20 @@
     return jnp.concatenate([found[j : j + 1] for j in range(blocks)], axis=1)
 
 
+def panels(lhs, rhs, emit):
+    width, n = lhs.shape[1], 0
+    for i in range(0, width, BLOCK):
+        panel = lax.dot_general(
+            lhs[:, i : i + BLOCK],
+            rhs[:, i:],
+            (((0,), (0,)), ((), ())),
+            preferred_element_type=F32,
+        )
+        for j in range(0, width - i, BLOCK):
+            emit(n, panel[:, j : j + BLOCK])
+            n += 1
+
+
 def spread(means, count, left_ref, right_ref, emit):
     centre = means[0]
     for mean in means[1:]:
@@ -165,26 +179,13 @@
             left_ref[at : at + 1, :] = lhs
             right_ref[at : at + 1, :] = rhs
     lhs, rhs = left_ref[...].astype(BF), right_ref[...].astype(BF)
-    for n, (i, j) in enumerate(pairs(lhs.shape[1])):
-        product = lax.dot_general(
-            lhs[:, i * BLOCK : (i + 1) * BLOCK],
-            rhs[:, j * BLOCK : (j + 1) * BLOCK],
-            (((0,), (0,)), ((), ())),
-            preferred_element_type=F32,
-        )
-        emit(n, product * float(count))
+    panels(lhs, rhs, lambda n, block: emit(n, block * float(count)))
     return centre
 
 
-def middle(dims, place, pool, far, near, w1_hbm, w2_hbm, *rest):
-    taps1, taps2, act1, slope1, act2, slope2, w1, w2, buf, sems = rest
+def middle(dims, place, pool, far, near, w1, w2, *rest):
+    taps1, taps2, act1, slope1, act2, slope2, buf = rest
     height, breadth, groups, limits = dims
-    loads = [
-        pltpu.make_async_copy(w1_hbm, w1, sems.at[0]),
-        pltpu.make_async_copy(w2_hbm, w2, sems.at[1]),
-    ]
-    for load in loads:
-        load.start()
     pitch = groups * 16
     left_core = place[0] == 0
     space = buf.shape[1] // height
@@ -198,15 +199,15 @@
         fold_row(taps1, r, buf, at, groups)
     low = 3 - place[2]
     inside = span(groups, low, low + limits[1])
-    loads[0].wait()
     for t in range(0, height - 2, 2):
         mask = pair_mask(inside, place, limits, t + 1)
         first_rows(
             lambda r: (taps1, t + r), w1, taps2, t, act1, slope1, t * pitch, groups, mask
         )
-    loads[1].wait()
-    for t in range(0, height - 4, 2):
-        second_rows(lambda r: (taps2, t + r), w2, act2, slope2, t * pitch, groups)
+        if t >= 2:
+            second_rows(
+                lambda r: (taps2, t - 2 + r), w2, act2, slope2, (t - 2) * pitch, groups
+            )
 
 
 def rim_taps(ref, rows, place, buf, groups):
@@ -222,11 +223,10 @@
 
 def front(dims, place, even, odd, taps1, taps2, act1, act2, w1, w2, *rest):
     (taps2b, act1b, slope1b, act2b, slope2b, keep, mine, sent) = rest[:8]
-    (rim, buf, gram, stat) = rest[8:]
+    (rim, buf, centred, stat) = rest[8:]
     height, breadth, groups, limits = dims
     pitch = groups * 16
     width = w1.shape[1]
-    blocks = width // BLOCK
     rows = [(odd, even, REACH - 2), (odd, even, REACH - 1), (even, odd, 0), (even, odd, 1)]
     rim_taps(rim, rows, place, buf, groups)
     low = 3 - place[2]
@@ -258,34 +258,27 @@
             for at in range(start, start + count, pitch):
                 total = total + ref[at : at + pitch, :]
         mean = jnp.sum(total * own, axis=0, keepdims=True) * (1.0 / cells)
-        centred = jnp.concatenate(
-            [
-                ((ref[at : at + pitch, :] - mean) * own).astype(BF)
-                for ref, start, count in parts
-                for at in range(start, start + count, pitch)
-            ],
-            axis=0,
-        )
         n = 0
-        for i in range(blocks):
-            panel = lax.dot_general(
-                centred[:, i * BLOCK : (i + 1) * BLOCK],
-                centred[:, i * BLOCK :],
-                (((0,), (0,)), ((), ())),
-                preferred_element_type=F32,
-            )
-            for j in range(i, blocks):
-                gram[layer, n * BLOCK : (n + 1) * BLOCK, :] = panel[
-                    :, (j - i) * BLOCK : (j - i + 1) * BLOCK
-                ]
-                n += 1
+        for ref, start, count in parts:
+            for at in range(start, start + count, pitch):
+                centred[layer, n : n + pitch, :] = ((ref[at : at + pitch, :] - mean) * own).astype(
+                    BF
+                )
+                n += pitch
         stat[layer] = jnp.zeros(stat.shape[1:], F32)
         put_mean(stat.at[layer, 0:EXTRA], mean, 2)
         put_mean(stat.at[layer, EXTRA : 2 * EXTRA], mean, 1)
     rows = keep.shape[0]
-    keep[...] = gram[place[0]]
+
+    def give(n, block):
+        sent[n * BLOCK : (n + 1) * BLOCK, :] = block.astype(BF)
+
+    def hold(n, block):
+        keep[n * BLOCK : (n + 1) * BLOCK, :] = block
+
+    for layer, emit in ((1 - place[0], give), (place[0], hold)):
+        panels(centred[layer], centred[layer], emit)
     mine[...] = stat[place[0], EXTRA : EXTRA + 8, :]
-    sent[0:rows, :] = gram[1 - place[0]].astype(BF)
     sent[rows:, :] = stat[1 - place[0], 0:EXTRA, :].astype(BF)
 
 
@@ -390,26 +383,31 @@
                 ref[j * BLOCK : (j + 1) * BLOCK, i * BLOCK : (i + 1) * BLOCK] = block.T
         means.append(get_mean(table[layer, packed:, :], blocks, 2))
     low = 2 - place[2]
-    inside = span(groups, low, low + limits[1])
-    tiles = [(act2r, slope2r, 0), (act2b, slope2b, 0)]
-    tiles += [(act2, slope2, t * pitch) for t in range(0, height - 4, 2)]
-    tiles += [(act2b, slope2b, step), (act2r, slope2r, step)]
-    for t, (act, slope, at) in enumerate(tiles):
+    inside2 = span(groups, low, low + limits[1])
+    tiles2 = [(act2r, slope2r, 0), (act2b, slope2b, 0)]
+    tiles2 += [(act2, slope2, t * pitch) for t in range(0, height - 4, 2)]
+    tiles2 += [(act2b, slope2b, step), (act2r, slope2r, step)]
+
+    def second(t):
+        act, slope, at = tiles2[t]
         centred = (act[at : at + step, :] - means[1]).astype(BF)
-        mask = wide(pair_mask(inside, place, limits, 2 * t - 2), 2 * BLOCK)
+        mask = wide(pair_mask(inside2, place, limits, 2 * t - 2), 2 * BLOCK)
         for lanes in halves(width):
             push = jnp.dot(centred, second_m[:, lanes], preferred_element_type=F32)
             grad = push * slope[at : at + step, lanes] * mask
             for r in range(2):
                 write_taps(taps2, 2 * t + r, grad[r * pitch : (r + 1) * pitch], groups, lanes)
+
     low = 1 - place[2]
-    inside = span(groups, low, low + limits[1])
-    tiles = [(act1b, slope1b, 0)]
-    tiles += [(act1, slope1, t * pitch) for t in range(0, height - 2, 2)]
-    tiles += [(act1b, slope1b, step)]
-    for t, (act, slope, at) in enumerate(tiles):
+    inside1 = span(groups, low, low + limits[1])
+    tiles1 = [(act1b, slope1b, 0)]
+    tiles1 += [(act1, slope1, t * pitch) for t in range(0, height - 2, 2)]
+    tiles1 += [(act1b, slope1b, step)]
+
+    def first(t):
+        act, slope, at = tiles1[t]
         centred = (act[at : at + step, :] - means[0]).astype(BF)
-        mask = wide(pair_mask(inside, place, limits, 2 * t - 1), 2 * BLOCK)
+        mask = wide(pair_mask(inside1, place, limits, 2 * t - 1), 2 * BLOCK)
         for lanes in halves(width):
             flow = conv(lambda r: (taps2, 2 * t + r), w2, groups, lanes) + jnp.dot(
                 centred, first_m[:, lanes], preferred_element_type=F32
@@ -417,28 +415,39 @@
             grad = flow * slope[at : at + step, lanes] * mask
             for r in range(2):
                 write_taps(taps1, 2 * t + r, grad[r * pitch : (r + 1) * pitch], groups, lanes)
-    for t in range(0, height, 2):
-        got = conv(lambda r: (taps1, t + r), w1, groups, slice(None))
+
+    def last(t):
+        got = conv(lambda r: (taps1, 2 * t + r), w1, groups, slice(None))
         for r in range(2):
-            at = (t + r) * pitch
-            for n in range(groups):
-                part = got[r * pitch + n * 16 : r * pitch + (n + 1) * 16]
-                for p in range(buf.shape[0]):
-                    lanes = slice(p * BLOCK, (p + 1) * BLOCK)
-                    buf[p, pl.ds(at + n, 16, stride=groups), :] = part[:, lanes]
+            at = (2 * t + r) * pitch
             for p in range(buf.shape[0]):
                 lanes = slice(p * BLOCK, (p + 1) * BLOCK)
-                out[t + r, :, lanes] = buf[p, at : at + breadth, :]
-
-
-def edges(place, pool_hbm, pool, far, near, sem):
-    load = pltpu.make_async_copy(pool_hbm, pool, sem)
-    load.start()
-    load.wait()
-    breadth = pool.shape[1]
+                for n in range(groups):
+                    part = got[r * pitch + n * 16 : r * pitch + (n + 1) * 16, lanes]
+                    buf[p, pl.ds(at + n, 16, stride=groups), :] = part
+                out[2 * t + r, :, lanes] = buf[p, at : at + breadth, :]
+
+    for t in range(len(tiles2)):
+        second(t)
+    for t in range(len(tiles1)):
+        first(t)
+    for t in range(height // 2):
+        last(t)
+
+
+def edges(place, pool_hbm, far, near, strips, sems):
+    breadth = pool_hbm.shape[1]
+    ends = (0, breadth - 8)
+    loads = [
+        pltpu.make_async_copy(pool_hbm.at[:, pl.ds(at, 8), :], strips.at[n], sems.at[n])
+        for n, at in enumerate(ends)
+    ]
+    for load in loads:
+        load.start()
+    for load in loads:
+        load.wait()
     left_core = place[0] == 0
-    left = pool[:, 0:REACH, :]
-    right = pool[:, breadth - REACH : breadth, :]
+    left, right = strips[0, :, 0:REACH, :], strips[1, :, 8 - REACH :, :]
     far[...] = jnp.where(left_core, left, right).astype(BF)
     near[...] = jnp.where(left_core, right, left).astype(BF)
 
@@ -522,18 +531,23 @@
     cross = cross + [(j, i) for i, j in cross]
 
     rim = shape((height, REACH, depth), BF)
-    pool, far, near = call(
+    far, near = call(
         edges,
         [place, pool_input],
-        [shape(pool_input.shape, F32)] + [rim] * 2,
-        [pltpu.SemaphoreType.DMA],
+        [rim] * 2,
+        [pltpu.VMEM((2, height, 8, depth), F32), pltpu.SemaphoreType.DMA((2,))],
+        flops=4 * 10**9,
         far=(1,),
     )
     far = lax.ppermute(far, "tile", cross)
     near = lax.ppermute(near, "tile", swap)
     band = shape((REACH, breadth + 2 * REACH, depth), BF)
     even, odd = call(
-        bands, [place, pool, far, near], [band] * 2, [pltpu.VMEM((breadth + 2 * REACH, depth), F32)]
+        bands,
+        [place, pool_input, far, near],
+        [band] * 2,
+        [pltpu.VMEM((breadth + 2 * REACH, depth), F32)],
+        flops=6 * 10**9,
     )
 
     def couples(start):
@@ -544,6 +558,8 @@
     odd = lax.ppermute(odd, "grp", couples(1))
 
     packed = len(pairs(width)) * BLOCK
+    w1 = weight_first.reshape(-1, width)
+    w2 = weight_second.reshape(-1, width)
     space = (fold * 15 + fold + 2 + 7) // 8 * 8
 
     def maps(rows):
@@ -552,18 +568,15 @@
     def cost(rows_first, rows_second):
         return 2 * 9 * width * pitch * (rows_first * depth + rows_second * width)
 
-    taps1, taps2, act1, slope1, act2, slope2, w1, w2 = call(
+    taps1, taps2, act1, slope1, act2, slope2 = call(
         functools.partial(middle, dims),
-        [place, pool, far, near]
-        + [weight_first.reshape(-1, width), weight_second.reshape(-1, width)],
+        [place, pool_input, far, near, w1, w2],
         [shape((height * wider, depth), BF), shape(((height - 2) * wider, width), BF)]
         + maps(height - 2)
-        + maps(height - 4)
-        + [shape((9 * depth, width), BF), shape((9 * width, width), BF)],
-        [pltpu.VMEM((depth // BLOCK, height * space, BLOCK), F32), pltpu.SemaphoreType.DMA((2,))],
+        + maps(height - 4),
+        [pltpu.VMEM((depth // BLOCK, height * space, BLOCK), F32)],
         flops=cost(height - 2, height - 4),
         limit=24,
-        far=(4, 5),
     )
     taps2b, act1b, slope1b, act2b, slope2b, keep, mine, sent = call(
         functools.partial(front, dims),
@@ -579,7 +592,7 @@
         [
             pltpu.VMEM((4 * wider, depth), BF),
             pltpu.VMEM((depth // BLOCK, 4 * space, BLOCK), F32),
-            pltpu.VMEM((2, packed, BLOCK), F32),
+            pltpu.VMEM((2, height * pitch, width), BF),
             pltpu.VMEM((2, 2 * EXTRA, BLOCK), F32),
         ],
         flops=cost(4, 4),

time: 67.2 us -> 66.9 us (level)
  Pallas kernels: 31.5 us -> 29.7 us
  waiting for transfers between devices: 14.5 us -> 15.8 us
    pallas_call x13, Pallas kernels: 31.5 us -> 29.7 us  [call(): pl.pallas_call(body, out_shape=tuple(outs), in_specs=[HBM if n in far els...]
    ppermute x3, starting transfers between devices: 5.18 us -> 6.37 us  [local(): lax.ppermute(sents[k - 1], 'grp', [(i, i ^ k) for i in range(groups)])]
    ppermute x3, waiting for transfers between devices: 3.07 us -> 4.17 us  [local(): lax.ppermute(sents[k - 1], 'grp', [(i, i ^ k) for i in range(groups)])]
    ppermute x3, starting transfers between devices: 4.3 us -> 3.61 us  [local(): lax.ppermute(sent, 'tile', [(i, i ^ 2 * k) for i in range(tiles)])]
  transfers between devices with their start and end apart: 15 -> 15, of which waited for: 9 -> 9; matrix products, arithmetic and copies ran while one was open for 0% -> 0% of each run, Pallas kernels for 20% -> 17%
where the time goes in v7:
time: 66.9 us; the launch traced here: 66.8 us
  Pallas kernels  29.7 us (44%)
  starting transfers between devices  21 us (31%)
  waiting for transfers between devices  15.8 us (24%)
    pallas_call x13, Pallas kernels, call(): pl.pallas_call(body, out_shape=tuple(outs), in_specs=[HBM if n in far els...  29.7 us
    ppermute x3, waiting for transfers between devices, local(): lax.ppermute(sent, 'tile', [(i, i ^ 2 * k) for i in range(tiles)])  6.43 us
    ppermute x3, starting transfers between devices, local(): lax.ppermute(sents[k - 1], 'grp', [(i, i ^ k) for i in range(groups)])  6.37 us
    ppermute x1, starting transfers between devices, local(): far = lax.ppermute(far, 'tile', cross)  4.58 us
    ppermute x3, waiting for transfers between devices, local(): lax.ppermute(sents[k - 1], 'grp', [(i, i ^ k) for i in range(groups)])  4.17 us
    ppermute x3, starting transfers between devices, local(): lax.ppermute(sent, 'tile', [(i, i ^ 2 * k) for i in range(tiles)])  3.61 us
    ppermute x3, starting transfers between devices, local(): lax.ppermute(share, 'grp', [(i, i ^ k) for i in range(groups)])  2.71 us
    ppermute x3, waiting for transfers between devices, local(): lax.ppermute(share, 'grp', [(i, i ^ k) for i in range(groups)])  2.55 us
  transfers between devices with their start and end apart: 15, of which 9 were waited for; matrix products, arithmetic and copies ran while one was open for 0% of the time, Pallas kernels for 17%

profile of v7, /device:TPU:1, one launch (start us, length us, event | category | flops | bytes accessed | tf_op | source)
XLA Modules:
  0.0 66.8 jit_solution(18023710794260853574)
XLA Ops:
  0.0 0.1 pad_add_fusion.place
  0.1 1.4 %shard_map.46 = (bf16[8,4,256]{2,1,0:T(4,128)(2,1)S(1)}, bf16[8,4,256]{2,1,0:T(4,128)(2,1)S(1)}) custom-call(s32[4]{0:T(128)S(1)} %pad_add_fusion.place, f32[8,64,256]{2,1,0:T(8,128)} %pool.3), custom_call_target="tpu_custom_call" | custom-call | flops 4000000000 | bytes 557072 | tf_op jit(solution)/shard_map/pallas_call | solution.py:498
  1.5 4.6 %collective-permute-start = (bf16[8,4,256]{2,1,0:T(4,128)(2,1)S(1)}, bf16[8,4,256]{2,1,0:T(4,128)(2,1)S(1)}, u32[]{:S(2)}, u32[]{:S(2)}) collective-permute-start(bf16[8,4,256]{2,1,0:T(4,128)(2,1)S(1)} %get-tuple-element.35), channel_id=1, source_target_pairs={{1,2},{3,4},{5,6},{2,1},{4,3},{6,5},{9,10},{11,12},{13,14},{10,9},... | collective-permute-start | bytes 49160 | tf_op jit(solution)/shard_map/ppermute | solution.py:542
  6.1 0.0 slice-start
  6.1 0.0 slice-start.1
  6.2 0.0 copy-start
  6.2 0.1 collective-permute-start.1
  6.2 1.3 %collective-permute-done.far = bf16[8,4,256]{2,1,0:T(4,128)(2,1)S(1)} collective-permute-done((bf16[8,4,256]{2,1,0:T(4,128)(2,1)S(1)}, bf16[8,4,256]{2,1,0:T(4,128)(2,1)S(1)}, u32[]{:S(2)}, u32[]{:S(2)}) %collective-permute-start) | collective-permute-done | bytes 16416 | tf_op jit(solution)/shard_map/ppermute | solution.py:542
  7.5 0.0 collective-permute-done.1.near
  7.5 0.6 shard_map.48
  8.2 1.3 %collective-permute-start.2 = (bf16[4,72,256]{2,1,0:T(8,128)(2,1)S(1)}, bf16[4,72,256]{2,1,0:T(8,128)(2,1)S(1)}, u32[]{:S(2)}, u32[]{:S(2)}) collective-permute-start(bf16[4,72,256]{2,1,0:T(8,128)(2,1)S(1)} %get-tuple-element.39), channel_id=1, source_target_pairs={{0,8},{16,24},{8,0},{24,16},{1,9},{17,25},{9,1},{25,17},{2,10},{18... | collective-permute-start | bytes 442376 | tf_op jit(solution)/shard_map/ppermute | solution.py:557
  9.4 0.7 collective-permute-start.3
  10.1 4.2 %shard_map.47 = (bf16[896,256]{1,0:T(8,128)(2,1)S(1)}, bf16[672,512]{1,0:T(8,128)(2,1)S(1)}, f32[480,512]{1,0:T(8,128)S(1)}, f32[480,512]{1,0:T(8,128)S(1)}, f32...) custom-call(s32[4]{0:T(128)S(1)} %pad_add_fusion.place, f32[8,64,256]{2,1,0:T(8,128)S(1)} %copy-done.2, ...), custom_call_target="tpu_custom_call" | custom-call | flops 2642411520 | bytes 12058640 | tf_op jit(solution)/shard_map/pallas_call | solution.py:498
  14.4 0.0 collective-permute-done.2.even
  14.4 0.0 collective-permute-done.3.odd
  14.4 0.0 copy-start.1
  14.4 4.8 %shard_map.49 = (bf16[448,512]{1,0:T(8,128)(2,1)S(1)}, f32[320,512]{1,0:T(8,128)S(1)}, f32[320,512]{1,0:T(8,128)S(1)}, f32[320,512]{1,0:T(8,128)S(1)}, f32[320,5...) custom-call(s32[4]{0:T(128)S(1)} %pad_add_fusion.place, ...), custom_call_target="tpu_custom_call" | custom-call | flops 2264924160 | bytes 14229520 | tf_op jit(solution)/shard_map/pallas_call | solution.py:498
  19.2 0.4 collective-permute-start.4
  19.6 1.3 %collective-permute-done.4.got = bf16[1296,128]{1,0:T(8,128)(2,1)S(1)} collective-permute-done((bf16[1296,128]{1,0:T(8,128)(2,1)S(1)}, bf16[1296,128]{1,0:T(8,128)(2,1)S(1)}, u32[]{:S(2)}, u32[]{:S(2)}) %collective-permute-start.4) | collective-permute-done | bytes 331808 | tf_op jit(solution)/shard_map/ppermute | solution.py:647
  20.9 0.9 %shard_map.51 = (f32[320,128]{1,0:T(8,128)S(1)}, f32[8,128]{1,0:T(8,128)S(1)}, bf16[336,128]{1,0:T(8,128)(2,1)S(1)}, bf16[336,128]{1,0:T(8,128)(2,1)S(1)}, bf16[336,128]{1,0:T(8,128)(2,1)S(1)}) custom-call(s32[4]{0:T(128)S(1)} %pad_add_fusion.place, f32[1280,128]{1,0:T(8,128)S(1)} %get-tuple-element.52.keep, f32[8,128]{1,0:T(8,128)S(1)} %get-tuple-element.53.mine, ...), custom_call_target="tpu_custom_call" | custom-call | bytes 1417232 | tf_op jit(solution)/shard_map/pallas_call | solution.py:498
  21.8 5.1 %collective-permute-start.5 = (bf16[336,128]{1,0:T(8,128)(2,1)S(1)}, bf16[336,128]{1,0:T(8,128)(2,1)S(1)}, u32[]{:S(2)}, u32[]{:S(2)}) collective-permute-start(bf16[336,128]{1,0:T(8,128)(2,1)S(1)} %get-tuple-element.57), channel_id=1, source_target_pairs={{0,8},{8,0},{16,24},{24,16},{1,9},{9,1},{17,25},{25,17},{2,10},{10... | collective-permute-start | bytes 258056 | tf_op jit(solution)/shard_map/ppermute | solution.py:655
  26.9 0.0 collective-permute-start.6
  26.9 1.3 %collective-permute-start.7 = (bf16[336,128]{1,0:T(8,128)(2,1)S(1)}, bf16[336,128]{1,0:T(8,128)(2,1)S(1)}, u32[]{:S(2)}, u32[]{:S(2)}) collective-permute-start(bf16[336,128]{1,0:T(8,128)(2,1)S(1)} %get-tuple-element.59), channel_id=1, source_target_pairs={{0,24},{8,16},{16,8},{24,0},{1,25},{9,17},{17,9},{25,1},{2,26},{10... | collective-permute-start | bytes 258056 | tf_op jit(solution)/shard_map/ppermute | solution.py:655
  28.1 1.3 %collective-permute-done.5.rest_0_ = bf16[336,128]{1,0:T(8,128)(2,1)S(1)} collective-permute-done((bf16[336,128]{1,0:T(8,128)(2,1)S(1)}, bf16[336,128]{1,0:T(8,128)(2,1)S(1)}, u32[]{:S(2)}, u32[]{:S(2)}) %collective-permute-start.5) | collective-permute-done | bytes 86048 | tf_op jit(solution)/shard_map/ppermute | solution.py:655
  29.4 0.8 %collective-permute-done.6.rest_1_ = bf16[336,128]{1,0:T(8,128)(2,1)S(1)} collective-permute-done((bf16[336,128]{1,0:T(8,128)(2,1)S(1)}, bf16[336,128]{1,0:T(8,128)(2,1)S(1)}, u32[]{:S(2)}, u32[]{:S(2)}) %collective-permute-start.6) | collective-permute-done | bytes 86048 | tf_op jit(solution)/shard_map/ppermute | solution.py:655
  30.2 2.1 %collective-permute-done.7.rest_2_ = bf16[336,128]{1,0:T(8,128)(2,1)S(1)} collective-permute-done((bf16[336,128]{1,0:T(8,128)(2,1)S(1)}, bf16[336,128]{1,0:T(8,128)(2,1)S(1)}, u32[]{:S(2)}, u32[]{:S(2)}) %collective-permute-start.7) | collective-permute-done | bytes 86048 | tf_op jit(solution)/shard_map/ppermute | solution.py:655
  32.3 0.9 %shard_map.52 = (f32[320,128]{1,0:T(8,128)S(1)}, f32[8,128]{1,0:T(8,128)S(1)}, bf16[336,128]{1,0:T(8,128)(2,1)S(1)}) custom-call(s32[4]{0:T(128)S(1)} %pad_add_fusion.place, f32[320,128]{1,0:T(8,128)S(1)} %get-tuple-element.55.share, f32[8,128]{1,0:T(8,128)S(1)} %get-tuple-element.56.mine, bf16[336,128]{1,0:T(8,128)(2,1)S(1)} %collective-permute-done.5.rest_0_, ...), custom_call_target="tpu_custom_call" | custom-call | bytes 679952 | tf_op jit(solution)/shard_map/pallas_call | solution.py:498
  33.2 3.1 %collective-permute-start.10 = (bf16[336,128]{1,0:T(8,128)(2,1)S(1)}, bf16[336,128]{1,0:T(8,128)(2,1)S(1)}, u32[]{:S(2)}, u32[]{:S(2)}) collective-permute-start(bf16[336,128]{1,0:T(8,128)(2,1)S(1)} %get-tuple-element.62), channel_id=1, source_target_pairs={{0,6},{1,7},{2,4},{3,5},{4,2},{5,3},{6,0},{7,1},{8,14},{9,15},{10,... | collective-permute-start | bytes 258056 | tf_op jit(solution)/shard_map/ppermute | solution.py:665
  36.3 0.0 collective-permute-start.9
  36.3 0.5 collective-permute-start.8
  36.8 0.8 %shard_map.53.rest_3_ = f32[320,128]{1,0:T(8,128)S(1)} custom-call(s32[4]{0:T(128)S(1)} %pad_add_fusion.place, f32[2,512,512]{2,1,0:T(8,128)S(1)} %copy-done.1), custom_call_target="tpu_custom_call" | custom-call | flops 200000000 | bytes 2261008 | tf_op jit(solution)/shard_map/pallas_call | solution.py:498
  37.6 0.9 %collective-permute-done.10.rest_2_ = bf16[336,128]{1,0:T(8,128)(2,1)S(1)} collective-permute-done((bf16[336,128]{1,0:T(8,128)(2,1)S(1)}, bf16[336,128]{1,0:T(8,128)(2,1)S(1)}, u32[]{:S(2)}, u32[]{:S(2)}) %collective-permute-start.10) | collective-permute-done | bytes 86048 | tf_op jit(solution)/shard_map/ppermute | solution.py:665
  38.5 5.5 %collective-permute-done.9.rest_1_ = bf16[336,128]{1,0:T(8,128)(2,1)S(1)} collective-permute-done((bf16[336,128]{1,0:T(8,128)(2,1)S(1)}, bf16[336,128]{1,0:T(8,128)(2,1)S(1)}, u32[]{:S(2)}, u32[]{:S(2)}) %collective-permute-start.9) | collective-permute-done | bytes 86048 | tf_op jit(solution)/shard_map/ppermute | solution.py:665
  44.1 0.0 collective-permute-done.8.rest_0_
  44.1 0.9 %shard_map.54 = (bf16[320,128]{1,0:T(8,128)(2,1)S(1)}, bf16[16,128]{1,0:T(8,128)(2,1)S(1)}) custom-call(s32[4]{0:T(128)S(1)} %pad_add_fusion.place, f32[320,128]{1,0:T(8,128)S(1)} %get-tuple-element.60.share, f32[8,128]{1,0:T(8,128)S(1)} %get-tuple-element.61.mine, bf16[336,128]{1,0:T(8,128)(2,1)S(1)} %collective-permute-done.8.rest_0_, ...), custom_call_target="tpu_custom_call" | custom-call | bytes 675856 | tf_op jit(solution)/shard_map/pallas_call | solution.py:498
  45.0 1.3 %collective-permute-start.13 = (bf16[320,128]{1,0:T(8,128)(2,1)S(1)}, bf16[320,128]{1,0:T(8,128)(2,1)S(1)}, u32[]{:S(2)}, u32[]{:S(2)}) collective-permute-start(bf16[320,128]{1,0:T(8,128)(2,1)S(1)} %get-tuple-element.63.share), channel_id=1, source_target_pairs={{0,24},{8,16},{16,8},{24,0},{1,25},{9,17},{17,9},{25,1},{2,26},{10... | collective-permute-start | bytes 245768 | tf_op jit(solution)/shard_map/ppermute | solution.py:675
  46.3 0.0 collective-permute-start.12
  46.3 1.4 %collective-permute-start.11 = (bf16[320,128]{1,0:T(8,128)(2,1)S(1)}, bf16[320,128]{1,0:T(8,128)(2,1)S(1)}, u32[]{:S(2)}, u32[]{:S(2)}) collective-permute-start(bf16[320,128]{1,0:T(8,128)(2,1)S(1)} %get-tuple-element.63.share), channel_id=1, source_target_pairs={{0,8},{8,0},{16,24},{24,16},{1,9},{9,1},{17,25},{25,17},{2,10},{10... | collective-permute-start | bytes 245768 | tf_op jit(solution)/shard_map/ppermute | solution.py:675
  47.7 1.1 %shard_map.57.rest_13_ = bf16[4608,256]{1,0:T(8,128)(2,1)S(1)} custom-call(bf16[9,256,512]{2,1,0:T(8,128)(2,1)S(1)} %bitcast.16), custom_call_target="tpu_custom_call" | custom-call | flops 2000000000 | bytes 4718592 | tf_op jit(solution)/shard_map/pallas_call | solution.py:498
  48.8 0.5 collective-permute-done.13.rest_2_
  49.3 2.1 %collective-permute-done.12.rest_1_ = bf16[320,128]{1,0:T(8,128)(2,1)S(1)} collective-permute-done((bf16[320,128]{1,0:T(8,128)(2,1)S(1)}, bf16[320,128]{1,0:T(8,128)(2,1)S(1)}, u32[]{:S(2)}, u32[]{:S(2)}) %collective-permute-start.12) | collective-permute-done | bytes 81952 | tf_op jit(solution)/shard_map/ppermute | solution.py:675
  51.3 0.0 collective-permute-done.11.rest_0_
  51.3 0.6 shard_map.55.rest_10_
  51.9 1.3 %collective-permute-start.14 = (bf16[1296,128]{1,0:T(8,128)(2,1)S(1)}, bf16[1296,128]{1,0:T(8,128)(2,1)S(1)}, u32[]{:S(2)}, u32[]{:S(2)}) collective-permute-start(bf16[1296,128]{1,0:T(8,128)(2,1)S(1)} %shard_map.55.rest_10_), channel_id=1, source_target_pairs={{0,1},{1,0},{2,3},{3,2},{4,5},{5,4},{6,7},{7,6},{8,9},{9,8},{10,11... | collective-permute-start | bytes 995336 | tf_op jit(solution)/shard_map/ppermute | solution.py:680
  53.2 1.7 %shard_map.56.rest_12_ = bf16[4608,512]{1,0:T(8,128)(2,1)S(1)} custom-call(bf16[9,512,512]{2,1,0:T(8,128)(2,1)S(1)} %bitcast.12), custom_call_target="tpu_custom_call" | custom-call | flops 2000000000 | bytes 9437184 | tf_op jit(solution)/shard_map/pallas_call | solution.py:498
  54.9 3.5 %shard_map.50 = (f32[320,512]{1,0:T(8,128)S(1)}, f32[320,512]{1,0:T(8,128)S(1)}) custom-call(s32[4]{0:T(128)S(1)} %pad_add_fusion.place, bf16[4,72,256]{2,1,0:T(8,128)(2,1)S(1)} %collective-permute-done.2.even, bf16[4,72,256]{2,1,0:T(8,128)(2,1)S(1)} %collective-permute-done.3.odd, bf16[448,512]{1,0:T(8,128)(2,1)S(1)} %get-tuple-element.49.taps2b, ...), custom_call_target="tpu_custom_call" | custom-call | flops 2264924160 | bytes 9142288 | tf_op jit(solution)/shard_map/pallas_call | solution.py:498
  58.5 0.0 collective-permute-done.14.rest_11_
  58.5 8.2 %shard_map.58 = f32[8,64,256]{2,1,0:T(8,128)} custom-call(s32[4]{0:T(128)S(1)} %pad_add_fusion.place, f32[480,512]{1,0:T(8,128)S(1)} %get-tuple-element.37.act1.rest_0_, f32[480,512]{1,0:T(8,128)S(1)} %get-tuple-element.38.rest_1_, f32[320,512]{1,0:T(8,128)S(1)} %get-tuple-element.44.rest_2_, f32[320,512]{1,0:T(8,128)S(1)} %get-tuple-element.45.rest_3_, ...), custom_call_target="tpu_custom_call" | custom-call | flops 5284823040 | bytes 15474704 | tf_op jit(solution)/shard_map/pallas_call | solution.py:498
  (7 shorter events, 0.0 us)
Async XLA Ops:
  0.1 7.5 %copy-start.2 = (f32[8,64,256]{2,1,0:T(8,128)S(1)}, f32[8,64,256]{2,1,0:T(8,128)}, u32[]{:S(2)}) copy-start(f32[8,64,256]{2,1,0:T(8,128)} %pool.3) | copy-start | bytes 1572868
  1.5 6.0 %collective-permute-start = (bf16[8,4,256]{2,1,0:T(4,128)(2,1)S(1)}, bf16[8,4,256]{2,1,0:T(4,128)(2,1)S(1)}, u32[]{:S(2)}, u32[]{:S(2)}) collective-permute-start(bf16[8,4,256]{2,1,0:T(4,128)(2,1)S(1)} %get-tuple-element.35), channel_id=1, source_target_pairs={{1,2},{3,4},{5,6},{2,1},{4,3},{6,5},{9,10},{11,12},{13,14},{10,9},... | collective-permute-start | bytes 49160 | tf_op jit(solution)/shard_map/ppermute | solution.py:542
  6.1 4.0 %slice-start = ((s8[4718592]{0:T(1024)(128)(4,1)}), s8[4194304]{0:T(1024)(128)(4,1)S(1)}, s32[]{:S(2)}) async-start(s8[4718592]{0:T(1024)(128)(4,1)} %bitcast.8), calls=%async_computation | async-start | bytes 8388608
  6.1 4.0 %slice-start.1 = ((s8[4718592]{0:T(1024)(128)(4,1)}), s8[524288]{0:T(1024)(128)(4,1)S(1)}, s32[]{:S(2)}) async-start(s8[4718592]{0:T(1024)(128)(4,1)} %bitcast.8), calls=%async_computation.1 | async-start | bytes 1048576
  6.2 4.0 %copy-start = (bf16[3,3,256,512]{3,2,1,0:T(8,128)(2,1)S(1)}, bf16[3,3,256,512]{3,2,1,0:T(8,128)(2,1)}, u32[]{:S(2)}) copy-start(bf16[3,3,256,512]{3,2,1,0:T(8,128)(2,1)} %param.5) | copy-start | bytes 7077892
  6.2 1.4 %collective-permute-start.1 = (bf16[8,4,256]{2,1,0:T(4,128)(2,1)S(1)}, bf16[8,4,256]{2,1,0:T(4,128)(2,1)S(1)}, u32[]{:S(2)}, u32[]{:S(2)}) collective-permute-start(bf16[8,4,256]{2,1,0:T(4,128)(2,1)S(1)} %get-tuple-element.36), channel_id=1, source_target_pairs={{0,1},{1,0},{2,3},{3,2},{4,5},{5,4},{6,7},{7,6},{8,9},{9,8},{10,11... | collective-permute-start | bytes 49160 | tf_op jit(solution)/shard_map/ppermute | solution.py:543
  8.2 6.2 %collective-permute-start.2 = (bf16[4,72,256]{2,1,0:T(8,128)(2,1)S(1)}, bf16[4,72,256]{2,1,0:T(8,128)(2,1)S(1)}, u32[]{:S(2)}, u32[]{:S(2)}) collective-permute-start(bf16[4,72,256]{2,1,0:T(8,128)(2,1)S(1)} %get-tuple-element.39), channel_id=1, source_target_pairs={{0,8},{16,24},{8,0},{24,16},{1,9},{17,25},{9,1},{25,17},{2,10},{18... | collective-permute-start | bytes 442376 | tf_op jit(solution)/shard_map/ppermute | solution.py:557
  9.4 5.0 %collective-permute-start.3 = (bf16[4,72,256]{2,1,0:T(8,128)(2,1)S(1)}, bf16[4,72,256]{2,1,0:T(8,128)(2,1)S(1)}, u32[]{:S(2)}, u32[]{:S(2)}) collective-permute-start(bf16[4,72,256]{2,1,0:T(8,128)(2,1)S(1)} %get-tuple-element.40), channel_id=1, source_target_pairs={{8,16},{16,8},{9,17},{17,9},{10,18},{18,10},{11,19},{19,11},{12,20... | collective-permute-start | bytes 442376 | tf_op jit(solution)/shard_map/ppermute | solution.py:558
  14.4 22.4 %copy-start.1 = (f32[2,512,512]{2,1,0:T(8,128)S(1)}, f32[2,512,512]{2,1,0:T(8,128)}, u32[]{:S(2)}) copy-start(f32[2,512,512]{2,1,0:T(8,128)} %targets.1) | copy-start | bytes 6291460
  19.2 1.7 %collective-permute-start.4 = (bf16[1296,128]{1,0:T(8,128)(2,1)S(1)}, bf16[1296,128]{1,0:T(8,128)(2,1)S(1)}, u32[]{:S(2)}, u32[]{:S(2)}) collective-permute-start(bf16[1296,128]{1,0:T(8,128)(2,1)S(1)} %get-tuple-element.54), channel_id=1, source_target_pairs={{0,1},{1,0},{2,3},{3,2},{4,5},{5,4},{6,7},{7,6},{8,9},{9,8},{10,11... | collective-permute-start | bytes 995336 | tf_op jit(solution)/shard_map/ppermute | solution.py:647
  21.8 7.6 %collective-permute-start.5 = (bf16[336,128]{1,0:T(8,128)(2,1)S(1)}, bf16[336,128]{1,0:T(8,128)(2,1)S(1)}, u32[]{:S(2)}, u32[]{:S(2)}) collective-permute-start(bf16[336,128]{1,0:T(8,128)(2,1)S(1)} %get-tuple-element.57), channel_id=1, source_target_pairs={{0,8},{8,0},{16,24},{24,16},{1,9},{9,1},{17,25},{25,17},{2,10},{10... | collective-permute-start | bytes 258056 | tf_op jit(solution)/shard_map/ppermute | solution.py:655
  26.9 3.3 %collective-permute-start.6 = (bf16[336,128]{1,0:T(8,128)(2,1)S(1)}, bf16[336,128]{1,0:T(8,128)(2,1)S(1)}, u32[]{:S(2)}, u32[]{:S(2)}) collective-permute-start(bf16[336,128]{1,0:T(8,128)(2,1)S(1)} %get-tuple-element.58), channel_id=1, source_target_pairs={{0,16},{8,24},{16,0},{24,8},{1,17},{9,25},{17,1},{25,9},{2,18},{10... | collective-permute-start | bytes 258056 | tf_op jit(solution)/shard_map/ppermute | solution.py:655
  26.9 5.4 %collective-permute-start.7 = (bf16[336,128]{1,0:T(8,128)(2,1)S(1)}, bf16[336,128]{1,0:T(8,128)(2,1)S(1)}, u32[]{:S(2)}, u32[]{:S(2)}) collective-permute-start(bf16[336,128]{1,0:T(8,128)(2,1)S(1)} %get-tuple-element.59), channel_id=1, source_target_pairs={{0,24},{8,16},{16,8},{24,0},{1,25},{9,17},{17,9},{25,1},{2,26},{10... | collective-permute-start | bytes 258056 | tf_op jit(solution)/shard_map/ppermute | solution.py:655
  33.2 5.3 %collective-permute-start.10 = (bf16[336,128]{1,0:T(8,128)(2,1)S(1)}, bf16[336,128]{1,0:T(8,128)(2,1)S(1)}, u32[]{:S(2)}, u32[]{:S(2)}) collective-permute-start(bf16[336,128]{1,0:T(8,128)(2,1)S(1)} %get-tuple-element.62), channel_id=1, source_target_pairs={{0,6},{1,7},{2,4},{3,5},{4,2},{5,3},{6,0},{7,1},{8,14},{9,15},{10,... | collective-permute-start | bytes 258056 | tf_op jit(solution)/shard_map/ppermute | solution.py:665
  36.3 7.8 %collective-permute-start.9 = (bf16[336,128]{1,0:T(8,128)(2,1)S(1)}, bf16[336,128]{1,0:T(8,128)(2,1)S(1)}, u32[]{:S(2)}, u32[]{:S(2)}) collective-permute-start(bf16[336,128]{1,0:T(8,128)(2,1)S(1)} %get-tuple-element.62), channel_id=1, source_target_pairs={{0,4},{1,5},{2,6},{3,7},{4,0},{5,1},{6,2},{7,3},{8,12},{9,13},{10,... | collective-permute-start | bytes 258056 | tf_op jit(solution)/shard_map/ppermute | solution.py:665
  36.3 7.8 %collective-permute-start.8 = (bf16[336,128]{1,0:T(8,128)(2,1)S(1)}, bf16[336,128]{1,0:T(8,128)(2,1)S(1)}, u32[]{:S(2)}, u32[]{:S(2)}) collective-permute-start(bf16[336,128]{1,0:T(8,128)(2,1)S(1)} %get-tuple-element.62), channel_id=1, source_target_pairs={{0,2},{1,3},{2,0},{3,1},{4,6},{5,7},{6,4},{7,5},{8,10},{9,11},{10,... | collective-permute-start | bytes 258056 | tf_op jit(solution)/shard_map/ppermute | solution.py:665
  45.0 4.3 %collective-permute-start.13 = (bf16[320,128]{1,0:T(8,128)(2,1)S(1)}, bf16[320,128]{1,0:T(8,128)(2,1)S(1)}, u32[]{:S(2)}, u32[]{:S(2)}) collective-permute-start(bf16[320,128]{1,0:T(8,128)(2,1)S(1)} %get-tuple-element.63.share), channel_id=1, source_target_pairs={{0,24},{8,16},{16,8},{24,0},{1,25},{9,17},{17,9},{25,1},{2,26},{10... | collective-permute-start | bytes 245768 | tf_op jit(solution)/shard_map/ppermute | solution.py:675
  46.3 5.0 %collective-permute-start.12 = (bf16[320,128]{1,0:T(8,128)(2,1)S(1)}, bf16[320,128]{1,0:T(8,128)(2,1)S(1)}, u32[]{:S(2)}, u32[]{:S(2)}) collective-permute-start(bf16[320,128]{1,0:T(8,128)(2,1)S(1)} %get-tuple-element.63.share), channel_id=1, source_target_pairs={{0,16},{8,24},{16,0},{24,8},{1,17},{9,25},{17,1},{25,9},{2,18},{10... | collective-permute-start | bytes 245768 | tf_op jit(solution)/shard_map/ppermute | solution.py:675
  46.3 5.0 %collective-permute-start.11 = (bf16[320,128]{1,0:T(8,128)(2,1)S(1)}, bf16[320,128]{1,0:T(8,128)(2,1)S(1)}, u32[]{:S(2)}, u32[]{:S(2)}) collective-permute-start(bf16[320,128]{1,0:T(8,128)(2,1)S(1)} %get-tuple-element.63.share), channel_id=1, source_target_pairs={{0,8},{8,0},{16,24},{24,16},{1,9},{9,1},{17,25},{25,17},{2,10},{10... | collective-permute-start | bytes 245768 | tf_op jit(solution)/shard_map/ppermute | solution.py:675
  51.9 6.6 %collective-permute-start.14 = (bf16[1296,128]{1,0:T(8,128)(2,1)S(1)}, bf16[1296,128]{1,0:T(8,128)(2,1)S(1)}, u32[]{:S(2)}, u32[]{:S(2)}) collective-permute-start(bf16[1296,128]{1,0:T(8,128)(2,1)S(1)} %shard_map.55.rest_10_), channel_id=1, source_target_pairs={{0,1},{1,0},{2,3},{3,2},{4,5},{5,4},{6,7},{7,6},{8,9},{9,8},{10,11... | collective-permute-start | bytes 995336 | tf_op jit(solution)/shard_map/ppermute | solution.py:680

commit v8 on v7

--- a/solution.py
+++ b/solution.py
@@ -16,7 +16,6 @@
 BF = jnp.bfloat16
 F32 = jnp.float32
 VMEM = pl.BlockSpec(memory_space=pltpu.VMEM)
-SMEM = pl.BlockSpec(memory_space=pltpu.SMEM)
 HBM = pl.BlockSpec(memory_space=pltpu.HBM)
 MIB = 2**20
 
@@ -487,7 +486,18 @@
     goal[...] = full[pl.ds(pl.multiple_of(place[3] * chunk, 16), chunk), :]
 
 
+def locate(height, breadth):
+    row, tile = lax.axis_index("grp"), lax.axis_index("tile")
+    return tile & 1, row * height, tile * breadth, row
+
+
 def call(body, ins, outs, scratch, flops=0, limit=None, far=()):
+    if isinstance(ins[0], tuple):
+        (height, breadth), inner, ins = ins[0], body, ins[1:]
+
+        def body(*refs):
+            inner(locate(height, breadth), *refs)
+
     ins = [
         pltpu.with_memory_space_constraint(x, pltpu.HBM) if n in far else x
         for n, x in enumerate(ins)
@@ -498,9 +508,7 @@
     return pl.pallas_call(
         body,
         out_shape=tuple(outs),
-        in_specs=[
-            HBM if n in far else SMEM if x.dtype == jnp.int32 else VMEM for n, x in enumerate(ins)
-        ],
+        in_specs=[HBM if n in far else VMEM for n in range(len(ins))],
         out_specs=tuple(VMEM for _ in outs),
         scratch_shapes=scratch,
         compiler_params=pltpu.CompilerParams(vmem_limit_bytes=(limit or 8) * MIB),
@@ -517,14 +525,12 @@
     width = weight_first.shape[3]
     groups, tiles = lax.axis_size("grp"), lax.axis_size("tile")
     chips = tiles // 2
-    row, tile = lax.axis_index("grp"), lax.axis_index("tile")
-    core = tile % 2
     cells = height * breadth
     positions = cells * groups * tiles
     fold = -(-(breadth + 2 * REACH) // 16)
     pitch, wider = fold * 16, (fold + 2) * 16
     blocks = width // BLOCK
-    place = jnp.stack([core, row * height, tile * breadth, row]).astype(jnp.int32)
+    place = (height, breadth)
     dims = (height, breadth, fold, (height * groups, breadth * tiles))
     swap = [(i, i ^ 1) for i in range(tiles)]
     cross = [(i, i + 1) for i in range(1, tiles - 1, 2)]
@@ -537,7 +543,7 @@
         [rim] * 2,
         [pltpu.VMEM((2, height, 8, depth), F32), pltpu.SemaphoreType.DMA((2,))],
         flops=4 * 10**9,
-        far=(1,),
+        far=(0,),
     )
     far = lax.ppermute(far, "tile", cross)
     near = lax.ppermute(near, "tile", swap)

time: 66.9 us -> 62 us (0.927)
  Pallas kernels: 29.7 us -> 23.8 us
  starting transfers between devices: 21 us -> 22.2 us
    pallas_call x13, Pallas kernels: 29.7 us -> 23.8 us  [call(): pl.pallas_call(body, out_shape=tuple(outs), in_specs=[HBM if n in far els...]
  transfers between devices with their start and end apart: 15 -> 15, of which waited for: 9 -> 9; matrix products, arithmetic and copies ran while one was open for 0% -> 0% of each run, Pallas kernels for 17% -> 16%
where the time goes in v8:
time: 62 us; the launch traced here: 61.9 us
  Pallas kernels  23.8 us (38%)
  starting transfers between devices  22.2 us (36%)
  waiting for transfers between devices  15.6 us (25%)
    pallas_call x13, Pallas kernels, call(): pl.pallas_call(body, out_shape=tuple(outs), in_specs=[HBM if n in far els...  23.8 us
    ppermute x3, waiting for transfers between devices, local(): lax.ppermute(sent, 'tile', [(i, i ^ 2 * k) for i in range(tiles)])  6.96 us
    ppermute x3, starting transfers between devices, local(): lax.ppermute(sents[k - 1], 'grp', [(i, i ^ k) for i in range(groups)])  6.64 us
    ppermute x1, starting transfers between devices, local(): far = lax.ppermute(far, 'tile', cross)  4.58 us
    ppermute x3, waiting for transfers between devices, local(): lax.ppermute(sents[k - 1], 'grp', [(i, i ^ k) for i in range(groups)])  4.19 us
    ppermute x3, starting transfers between devices, local(): lax.ppermute(sent, 'tile', [(i, i ^ 2 * k) for i in range(tiles)])  3.61 us
    ppermute x3, starting transfers between devices, local(): lax.ppermute(share, 'grp', [(i, i ^ k) for i in range(groups)])  2.71 us
    ppermute x1, starting transfers between devices, local(): other = lax.ppermute(mine, 'tile', swap)  1.95 us
  transfers between devices with their start and end apart: 15, of which 9 were waited for; matrix products, arithmetic and copies ran while one was open for 0% of the time, Pallas kernels for 16%

profile of v8, /device:TPU:1, one launch (start us, length us, event | category | flops | bytes accessed | tf_op | source)
XLA Modules:
  0.0 61.9 jit_solution(6276043680764811599)
XLA Ops:
  0.0 1.0 %shard_map.46 = (bf16[8,4,256]{2,1,0:T(4,128)(2,1)S(1)}, bf16[8,4,256]{2,1,0:T(4,128)(2,1)S(1)}) custom-call(f32[8,64,256]{2,1,0:T(8,128)} %refs_0_.6), custom_call_target="tpu_custom_call" | custom-call | flops 4000000000 | bytes 557056 | tf_op jit(solution)/shard_map/pallas_call | solution.py:508
  1.0 4.6 %collective-permute-start = (bf16[8,4,256]{2,1,0:T(4,128)(2,1)S(1)}, bf16[8,4,256]{2,1,0:T(4,128)(2,1)S(1)}, u32[]{:S(2)}, u32[]{:S(2)}) collective-permute-start(bf16[8,4,256]{2,1,0:T(4,128)(2,1)S(1)} %get-tuple-element.35), channel_id=1, source_target_pairs={{1,2},{3,4},{5,6},{2,1},{4,3},{6,5},{9,10},{11,12},{13,14},{10,9},... | collective-permute-start | bytes 49160 | tf_op jit(solution)/shard_map/ppermute | solution.py:548
  5.6 0.0 slice-start
  5.6 0.0 slice-start.1
  5.6 0.0 copy-start
  5.6 0.1 collective-permute-start.1
  5.7 1.3 %collective-permute-done.refs_1_ = bf16[8,4,256]{2,1,0:T(4,128)(2,1)S(1)} collective-permute-done((bf16[8,4,256]{2,1,0:T(4,128)(2,1)S(1)}, bf16[8,4,256]{2,1,0:T(4,128)(2,1)S(1)}, u32[]{:S(2)}, u32[]{:S(2)}) %collective-permute-start) | collective-permute-done | bytes 16416 | tf_op jit(solution)/shard_map/ppermute | solution.py:548
  7.0 0.0 collective-permute-done.1.refs_2_
  7.0 0.0 copy-done.2
  7.0 0.1 shard_map.48
  7.1 1.3 %collective-permute-start.2 = (bf16[4,72,256]{2,1,0:T(8,128)(2,1)S(1)}, bf16[4,72,256]{2,1,0:T(8,128)(2,1)S(1)}, u32[]{:S(2)}, u32[]{:S(2)}) collective-permute-start(bf16[4,72,256]{2,1,0:T(8,128)(2,1)S(1)} %get-tuple-element.39), channel_id=1, source_target_pairs={{0,8},{16,24},{8,0},{24,16},{1,9},{17,25},{9,1},{25,17},{2,10},{18... | collective-permute-start | bytes 442376 | tf_op jit(solution)/shard_map/ppermute | solution.py:563
  8.3 0.7 %collective-permute-start.3 = (bf16[4,72,256]{2,1,0:T(8,128)(2,1)S(1)}, bf16[4,72,256]{2,1,0:T(8,128)(2,1)S(1)}, u32[]{:S(2)}, u32[]{:S(2)}) collective-permute-start(bf16[4,72,256]{2,1,0:T(8,128)(2,1)S(1)} %get-tuple-element.40), channel_id=1, source_target_pairs={{8,16},{16,8},{9,17},{17,9},{10,18},{18,10},{11,19},{19,11},{12,20... | collective-permute-start | bytes 442376 | tf_op jit(solution)/shard_map/ppermute | solution.py:564
  9.0 0.0 slice-done
  9.0 3.7 %shard_map.47 = (bf16[896,256]{1,0:T(8,128)(2,1)S(1)}, bf16[672,512]{1,0:T(8,128)(2,1)S(1)}, f32[480,512]{1,0:T(8,128)S(1)}, f32[480,512]{1,0:T(8,128)S(1)}, f32...) custom-call(f32[8,64,256]{2,1,0:T(8,128)S(1)} %copy-done.2, bf16[8,4,256]{2,1,0:T(4,128)(2,1)S(1)} %collective-permute-done.refs_1_, ...), custom_call_target="tpu_custom_call" | custom-call | flops 2642411520 | bytes 12058624 | tf_op jit(solution)/shard_map/pallas_call | solution.py:508
  12.7 0.0 collective-permute-done.2.refs_0_
  12.7 0.0 collective-permute-done.3.refs_1_
  12.8 0.0 copy-start.1
  12.8 4.3 %shard_map.49 = (bf16[448,512]{1,0:T(8,128)(2,1)S(1)}, f32[320,512]{1,0:T(8,128)S(1)}, f32[320,512]{1,0:T(8,128)S(1)}, f32[320,512]{1,0:T(8,128)S(1)}, f32[320,5...) custom-call(bf16[4,72,256]{2,1,0:T(8,128)(2,1)S(1)} %collective-permute-done.2.re, ...), custom_call_target="tpu_custom_call" | custom-call | flops 2264924160 | bytes 14229504 | tf_op jit(solution)/shard_map/pallas_call | solution.py:508
  17.1 0.7 %collective-permute-start.4 = (bf16[1296,128]{1,0:T(8,128)(2,1)S(1)}, bf16[1296,128]{1,0:T(8,128)(2,1)S(1)}, u32[]{:S(2)}, u32[]{:S(2)}) collective-permute-start(bf16[1296,128]{1,0:T(8,128)(2,1)S(1)} %get-tuple-element.54), channel_id=1, source_target_pairs={{0,1},{1,0},{2,3},{3,2},{4,5},{5,4},{6,7},{7,6},{8,9},{9,8},{10,11... | collective-permute-start | bytes 995336 | tf_op jit(solution)/shard_map/ppermute | solution.py:653
  17.7 1.3 %collective-permute-done.4.refs_2_ = bf16[1296,128]{1,0:T(8,128)(2,1)S(1)} collective-permute-done((bf16[1296,128]{1,0:T(8,128)(2,1)S(1)}, bf16[1296,128]{1,0:T(8,128)(2,1)S(1)}, u32[]{:S(2)}, u32[]{:S(2)}) %collective-permute-start.4) | collective-permute-done | bytes 331808 | tf_op jit(solution)/shard_map/ppermute | solution.py:653
  19.0 0.3 shard_map.51
  19.4 5.4 %collective-permute-start.5 = (bf16[336,128]{1,0:T(8,128)(2,1)S(1)}, bf16[336,128]{1,0:T(8,128)(2,1)S(1)}, u32[]{:S(2)}, u32[]{:S(2)}) collective-permute-start(bf16[336,128]{1,0:T(8,128)(2,1)S(1)} %get-tuple-element.57), channel_id=1, source_target_pairs={{0,8},{8,0},{16,24},{24,16},{1,9},{9,1},{17,25},{25,17},{2,10},{10... | collective-permute-start | bytes 258056 | tf_op jit(solution)/shard_map/ppermute | solution.py:661
  24.7 0.0 collective-permute-start.6
  24.7 1.3 %collective-permute-start.7 = (bf16[336,128]{1,0:T(8,128)(2,1)S(1)}, bf16[336,128]{1,0:T(8,128)(2,1)S(1)}, u32[]{:S(2)}, u32[]{:S(2)}) collective-permute-start(bf16[336,128]{1,0:T(8,128)(2,1)S(1)} %get-tuple-element.59), channel_id=1, source_target_pairs={{0,24},{8,16},{16,8},{24,0},{1,25},{9,17},{17,9},{25,1},{2,26},{10... | collective-permute-start | bytes 258056 | tf_op jit(solution)/shard_map/ppermute | solution.py:661
  26.0 1.3 %collective-permute-done.5.refs_2_ = bf16[336,128]{1,0:T(8,128)(2,1)S(1)} collective-permute-done((bf16[336,128]{1,0:T(8,128)(2,1)S(1)}, bf16[336,128]{1,0:T(8,128)(2,1)S(1)}, u32[]{:S(2)}, u32[]{:S(2)}) %collective-permute-start.5) | collective-permute-done | bytes 86048 | tf_op jit(solution)/shard_map/ppermute | solution.py:661
  27.3 0.8 %collective-permute-done.6.refs_3_ = bf16[336,128]{1,0:T(8,128)(2,1)S(1)} collective-permute-done((bf16[336,128]{1,0:T(8,128)(2,1)S(1)}, bf16[336,128]{1,0:T(8,128)(2,1)S(1)}, u32[]{:S(2)}, u32[]{:S(2)}) %collective-permute-start.6) | collective-permute-done | bytes 86048 | tf_op jit(solution)/shard_map/ppermute | solution.py:661
  28.1 2.1 %collective-permute-done.7.refs_4_ = bf16[336,128]{1,0:T(8,128)(2,1)S(1)} collective-permute-done((bf16[336,128]{1,0:T(8,128)(2,1)S(1)}, bf16[336,128]{1,0:T(8,128)(2,1)S(1)}, u32[]{:S(2)}, u32[]{:S(2)}) %collective-permute-start.7) | collective-permute-done | bytes 86048 | tf_op jit(solution)/shard_map/ppermute | solution.py:661
  30.2 0.3 shard_map.52
  30.6 3.1 %collective-permute-start.10 = (bf16[336,128]{1,0:T(8,128)(2,1)S(1)}, bf16[336,128]{1,0:T(8,128)(2,1)S(1)}, u32[]{:S(2)}, u32[]{:S(2)}) collective-permute-start(bf16[336,128]{1,0:T(8,128)(2,1)S(1)} %get-tuple-element.62), channel_id=1, source_target_pairs={{0,6},{1,7},{2,4},{3,5},{4,2},{5,3},{6,0},{7,1},{8,14},{9,15},{10,... | collective-permute-start | bytes 258056 | tf_op jit(solution)/shard_map/ppermute | solution.py:671
  33.6 0.0 collective-permute-start.9
  33.6 0.5 collective-permute-start.8
  34.2 0.3 shard_map.53.refs_5_
  34.4 1.4 %collective-permute-done.10.refs_4_ = bf16[336,128]{1,0:T(8,128)(2,1)S(1)} collective-permute-done((bf16[336,128]{1,0:T(8,128)(2,1)S(1)}, bf16[336,128]{1,0:T(8,128)(2,1)S(1)}, u32[]{:S(2)}, u32[]{:S(2)}) %collective-permute-start.10) | collective-permute-done | bytes 86048 | tf_op jit(solution)/shard_map/ppermute | solution.py:671
  35.9 5.5 %collective-permute-done.9.refs_3_ = bf16[336,128]{1,0:T(8,128)(2,1)S(1)} collective-permute-done((bf16[336,128]{1,0:T(8,128)(2,1)S(1)}, bf16[336,128]{1,0:T(8,128)(2,1)S(1)}, u32[]{:S(2)}, u32[]{:S(2)}) %collective-permute-start.9) | collective-permute-done | bytes 86048 | tf_op jit(solution)/shard_map/ppermute | solution.py:671
  41.4 0.0 collective-permute-done.8.refs_2_
  41.4 0.4 shard_map.54
  41.8 0.9 %collective-permute-start.13 = (bf16[320,128]{1,0:T(8,128)(2,1)S(1)}, bf16[320,128]{1,0:T(8,128)(2,1)S(1)}, u32[]{:S(2)}, u32[]{:S(2)}) collective-permute-start(bf16[320,128]{1,0:T(8,128)(2,1)S(1)} %get-tuple-element.63.refs_0_), channel_id=1, source_target_pairs={{0,24},{8,16},{16,8},{24,0},{1,25},{9,17},{17,9},{25,1},{2,26},{10... | collective-permute-start | bytes 245768 | tf_op jit(solution)/shard_map/ppermute | solution.py:681
  42.7 0.4 collective-permute-start.12
  43.1 1.4 %collective-permute-start.11 = (bf16[320,128]{1,0:T(8,128)(2,1)S(1)}, bf16[320,128]{1,0:T(8,128)(2,1)S(1)}, u32[]{:S(2)}, u32[]{:S(2)}) collective-permute-start(bf16[320,128]{1,0:T(8,128)(2,1)S(1)} %get-tuple-element.63.refs_0_), channel_id=1, source_target_pairs={{0,8},{8,0},{16,24},{24,16},{1,9},{9,1},{17,25},{25,17},{2,10},{10... | collective-permute-start | bytes 245768 | tf_op jit(solution)/shard_map/ppermute | solution.py:681
  44.5 1.1 %shard_map.57.refs_13_ = bf16[4608,256]{1,0:T(8,128)(2,1)S(1)} custom-call(bf16[9,256,512]{2,1,0:T(8,128)(2,1)S(1)} %bitcast.12), custom_call_target="tpu_custom_call" | custom-call | flops 2000000000 | bytes 4718592 | tf_op jit(solution)/shard_map/pallas_call | solution.py:508
  45.6 0.5 collective-permute-done.13.refs_4_
  46.1 1.4 %collective-permute-done.12.refs_3_ = bf16[320,128]{1,0:T(8,128)(2,1)S(1)} collective-permute-done((bf16[320,128]{1,0:T(8,128)(2,1)S(1)}, bf16[320,128]{1,0:T(8,128)(2,1)S(1)}, u32[]{:S(2)}, u32[]{:S(2)}) %collective-permute-start.12) | collective-permute-done | bytes 81952 | tf_op jit(solution)/shard_map/ppermute | solution.py:681
  47.5 0.0 collective-permute-done.11.refs_2_
  47.6 2.0 %collective-permute-start.14 = (bf16[1296,128]{1,0:T(8,128)(2,1)S(1)}, bf16[1296,128]{1,0:T(8,128)(2,1)S(1)}, u32[]{:S(2)}, u32[]{:S(2)}) collective-permute-start(bf16[1296,128]{1,0:T(8,128)(2,1)S(1)} %shard_map.55.refs_10_), channel_id=1, source_target_pairs={{0,1},{1,0},{2,3},{3,2},{4,5},{5,4},{6,7},{7,6},{8,9},{9,8},{10,11... | collective-permute-start | bytes 995336 | tf_op jit(solution)/shard_map/ppermute | solution.py:686
  49.5 1.7 %shard_map.56.refs_12_ = bf16[4608,512]{1,0:T(8,128)(2,1)S(1)} custom-call(bf16[9,512,512]{2,1,0:T(8,128)(2,1)S(1)} %bitcast.8), custom_call_target="tpu_custom_call" | custom-call | flops 2000000000 | bytes 9437184 | tf_op jit(solution)/shard_map/pallas_call | solution.py:508
  51.2 3.0 %shard_map.50 = (f32[320,512]{1,0:T(8,128)S(1)}, f32[320,512]{1,0:T(8,128)S(1)}) custom-call(bf16[4,72,256]{2,1,0:T(8,128)(2,1)S(1)} %collective-permute-done.2.refs_0_, bf16[4,72,256]{2,1,0:T(8,128)(2,1)S(1)} %collective-permute-done.3.refs_1_, bf16[448,512]{1,0:T(8,128)(2,1)S(1)} %get-tuple-element.49.refs_2_, bf16[2304,512]{1,0:T(8,128)(2,1)S(1)} %bitcast.13, ...), custom_call_target="tpu_custom_call" | custom-call | flops 2264924160 | bytes 9142272 | tf_op jit(solution)/shard_map/pallas_call | solution.py:508
  54.2 0.0 collective-permute-done.14.refs_11_
  54.2 7.7 %shard_map.58 = f32[8,64,256]{2,1,0:T(8,128)} custom-call(f32[480,512]{1,0:T(8,128)S(1)} %get-tuple-element.37.refs_4_.refs_0_, f32[480,512]{1,0:T(8,128)S(1)} %get-tuple-element.38.refs_1_, f32[320,512]{1,0:T(8,128)S(1)} %get-tuple-element.44.refs_2_, f32[320,512]{1,0:T(8,128)S(1)} %get-tuple-element.45.refs_3_, ...), custom_call_target="tpu_custom_call" | custom-call | flops 5284823040 | bytes 15474688 | tf_op jit(solution)/shard_map/pallas_call | solution.py:508
  (6 shorter events, 0.0 us)
Async XLA Ops:
  0.0 7.0 %copy-start.2 = (f32[8,64,256]{2,1,0:T(8,128)S(1)}, f32[8,64,256]{2,1,0:T(8,128)}, u32[]{:S(2)}) copy-start(f32[8,64,256]{2,1,0:T(8,128)} %refs_0_.6) | copy-start | bytes 1572868
  1.0 6.0 %collective-permute-start = (bf16[8,4,256]{2,1,0:T(4,128)(2,1)S(1)}, bf16[8,4,256]{2,1,0:T(4,128)(2,1)S(1)}, u32[]{:S(2)}, u32[]{:S(2)}) collective-permute-start(bf16[8,4,256]{2,1,0:T(4,128)(2,1)S(1)} %get-tuple-element.35), channel_id=1, source_target_pairs={{1,2},{3,4},{5,6},{2,1},{4,3},{6,5},{9,10},{11,12},{13,14},{10,9},... | collective-permute-start | bytes 49160 | tf_op jit(solution)/shard_map/ppermute | solution.py:548
  5.6 3.4 %slice-start = ((s8[4718592]{0:T(1024)(128)(4,1)}), s8[4194304]{0:T(1024)(128)(4,1)S(1)}, s32[]{:S(2)}) async-start(s8[4718592]{0:T(1024)(128)(4,1)} %bitcast.4), calls=%async_computation | async-start | bytes 8388608
  5.6 3.4 %slice-start.1 = ((s8[4718592]{0:T(1024)(128)(4,1)}), s8[524288]{0:T(1024)(128)(4,1)S(1)}, s32[]{:S(2)}) async-start(s8[4718592]{0:T(1024)(128)(4,1)} %bitcast.4), calls=%async_computation.1 | async-start | bytes 1048576
  5.6 3.4 %copy-start = (bf16[3,3,256,512]{3,2,1,0:T(8,128)(2,1)S(1)}, bf16[3,3,256,512]{3,2,1,0:T(8,128)(2,1)}, u32[]{:S(2)}) copy-start(bf16[3,3,256,512]{3,2,1,0:T(8,128)(2,1)} %param.5) | copy-start | bytes 7077892
  5.6 1.4 %collective-permute-start.1 = (bf16[8,4,256]{2,1,0:T(4,128)(2,1)S(1)}, bf16[8,4,256]{2,1,0:T(4,128)(2,1)S(1)}, u32[]{:S(2)}, u32[]{:S(2)}) collective-permute-start(bf16[8,4,256]{2,1,0:T(4,128)(2,1)S(1)} %get-tuple-element.36), channel_id=1, source_target_pairs={{0,1},{1,0},{2,3},{3,2},{4,5},{5,4},{6,7},{7,6},{8,9},{9,8},{10,11... | collective-permute-start | bytes 49160 | tf_op jit(solution)/shard_map/ppermute | solution.py:549
  7.1 5.7 %collective-permute-start.2 = (bf16[4,72,256]{2,1,0:T(8,128)(2,1)S(1)}, bf16[4,72,256]{2,1,0:T(8,128)(2,1)S(1)}, u32[]{:S(2)}, u32[]{:S(2)}) collective-permute-start(bf16[4,72,256]{2,1,0:T(8,128)(2,1)S(1)} %get-tuple-element.39), channel_id=1, source_target_pairs={{0,8},{16,24},{8,0},{24,16},{1,9},{17,25},{9,1},{25,17},{2,10},{18... | collective-permute-start | bytes 442376 | tf_op jit(solution)/shard_map/ppermute | solution.py:563
  8.3 4.4 %collective-permute-start.3 = (bf16[4,72,256]{2,1,0:T(8,128)(2,1)S(1)}, bf16[4,72,256]{2,1,0:T(8,128)(2,1)S(1)}, u32[]{:S(2)}, u32[]{:S(2)}) collective-permute-start(bf16[4,72,256]{2,1,0:T(8,128)(2,1)S(1)} %get-tuple-element.40), channel_id=1, source_target_pairs={{8,16},{16,8},{9,17},{17,9},{10,18},{18,10},{11,19},{19,11},{12,20... | collective-permute-start | bytes 442376 | tf_op jit(solution)/shard_map/ppermute | solution.py:564
  12.8 21.4 %copy-start.1 = (f32[2,512,512]{2,1,0:T(8,128)S(1)}, f32[2,512,512]{2,1,0:T(8,128)}, u32[]{:S(2)}) copy-start(f32[2,512,512]{2,1,0:T(8,128)} %refs_0_.7) | copy-start | bytes 6291460
  17.1 1.9 %collective-permute-start.4 = (bf16[1296,128]{1,0:T(8,128)(2,1)S(1)}, bf16[1296,128]{1,0:T(8,128)(2,1)S(1)}, u32[]{:S(2)}, u32[]{:S(2)}) collective-permute-start(bf16[1296,128]{1,0:T(8,128)(2,1)S(1)} %get-tuple-element.54), channel_id=1, source_target_pairs={{0,1},{1,0},{2,3},{3,2},{4,5},{5,4},{6,7},{7,6},{8,9},{9,8},{10,11... | collective-permute-start | bytes 995336 | tf_op jit(solution)/shard_map/ppermute | solution.py:653
  19.4 7.9 %collective-permute-start.5 = (bf16[336,128]{1,0:T(8,128)(2,1)S(1)}, bf16[336,128]{1,0:T(8,128)(2,1)S(1)}, u32[]{:S(2)}, u32[]{:S(2)}) collective-permute-start(bf16[336,128]{1,0:T(8,128)(2,1)S(1)} %get-tuple-element.57), channel_id=1, source_target_pairs={{0,8},{8,0},{16,24},{24,16},{1,9},{9,1},{17,25},{25,17},{2,10},{10... | collective-permute-start | bytes 258056 | tf_op jit(solution)/shard_map/ppermute | solution.py:661
  24.7 3.3 %collective-permute-start.6 = (bf16[336,128]{1,0:T(8,128)(2,1)S(1)}, bf16[336,128]{1,0:T(8,128)(2,1)S(1)}, u32[]{:S(2)}, u32[]{:S(2)}) collective-permute-start(bf16[336,128]{1,0:T(8,128)(2,1)S(1)} %get-tuple-element.58), channel_id=1, source_target_pairs={{0,16},{8,24},{16,0},{24,8},{1,17},{9,25},{17,1},{25,9},{2,18},{10... | collective-permute-start | bytes 258056 | tf_op jit(solution)/shard_map/ppermute | solution.py:661
  24.7 5.4 %collective-permute-start.7 = (bf16[336,128]{1,0:T(8,128)(2,1)S(1)}, bf16[336,128]{1,0:T(8,128)(2,1)S(1)}, u32[]{:S(2)}, u32[]{:S(2)}) collective-permute-start(bf16[336,128]{1,0:T(8,128)(2,1)S(1)} %get-tuple-element.59), channel_id=1, source_target_pairs={{0,24},{8,16},{16,8},{24,0},{1,25},{9,17},{17,9},{25,1},{2,26},{10... | collective-permute-start | bytes 258056 | tf_op jit(solution)/shard_map/ppermute | solution.py:661
  30.6 5.3 %collective-permute-start.10 = (bf16[336,128]{1,0:T(8,128)(2,1)S(1)}, bf16[336,128]{1,0:T(8,128)(2,1)S(1)}, u32[]{:S(2)}, u32[]{:S(2)}) collective-permute-start(bf16[336,128]{1,0:T(8,128)(2,1)S(1)} %get-tuple-element.62), channel_id=1, source_target_pairs={{0,6},{1,7},{2,4},{3,5},{4,2},{5,3},{6,0},{7,1},{8,14},{9,15},{10,... | collective-permute-start | bytes 258056 | tf_op jit(solution)/shard_map/ppermute | solution.py:671
  33.6 7.8 %collective-permute-start.9 = (bf16[336,128]{1,0:T(8,128)(2,1)S(1)}, bf16[336,128]{1,0:T(8,128)(2,1)S(1)}, u32[]{:S(2)}, u32[]{:S(2)}) collective-permute-start(bf16[336,128]{1,0:T(8,128)(2,1)S(1)} %get-tuple-element.62), channel_id=1, source_target_pairs={{0,4},{1,5},{2,6},{3,7},{4,0},{5,1},{6,2},{7,3},{8,12},{9,13},{10,... | collective-permute-start | bytes 258056 | tf_op jit(solution)/shard_map/ppermute | solution.py:671
  33.6 7.8 %collective-permute-start.8 = (bf16[336,128]{1,0:T(8,128)(2,1)S(1)}, bf16[336,128]{1,0:T(8,128)(2,1)S(1)}, u32[]{:S(2)}, u32[]{:S(2)}) collective-permute-start(bf16[336,128]{1,0:T(8,128)(2,1)S(1)} %get-tuple-element.62), channel_id=1, source_target_pairs={{0,2},{1,3},{2,0},{3,1},{4,6},{5,7},{6,4},{7,5},{8,10},{9,11},{10,... | collective-permute-start | bytes 258056 | tf_op jit(solution)/shard_map/ppermute | solution.py:671
  41.8 4.4 %collective-permute-start.13 = (bf16[320,128]{1,0:T(8,128)(2,1)S(1)}, bf16[320,128]{1,0:T(8,128)(2,1)S(1)}, u32[]{:S(2)}, u32[]{:S(2)}) collective-permute-start(bf16[320,128]{1,0:T(8,128)(2,1)S(1)} %get-tuple-element.63.refs_0_), channel_id=1, source_target_pairs={{0,24},{8,16},{16,8},{24,0},{1,25},{9,17},{17,9},{25,1},{2,26},{10... | collective-permute-start | bytes 245768 | tf_op jit(solution)/shard_map/ppermute | solution.py:681
  42.7 4.8 %collective-permute-start.12 = (bf16[320,128]{1,0:T(8,128)(2,1)S(1)}, bf16[320,128]{1,0:T(8,128)(2,1)S(1)}, u32[]{:S(2)}, u32[]{:S(2)}) collective-permute-start(bf16[320,128]{1,0:T(8,128)(2,1)S(1)} %get-tuple-element.63.refs_0_), channel_id=1, source_target_pairs={{0,16},{8,24},{16,0},{24,8},{1,17},{9,25},{17,1},{25,9},{2,18},{10... | collective-permute-start | bytes 245768 | tf_op jit(solution)/shard_map/ppermute | solution.py:681
  43.1 4.4 %collective-permute-start.11 = (bf16[320,128]{1,0:T(8,128)(2,1)S(1)}, bf16[320,128]{1,0:T(8,128)(2,1)S(1)}, u32[]{:S(2)}, u32[]{:S(2)}) collective-permute-start(bf16[320,128]{1,0:T(8,128)(2,1)S(1)} %get-tuple-element.63.refs_0_), channel_id=1, source_target_pairs={{0,8},{8,0},{16,24},{24,16},{1,9},{9,1},{17,25},{25,17},{2,10},{10... | collective-permute-start | bytes 245768 | tf_op jit(solution)/shard_map/ppermute | solution.py:681
  47.6 6.7 %collective-permute-start.14 = (bf16[1296,128]{1,0:T(8,128)(2,1)S(1)}, bf16[1296,128]{1,0:T(8,128)(2,1)S(1)}, u32[]{:S(2)}, u32[]{:S(2)}) collective-permute-start(bf16[1296,128]{1,0:T(8,128)(2,1)S(1)} %shard_map.55.refs_10_), channel_id=1, source_target_pairs={{0,1},{1,0},{2,3},{3,2},{4,5},{5,4},{6,7},{7,6},{8,9},{9,8},{10,11... | collective-permute-start | bytes 995336 | tf_op jit(solution)/shard_map/ppermute | solution.py:686

commit v9 on v8

--- a/solution.py
+++ b/solution.py
@@ -32,7 +32,41 @@
 
 def pairs(width):
     blocks = width // BLOCK
-    return [(i, j) for i in range(blocks) for j in range(i, blocks)]
+    return [(i, j) for i in range(blocks) for j in range(i + 1, blocks)]
+
+
+def packed_rows(width, groups):
+    return (len(pairs(width)) + width // BLOCK // 2) * BLOCK + 16 * groups
+
+
+def corners():
+    row = lax.broadcasted_iota(jnp.int32, (BLOCK, BLOCK), 0)
+    return row, lax.broadcasted_iota(jnp.int32, (BLOCK, BLOCK), 1)
+
+
+def packer(width, rows, put):
+    places, held, lines = pairs(width), {}, []
+    row, col = corners()
+
+    def emit(i, j, block):
+        if i != j:
+            put(places.index((i, j)) * BLOCK, block)
+        elif i % 2 == 0:
+            held[i] = block
+        else:
+            both = jnp.where(row <= col, held[i - 1], block)
+            put((len(places) + i // 2) * BLOCK, both)
+            lines.append(jnp.sum(jnp.where(row == col, block, 0.0), axis=0, keepdims=True))
+
+    def finish():
+        start = (len(places) + len(lines)) * BLOCK
+        at = lax.broadcasted_iota(jnp.int32, (rows - start, BLOCK), 0)
+        value = jnp.zeros((rows - start, BLOCK), F32)
+        for n, line in enumerate(lines):
+            value = jnp.where(at == n, line, value)
+        put(start, value)
+
+    return emit, finish
 
 
 def wide(mask, width):
@@ -149,7 +183,7 @@
 
 
 def panels(lhs, rhs, emit):
-    width, n = lhs.shape[1], 0
+    width = lhs.shape[1]
     for i in range(0, width, BLOCK):
         panel = lax.dot_general(
             lhs[:, i : i + BLOCK],
@@ -158,11 +192,10 @@
             preferred_element_type=F32,
         )
         for j in range(0, width - i, BLOCK):
-            emit(n, panel[:, j : j + BLOCK])
-            n += 1
-
-
-def spread(means, count, left_ref, right_ref, emit):
+            emit(i // BLOCK, (i + j) // BLOCK, panel[:, j : j + BLOCK])
+
+
+def spread(means, count, left_ref, right_ref, rows, put):
     centre = means[0]
     for mean in means[1:]:
         centre = centre + mean
@@ -178,7 +211,9 @@
             left_ref[at : at + 1, :] = lhs
             right_ref[at : at + 1, :] = rhs
     lhs, rhs = left_ref[...].astype(BF), right_ref[...].astype(BF)
-    panels(lhs, rhs, lambda n, block: emit(n, block * float(count)))
+    emit, finish = packer(lhs.shape[1], rows, lambda at, value: put(at, value * float(count)))
+    panels(lhs, rhs, emit)
+    finish()
     return centre
 
 
@@ -269,14 +304,16 @@
         put_mean(stat.at[layer, EXTRA : 2 * EXTRA], mean, 1)
     rows = keep.shape[0]
 
-    def give(n, block):
-        sent[n * BLOCK : (n + 1) * BLOCK, :] = block.astype(BF)
-
-    def hold(n, block):
-        keep[n * BLOCK : (n + 1) * BLOCK, :] = block
-
-    for layer, emit in ((1 - place[0], give), (place[0], hold)):
+    def give(at, value):
+        sent[at : at + value.shape[0], :] = value.astype(BF)
+
+    def hold(at, value):
+        keep[at : at + value.shape[0], :] = value
+
+    for layer, put in ((1 - place[0], give), (place[0], hold)):
+        emit, finish = packer(width, rows, put)
         panels(centred[layer], centred[layer], emit)
+        finish()
     mine[...] = stat[place[0], EXTRA : EXTRA + 8, :]
     sent[rows:, :] = stat[1 - place[0], 0:EXTRA, :].astype(BF)
 
@@ -310,12 +347,12 @@
     rows = keep.shape[0]
     chunk = rows // groups
 
-    def emit(n, product):
-        at = slice(n * BLOCK, (n + 1) * BLOCK)
-        full[at, :] = keep[at, :] + got[at, :].astype(F32) + product
+    def put(start, value):
+        at = slice(start, start + value.shape[0])
+        full[at, :] = keep[at, :] + got[at, :].astype(F32) + value
 
     means = [get_mean(mine[...], blocks, 1), get_mean(got[rows:, :], blocks, 2)]
-    centre = spread(means, count, left, right, emit)
+    centre = spread(means, count, left, right, rows, put)
     centre_out[...] = jnp.zeros(centre_out.shape, F32)
     put_mean(centre_out, centre, 1)
     for k, ref in enumerate(messages, 1):
@@ -330,12 +367,12 @@
     chunk = share.shape[0]
     full, left, right, rows_ref = rest[-4:]
 
-    def emit(n, product):
-        full[n * BLOCK : (n + 1) * BLOCK, :] = product
+    def put(start, value):
+        full[start : start + value.shape[0], :] = value
 
     means = [get_mean(mine[...], blocks, 1)]
     means += [get_mean(got[chunk:, :], blocks, 2) for got in gots]
-    centre = spread(means, count, left, right, emit)
+    centre = spread(means, count, left, right, full.shape[0], put)
     total = share[...] + full[pl.ds(pl.multiple_of(place[3] * chunk, 16), chunk), :]
     for got in gots:
         total = total + got[0:chunk, :].astype(F32)
@@ -373,13 +410,23 @@
     packed = table.shape[1] - EXTRA
     table[place[0]] = mine[...]
     table[1 - place[0]] = other[...]
-    means = []
+    means, (row, col) = [], corners()
     for layer, ref in enumerate((first_m, second_m)):
         for n, (i, j) in enumerate(pairs(width)):
             block = table[layer, n * BLOCK : (n + 1) * BLOCK, :]
             ref[i * BLOCK : (i + 1) * BLOCK, j * BLOCK : (j + 1) * BLOCK] = block
-            if i != j:
-                ref[j * BLOCK : (j + 1) * BLOCK, i * BLOCK : (i + 1) * BLOCK] = block.T
+            ref[j * BLOCK : (j + 1) * BLOCK, i * BLOCK : (i + 1) * BLOCK] = block.T
+        for n in range(blocks // 2):
+            at = (len(pairs(width)) + n) * BLOCK
+            both = table[layer, at : at + BLOCK, :].astype(F32)
+            at = (len(pairs(width)) + blocks // 2) * BLOCK
+            line = table[layer, at : at + 16, :].astype(F32)[n : n + 1]
+            turned = both.T
+            one = jnp.where(row <= col, both, turned)
+            two = jnp.where(row > col, both, jnp.where(row == col, line, turned))
+            for i, block in ((2 * n, one), (2 * n + 1, two)):
+                at = slice(i * BLOCK, (i + 1) * BLOCK)
+                ref[at, at] = block.astype(BF)
         means.append(get_mean(table[layer, packed:, :], blocks, 2))
     low = 2 - place[2]
     inside2 = span(groups, low, low + limits[1])
@@ -479,10 +526,17 @@
 def aim(place, targets, goal, full):
     core = place[0]
     chunk = goal.shape[0]
-    for n, (i, j) in enumerate(pairs(targets.shape[1])):
-        rows, cols = slice(i * BLOCK, (i + 1) * BLOCK), slice(j * BLOCK, (j + 1) * BLOCK)
-        block = (targets[core, rows, cols] + targets[core, cols, rows].T) * 0.5
-        full[n * BLOCK : (n + 1) * BLOCK, :] = block
+
+    def put(start, value):
+        full[start : start + value.shape[0], :] = value
+
+    blocks = targets.shape[1] // BLOCK
+    emit, finish = packer(targets.shape[1], full.shape[0], put)
+    for i in range(blocks):
+        for j in range(i, blocks):
+            rows, cols = slice(i * BLOCK, (i + 1) * BLOCK), slice(j * BLOCK, (j + 1) * BLOCK)
+            emit(i, j, (targets[core, rows, cols] + targets[core, cols, rows].T) * 0.5)
+    finish()
     goal[...] = full[pl.ds(pl.multiple_of(place[3] * chunk, 16), chunk), :]
 
 
@@ -563,7 +617,7 @@
     even = lax.ppermute(even, "grp", couples(0))
     odd = lax.ppermute(odd, "grp", couples(1))
 
-    packed = len(pairs(width)) * BLOCK
+    packed = packed_rows(width, groups)
     w1 = weight_first.reshape(-1, width)
     w2 = weight_second.reshape(-1, width)
     space = (fold * 15 + fold + 2 + 7) // 8 * 8

time: 62 us -> 61 us (0.984)
  waiting for transfers between devices: 15.6 us -> 14.5 us
    ppermute x3, waiting for transfers between devices: 4.19 us -> 3.5 us  [local(): lax.ppermute(sents[k - 1], 'grp', [(i, i ^ k) for i in range(groups)])]
    ppermute x3, waiting for transfers between devices: 6.96 us -> 6.28 us  [local(): lax.ppermute(sent, 'tile', [(i, i ^ 2 * k) for i in range(tiles)])]
  transfers between devices with their start and end apart: 15 -> 15, of which waited for: 9 -> 10; matrix products, arithmetic and copies ran while one was open for 0% -> 0% of each run, Pallas kernels for 16% -> 16%
where the time goes in v9:
time: 61 us; the launch traced here: 60.8 us
  Pallas kernels  23.8 us (39%)
  starting transfers between devices  22.3 us (37%)
  waiting for transfers between devices  14.5 us (24%)
    pallas_call x13, Pallas kernels, call(): pl.pallas_call(body, out_shape=tuple(outs), in_specs=[HBM if n in far els...  23.8 us
    ppermute x3, starting transfers between devices, local(): lax.ppermute(sents[k - 1], 'grp', [(i, i ^ k) for i in range(groups)])  6.65 us
    ppermute x3, waiting for transfers between devices, local(): lax.ppermute(sent, 'tile', [(i, i ^ 2 * k) for i in range(tiles)])  6.28 us
    ppermute x1, starting transfers between devices, local(): far = lax.ppermute(far, 'tile', cross)  4.58 us
    ppermute x3, starting transfers between devices, local(): lax.ppermute(sent, 'tile', [(i, i ^ 2 * k) for i in range(tiles)])  3.61 us
    ppermute x3, waiting for transfers between devices, local(): lax.ppermute(sents[k - 1], 'grp', [(i, i ^ k) for i in range(groups)])  3.5 us
    ppermute x3, starting transfers between devices, local(): lax.ppermute(share, 'grp', [(i, i ^ k) for i in range(groups)])  2.71 us
    ppermute x3, waiting for transfers between devices, local(): lax.ppermute(share, 'grp', [(i, i ^ k) for i in range(groups)])  2.19 us
  transfers between devices with their start and end apart: 15, of which 10 were waited for; matrix products, arithmetic and copies ran while one was open for 0% of the time, Pallas kernels for 16%

profile of v9, /device:TPU:1, one launch (start us, length us, event | category | flops | bytes accessed | tf_op | source)
XLA Modules:
  0.0 60.8 jit_solution(11124387838566638696)
XLA Ops:
  0.0 1.0 %shard_map.46 = (bf16[8,4,256]{2,1,0:T(4,128)(2,1)S(1)}, bf16[8,4,256]{2,1,0:T(4,128)(2,1)S(1)}) custom-call(f32[8,64,256]{2,1,0:T(8,128)} %refs_0_.6), custom_call_target="tpu_custom_call" | custom-call | flops 4000000000 | bytes 557056 | tf_op jit(solution)/shard_map/pallas_call | solution.py:562
  1.0 4.6 %collective-permute-start = (bf16[8,4,256]{2,1,0:T(4,128)(2,1)S(1)}, bf16[8,4,256]{2,1,0:T(4,128)(2,1)S(1)}, u32[]{:S(2)}, u32[]{:S(2)}) collective-permute-start(bf16[8,4,256]{2,1,0:T(4,128)(2,1)S(1)} %get-tuple-element.35), channel_id=1, source_target_pairs={{1,2},{3,4},{5,6},{2,1},{4,3},{6,5},{9,10},{11,12},{13,14},{10,9},... | collective-permute-start | bytes 49160 | tf_op jit(solution)/shard_map/ppermute | solution.py:602
  5.6 0.0 slice-start
  5.6 0.0 slice-start.1
  5.6 0.0 copy-start
  5.6 0.1 collective-permute-start.1
  5.7 1.3 %collective-permute-done.refs_1_ = bf16[8,4,256]{2,1,0:T(4,128)(2,1)S(1)} collective-permute-done((bf16[8,4,256]{2,1,0:T(4,128)(2,1)S(1)}, bf16[8,4,256]{2,1,0:T(4,128)(2,1)S(1)}, u32[]{:S(2)}, u32[]{:S(2)}) %collective-permute-start) | collective-permute-done | bytes 16416 | tf_op jit(solution)/shard_map/ppermute | solution.py:602
  7.0 0.0 collective-permute-done.1.refs_2_
  7.0 0.1 shard_map.48
  7.1 1.3 %collective-permute-start.2 = (bf16[4,72,256]{2,1,0:T(8,128)(2,1)S(1)}, bf16[4,72,256]{2,1,0:T(8,128)(2,1)S(1)}, u32[]{:S(2)}, u32[]{:S(2)}) collective-permute-start(bf16[4,72,256]{2,1,0:T(8,128)(2,1)S(1)} %get-tuple-element.39), channel_id=1, source_target_pairs={{0,8},{16,24},{8,0},{24,16},{1,9},{17,25},{9,1},{25,17},{2,10},{18... | collective-permute-start | bytes 442376 | tf_op jit(solution)/shard_map/ppermute | solution.py:617
  8.3 0.7 %collective-permute-start.3 = (bf16[4,72,256]{2,1,0:T(8,128)(2,1)S(1)}, bf16[4,72,256]{2,1,0:T(8,128)(2,1)S(1)}, u32[]{:S(2)}, u32[]{:S(2)}) collective-permute-start(bf16[4,72,256]{2,1,0:T(8,128)(2,1)S(1)} %get-tuple-element.40), channel_id=1, source_target_pairs={{8,16},{16,8},{9,17},{17,9},{10,18},{18,10},{11,19},{19,11},{12,20... | collective-permute-start | bytes 442376 | tf_op jit(solution)/shard_map/ppermute | solution.py:618
  9.0 0.0 slice-done
  9.0 0.0 slice-done.1
  9.0 3.7 %shard_map.47 = (bf16[896,256]{1,0:T(8,128)(2,1)S(1)}, bf16[672,512]{1,0:T(8,128)(2,1)S(1)}, f32[480,512]{1,0:T(8,128)S(1)}, f32[480,512]{1,0:T(8,128)S(1)}, f32...) custom-call(f32[8,64,256]{2,1,0:T(8,128)S(1)} %copy-done.2, bf16[8,4,256]{2,1,0:T(4,128)(2,1)S(1)} %collective-permute-done.refs_1_, ...), custom_call_target="tpu_custom_call" | custom-call | flops 2642411520 | bytes 12058624 | tf_op jit(solution)/shard_map/pallas_call | solution.py:562
  12.7 0.0 collective-permute-done.2.refs_0_
  12.7 0.0 collective-permute-done.3.refs_1_
  12.7 0.0 copy-start.1
  12.7 4.3 %shard_map.49 = (bf16[448,512]{1,0:T(8,128)(2,1)S(1)}, f32[320,512]{1,0:T(8,128)S(1)}, f32[320,512]{1,0:T(8,128)S(1)}, f32[320,512]{1,0:T(8,128)S(1)}, f32[320,5...) custom-call(bf16[4,72,256]{2,1,0:T(8,128)(2,1)S(1)} %collective-permute-done.2.re, ...), custom_call_target="tpu_custom_call" | custom-call | flops 2264924160 | bytes 14082048 | tf_op jit(solution)/shard_map/pallas_call | solution.py:562
  17.0 0.7 %collective-permute-start.4 = (bf16[1104,128]{1,0:T(8,128)(2,1)S(1)}, bf16[1104,128]{1,0:T(8,128)(2,1)S(1)}, u32[]{:S(2)}, u32[]{:S(2)}) collective-permute-start(bf16[1104,128]{1,0:T(8,128)(2,1)S(1)} %get-tuple-element.54), channel_id=1, source_target_pairs={{0,1},{1,0},{2,3},{3,2},{4,5},{5,4},{6,7},{7,6},{8,9},{9,8},{10,11... | collective-permute-start | bytes 847880 | tf_op jit(solution)/shard_map/ppermute | solution.py:707
  17.8 1.2 %collective-permute-done.4.refs_2_ = bf16[1104,128]{1,0:T(8,128)(2,1)S(1)} collective-permute-done((bf16[1104,128]{1,0:T(8,128)(2,1)S(1)}, bf16[1104,128]{1,0:T(8,128)(2,1)S(1)}, u32[]{:S(2)}, u32[]{:S(2)}) %collective-permute-start.4) | collective-permute-done | bytes 282656 | tf_op jit(solution)/shard_map/ppermute | solution.py:707
  18.9 0.4 shard_map.51
  19.3 5.4 %collective-permute-start.5 = (bf16[288,128]{1,0:T(8,128)(2,1)S(1)}, bf16[288,128]{1,0:T(8,128)(2,1)S(1)}, u32[]{:S(2)}, u32[]{:S(2)}) collective-permute-start(bf16[288,128]{1,0:T(8,128)(2,1)S(1)} %get-tuple-element.57), channel_id=1, source_target_pairs={{0,8},{8,0},{16,24},{24,16},{1,9},{9,1},{17,25},{25,17},{2,10},{10... | collective-permute-start | bytes 221192 | tf_op jit(solution)/shard_map/ppermute | solution.py:715
  24.7 0.0 collective-permute-start.6
  24.7 1.3 %collective-permute-start.7 = (bf16[288,128]{1,0:T(8,128)(2,1)S(1)}, bf16[288,128]{1,0:T(8,128)(2,1)S(1)}, u32[]{:S(2)}, u32[]{:S(2)}) collective-permute-start(bf16[288,128]{1,0:T(8,128)(2,1)S(1)} %get-tuple-element.59), channel_id=1, source_target_pairs={{0,24},{8,16},{16,8},{24,0},{1,25},{9,17},{17,9},{25,1},{2,26},{10... | collective-permute-start | bytes 221192 | tf_op jit(solution)/shard_map/ppermute | solution.py:715
  26.0 1.0 %collective-permute-done.5.refs_2_ = bf16[288,128]{1,0:T(8,128)(2,1)S(1)} collective-permute-done((bf16[288,128]{1,0:T(8,128)(2,1)S(1)}, bf16[288,128]{1,0:T(8,128)(2,1)S(1)}, u32[]{:S(2)}, u32[]{:S(2)}) %collective-permute-start.5) | collective-permute-done | bytes 73760 | tf_op jit(solution)/shard_map/ppermute | solution.py:715
  27.0 0.9 %collective-permute-done.6.refs_3_ = bf16[288,128]{1,0:T(8,128)(2,1)S(1)} collective-permute-done((bf16[288,128]{1,0:T(8,128)(2,1)S(1)}, bf16[288,128]{1,0:T(8,128)(2,1)S(1)}, u32[]{:S(2)}, u32[]{:S(2)}) %collective-permute-start.6) | collective-permute-done | bytes 73760 | tf_op jit(solution)/shard_map/ppermute | solution.py:715
  27.9 1.6 %collective-permute-done.7.refs_4_ = bf16[288,128]{1,0:T(8,128)(2,1)S(1)} collective-permute-done((bf16[288,128]{1,0:T(8,128)(2,1)S(1)}, bf16[288,128]{1,0:T(8,128)(2,1)S(1)}, u32[]{:S(2)}, u32[]{:S(2)}) %collective-permute-start.7) | collective-permute-done | bytes 73760 | tf_op jit(solution)/shard_map/ppermute | solution.py:715
  29.5 0.4 shard_map.52
  29.8 3.1 %collective-permute-start.10 = (bf16[288,128]{1,0:T(8,128)(2,1)S(1)}, bf16[288,128]{1,0:T(8,128)(2,1)S(1)}, u32[]{:S(2)}, u32[]{:S(2)}) collective-permute-start(bf16[288,128]{1,0:T(8,128)(2,1)S(1)} %get-tuple-element.62), channel_id=1, source_target_pairs={{0,6},{1,7},{2,4},{3,5},{4,2},{5,3},{6,0},{7,1},{8,14},{9,15},{10,... | collective-permute-start | bytes 221192 | tf_op jit(solution)/shard_map/ppermute | solution.py:725
  33.0 0.0 collective-permute-start.9
  33.0 0.5 collective-permute-start.8
  33.5 0.3 shard_map.53.refs_5_
  33.8 1.3 %collective-permute-done.10.refs_4_ = bf16[288,128]{1,0:T(8,128)(2,1)S(1)} collective-permute-done((bf16[288,128]{1,0:T(8,128)(2,1)S(1)}, bf16[288,128]{1,0:T(8,128)(2,1)S(1)}, u32[]{:S(2)}, u32[]{:S(2)}) %collective-permute-start.10) | collective-permute-done | bytes 73760 | tf_op jit(solution)/shard_map/ppermute | solution.py:725
  35.0 5.0 %collective-permute-done.9.refs_3_ = bf16[288,128]{1,0:T(8,128)(2,1)S(1)} collective-permute-done((bf16[288,128]{1,0:T(8,128)(2,1)S(1)}, bf16[288,128]{1,0:T(8,128)(2,1)S(1)}, u32[]{:S(2)}, u32[]{:S(2)}) %collective-permute-start.9) | collective-permute-done | bytes 73760 | tf_op jit(solution)/shard_map/ppermute | solution.py:725
  40.0 0.0 collective-permute-done.8.refs_2_
  40.0 0.4 shard_map.54
  40.4 0.6 %collective-permute-start.13 = (bf16[272,128]{1,0:T(8,128)(2,1)S(1)}, bf16[272,128]{1,0:T(8,128)(2,1)S(1)}, u32[]{:S(2)}, u32[]{:S(2)}) collective-permute-start(bf16[272,128]{1,0:T(8,128)(2,1)S(1)} %get-tuple-element.63.refs_0_), channel_id=1, source_target_pairs={{0,24},{8,16},{16,8},{24,0},{1,25},{9,17},{17,9},{25,1},{2,26},{10... | collective-permute-start | bytes 208904 | tf_op jit(solution)/shard_map/ppermute | solution.py:735
  41.1 1.3 %collective-permute-start.12 = (bf16[272,128]{1,0:T(8,128)(2,1)S(1)}, bf16[272,128]{1,0:T(8,128)(2,1)S(1)}, u32[]{:S(2)}, u32[]{:S(2)}) collective-permute-start(bf16[272,128]{1,0:T(8,128)(2,1)S(1)} %get-tuple-element.63.refs_0_), channel_id=1, source_target_pairs={{0,16},{8,24},{16,0},{24,8},{1,17},{9,25},{17,1},{25,9},{2,18},{10... | collective-permute-start | bytes 208904 | tf_op jit(solution)/shard_map/ppermute | solution.py:735
  42.3 0.8 %collective-permute-start.11 = (bf16[272,128]{1,0:T(8,128)(2,1)S(1)}, bf16[272,128]{1,0:T(8,128)(2,1)S(1)}, u32[]{:S(2)}, u32[]{:S(2)}) collective-permute-start(bf16[272,128]{1,0:T(8,128)(2,1)S(1)} %get-tuple-element.63.refs_0_), channel_id=1, source_target_pairs={{0,8},{8,0},{16,24},{24,16},{1,9},{9,1},{17,25},{25,17},{2,10},{10... | collective-permute-start | bytes 208904 | tf_op jit(solution)/shard_map/ppermute | solution.py:735
  43.1 1.1 %shard_map.57.refs_13_ = bf16[4608,256]{1,0:T(8,128)(2,1)S(1)} custom-call(bf16[9,256,512]{2,1,0:T(8,128)(2,1)S(1)} %bitcast.12), custom_call_target="tpu_custom_call" | custom-call | flops 2000000000 | bytes 4718592 | tf_op jit(solution)/shard_map/pallas_call | solution.py:562
  44.2 0.4 collective-permute-done.13.refs_4_
  44.7 0.3 collective-permute-done.12.refs_3_
  45.0 1.5 %collective-permute-done.11.refs_2_ = bf16[272,128]{1,0:T(8,128)(2,1)S(1)} collective-permute-done((bf16[272,128]{1,0:T(8,128)(2,1)S(1)}, bf16[272,128]{1,0:T(8,128)(2,1)S(1)}, u32[]{:S(2)}, u32[]{:S(2)}) %collective-permute-start.11) | collective-permute-done | bytes 69664 | tf_op jit(solution)/shard_map/ppermute | solution.py:735
  46.5 2.0 %collective-permute-start.14 = (bf16[1104,128]{1,0:T(8,128)(2,1)S(1)}, bf16[1104,128]{1,0:T(8,128)(2,1)S(1)}, u32[]{:S(2)}, u32[]{:S(2)}) collective-permute-start(bf16[1104,128]{1,0:T(8,128)(2,1)S(1)} %shard_map.55.refs_10_), channel_id=1, source_target_pairs={{0,1},{1,0},{2,3},{3,2},{4,5},{5,4},{6,7},{7,6},{8,9},{9,8},{10,11... | collective-permute-start | bytes 847880 | tf_op jit(solution)/shard_map/ppermute | solution.py:740
  48.5 1.7 %shard_map.56.refs_12_ = bf16[4608,512]{1,0:T(8,128)(2,1)S(1)} custom-call(bf16[9,512,512]{2,1,0:T(8,128)(2,1)S(1)} %bitcast.8), custom_call_target="tpu_custom_call" | custom-call | flops 2000000000 | bytes 9437184 | tf_op jit(solution)/shard_map/pallas_call | solution.py:562
  50.2 3.0 %shard_map.50 = (f32[320,512]{1,0:T(8,128)S(1)}, f32[320,512]{1,0:T(8,128)S(1)}) custom-call(bf16[4,72,256]{2,1,0:T(8,128)(2,1)S(1)} %collective-permute-done.2.refs_0_, bf16[4,72,256]{2,1,0:T(8,128)(2,1)S(1)} %collective-permute-done.3.refs_1_, bf16[448,512]{1,0:T(8,128)(2,1)S(1)} %get-tuple-element.49.refs_2_, bf16[2304,512]{1,0:T(8,128)(2,1)S(1)} %bitcast.13, ...), custom_call_target="tpu_custom_call" | custom-call | flops 2264924160 | bytes 9142272 | tf_op jit(solution)/shard_map/pallas_call | solution.py:562
  53.1 0.0 collective-permute-done.14.refs_11_
  53.1 7.7 %shard_map.58 = f32[8,64,256]{2,1,0:T(8,128)} custom-call(f32[480,512]{1,0:T(8,128)S(1)} %get-tuple-element.37.refs_4_.refs_0_, f32[480,512]{1,0:T(8,128)S(1)} %get-tuple-element.38.refs_1_, f32[320,512]{1,0:T(8,128)S(1)} %get-tuple-element.44.refs_2_, f32[320,512]{1,0:T(8,128)S(1)} %get-tuple-element.45.refs_3_, ...), custom_call_target="tpu_custom_call" | custom-call | flops 5284823040 | bytes 15376384 | tf_op jit(solution)/shard_map/pallas_call | solution.py:562
  (6 shorter events, 0.0 us)
Async XLA Ops:
  0.0 7.0 %copy-start.2 = (f32[8,64,256]{2,1,0:T(8,128)S(1)}, f32[8,64,256]{2,1,0:T(8,128)}, u32[]{:S(2)}) copy-start(f32[8,64,256]{2,1,0:T(8,128)} %refs_0_.6) | copy-start | bytes 1572868
  1.0 6.0 %collective-permute-start = (bf16[8,4,256]{2,1,0:T(4,128)(2,1)S(1)}, bf16[8,4,256]{2,1,0:T(4,128)(2,1)S(1)}, u32[]{:S(2)}, u32[]{:S(2)}) collective-permute-start(bf16[8,4,256]{2,1,0:T(4,128)(2,1)S(1)} %get-tuple-element.35), channel_id=1, source_target_pairs={{1,2},{3,4},{5,6},{2,1},{4,3},{6,5},{9,10},{11,12},{13,14},{10,9},... | collective-permute-start | bytes 49160 | tf_op jit(solution)/shard_map/ppermute | solution.py:602
  5.6 3.4 %slice-start = ((s8[4718592]{0:T(1024)(128)(4,1)}), s8[4194304]{0:T(1024)(128)(4,1)S(1)}, s32[]{:S(2)}) async-start(s8[4718592]{0:T(1024)(128)(4,1)} %bitcast.4), calls=%async_computation | async-start | bytes 8388608
  5.6 3.4 %slice-start.1 = ((s8[4718592]{0:T(1024)(128)(4,1)}), s8[524288]{0:T(1024)(128)(4,1)S(1)}, s32[]{:S(2)}) async-start(s8[4718592]{0:T(1024)(128)(4,1)} %bitcast.4), calls=%async_computation.1 | async-start | bytes 1048576
  5.6 3.4 %copy-start = (bf16[3,3,256,512]{3,2,1,0:T(8,128)(2,1)S(1)}, bf16[3,3,256,512]{3,2,1,0:T(8,128)(2,1)}, u32[]{:S(2)}) copy-start(bf16[3,3,256,512]{3,2,1,0:T(8,128)(2,1)} %param.5) | copy-start | bytes 7077892
  5.6 1.4 %collective-permute-start.1 = (bf16[8,4,256]{2,1,0:T(4,128)(2,1)S(1)}, bf16[8,4,256]{2,1,0:T(4,128)(2,1)S(1)}, u32[]{:S(2)}, u32[]{:S(2)}) collective-permute-start(bf16[8,4,256]{2,1,0:T(4,128)(2,1)S(1)} %get-tuple-element.36), channel_id=1, source_target_pairs={{0,1},{1,0},{2,3},{3,2},{4,5},{5,4},{6,7},{7,6},{8,9},{9,8},{10,11... | collective-permute-start | bytes 49160 | tf_op jit(solution)/shard_map/ppermute | solution.py:603
  7.1 5.7 %collective-permute-start.2 = (bf16[4,72,256]{2,1,0:T(8,128)(2,1)S(1)}, bf16[4,72,256]{2,1,0:T(8,128)(2,1)S(1)}, u32[]{:S(2)}, u32[]{:S(2)}) collective-permute-start(bf16[4,72,256]{2,1,0:T(8,128)(2,1)S(1)} %get-tuple-element.39), channel_id=1, source_target_pairs={{0,8},{16,24},{8,0},{24,16},{1,9},{17,25},{9,1},{25,17},{2,10},{18... | collective-permute-start | bytes 442376 | tf_op jit(solution)/shard_map/ppermute | solution.py:617
  8.3 4.4 %collective-permute-start.3 = (bf16[4,72,256]{2,1,0:T(8,128)(2,1)S(1)}, bf16[4,72,256]{2,1,0:T(8,128)(2,1)S(1)}, u32[]{:S(2)}, u32[]{:S(2)}) collective-permute-start(bf16[4,72,256]{2,1,0:T(8,128)(2,1)S(1)} %get-tuple-element.40), channel_id=1, source_target_pairs={{8,16},{16,8},{9,17},{17,9},{10,18},{18,10},{11,19},{19,11},{12,20... | collective-permute-start | bytes 442376 | tf_op jit(solution)/shard_map/ppermute | solution.py:618
  12.7 20.7 %copy-start.1 = (f32[2,512,512]{2,1,0:T(8,128)S(1)}, f32[2,512,512]{2,1,0:T(8,128)}, u32[]{:S(2)}) copy-start(f32[2,512,512]{2,1,0:T(8,128)} %refs_0_.7) | copy-start | bytes 6291460
  17.0 1.9 %collective-permute-start.4 = (bf16[1104,128]{1,0:T(8,128)(2,1)S(1)}, bf16[1104,128]{1,0:T(8,128)(2,1)S(1)}, u32[]{:S(2)}, u32[]{:S(2)}) collective-permute-start(bf16[1104,128]{1,0:T(8,128)(2,1)S(1)} %get-tuple-element.54), channel_id=1, source_target_pairs={{0,1},{1,0},{2,3},{3,2},{4,5},{5,4},{6,7},{7,6},{8,9},{9,8},{10,11... | collective-permute-start | bytes 847880 | tf_op jit(solution)/shard_map/ppermute | solution.py:707
  19.3 7.7 %collective-permute-start.5 = (bf16[288,128]{1,0:T(8,128)(2,1)S(1)}, bf16[288,128]{1,0:T(8,128)(2,1)S(1)}, u32[]{:S(2)}, u32[]{:S(2)}) collective-permute-start(bf16[288,128]{1,0:T(8,128)(2,1)S(1)} %get-tuple-element.57), channel_id=1, source_target_pairs={{0,8},{8,0},{16,24},{24,16},{1,9},{9,1},{17,25},{25,17},{2,10},{10... | collective-permute-start | bytes 221192 | tf_op jit(solution)/shard_map/ppermute | solution.py:715
  24.7 3.2 %collective-permute-start.6 = (bf16[288,128]{1,0:T(8,128)(2,1)S(1)}, bf16[288,128]{1,0:T(8,128)(2,1)S(1)}, u32[]{:S(2)}, u32[]{:S(2)}) collective-permute-start(bf16[288,128]{1,0:T(8,128)(2,1)S(1)} %get-tuple-element.58), channel_id=1, source_target_pairs={{0,16},{8,24},{16,0},{24,8},{1,17},{9,25},{17,1},{25,9},{2,18},{10... | collective-permute-start | bytes 221192 | tf_op jit(solution)/shard_map/ppermute | solution.py:715
  24.7 4.8 %collective-permute-start.7 = (bf16[288,128]{1,0:T(8,128)(2,1)S(1)}, bf16[288,128]{1,0:T(8,128)(2,1)S(1)}, u32[]{:S(2)}, u32[]{:S(2)}) collective-permute-start(bf16[288,128]{1,0:T(8,128)(2,1)S(1)} %get-tuple-element.59), channel_id=1, source_target_pairs={{0,24},{8,16},{16,8},{24,0},{1,25},{9,17},{17,9},{25,1},{2,26},{10... | collective-permute-start | bytes 221192 | tf_op jit(solution)/shard_map/ppermute | solution.py:715
  29.8 5.2 %collective-permute-start.10 = (bf16[288,128]{1,0:T(8,128)(2,1)S(1)}, bf16[288,128]{1,0:T(8,128)(2,1)S(1)}, u32[]{:S(2)}, u32[]{:S(2)}) collective-permute-start(bf16[288,128]{1,0:T(8,128)(2,1)S(1)} %get-tuple-element.62), channel_id=1, source_target_pairs={{0,6},{1,7},{2,4},{3,5},{4,2},{5,3},{6,0},{7,1},{8,14},{9,15},{10,... | collective-permute-start | bytes 221192 | tf_op jit(solution)/shard_map/ppermute | solution.py:725
  33.0 7.1 %collective-permute-start.9 = (bf16[288,128]{1,0:T(8,128)(2,1)S(1)}, bf16[288,128]{1,0:T(8,128)(2,1)S(1)}, u32[]{:S(2)}, u32[]{:S(2)}) collective-permute-start(bf16[288,128]{1,0:T(8,128)(2,1)S(1)} %get-tuple-element.62), channel_id=1, source_target_pairs={{0,4},{1,5},{2,6},{3,7},{4,0},{5,1},{6,2},{7,3},{8,12},{9,13},{10,... | collective-permute-start | bytes 221192 | tf_op jit(solution)/shard_map/ppermute | solution.py:725
  33.0 7.1 %collective-permute-start.8 = (bf16[288,128]{1,0:T(8,128)(2,1)S(1)}, bf16[288,128]{1,0:T(8,128)(2,1)S(1)}, u32[]{:S(2)}, u32[]{:S(2)}) collective-permute-start(bf16[288,128]{1,0:T(8,128)(2,1)S(1)} %get-tuple-element.62), channel_id=1, source_target_pairs={{0,2},{1,3},{2,0},{3,1},{4,6},{5,7},{6,4},{7,5},{8,10},{9,11},{10,... | collective-permute-start | bytes 221192 | tf_op jit(solution)/shard_map/ppermute | solution.py:725
  40.4 4.2 %collective-permute-start.13 = (bf16[272,128]{1,0:T(8,128)(2,1)S(1)}, bf16[272,128]{1,0:T(8,128)(2,1)S(1)}, u32[]{:S(2)}, u32[]{:S(2)}) collective-permute-start(bf16[272,128]{1,0:T(8,128)(2,1)S(1)} %get-tuple-element.63.refs_0_), channel_id=1, source_target_pairs={{0,24},{8,16},{16,8},{24,0},{1,25},{9,17},{17,9},{25,1},{2,26},{10... | collective-permute-start | bytes 208904 | tf_op jit(solution)/shard_map/ppermute | solution.py:735
  41.1 3.9 %collective-permute-start.12 = (bf16[272,128]{1,0:T(8,128)(2,1)S(1)}, bf16[272,128]{1,0:T(8,128)(2,1)S(1)}, u32[]{:S(2)}, u32[]{:S(2)}) collective-permute-start(bf16[272,128]{1,0:T(8,128)(2,1)S(1)} %get-tuple-element.63.refs_0_), channel_id=1, source_target_pairs={{0,16},{8,24},{16,0},{24,8},{1,17},{9,25},{17,1},{25,9},{2,18},{10... | collective-permute-start | bytes 208904 | tf_op jit(solution)/shard_map/ppermute | solution.py:735
  42.3 4.1 %collective-permute-start.11 = (bf16[272,128]{1,0:T(8,128)(2,1)S(1)}, bf16[272,128]{1,0:T(8,128)(2,1)S(1)}, u32[]{:S(2)}, u32[]{:S(2)}) collective-permute-start(bf16[272,128]{1,0:T(8,128)(2,1)S(1)} %get-tuple-element.63.refs_0_), channel_id=1, source_target_pairs={{0,8},{8,0},{16,24},{24,16},{1,9},{9,1},{17,25},{25,17},{2,10},{10... | collective-permute-start | bytes 208904 | tf_op jit(solution)/shard_map/ppermute | solution.py:735
  46.5 6.7 %collective-permute-start.14 = (bf16[1104,128]{1,0:T(8,128)(2,1)S(1)}, bf16[1104,128]{1,0:T(8,128)(2,1)S(1)}, u32[]{:S(2)}, u32[]{:S(2)}) collective-permute-start(bf16[1104,128]{1,0:T(8,128)(2,1)S(1)} %shard_map.55.refs_10_), channel_id=1, source_target_pairs={{0,1},{1,0},{2,3},{3,2},{4,5},{5,4},{6,7},{7,6},{8,9},{9,8},{10,11... | collective-permute-start | bytes 847880 | tf_op jit(solution)/shard_map/ppermute | solution.py:740

commit v10 on v9

--- a/solution.py
+++ b/solution.py
@@ -256,8 +256,8 @@
 
 
 def front(dims, place, even, odd, taps1, taps2, act1, act2, w1, w2, *rest):
-    (taps2b, act1b, slope1b, act2b, slope2b, keep, mine, sent) = rest[:8]
-    (rim, buf, centred, stat) = rest[8:]
+    (taps2b, act1b, slope1b, act2b, slope2b, centred, mine, sent) = rest[:8]
+    (rim, buf, stat) = rest[8:]
     height, breadth, groups, limits = dims
     pitch = groups * 16
     width = w1.shape[1]
@@ -302,20 +302,27 @@
         stat[layer] = jnp.zeros(stat.shape[1:], F32)
         put_mean(stat.at[layer, 0:EXTRA], mean, 2)
         put_mean(stat.at[layer, EXTRA : 2 * EXTRA], mean, 1)
-    rows = keep.shape[0]
-
-    def give(at, value):
+    rows = sent.shape[0] - EXTRA
+
+    def put(at, value):
         sent[at : at + value.shape[0], :] = value.astype(BF)
 
-    def hold(at, value):
-        keep[at : at + value.shape[0], :] = value
-
-    for layer, put in ((1 - place[0], give), (place[0], hold)):
-        emit, finish = packer(width, rows, put)
-        panels(centred[layer], centred[layer], emit)
-        finish()
+    emit, finish = packer(width, rows, put)
+    other = centred[1 - place[0]]
+    panels(other, other, emit)
+    finish()
     mine[...] = stat[place[0], EXTRA : EXTRA + 8, :]
     sent[rows:, :] = stat[1 - place[0], 0:EXTRA, :].astype(BF)
+
+
+def hold(place, centred, keep):
+    def put(at, value):
+        keep[at : at + value.shape[0], :] = value
+
+    own = centred[place[0]]
+    emit, finish = packer(own.shape[1], keep.shape[0], put)
+    panels(own, own, emit)
+    finish()
 
 
 def ring(dims, place, even, odd, taps2b, w1, w2, act2, slope2, rim, outer, buf):
@@ -638,21 +645,20 @@
         flops=cost(height - 2, height - 4),
         limit=24,
     )
-    taps2b, act1b, slope1b, act2b, slope2b, keep, mine, sent = call(
+    taps2b, act1b, slope1b, act2b, slope2b, centred, mine, sent = call(
         functools.partial(front, dims),
         [place, even, odd, taps1, taps2, act1, act2, w1, w2],
         [shape((4 * wider, width), BF)]
         + maps(4)
         + maps(4)
         + [
-            shape((packed, BLOCK), F32),
+            shape((2, height * pitch, width), BF),
             shape((8, BLOCK), F32),
             shape((packed + EXTRA, BLOCK), BF),
         ],
         [
             pltpu.VMEM((4 * wider, depth), BF),
             pltpu.VMEM((depth // BLOCK, 4 * space, BLOCK), F32),
-            pltpu.VMEM((2, height * pitch, width), BF),
             pltpu.VMEM((2, 2 * EXTRA, BLOCK), F32),
         ],
         flops=cost(4, 4),
@@ -705,6 +711,13 @@
     message = shape((chunk + EXTRA, BLOCK), BF)
     part, centre = shape((chunk, BLOCK), F32), shape((8, BLOCK), F32)
     got = lax.ppermute(sent, "tile", swap)
+    (keep,) = call(
+        hold,
+        [place, centred],
+        [shape((packed, BLOCK), F32)],
+        [],
+        flops=2 * width * width * height * pitch,
+    )
     share, mean, *sents = call(
         functools.partial(merge_pair, (cells, groups, blocks)),
         [place, keep, mine, got],

time: 61 us -> 60.8 us (level)
    pallas_call x13 -> x14, Pallas kernels: 23.8 us -> 24.1 us  [call(): pl.pallas_call(body, out_shape=tuple(outs), in_specs=[HBM if n in far els...]
  transfers between devices with their start and end apart: 15 -> 15, of which waited for: 10 -> 10; matrix products, arithmetic and copies ran while one was open for 0% -> 0% of each run, Pallas kernels for 16% -> 17%
where the time goes in v10:
time: 60.8 us; the launch traced here: 60.6 us
  Pallas kernels  24.1 us (40%)
  starting transfers between devices  22.2 us (37%)
  waiting for transfers between devices  14 us (23%)
    pallas_call x14, Pallas kernels, call(): pl.pallas_call(body, out_shape=tuple(outs), in_specs=[HBM if n in far els...  24.1 us
    ppermute x3, starting transfers between devices, local(): lax.ppermute(sents[k - 1], 'grp', [(i, i ^ k) for i in range(groups)])  6.64 us
    ppermute x3, waiting for transfers between devices, local(): lax.ppermute(sent, 'tile', [(i, i ^ 2 * k) for i in range(tiles)])  6.28 us
    ppermute x1, starting transfers between devices, local(): far = lax.ppermute(far, 'tile', cross)  4.58 us
    ppermute x3, starting transfers between devices, local(): lax.ppermute(sent, 'tile', [(i, i ^ 2 * k) for i in range(tiles)])  3.61 us
    ppermute x3, waiting for transfers between devices, local(): lax.ppermute(sents[k - 1], 'grp', [(i, i ^ k) for i in range(groups)])  3.53 us
    ppermute x3, starting transfers between devices, local(): lax.ppermute(share, 'grp', [(i, i ^ k) for i in range(groups)])  2.71 us
    ppermute x3, waiting for transfers between devices, local(): lax.ppermute(share, 'grp', [(i, i ^ k) for i in range(groups)])  2.2 us
  transfers between devices with their start and end apart: 15, of which 10 were waited for; matrix products, arithmetic and copies ran while one was open for 0% of the time, Pallas kernels for 17%

profile of v10, /device:TPU:1, one launch (start us, length us, event | category | flops | bytes accessed | tf_op | source)
XLA Modules:
  0.0 60.6 jit_solution(12018895830584920779)
XLA Ops:
  0.0 1.0 %shard_map.46 = (bf16[8,4,256]{2,1,0:T(4,128)(2,1)S(1)}, bf16[8,4,256]{2,1,0:T(4,128)(2,1)S(1)}) custom-call(f32[8,64,256]{2,1,0:T(8,128)} %refs_0_.6), custom_call_target="tpu_custom_call" | custom-call | flops 4000000000 | bytes 557056 | tf_op jit(solution)/shard_map/pallas_call | solution.py:569
  1.0 4.6 %collective-permute-start = (bf16[8,4,256]{2,1,0:T(4,128)(2,1)S(1)}, bf16[8,4,256]{2,1,0:T(4,128)(2,1)S(1)}, u32[]{:S(2)}, u32[]{:S(2)}) collective-permute-start(bf16[8,4,256]{2,1,0:T(4,128)(2,1)S(1)} %get-tuple-element.35), channel_id=1, source_target_pairs={{1,2},{3,4},{5,6},{2,1},{4,3},{6,5},{9,10},{11,12},{13,14},{10,9},... | collective-permute-start | bytes 49160 | tf_op jit(solution)/shard_map/ppermute | solution.py:609
  5.6 0.0 slice-start
  5.6 0.0 slice-start.1
  5.6 0.0 copy-start
  5.6 0.1 collective-permute-start.1
  5.7 1.3 %collective-permute-done.refs_1_ = bf16[8,4,256]{2,1,0:T(4,128)(2,1)S(1)} collective-permute-done((bf16[8,4,256]{2,1,0:T(4,128)(2,1)S(1)}, bf16[8,4,256]{2,1,0:T(4,128)(2,1)S(1)}, u32[]{:S(2)}, u32[]{:S(2)}) %collective-permute-start) | collective-permute-done | bytes 16416 | tf_op jit(solution)/shard_map/ppermute | solution.py:609
  7.0 0.0 collective-permute-done.1.refs_2_
  7.0 0.0 copy-done.2
  7.0 0.1 shard_map.48
  7.1 1.3 %collective-permute-start.2 = (bf16[4,72,256]{2,1,0:T(8,128)(2,1)S(1)}, bf16[4,72,256]{2,1,0:T(8,128)(2,1)S(1)}, u32[]{:S(2)}, u32[]{:S(2)}) collective-permute-start(bf16[4,72,256]{2,1,0:T(8,128)(2,1)S(1)} %get-tuple-element.39), channel_id=1, source_target_pairs={{0,8},{16,24},{8,0},{24,16},{1,9},{17,25},{9,1},{25,17},{2,10},{18... | collective-permute-start | bytes 442376 | tf_op jit(solution)/shard_map/ppermute | solution.py:624
  8.3 0.7 %collective-permute-start.3 = (bf16[4,72,256]{2,1,0:T(8,128)(2,1)S(1)}, bf16[4,72,256]{2,1,0:T(8,128)(2,1)S(1)}, u32[]{:S(2)}, u32[]{:S(2)}) collective-permute-start(bf16[4,72,256]{2,1,0:T(8,128)(2,1)S(1)} %get-tuple-element.40), channel_id=1, source_target_pairs={{8,16},{16,8},{9,17},{17,9},{10,18},{18,10},{11,19},{19,11},{12,20... | collective-permute-start | bytes 442376 | tf_op jit(solution)/shard_map/ppermute | solution.py:625
  9.0 3.7 %shard_map.47 = (bf16[896,256]{1,0:T(8,128)(2,1)S(1)}, bf16[672,512]{1,0:T(8,128)(2,1)S(1)}, f32[480,512]{1,0:T(8,128)S(1)}, f32[480,512]{1,0:T(8,128)S(1)}, f32...) custom-call(f32[8,64,256]{2,1,0:T(8,128)S(1)} %copy-done.2, bf16[8,4,256]{2,1,0:T(4,128)(2,1)S(1)} %collective-permute-done.refs_1_, ...), custom_call_target="tpu_custom_call" | custom-call | flops 2642411520 | bytes 12058624 | tf_op jit(solution)/shard_map/pallas_call | solution.py:569
  12.7 0.0 collective-permute-done.2.refs_0_
  12.7 0.0 collective-permute-done.3.refs_1_
  12.7 4.0 %shard_map.49 = (bf16[448,512]{1,0:T(8,128)(2,1)S(1)}, f32[320,512]{1,0:T(8,128)S(1)}, f32[320,512]{1,0:T(8,128)S(1)}, f32[320,512]{1,0:T(8,128)S(1)}, f32[320,5...) custom-call(bf16[4,72,256]{2,1,0:T(8,128)(2,1)S(1)} %collective-permute-, ...), custom_call_target="tpu_custom_call" | custom-call | flops 2264924160 | bytes 14835712 | tf_op jit(solution)/shard_map/pallas_call | solution.py:569
  16.8 0.0 copy-start.1
  16.8 0.7 %collective-permute-start.4 = (bf16[1104,128]{1,0:T(8,128)(2,1)S(1)}, bf16[1104,128]{1,0:T(8,128)(2,1)S(1)}, u32[]{:S(2)}, u32[]{:S(2)}) collective-permute-start(bf16[1104,128]{1,0:T(8,128)(2,1)S(1)} %get-tuple-element.54), channel_id=1, source_target_pairs={{0,1},{1,0},{2,3},{3,2},{4,5},{5,4},{6,7},{7,6},{8,9},{9,8},{10,11... | collective-permute-start | bytes 847880 | tf_op jit(solution)/shard_map/ppermute | solution.py:713
  17.5 0.5 shard_map.51.refs_0_
  18.0 0.7 %collective-permute-done.4.refs_2_ = bf16[1104,128]{1,0:T(8,128)(2,1)S(1)} collective-permute-done((bf16[1104,128]{1,0:T(8,128)(2,1)S(1)}, bf16[1104,128]{1,0:T(8,128)(2,1)S(1)}, u32[]{:S(2)}, u32[]{:S(2)}) %collective-permute-start.4) | collective-permute-done | bytes 282656 | tf_op jit(solution)/shard_map/ppermute | solution.py:713
  18.7 0.4 shard_map.52
  19.1 5.4 %collective-permute-start.5 = (bf16[288,128]{1,0:T(8,128)(2,1)S(1)}, bf16[288,128]{1,0:T(8,128)(2,1)S(1)}, u32[]{:S(2)}, u32[]{:S(2)}) collective-permute-start(bf16[288,128]{1,0:T(8,128)(2,1)S(1)} %get-tuple-element.57), channel_id=1, source_target_pairs={{0,8},{8,0},{16,24},{24,16},{1,9},{9,1},{17,25},{25,17},{2,10},{10... | collective-permute-start | bytes 221192 | tf_op jit(solution)/shard_map/ppermute | solution.py:728
  24.5 0.0 collective-permute-start.6
  24.5 1.3 %collective-permute-start.7 = (bf16[288,128]{1,0:T(8,128)(2,1)S(1)}, bf16[288,128]{1,0:T(8,128)(2,1)S(1)}, u32[]{:S(2)}, u32[]{:S(2)}) collective-permute-start(bf16[288,128]{1,0:T(8,128)(2,1)S(1)} %get-tuple-element.59), channel_id=1, source_target_pairs={{0,24},{8,16},{16,8},{24,0},{1,25},{9,17},{17,9},{25,1},{2,26},{10... | collective-permute-start | bytes 221192 | tf_op jit(solution)/shard_map/ppermute | solution.py:728
  25.7 1.0 %collective-permute-done.5.refs_2_ = bf16[288,128]{1,0:T(8,128)(2,1)S(1)} collective-permute-done((bf16[288,128]{1,0:T(8,128)(2,1)S(1)}, bf16[288,128]{1,0:T(8,128)(2,1)S(1)}, u32[]{:S(2)}, u32[]{:S(2)}) %collective-permute-start.5) | collective-permute-done | bytes 73760 | tf_op jit(solution)/shard_map/ppermute | solution.py:728
  26.7 0.9 %collective-permute-done.6.refs_3_ = bf16[288,128]{1,0:T(8,128)(2,1)S(1)} collective-permute-done((bf16[288,128]{1,0:T(8,128)(2,1)S(1)}, bf16[288,128]{1,0:T(8,128)(2,1)S(1)}, u32[]{:S(2)}, u32[]{:S(2)}) %collective-permute-start.6) | collective-permute-done | bytes 73760 | tf_op jit(solution)/shard_map/ppermute | solution.py:728
  27.7 1.6 %collective-permute-done.7.refs_4_ = bf16[288,128]{1,0:T(8,128)(2,1)S(1)} collective-permute-done((bf16[288,128]{1,0:T(8,128)(2,1)S(1)}, bf16[288,128]{1,0:T(8,128)(2,1)S(1)}, u32[]{:S(2)}, u32[]{:S(2)}) %collective-permute-start.7) | collective-permute-done | bytes 73760 | tf_op jit(solution)/shard_map/ppermute | solution.py:728
  29.3 0.4 shard_map.53
  29.6 3.1 %collective-permute-start.10 = (bf16[288,128]{1,0:T(8,128)(2,1)S(1)}, bf16[288,128]{1,0:T(8,128)(2,1)S(1)}, u32[]{:S(2)}, u32[]{:S(2)}) collective-permute-start(bf16[288,128]{1,0:T(8,128)(2,1)S(1)} %get-tuple-element.62), channel_id=1, source_target_pairs={{0,6},{1,7},{2,4},{3,5},{4,2},{5,3},{6,0},{7,1},{8,14},{9,15},{10,... | collective-permute-start | bytes 221192 | tf_op jit(solution)/shard_map/ppermute | solution.py:738
  32.8 0.0 collective-permute-start.9
  32.8 0.5 collective-permute-start.8
  33.3 0.3 shard_map.54.refs_5_
  33.6 1.3 %collective-permute-done.10.refs_4_ = bf16[288,128]{1,0:T(8,128)(2,1)S(1)} collective-permute-done((bf16[288,128]{1,0:T(8,128)(2,1)S(1)}, bf16[288,128]{1,0:T(8,128)(2,1)S(1)}, u32[]{:S(2)}, u32[]{:S(2)}) %collective-permute-start.10) | collective-permute-done | bytes 73760 | tf_op jit(solution)/shard_map/ppermute | solution.py:738
  34.8 5.0 %collective-permute-done.9.refs_3_ = bf16[288,128]{1,0:T(8,128)(2,1)S(1)} collective-permute-done((bf16[288,128]{1,0:T(8,128)(2,1)S(1)}, bf16[288,128]{1,0:T(8,128)(2,1)S(1)}, u32[]{:S(2)}, u32[]{:S(2)}) %collective-permute-start.9) | collective-permute-done | bytes 73760 | tf_op jit(solution)/shard_map/ppermute | solution.py:738
  39.8 0.0 collective-permute-done.8.refs_2_
  39.8 0.4 shard_map.55
  40.2 0.6 %collective-permute-start.13 = (bf16[272,128]{1,0:T(8,128)(2,1)S(1)}, bf16[272,128]{1,0:T(8,128)(2,1)S(1)}, u32[]{:S(2)}, u32[]{:S(2)}) collective-permute-start(bf16[272,128]{1,0:T(8,128)(2,1)S(1)} %get-tuple-element.63.refs_0_), channel_id=1, source_target_pairs={{0,24},{8,16},{16,8},{24,0},{1,25},{9,17},{17,9},{25,1},{2,26},{10... | collective-permute-start | bytes 208904 | tf_op jit(solution)/shard_map/ppermute | solution.py:748
  40.9 1.2 %collective-permute-start.12 = (bf16[272,128]{1,0:T(8,128)(2,1)S(1)}, bf16[272,128]{1,0:T(8,128)(2,1)S(1)}, u32[]{:S(2)}, u32[]{:S(2)}) collective-permute-start(bf16[272,128]{1,0:T(8,128)(2,1)S(1)} %get-tuple-element.63.refs_0_), channel_id=1, source_target_pairs={{0,16},{8,24},{16,0},{24,8},{1,17},{9,25},{17,1},{25,9},{2,18},{10... | collective-permute-start | bytes 208904 | tf_op jit(solution)/shard_map/ppermute | solution.py:748
  42.1 0.8 %collective-permute-start.11 = (bf16[272,128]{1,0:T(8,128)(2,1)S(1)}, bf16[272,128]{1,0:T(8,128)(2,1)S(1)}, u32[]{:S(2)}, u32[]{:S(2)}) collective-permute-start(bf16[272,128]{1,0:T(8,128)(2,1)S(1)} %get-tuple-element.63.refs_0_), channel_id=1, source_target_pairs={{0,8},{8,0},{16,24},{24,16},{1,9},{9,1},{17,25},{25,17},{2,10},{10... | collective-permute-start | bytes 208904 | tf_op jit(solution)/shard_map/ppermute | solution.py:748
  42.9 1.1 %shard_map.58.refs_13_ = bf16[4608,256]{1,0:T(8,128)(2,1)S(1)} custom-call(bf16[9,256,512]{2,1,0:T(8,128)(2,1)S(1)} %bitcast.12), custom_call_target="tpu_custom_call" | custom-call | flops 2000000000 | bytes 4718592 | tf_op jit(solution)/shard_map/pallas_call | solution.py:569
  44.0 0.4 collective-permute-done.13.refs_4_
  44.5 0.3 collective-permute-done.12.refs_3_
  44.8 1.5 %collective-permute-done.11.refs_2_ = bf16[272,128]{1,0:T(8,128)(2,1)S(1)} collective-permute-done((bf16[272,128]{1,0:T(8,128)(2,1)S(1)}, bf16[272,128]{1,0:T(8,128)(2,1)S(1)}, u32[]{:S(2)}, u32[]{:S(2)}) %collective-permute-start.11) | collective-permute-done | bytes 69664 | tf_op jit(solution)/shard_map/ppermute | solution.py:748
  46.3 2.0 %collective-permute-start.14 = (bf16[1104,128]{1,0:T(8,128)(2,1)S(1)}, bf16[1104,128]{1,0:T(8,128)(2,1)S(1)}, u32[]{:S(2)}, u32[]{:S(2)}) collective-permute-start(bf16[1104,128]{1,0:T(8,128)(2,1)S(1)} %shard_map.56.refs_10_), channel_id=1, source_target_pairs={{0,1},{1,0},{2,3},{3,2},{4,5},{5,4},{6,7},{7,6},{8,9},{9,8},{10,11... | collective-permute-start | bytes 847880 | tf_op jit(solution)/shard_map/ppermute | solution.py:753
  48.2 1.7 %shard_map.57.refs_12_ = bf16[4608,512]{1,0:T(8,128)(2,1)S(1)} custom-call(bf16[9,512,512]{2,1,0:T(8,128)(2,1)S(1)} %bitcast.8), custom_call_target="tpu_custom_call" | custom-call | flops 2000000000 | bytes 9437184 | tf_op jit(solution)/shard_map/pallas_call | solution.py:569
  50.0 3.0 %shard_map.50 = (f32[320,512]{1,0:T(8,128)S(1)}, f32[320,512]{1,0:T(8,128)S(1)}) custom-call(bf16[4,72,256]{2,1,0:T(8,128)(2,1)S(1)} %collective-permute-done.2.refs_0_, bf16[4,72,256]{2,1,0:T(8,128)(2,1)S(1)} %collective-permute-done.3.refs_1_, bf16[448,512]{1,0:T(8,128)(2,1)S(1)} %get-tuple-element.49.refs_2_, bf16[2304,512]{1,0:T(8,128)(2,1)S(1)} %bitcast.13, ...), custom_call_target="tpu_custom_call" | custom-call | flops 2264924160 | bytes 9142272 | tf_op jit(solution)/shard_map/pallas_call | solution.py:569
  52.9 0.0 collective-permute-done.14.refs_11_
  52.9 7.6 %shard_map.59 = f32[8,64,256]{2,1,0:T(8,128)} custom-call(f32[480,512]{1,0:T(8,128)S(1)} %get-tuple-element.37.refs_4_.refs_0_, f32[480,512]{1,0:T(8,128)S(1)} %get-tuple-element.38.refs_1_, f32[320,512]{1,0:T(8,128)S(1)} %get-tuple-element.44.refs_2_, f32[320,512]{1,0:T(8,128)S(1)} %get-tuple-element.45.refs_3_, ...), custom_call_target="tpu_custom_call" | custom-call | flops 5284823040 | bytes 15376384 | tf_op jit(solution)/shard_map/pallas_call | solution.py:569
  (7 shorter events, 0.0 us)
Async XLA Ops:
  0.0 7.0 %copy-start.2 = (f32[8,64,256]{2,1,0:T(8,128)S(1)}, f32[8,64,256]{2,1,0:T(8,128)}, u32[]{:S(2)}) copy-start(f32[8,64,256]{2,1,0:T(8,128)} %refs_0_.6) | copy-start | bytes 1572868
  1.0 6.0 %collective-permute-start = (bf16[8,4,256]{2,1,0:T(4,128)(2,1)S(1)}, bf16[8,4,256]{2,1,0:T(4,128)(2,1)S(1)}, u32[]{:S(2)}, u32[]{:S(2)}) collective-permute-start(bf16[8,4,256]{2,1,0:T(4,128)(2,1)S(1)} %get-tuple-element.35), channel_id=1, source_target_pairs={{1,2},{3,4},{5,6},{2,1},{4,3},{6,5},{9,10},{11,12},{13,14},{10,9},... | collective-permute-start | bytes 49160 | tf_op jit(solution)/shard_map/ppermute | solution.py:609
  5.6 3.4 %slice-start = ((s8[4718592]{0:T(1024)(128)(4,1)}), s8[4194304]{0:T(1024)(128)(4,1)S(1)}, s32[]{:S(2)}) async-start(s8[4718592]{0:T(1024)(128)(4,1)} %bitcast.4), calls=%async_computation | async-start | bytes 8388608
  5.6 3.4 %slice-start.1 = ((s8[4718592]{0:T(1024)(128)(4,1)}), s8[524288]{0:T(1024)(128)(4,1)S(1)}, s32[]{:S(2)}) async-start(s8[4718592]{0:T(1024)(128)(4,1)} %bitcast.4), calls=%async_computation.1 | async-start | bytes 1048576
  5.6 3.4 %copy-start = (bf16[3,3,256,512]{3,2,1,0:T(8,128)(2,1)S(1)}, bf16[3,3,256,512]{3,2,1,0:T(8,128)(2,1)}, u32[]{:S(2)}) copy-start(bf16[3,3,256,512]{3,2,1,0:T(8,128)(2,1)} %param.5) | copy-start | bytes 7077892
  5.6 1.4 %collective-permute-start.1 = (bf16[8,4,256]{2,1,0:T(4,128)(2,1)S(1)}, bf16[8,4,256]{2,1,0:T(4,128)(2,1)S(1)}, u32[]{:S(2)}, u32[]{:S(2)}) collective-permute-start(bf16[8,4,256]{2,1,0:T(4,128)(2,1)S(1)} %get-tuple-element.36), channel_id=1, source_target_pairs={{0,1},{1,0},{2,3},{3,2},{4,5},{5,4},{6,7},{7,6},{8,9},{9,8},{10,11... | collective-permute-start | bytes 49160 | tf_op jit(solution)/shard_map/ppermute | solution.py:610
  7.1 5.7 %collective-permute-start.2 = (bf16[4,72,256]{2,1,0:T(8,128)(2,1)S(1)}, bf16[4,72,256]{2,1,0:T(8,128)(2,1)S(1)}, u32[]{:S(2)}, u32[]{:S(2)}) collective-permute-start(bf16[4,72,256]{2,1,0:T(8,128)(2,1)S(1)} %get-tuple-element.39), channel_id=1, source_target_pairs={{0,8},{16,24},{8,0},{24,16},{1,9},{17,25},{9,1},{25,17},{2,10},{18... | collective-permute-start | bytes 442376 | tf_op jit(solution)/shard_map/ppermute | solution.py:624
  8.3 4.4 %collective-permute-start.3 = (bf16[4,72,256]{2,1,0:T(8,128)(2,1)S(1)}, bf16[4,72,256]{2,1,0:T(8,128)(2,1)S(1)}, u32[]{:S(2)}, u32[]{:S(2)}) collective-permute-start(bf16[4,72,256]{2,1,0:T(8,128)(2,1)S(1)} %get-tuple-element.40), channel_id=1, source_target_pairs={{8,16},{16,8},{9,17},{17,9},{10,18},{18,10},{11,19},{19,11},{12,20... | collective-permute-start | bytes 442376 | tf_op jit(solution)/shard_map/ppermute | solution.py:625
  16.8 16.5 %copy-start.1 = (f32[2,512,512]{2,1,0:T(8,128)S(1)}, f32[2,512,512]{2,1,0:T(8,128)}, u32[]{:S(2)}) copy-start(f32[2,512,512]{2,1,0:T(8,128)} %refs_0_.7) | copy-start | bytes 6291460
  16.8 1.9 %collective-permute-start.4 = (bf16[1104,128]{1,0:T(8,128)(2,1)S(1)}, bf16[1104,128]{1,0:T(8,128)(2,1)S(1)}, u32[]{:S(2)}, u32[]{:S(2)}) collective-permute-start(bf16[1104,128]{1,0:T(8,128)(2,1)S(1)} %get-tuple-element.54), channel_id=1, source_target_pairs={{0,1},{1,0},{2,3},{3,2},{4,5},{5,4},{6,7},{7,6},{8,9},{9,8},{10,11... | collective-permute-start | bytes 847880 | tf_op jit(solution)/shard_map/ppermute | solution.py:713
  19.1 7.7 %collective-permute-start.5 = (bf16[288,128]{1,0:T(8,128)(2,1)S(1)}, bf16[288,128]{1,0:T(8,128)(2,1)S(1)}, u32[]{:S(2)}, u32[]{:S(2)}) collective-permute-start(bf16[288,128]{1,0:T(8,128)(2,1)S(1)} %get-tuple-element.57), channel_id=1, source_target_pairs={{0,8},{8,0},{16,24},{24,16},{1,9},{9,1},{17,25},{25,17},{2,10},{10... | collective-permute-start | bytes 221192 | tf_op jit(solution)/shard_map/ppermute | solution.py:728
  24.5 3.2 %collective-permute-start.6 = (bf16[288,128]{1,0:T(8,128)(2,1)S(1)}, bf16[288,128]{1,0:T(8,128)(2,1)S(1)}, u32[]{:S(2)}, u32[]{:S(2)}) collective-permute-start(bf16[288,128]{1,0:T(8,128)(2,1)S(1)} %get-tuple-element.58), channel_id=1, source_target_pairs={{0,16},{8,24},{16,0},{24,8},{1,17},{9,25},{17,1},{25,9},{2,18},{10... | collective-permute-start | bytes 221192 | tf_op jit(solution)/shard_map/ppermute | solution.py:728
  24.5 4.8 %collective-permute-start.7 = (bf16[288,128]{1,0:T(8,128)(2,1)S(1)}, bf16[288,128]{1,0:T(8,128)(2,1)S(1)}, u32[]{:S(2)}, u32[]{:S(2)}) collective-permute-start(bf16[288,128]{1,0:T(8,128)(2,1)S(1)} %get-tuple-element.59), channel_id=1, source_target_pairs={{0,24},{8,16},{16,8},{24,0},{1,25},{9,17},{17,9},{25,1},{2,26},{10... | collective-permute-start | bytes 221192 | tf_op jit(solution)/shard_map/ppermute | solution.py:728
  29.6 5.2 %collective-permute-start.10 = (bf16[288,128]{1,0:T(8,128)(2,1)S(1)}, bf16[288,128]{1,0:T(8,128)(2,1)S(1)}, u32[]{:S(2)}, u32[]{:S(2)}) collective-permute-start(bf16[288,128]{1,0:T(8,128)(2,1)S(1)} %get-tuple-element.62), channel_id=1, source_target_pairs={{0,6},{1,7},{2,4},{3,5},{4,2},{5,3},{6,0},{7,1},{8,14},{9,15},{10,... | collective-permute-start | bytes 221192 | tf_op jit(solution)/shard_map/ppermute | solution.py:738
  32.8 7.1 %collective-permute-start.9 = (bf16[288,128]{1,0:T(8,128)(2,1)S(1)}, bf16[288,128]{1,0:T(8,128)(2,1)S(1)}, u32[]{:S(2)}, u32[]{:S(2)}) collective-permute-start(bf16[288,128]{1,0:T(8,128)(2,1)S(1)} %get-tuple-element.62), channel_id=1, source_target_pairs={{0,4},{1,5},{2,6},{3,7},{4,0},{5,1},{6,2},{7,3},{8,12},{9,13},{10,... | collective-permute-start | bytes 221192 | tf_op jit(solution)/shard_map/ppermute | solution.py:738
  32.8 7.1 %collective-permute-start.8 = (bf16[288,128]{1,0:T(8,128)(2,1)S(1)}, bf16[288,128]{1,0:T(8,128)(2,1)S(1)}, u32[]{:S(2)}, u32[]{:S(2)}) collective-permute-start(bf16[288,128]{1,0:T(8,128)(2,1)S(1)} %get-tuple-element.62), channel_id=1, source_target_pairs={{0,2},{1,3},{2,0},{3,1},{4,6},{5,7},{6,4},{7,5},{8,10},{9,11},{10,... | collective-permute-start | bytes 221192 | tf_op jit(solution)/shard_map/ppermute | solution.py:738
  40.2 4.2 %collective-permute-start.13 = (bf16[272,128]{1,0:T(8,128)(2,1)S(1)}, bf16[272,128]{1,0:T(8,128)(2,1)S(1)}, u32[]{:S(2)}, u32[]{:S(2)}) collective-permute-start(bf16[272,128]{1,0:T(8,128)(2,1)S(1)} %get-tuple-element.63.refs_0_), channel_id=1, source_target_pairs={{0,24},{8,16},{16,8},{24,0},{1,25},{9,17},{17,9},{25,1},{2,26},{10... | collective-permute-start | bytes 208904 | tf_op jit(solution)/shard_map/ppermute | solution.py:748
  40.9 3.9 %collective-permute-start.12 = (bf16[272,128]{1,0:T(8,128)(2,1)S(1)}, bf16[272,128]{1,0:T(8,128)(2,1)S(1)}, u32[]{:S(2)}, u32[]{:S(2)}) collective-permute-start(bf16[272,128]{1,0:T(8,128)(2,1)S(1)} %get-tuple-element.63.refs_0_), channel_id=1, source_target_pairs={{0,16},{8,24},{16,0},{24,8},{1,17},{9,25},{17,1},{25,9},{2,18},{10... | collective-permute-start | bytes 208904 | tf_op jit(solution)/shard_map/ppermute | solution.py:748
  42.1 4.1 %collective-permute-start.11 = (bf16[272,128]{1,0:T(8,128)(2,1)S(1)}, bf16[272,128]{1,0:T(8,128)(2,1)S(1)}, u32[]{:S(2)}, u32[]{:S(2)}) collective-permute-start(bf16[272,128]{1,0:T(8,128)(2,1)S(1)} %get-tuple-element.63.refs_0_), channel_id=1, source_target_pairs={{0,8},{8,0},{16,24},{24,16},{1,9},{9,1},{17,25},{25,17},{2,10},{10... | collective-permute-start | bytes 208904 | tf_op jit(solution)/shard_map/ppermute | solution.py:748
  46.3 6.6 %collective-permute-start.14 = (bf16[1104,128]{1,0:T(8,128)(2,1)S(1)}, bf16[1104,128]{1,0:T(8,128)(2,1)S(1)}, u32[]{:S(2)}, u32[]{:S(2)}) collective-permute-start(bf16[1104,128]{1,0:T(8,128)(2,1)S(1)} %shard_map.56.refs_10_), channel_id=1, source_target_pairs={{0,1},{1,0},{2,3},{3,2},{4,5},{5,4},{6,7},{7,6},{8,9},{9,8},{10,11... | collective-permute-start | bytes 847880 | tf_op jit(solution)/shard_map/ppermute | solution.py:753

commit v11 on v10

--- a/solution.py
+++ b/solution.py
@@ -390,33 +390,29 @@
         put_mean(centre_out, centre, 1)
         write_message(sent, total, rows_ref, centre)
     else:
-        goal, sent, centre_out = rest[:3]
-        rows_ref[...] = jnp.zeros(rows_ref.shape, F32)
-        put_mean(rows_ref, centre, 2)
-        centre_out[...] = rows_ref[...].astype(BF)
-        sent[...] = (total * (1.0 / final) - goal[...]).astype(BF)
-
-
-def assemble(place, share, centre, *rest):
-    gots, out = rest[:-1], rest[-1]
-    chunk = share.shape[0]
-    for k, ref in enumerate((share,) + tuple(gots)):
-        out[pl.ds(pl.multiple_of((place[3] ^ k) * chunk, 16), chunk), :] = ref[...]
-    rows = chunk * (len(gots) + 1)
-    out[rows:, :] = centre[...]
-
-
-def back(dims, place, *rest):
+        goal, sent, both = rest[:3]
+        part = total * (1.0 / final) - goal[...]
+        sent[...] = part.astype(BF)
+        write_message(both, part, rows_ref, centre)
+
+
+def back(dims, members, place, *rest):
     (act1, slope1, act1b, slope1b, act2, slope2, act2b, slope2b, act2r, slope2r) = rest[:10]
-    (mine, other, w2, w1, out, taps2, taps1, first_m, second_m, table, buf) = rest[10:]
+    pieces, rest = rest[10 : 10 + 2 * members], rest[10 + 2 * members :]
+    (w2, w1, out, taps2, taps1, first_m, second_m, table, buf) = rest
     height, breadth, groups, limits = dims
     pitch = groups * 16
     step = 2 * pitch
     width = act1.shape[1]
     blocks = width // BLOCK
     packed = table.shape[1] - EXTRA
-    table[place[0]] = mine[...]
-    table[1 - place[0]] = other[...]
+    chunk = packed // members
+    for n, ref in enumerate(pieces):
+        core = place[0] if n < members else 1 - place[0]
+        at = pl.multiple_of((place[3] ^ (n % members)) * chunk, 16)
+        table[core, pl.ds(at, chunk), :] = ref[0:chunk, :]
+        if n % members == 0:
+            table[core, packed:, :] = ref[chunk:, :]
     means, (row, col) = [], corners()
     for layer, ref in enumerate((first_m, second_m)):
         for n, (i, j) in enumerate(pairs(width)):
@@ -738,23 +734,22 @@
         lax.ppermute(sent, "tile", [(i, i ^ (2 * k)) for i in range(tiles)])
         for k in range(1, chips)
     ]
-    share, mean = call(
+    share, both = call(
         functools.partial(merge_many, (2 * groups * cells, chips, blocks), positions),
         [place, share, mean] + gots + [goal],
-        [shape((chunk, BLOCK), BF), shape((EXTRA, BLOCK), BF)],
+        [shape((chunk, BLOCK), BF), message],
         helpers(chips),
     )
     gots = [
         lax.ppermute(share, "grp", [(i, i ^ k) for i in range(groups)])
         for k in range(1, groups)
     ]
-    table = shape((packed + EXTRA, BLOCK), BF)
-    (mine,) = call(assemble, [place, share, mean] + gots, [table], [])
-    other = lax.ppermute(mine, "tile", swap)
+    mine = [both] + gots
+    other = [lax.ppermute(piece, "tile", swap) for piece in mine]
     maps_in = [act1, slope1, act1b, slope1b, act2, slope2, act2b, slope2b, act2r, slope2r]
     (out,) = call(
-        functools.partial(back, dims),
-        [place] + maps_in + [mine, other, back2, back1],
+        functools.partial(back, dims, groups),
+        [place] + maps_in + mine + other + [back2, back1],
         [shape(pool_input.shape, F32)],
         [
             pltpu.VMEM(((height + 4) * wider, width), BF),

time: 60.8 us -> 58.9 us (0.969)
  waiting for transfers between devices: 14 us -> 10.2 us
  starting transfers between devices: 22.2 us -> 23.8 us
    ppermute x3, waiting for transfers between devices: 2.2 us -> 0.01 us  [local(): lax.ppermute(share, 'grp', [(i, i ^ k) for i in range(groups)])]
    ppermute x3, waiting for transfers between devices: 6.28 us -> 4.68 us  [local(): lax.ppermute(sent, 'tile', [(i, i ^ 2 * k) for i in range(tiles)])]
    ppermute x1 -> x4, starting transfers between devices: 1.96 us -> 3.48 us  [local(): other = [lax.ppermute(piece, 'tile', swap) for piece in mine]]
    pallas_call x14 -> x13, Pallas kernels: 24.1 us -> 24 us  [call(): pl.pallas_call(body, out_shape=tuple(outs), in_specs=[HBM if n in far els...]
  transfers between devices with their start and end apart: 15 -> 18, of which waited for: 10 -> 6; matrix products, arithmetic and copies ran while one was open for 0% -> 0% of each run, Pallas kernels for 17% -> 17%
where the time goes in v11:
time: 58.9 us; the launch traced here: 58.7 us
  Pallas kernels  24 us (41%)
  starting transfers between devices  23.8 us (40%)
  waiting for transfers between devices  10.2 us (17%)
    pallas_call x13, Pallas kernels, call(): pl.pallas_call(body, out_shape=tuple(outs), in_specs=[HBM if n in far els...  24 us
    ppermute x3, starting transfers between devices, local(): lax.ppermute(sents[k - 1], 'grp', [(i, i ^ k) for i in range(groups)])  6.64 us
    ppermute x3, waiting for transfers between devices, local(): lax.ppermute(sent, 'tile', [(i, i ^ 2 * k) for i in range(tiles)])  4.68 us
    ppermute x1, starting transfers between devices, local(): far = lax.ppermute(far, 'tile', cross)  4.58 us
    ppermute x3, starting transfers between devices, local(): lax.ppermute(sent, 'tile', [(i, i ^ 2 * k) for i in range(tiles)])  3.61 us
    ppermute x3, waiting for transfers between devices, local(): lax.ppermute(sents[k - 1], 'grp', [(i, i ^ k) for i in range(groups)])  3.53 us
    ppermute x4, starting transfers between devices, local(): other = [lax.ppermute(piece, 'tile', swap) for piece in mine]  3.48 us
    ppermute x3, starting transfers between devices, local(): lax.ppermute(share, 'grp', [(i, i ^ k) for i in range(groups)])  2.71 us
  transfers between devices with their start and end apart: 18, of which 6 were waited for; matrix products, arithmetic and copies ran while one was open for 0% of the time, Pallas kernels for 17%

profile of v11, /device:TPU:1, one launch (start us, length us, event | category | flops | bytes accessed | tf_op | source)
XLA Modules:
  0.0 58.7 jit_solution(5421528633070195677)
XLA Ops:
  0.0 1.0 %shard_map.46 = (bf16[8,4,256]{2,1,0:T(4,128)(2,1)S(1)}, bf16[8,4,256]{2,1,0:T(4,128)(2,1)S(1)}) custom-call(f32[8,64,256]{2,1,0:T(8,128)} %refs_0_.6), custom_call_target="tpu_custom_call" | custom-call | flops 4000000000 | bytes 557056 | tf_op jit(solution)/shard_map/pallas_call | solution.py:565
  1.0 4.6 %collective-permute-start = (bf16[8,4,256]{2,1,0:T(4,128)(2,1)S(1)}, bf16[8,4,256]{2,1,0:T(4,128)(2,1)S(1)}, u32[]{:S(2)}, u32[]{:S(2)}) collective-permute-start(bf16[8,4,256]{2,1,0:T(4,128)(2,1)S(1)} %get-tuple-element.35), channel_id=1, source_target_pairs={{1,2},{3,4},{5,6},{2,1},{4,3},{6,5},{9,10},{11,12},{13,14},{10,9},... | collective-permute-start | bytes 49160 | tf_op jit(solution)/shard_map/ppermute | solution.py:605
  5.6 0.0 slice-start
  5.6 0.0 slice-start.1
  5.6 0.0 copy-start
  5.6 0.1 collective-permute-start.1
  5.7 1.3 %collective-permute-done.refs_1_ = bf16[8,4,256]{2,1,0:T(4,128)(2,1)S(1)} collective-permute-done((bf16[8,4,256]{2,1,0:T(4,128)(2,1)S(1)}, bf16[8,4,256]{2,1,0:T(4,128)(2,1)S(1)}, u32[]{:S(2)}, u32[]{:S(2)}) %collective-permute-start) | collective-permute-done | bytes 16416 | tf_op jit(solution)/shard_map/ppermute | solution.py:605
  7.0 0.0 collective-permute-done.1.refs_2_
  7.0 0.1 shard_map.48
  7.1 1.3 %collective-permute-start.2 = (bf16[4,72,256]{2,1,0:T(8,128)(2,1)S(1)}, bf16[4,72,256]{2,1,0:T(8,128)(2,1)S(1)}, u32[]{:S(2)}, u32[]{:S(2)}) collective-permute-start(bf16[4,72,256]{2,1,0:T(8,128)(2,1)S(1)} %get-tuple-element.39), channel_id=1, source_target_pairs={{0,8},{16,24},{8,0},{24,16},{1,9},{17,25},{9,1},{25,17},{2,10},{18... | collective-permute-start | bytes 442376 | tf_op jit(solution)/shard_map/ppermute | solution.py:620
  8.3 0.7 %collective-permute-start.3 = (bf16[4,72,256]{2,1,0:T(8,128)(2,1)S(1)}, bf16[4,72,256]{2,1,0:T(8,128)(2,1)S(1)}, u32[]{:S(2)}, u32[]{:S(2)}) collective-permute-start(bf16[4,72,256]{2,1,0:T(8,128)(2,1)S(1)} %get-tuple-element.40), channel_id=1, source_target_pairs={{8,16},{16,8},{9,17},{17,9},{10,18},{18,10},{11,19},{19,11},{12,20... | collective-permute-start | bytes 442376 | tf_op jit(solution)/shard_map/ppermute | solution.py:621
  9.0 3.7 %shard_map.47 = (bf16[896,256]{1,0:T(8,128)(2,1)S(1)}, bf16[672,512]{1,0:T(8,128)(2,1)S(1)}, f32[480,512]{1,0:T(8,128)S(1)}, f32[480,512]{1,0:T(8,128)S(1)}, f32...) custom-call(f32[8,64,256]{2,1,0:T(8,128)S(1)} %copy-done.2, bf16[8,4,256]{2,1,0:T(4,128)(2,1)S(1)} %collective-permute-done.refs_1_, ...), custom_call_target="tpu_custom_call" | custom-call | flops 2642411520 | bytes 12058624 | tf_op jit(solution)/shard_map/pallas_call | solution.py:565
  12.7 0.0 collective-permute-done.2.refs_0_
  12.7 4.0 %shard_map.49 = (bf16[448,512]{1,0:T(8,128)(2,1)S(1)}, f32[320,512]{1,0:T(8,128)S(1)}, f32[320,512]{1,0:T(8,128)S(1)}, f32[320,512]{1,0:T(8,128)S(1)}, f32[320,5...) custom-call(bf16[4,72,256]{2,1,0:T(8,128)(2,1)S(1)} %collective-permute-, ...), custom_call_target="tpu_custom_call" | custom-call | flops 2264924160 | bytes 14835712 | tf_op jit(solution)/shard_map/pallas_call | solution.py:565
  16.8 0.7 %collective-permute-start.4 = (bf16[1104,128]{1,0:T(8,128)(2,1)S(1)}, bf16[1104,128]{1,0:T(8,128)(2,1)S(1)}, u32[]{:S(2)}, u32[]{:S(2)}) collective-permute-start(bf16[1104,128]{1,0:T(8,128)(2,1)S(1)} %get-tuple-element.54), channel_id=1, source_target_pairs={{0,1},{1,0},{2,3},{3,2},{4,5},{5,4},{6,7},{7,6},{8,9},{9,8},{10,11... | collective-permute-start | bytes 847880 | tf_op jit(solution)/shard_map/ppermute | solution.py:709
  17.5 0.5 shard_map.51.refs_0_
  18.0 0.7 %collective-permute-done.4.refs_2_ = bf16[1104,128]{1,0:T(8,128)(2,1)S(1)} collective-permute-done((bf16[1104,128]{1,0:T(8,128)(2,1)S(1)}, bf16[1104,128]{1,0:T(8,128)(2,1)S(1)}, u32[]{:S(2)}, u32[]{:S(2)}) %collective-permute-start.4) | collective-permute-done | bytes 282656 | tf_op jit(solution)/shard_map/ppermute | solution.py:709
  18.7 0.4 shard_map.52
  19.1 5.4 %collective-permute-start.5 = (bf16[288,128]{1,0:T(8,128)(2,1)S(1)}, bf16[288,128]{1,0:T(8,128)(2,1)S(1)}, u32[]{:S(2)}, u32[]{:S(2)}) collective-permute-start(bf16[288,128]{1,0:T(8,128)(2,1)S(1)} %get-tuple-element.57), channel_id=1, source_target_pairs={{0,8},{8,0},{16,24},{24,16},{1,9},{9,1},{17,25},{25,17},{2,10},{10... | collective-permute-start | bytes 221192 | tf_op jit(solution)/shard_map/ppermute | solution.py:724
  24.4 0.0 collective-permute-start.6
  24.4 1.3 %collective-permute-start.7 = (bf16[288,128]{1,0:T(8,128)(2,1)S(1)}, bf16[288,128]{1,0:T(8,128)(2,1)S(1)}, u32[]{:S(2)}, u32[]{:S(2)}) collective-permute-start(bf16[288,128]{1,0:T(8,128)(2,1)S(1)} %get-tuple-element.59), channel_id=1, source_target_pairs={{0,24},{8,16},{16,8},{24,0},{1,25},{9,17},{17,9},{25,1},{2,26},{10... | collective-permute-start | bytes 221192 | tf_op jit(solution)/shard_map/ppermute | solution.py:724
  25.7 1.0 %collective-permute-done.5.refs_2_ = bf16[288,128]{1,0:T(8,128)(2,1)S(1)} collective-permute-done((bf16[288,128]{1,0:T(8,128)(2,1)S(1)}, bf16[288,128]{1,0:T(8,128)(2,1)S(1)}, u32[]{:S(2)}, u32[]{:S(2)}) %collective-permute-start.5) | collective-permute-done | bytes 73760 | tf_op jit(solution)/shard_map/ppermute | solution.py:724
  26.7 0.9 %collective-permute-done.6.refs_3_ = bf16[288,128]{1,0:T(8,128)(2,1)S(1)} collective-permute-done((bf16[288,128]{1,0:T(8,128)(2,1)S(1)}, bf16[288,128]{1,0:T(8,128)(2,1)S(1)}, u32[]{:S(2)}, u32[]{:S(2)}) %collective-permute-start.6) | collective-permute-done | bytes 73760 | tf_op jit(solution)/shard_map/ppermute | solution.py:724
  27.6 1.6 %collective-permute-done.7.refs_4_ = bf16[288,128]{1,0:T(8,128)(2,1)S(1)} collective-permute-done((bf16[288,128]{1,0:T(8,128)(2,1)S(1)}, bf16[288,128]{1,0:T(8,128)(2,1)S(1)}, u32[]{:S(2)}, u32[]{:S(2)}) %collective-permute-start.7) | collective-permute-done | bytes 73760 | tf_op jit(solution)/shard_map/ppermute | solution.py:724
  29.2 0.4 shard_map.53
  29.6 3.1 %collective-permute-start.10 = (bf16[288,128]{1,0:T(8,128)(2,1)S(1)}, bf16[288,128]{1,0:T(8,128)(2,1)S(1)}, u32[]{:S(2)}, u32[]{:S(2)}) collective-permute-start(bf16[288,128]{1,0:T(8,128)(2,1)S(1)} %get-tuple-element.62), channel_id=1, source_target_pairs={{0,6},{1,7},{2,4},{3,5},{4,2},{5,3},{6,0},{7,1},{8,14},{9,15},{10,... | collective-permute-start | bytes 221192 | tf_op jit(solution)/shard_map/ppermute | solution.py:734
  32.7 0.0 collective-permute-start.9
  32.7 0.5 collective-permute-start.8
  33.2 1.1 %shard_map.57.refs_19_ = bf16[4608,256]{1,0:T(8,128)(2,1)S(1)} custom-call(bf16[9,256,512]{2,1,0:T(8,128)(2,1)S(1)} %bitcast.12), custom_call_target="tpu_custom_call" | custom-call | flops 2000000000 | bytes 4718592 | tf_op jit(solution)/shard_map/pallas_call | solution.py:565
  34.3 0.5 copy-done.1
  34.8 0.3 shard_map.54.refs_5_
  35.1 0.0 collective-permute-done.10.refs_4_
  35.1 4.7 %collective-permute-done.9.refs_3_ = bf16[288,128]{1,0:T(8,128)(2,1)S(1)} collective-permute-done((bf16[288,128]{1,0:T(8,128)(2,1)S(1)}, bf16[288,128]{1,0:T(8,128)(2,1)S(1)}, u32[]{:S(2)}, u32[]{:S(2)}) %collective-permute-start.9) | collective-permute-done | bytes 73760 | tf_op jit(solution)/shard_map/ppermute | solution.py:734
  39.8 0.4 shard_map.55
  40.2 0.6 %collective-permute-start.13 = (bf16[272,128]{1,0:T(8,128)(2,1)S(1)}, bf16[272,128]{1,0:T(8,128)(2,1)S(1)}, u32[]{:S(2)}, u32[]{:S(2)}) collective-permute-start(bf16[272,128]{1,0:T(8,128)(2,1)S(1)} %get-tuple-element.64), channel_id=1, source_target_pairs={{0,24},{8,16},{16,8},{24,0},{1,25},{9,17},{17,9},{25,1},{2,26},{10... | collective-permute-start | bytes 208904 | tf_op jit(solution)/shard_map/ppermute | solution.py:744
  40.8 1.2 %collective-permute-start.12 = (bf16[272,128]{1,0:T(8,128)(2,1)S(1)}, bf16[272,128]{1,0:T(8,128)(2,1)S(1)}, u32[]{:S(2)}, u32[]{:S(2)}) collective-permute-start(bf16[272,128]{1,0:T(8,128)(2,1)S(1)} %get-tuple-element.64), channel_id=1, source_target_pairs={{0,16},{8,24},{16,0},{24,8},{1,17},{9,25},{17,1},{25,9},{2,18},{10... | collective-permute-start | bytes 208904 | tf_op jit(solution)/shard_map/ppermute | solution.py:744
  42.1 0.8 %collective-permute-start.11 = (bf16[272,128]{1,0:T(8,128)(2,1)S(1)}, bf16[272,128]{1,0:T(8,128)(2,1)S(1)}, u32[]{:S(2)}, u32[]{:S(2)}) collective-permute-start(bf16[272,128]{1,0:T(8,128)(2,1)S(1)} %get-tuple-element.64), channel_id=1, source_target_pairs={{0,8},{8,0},{16,24},{24,16},{1,9},{9,1},{17,25},{25,17},{2,10},{10... | collective-permute-start | bytes 208904 | tf_op jit(solution)/shard_map/ppermute | solution.py:744
  42.9 1.7 %shard_map.56.refs_18_ = bf16[4608,512]{1,0:T(8,128)(2,1)S(1)} custom-call(bf16[9,512,512]{2,1,0:T(8,128)(2,1)S(1)} %bitcast.8), custom_call_target="tpu_custom_call" | custom-call | flops 2000000000 | bytes 9437184 | tf_op jit(solution)/shard_map/pallas_call | solution.py:565
  44.6 2.0 %collective-permute-start.14 = (bf16[288,128]{1,0:T(8,128)(2,1)S(1)}, bf16[288,128]{1,0:T(8,128)(2,1)S(1)}, u32[]{:S(2)}, u32[]{:S(2)}) collective-permute-start(bf16[288,128]{1,0:T(8,128)(2,1)S(1)} %get-tuple-element.63.refs_10_), channel_id=1, source_target_pairs={{0,1},{1,0},{2,3},{3,2},{4,5},{5,4},{6,7},{7,6},{8,9},{9,8},{10,11... | collective-permute-start | bytes 221192 | tf_op jit(solution)/shard_map/ppermute | solution.py:748
  46.6 0.0 collective-permute-done.13.refs_13_
  46.6 0.1 collective-permute-start.17
  46.7 0.0 collective-permute-done.12.refs_12_
  46.7 0.7 %collective-permute-start.16 = (bf16[272,128]{1,0:T(8,128)(2,1)S(1)}, bf16[272,128]{1,0:T(8,128)(2,1)S(1)}, u32[]{:S(2)}, u32[]{:S(2)}) collective-permute-start(bf16[272,128]{1,0:T(8,128)(2,1)S(1)} %collective-permute-done.12.refs_12_), channel_id=1, source_target_pairs={{0,1},{1,0},{2,3},{3,2},{4,5},{5,4},{6,7},{7,6},{8,9},{9,8},{10,11... | collective-permute-start | bytes 208904 | tf_op jit(solution)/shard_map/ppermute | solution.py:748
  47.4 0.8 %collective-permute-start.15 = (bf16[272,128]{1,0:T(8,128)(2,1)S(1)}, bf16[272,128]{1,0:T(8,128)(2,1)S(1)}, u32[]{:S(2)}, u32[]{:S(2)}) collective-permute-start(bf16[272,128]{1,0:T(8,128)(2,1)S(1)} %collective-permute-done.11.refs_11_), channel_id=1, source_target_pairs={{0,1},{1,0},{2,3},{3,2},{4,5},{5,4},{6,7},{7,6},{8,9},{9,8},{10,11... | collective-permute-start | bytes 208904 | tf_op jit(solution)/shard_map/ppermute | solution.py:748
  48.1 3.0 %shard_map.50 = (f32[320,512]{1,0:T(8,128)S(1)}, f32[320,512]{1,0:T(8,128)S(1)}) custom-call(bf16[4,72,256]{2,1,0:T(8,128)(2,1)S(1)} %collective-permute-done.2.refs_0_, bf16[4,72,256]{2,1,0:T(8,128)(2,1)S(1)} %collective-permute-done.3.refs_1_, bf16[448,512]{1,0:T(8,128)(2,1)S(1)} %get-tuple-element.49.refs_2_, bf16[2304,512]{1,0:T(8,128)(2,1)S(1)} %bitcast.13, ...), custom_call_target="tpu_custom_call" | custom-call | flops 2264924160 | bytes 9142272 | tf_op jit(solution)/shard_map/pallas_call | solution.py:565
  51.1 0.0 collective-permute-done.14.refs_14_
  51.1 0.0 collective-permute-done.15.refs_15_
  51.1 7.6 %shard_map.58 = f32[8,64,256]{2,1,0:T(8,128)} custom-call(f32[480,512]{1,0:T(8,128)S(1)} %get-tuple-element.37.refs_4_.refs_0_, f32[480,512]{1,0:T(8,128)S(1)} %get-tuple-element.38.refs_1_, f32[320,512]{1,0:T(8,128)S(1)} %get-tuple-element.44.refs_2_, f32[320,512]{1,0:T(8,128)S(1)} %get-tuple-element.45.refs_3_, ...), custom_call_target="tpu_custom_call" | custom-call | flops 5284823040 | bytes 15376384 | tf_op jit(solution)/shard_map/pallas_call | solution.py:565
  (12 shorter events, 0.0 us)
Async XLA Ops:
  0.0 7.0 %copy-start.2 = (f32[8,64,256]{2,1,0:T(8,128)S(1)}, f32[8,64,256]{2,1,0:T(8,128)}, u32[]{:S(2)}) copy-start(f32[8,64,256]{2,1,0:T(8,128)} %refs_0_.6) | copy-start | bytes 1572868
  1.0 6.0 %collective-permute-start = (bf16[8,4,256]{2,1,0:T(4,128)(2,1)S(1)}, bf16[8,4,256]{2,1,0:T(4,128)(2,1)S(1)}, u32[]{:S(2)}, u32[]{:S(2)}) collective-permute-start(bf16[8,4,256]{2,1,0:T(4,128)(2,1)S(1)} %get-tuple-element.35), channel_id=1, source_target_pairs={{1,2},{3,4},{5,6},{2,1},{4,3},{6,5},{9,10},{11,12},{13,14},{10,9},... | collective-permute-start | bytes 49160 | tf_op jit(solution)/shard_map/ppermute | solution.py:605
  5.6 3.4 %slice-start = ((s8[4718592]{0:T(1024)(128)(4,1)}), s8[4194304]{0:T(1024)(128)(4,1)S(1)}, s32[]{:S(2)}) async-start(s8[4718592]{0:T(1024)(128)(4,1)} %bitcast.4), calls=%async_computation | async-start | bytes 8388608
  5.6 3.4 %slice-start.1 = ((s8[4718592]{0:T(1024)(128)(4,1)}), s8[524288]{0:T(1024)(128)(4,1)S(1)}, s32[]{:S(2)}) async-start(s8[4718592]{0:T(1024)(128)(4,1)} %bitcast.4), calls=%async_computation.1 | async-start | bytes 1048576
  5.6 3.4 %copy-start = (bf16[3,3,256,512]{3,2,1,0:T(8,128)(2,1)S(1)}, bf16[3,3,256,512]{3,2,1,0:T(8,128)(2,1)}, u32[]{:S(2)}) copy-start(bf16[3,3,256,512]{3,2,1,0:T(8,128)(2,1)} %param.5) | copy-start | bytes 7077892
  5.6 1.4 %collective-permute-start.1 = (bf16[8,4,256]{2,1,0:T(4,128)(2,1)S(1)}, bf16[8,4,256]{2,1,0:T(4,128)(2,1)S(1)}, u32[]{:S(2)}, u32[]{:S(2)}) collective-permute-start(bf16[8,4,256]{2,1,0:T(4,128)(2,1)S(1)} %get-tuple-element.36), channel_id=1, source_target_pairs={{0,1},{1,0},{2,3},{3,2},{4,5},{5,4},{6,7},{7,6},{8,9},{9,8},{10,11... | collective-permute-start | bytes 49160 | tf_op jit(solution)/shard_map/ppermute | solution.py:606
  7.1 5.7 %collective-permute-start.2 = (bf16[4,72,256]{2,1,0:T(8,128)(2,1)S(1)}, bf16[4,72,256]{2,1,0:T(8,128)(2,1)S(1)}, u32[]{:S(2)}, u32[]{:S(2)}) collective-permute-start(bf16[4,72,256]{2,1,0:T(8,128)(2,1)S(1)} %get-tuple-element.39), channel_id=1, source_target_pairs={{0,8},{16,24},{8,0},{24,16},{1,9},{17,25},{9,1},{25,17},{2,10},{18... | collective-permute-start | bytes 442376 | tf_op jit(solution)/shard_map/ppermute | solution.py:620
  8.3 4.4 %collective-permute-start.3 = (bf16[4,72,256]{2,1,0:T(8,128)(2,1)S(1)}, bf16[4,72,256]{2,1,0:T(8,128)(2,1)S(1)}, u32[]{:S(2)}, u32[]{:S(2)}) collective-permute-start(bf16[4,72,256]{2,1,0:T(8,128)(2,1)S(1)} %get-tuple-element.40), channel_id=1, source_target_pairs={{8,16},{16,8},{9,17},{17,9},{10,18},{18,10},{11,19},{19,11},{12,20... | collective-permute-start | bytes 442376 | tf_op jit(solution)/shard_map/ppermute | solution.py:621
  16.8 1.9 %collective-permute-start.4 = (bf16[1104,128]{1,0:T(8,128)(2,1)S(1)}, bf16[1104,128]{1,0:T(8,128)(2,1)S(1)}, u32[]{:S(2)}, u32[]{:S(2)}) collective-permute-start(bf16[1104,128]{1,0:T(8,128)(2,1)S(1)} %get-tuple-element.54), channel_id=1, source_target_pairs={{0,1},{1,0},{2,3},{3,2},{4,5},{5,4},{6,7},{7,6},{8,9},{9,8},{10,11... | collective-permute-start | bytes 847880 | tf_op jit(solution)/shard_map/ppermute | solution.py:709
  19.1 7.6 %collective-permute-start.5 = (bf16[288,128]{1,0:T(8,128)(2,1)S(1)}, bf16[288,128]{1,0:T(8,128)(2,1)S(1)}, u32[]{:S(2)}, u32[]{:S(2)}) collective-permute-start(bf16[288,128]{1,0:T(8,128)(2,1)S(1)} %get-tuple-element.57), channel_id=1, source_target_pairs={{0,8},{8,0},{16,24},{24,16},{1,9},{9,1},{17,25},{25,17},{2,10},{10... | collective-permute-start | bytes 221192 | tf_op jit(solution)/shard_map/ppermute | solution.py:724
  24.4 3.2 %collective-permute-start.6 = (bf16[288,128]{1,0:T(8,128)(2,1)S(1)}, bf16[288,128]{1,0:T(8,128)(2,1)S(1)}, u32[]{:S(2)}, u32[]{:S(2)}) collective-permute-start(bf16[288,128]{1,0:T(8,128)(2,1)S(1)} %get-tuple-element.58), channel_id=1, source_target_pairs={{0,16},{8,24},{16,0},{24,8},{1,17},{9,25},{17,1},{25,9},{2,18},{10... | collective-permute-start | bytes 221192 | tf_op jit(solution)/shard_map/ppermute | solution.py:724
  24.4 4.8 %collective-permute-start.7 = (bf16[288,128]{1,0:T(8,128)(2,1)S(1)}, bf16[288,128]{1,0:T(8,128)(2,1)S(1)}, u32[]{:S(2)}, u32[]{:S(2)}) collective-permute-start(bf16[288,128]{1,0:T(8,128)(2,1)S(1)} %get-tuple-element.59), channel_id=1, source_target_pairs={{0,24},{8,16},{16,8},{24,0},{1,25},{9,17},{17,9},{25,1},{2,26},{10... | collective-permute-start | bytes 221192 | tf_op jit(solution)/shard_map/ppermute | solution.py:724
  29.6 5.5 %collective-permute-start.10 = (bf16[288,128]{1,0:T(8,128)(2,1)S(1)}, bf16[288,128]{1,0:T(8,128)(2,1)S(1)}, u32[]{:S(2)}, u32[]{:S(2)}) collective-permute-start(bf16[288,128]{1,0:T(8,128)(2,1)S(1)} %get-tuple-element.62), channel_id=1, source_target_pairs={{0,6},{1,7},{2,4},{3,5},{4,2},{5,3},{6,0},{7,1},{8,14},{9,15},{10,... | collective-permute-start | bytes 221192 | tf_op jit(solution)/shard_map/ppermute | solution.py:734
  32.7 7.1 %collective-permute-start.9 = (bf16[288,128]{1,0:T(8,128)(2,1)S(1)}, bf16[288,128]{1,0:T(8,128)(2,1)S(1)}, u32[]{:S(2)}, u32[]{:S(2)}) collective-permute-start(bf16[288,128]{1,0:T(8,128)(2,1)S(1)} %get-tuple-element.62), channel_id=1, source_target_pairs={{0,4},{1,5},{2,6},{3,7},{4,0},{5,1},{6,2},{7,3},{8,12},{9,13},{10,... | collective-permute-start | bytes 221192 | tf_op jit(solution)/shard_map/ppermute | solution.py:734
  32.7 7.1 %collective-permute-start.8 = (bf16[288,128]{1,0:T(8,128)(2,1)S(1)}, bf16[288,128]{1,0:T(8,128)(2,1)S(1)}, u32[]{:S(2)}, u32[]{:S(2)}) collective-permute-start(bf16[288,128]{1,0:T(8,128)(2,1)S(1)} %get-tuple-element.62), channel_id=1, source_target_pairs={{0,2},{1,3},{2,0},{3,1},{4,6},{5,7},{6,4},{7,5},{8,10},{9,11},{10,... | collective-permute-start | bytes 221192 | tf_op jit(solution)/shard_map/ppermute | solution.py:734
  33.2 1.6 %copy-start.1 = (f32[2,512,512]{2,1,0:T(8,128)S(1)}, f32[2,512,512]{2,1,0:T(8,128)}, u32[]{:S(2)}) copy-start(f32[2,512,512]{2,1,0:T(8,128)} %refs_0_.7) | copy-start | bytes 6291460
  40.2 6.4 %collective-permute-start.13 = (bf16[272,128]{1,0:T(8,128)(2,1)S(1)}, bf16[272,128]{1,0:T(8,128)(2,1)S(1)}, u32[]{:S(2)}, u32[]{:S(2)}) collective-permute-start(bf16[272,128]{1,0:T(8,128)(2,1)S(1)} %get-tuple-element.64), channel_id=1, source_target_pairs={{0,24},{8,16},{16,8},{24,0},{1,25},{9,17},{17,9},{25,1},{2,26},{10... | collective-permute-start | bytes 208904 | tf_op jit(solution)/shard_map/ppermute | solution.py:744
  40.8 5.9 %collective-permute-start.12 = (bf16[272,128]{1,0:T(8,128)(2,1)S(1)}, bf16[272,128]{1,0:T(8,128)(2,1)S(1)}, u32[]{:S(2)}, u32[]{:S(2)}) collective-permute-start(bf16[272,128]{1,0:T(8,128)(2,1)S(1)} %get-tuple-element.64), channel_id=1, source_target_pairs={{0,16},{8,24},{16,0},{24,8},{1,17},{9,25},{17,1},{25,9},{2,18},{10... | collective-permute-start | bytes 208904 | tf_op jit(solution)/shard_map/ppermute | solution.py:744
  42.1 5.3 %collective-permute-start.11 = (bf16[272,128]{1,0:T(8,128)(2,1)S(1)}, bf16[272,128]{1,0:T(8,128)(2,1)S(1)}, u32[]{:S(2)}, u32[]{:S(2)}) collective-permute-start(bf16[272,128]{1,0:T(8,128)(2,1)S(1)} %get-tuple-element.64), channel_id=1, source_target_pairs={{0,8},{8,0},{16,24},{24,16},{1,9},{9,1},{17,25},{25,17},{2,10},{10... | collective-permute-start | bytes 208904 | tf_op jit(solution)/shard_map/ppermute | solution.py:744
  44.6 6.5 %collective-permute-start.14 = (bf16[288,128]{1,0:T(8,128)(2,1)S(1)}, bf16[288,128]{1,0:T(8,128)(2,1)S(1)}, u32[]{:S(2)}, u32[]{:S(2)}) collective-permute-start(bf16[288,128]{1,0:T(8,128)(2,1)S(1)} %get-tuple-element.63.refs_10_), channel_id=1, source_target_pairs={{0,1},{1,0},{2,3},{3,2},{4,5},{5,4},{6,7},{7,6},{8,9},{9,8},{10,11... | collective-permute-start | bytes 221192 | tf_op jit(solution)/shard_map/ppermute | solution.py:748
  46.6 4.5 %collective-permute-start.17 = (bf16[272,128]{1,0:T(8,128)(2,1)S(1)}, bf16[272,128]{1,0:T(8,128)(2,1)S(1)}, u32[]{:S(2)}, u32[]{:S(2)}) collective-permute-start(bf16[272,128]{1,0:T(8,128)(2,1)S(1)} %collective-permute-done.13.refs_13_), channel_id=1, source_target_pairs={{0,1},{1,0},{2,3},{3,2},{4,5},{5,4},{6,7},{7,6},{8,9},{9,8},{10,11... | collective-permute-start | bytes 208904 | tf_op jit(solution)/shard_map/ppermute | solution.py:748
  46.7 4.4 %collective-permute-start.16 = (bf16[272,128]{1,0:T(8,128)(2,1)S(1)}, bf16[272,128]{1,0:T(8,128)(2,1)S(1)}, u32[]{:S(2)}, u32[]{:S(2)}) collective-permute-start(bf16[272,128]{1,0:T(8,128)(2,1)S(1)} %collective-permute-done.12.refs_12_), channel_id=1, source_target_pairs={{0,1},{1,0},{2,3},{3,2},{4,5},{5,4},{6,7},{7,6},{8,9},{9,8},{10,11... | collective-permute-start | bytes 208904 | tf_op jit(solution)/shard_map/ppermute | solution.py:748
  47.4 3.8 %collective-permute-start.15 = (bf16[272,128]{1,0:T(8,128)(2,1)S(1)}, bf16[272,128]{1,0:T(8,128)(2,1)S(1)}, u32[]{:S(2)}, u32[]{:S(2)}) collective-permute-start(bf16[272,128]{1,0:T(8,128)(2,1)S(1)} %collective-permute-done.11.refs_11_), channel_id=1, source_target_pairs={{0,1},{1,0},{2,3},{3,2},{4,5},{5,4},{6,7},{7,6},{8,9},{9,8},{10,11... | collective-permute-start | bytes 208904 | tf_op jit(solution)/shard_map/ppermute | solution.py:748

commit v12 on v11

--- a/solution.py
+++ b/solution.py
@@ -255,12 +255,33 @@
         fold_row(ref, n, buf, at, groups)
 
 
+def cell_parts(act1b, act1, act2b, act2, height, pitch):
+    return (
+        ([(act1b, pitch, 2 * pitch), (act1, 0, (height - 2) * pitch)], 1),
+        ([(act2b, 0, 4 * pitch), (act2, 0, (height - 4) * pitch)], 2),
+    )
+
+
+def centre_cells(layers, which, mean, breadth, groups, out):
+    pitch = groups * 16
+    for layer, (parts, offset) in enumerate(layers):
+
+        @pl.when(which == layer)
+        def _(parts=parts, offset=offset):
+            own, n = wide(span(groups, offset, offset + breadth), out.shape[1]), 0
+            for ref, start, count in parts:
+                for at in range(start, start + count, pitch):
+                    out[n : n + pitch, :] = ((ref[at : at + pitch, :] - mean) * own).astype(BF)
+                    n += pitch
+
+
 def front(dims, place, even, odd, taps1, taps2, act1, act2, w1, w2, *rest):
-    (taps2b, act1b, slope1b, act2b, slope2b, centred, mine, sent) = rest[:8]
-    (rim, buf, stat) = rest[8:]
+    (taps2b, act1b, slope1b, act2b, slope2b, mine, sent) = rest[:7]
+    (rim, buf, stat, centred) = rest[7:]
     height, breadth, groups, limits = dims
     pitch = groups * 16
     width = w1.shape[1]
+    blocks = width // BLOCK
     rows = [(odd, even, REACH - 2), (odd, even, REACH - 1), (even, odd, 0), (even, odd, 1)]
     rim_taps(rim, rows, place, buf, groups)
     low = 3 - place[2]
@@ -283,45 +304,42 @@
     for n in range(2):
         second_rows(finds[n], w2, act2b, slope2b, 2 * n * pitch, groups)
     cells = height * breadth
-    first_parts = [(act1b, pitch, 2 * pitch), (act1, 0, (height - 2) * pitch)]
-    second_parts = [(act2b, 0, 4 * pitch), (act2, 0, (height - 4) * pitch)]
-    for layer, (parts, offset) in enumerate(((first_parts, 1), (second_parts, 2))):
+    layers = cell_parts(act1b, act1, act2b, act2, height, pitch)
+    for layer, (parts, offset) in enumerate(layers):
         own = wide(span(groups, offset, offset + breadth), width)
         total = jnp.zeros((pitch, width), F32)
         for ref, start, count in parts:
             for at in range(start, start + count, pitch):
                 total = total + ref[at : at + pitch, :]
         mean = jnp.sum(total * own, axis=0, keepdims=True) * (1.0 / cells)
-        n = 0
-        for ref, start, count in parts:
-            for at in range(start, start + count, pitch):
-                centred[layer, n : n + pitch, :] = ((ref[at : at + pitch, :] - mean) * own).astype(
-                    BF
-                )
-                n += pitch
         stat[layer] = jnp.zeros(stat.shape[1:], F32)
         put_mean(stat.at[layer, 0:EXTRA], mean, 2)
         put_mean(stat.at[layer, EXTRA : 2 * EXTRA], mean, 1)
+    mean = get_mean(stat[1 - place[0], EXTRA : EXTRA + 8, :], blocks, 1)
+    centre_cells(layers, 1 - place[0], mean, breadth, groups, centred)
     rows = sent.shape[0] - EXTRA
 
     def put(at, value):
         sent[at : at + value.shape[0], :] = value.astype(BF)
 
     emit, finish = packer(width, rows, put)
-    other = centred[1 - place[0]]
-    panels(other, other, emit)
+    panels(centred[...], centred[...], emit)
     finish()
     mine[...] = stat[place[0], EXTRA : EXTRA + 8, :]
     sent[rows:, :] = stat[1 - place[0], 0:EXTRA, :].astype(BF)
 
 
-def hold(place, centred, keep):
+def hold(dims, place, act1b, act1, act2b, act2, mine, keep, centred):
+    height, breadth, groups, _ = dims
+    layers = cell_parts(act1b, act1, act2b, act2, height, groups * 16)
+    mean = get_mean(mine[...], centred.shape[1] // BLOCK, 1)
+    centre_cells(layers, place[0], mean, breadth, groups, centred)
+
     def put(at, value):
         keep[at : at + value.shape[0], :] = value
 
-    own = centred[place[0]]
-    emit, finish = packer(own.shape[1], keep.shape[0], put)
-    panels(own, own, emit)
+    emit, finish = packer(centred.shape[1], keep.shape[0], put)
+    panels(centred[...], centred[...], emit)
     finish()
 
 
@@ -641,14 +659,13 @@
         flops=cost(height - 2, height - 4),
         limit=24,
     )
-    taps2b, act1b, slope1b, act2b, slope2b, centred, mine, sent = call(
+    taps2b, act1b, slope1b, act2b, slope2b, mine, sent = call(
         functools.partial(front, dims),
         [place, even, odd, taps1, taps2, act1, act2, w1, w2],
         [shape((4 * wider, width), BF)]
         + maps(4)
         + maps(4)
         + [
-            shape((2, height * pitch, width), BF),
             shape((8, BLOCK), F32),
             shape((packed + EXTRA, BLOCK), BF),
         ],
@@ -656,6 +673,7 @@
             pltpu.VMEM((4 * wider, depth), BF),
             pltpu.VMEM((depth // BLOCK, 4 * space, BLOCK), F32),
             pltpu.VMEM((2, 2 * EXTRA, BLOCK), F32),
+            pltpu.VMEM((height * pitch, width), BF),
         ],
         flops=cost(4, 4),
         limit=24,
@@ -708,10 +726,10 @@
     part, centre = shape((chunk, BLOCK), F32), shape((8, BLOCK), F32)
     got = lax.ppermute(sent, "tile", swap)
     (keep,) = call(
-        hold,
-        [place, centred],
+        functools.partial(hold, dims),
+        [place, act1b, act1, act2b, act2, mine],
         [shape((packed, BLOCK), F32)],
-        [],
+        [pltpu.VMEM((height * pitch, width), BF)],
         flops=2 * width * width * height * pitch,
     )
     share, mean, *sents = call(

time: 58.9 us -> 58.7 us (level)
  transfers between devices with their start and end apart: 18 -> 18, of which waited for: 6 -> 6; matrix products, arithmetic and copies ran while one was open for 0% -> 0% of each run, Pallas kernels for 17% -> 18%
where the time goes in v12:
time: 58.7 us; the launch traced here: 58.5 us
  Pallas kernels  24.1 us (41%)
  starting transfers between devices  23.7 us (40%)
  waiting for transfers between devices  9.92 us (17%)
    pallas_call x13, Pallas kernels, call(): pl.pallas_call(body, out_shape=tuple(outs), in_specs=[HBM if n in far els...  24.1 us
    ppermute x3, starting transfers between devices, local(): lax.ppermute(sents[k - 1], 'grp', [(i, i ^ k) for i in range(groups)])  6.62 us
    ppermute x3, waiting for transfers between devices, local(): lax.ppermute(sent, 'tile', [(i, i ^ 2 * k) for i in range(tiles)])  4.69 us
    ppermute x1, starting transfers between devices, local(): far = lax.ppermute(far, 'tile', cross)  4.58 us
    ppermute x3, starting transfers between devices, local(): lax.ppermute(sent, 'tile', [(i, i ^ 2 * k) for i in range(tiles)])  3.61 us
    ppermute x3, waiting for transfers between devices, local(): lax.ppermute(sents[k - 1], 'grp', [(i, i ^ k) for i in range(groups)])  3.52 us
    ppermute x4, starting transfers between devices, local(): other = [lax.ppermute(piece, 'tile', swap) for piece in mine]  3.48 us
    ppermute x3, starting transfers between devices, local(): lax.ppermute(share, 'grp', [(i, i ^ k) for i in range(groups)])  2.71 us
  transfers between devices with their start and end apart: 18, of which 6 were waited for; matrix products, arithmetic and copies ran while one was open for 0% of the time, Pallas kernels for 18%

profile of v12, /device:TPU:1, one launch (start us, length us, event | category | flops | bytes accessed | tf_op | source)
XLA Modules:
  0.0 58.5 jit_solution(15087179825084966358)
XLA Ops:
  0.0 1.0 %shard_map.46 = (bf16[8,4,256]{2,1,0:T(4,128)(2,1)S(1)}, bf16[8,4,256]{2,1,0:T(4,128)(2,1)S(1)}) custom-call(f32[8,64,256]{2,1,0:T(8,128)} %refs_0_.6), custom_call_target="tpu_custom_call" | custom-call | flops 4000000000 | bytes 557056 | tf_op jit(solution)/shard_map/pallas_call | solution.py:583
  1.0 4.6 %collective-permute-start = (bf16[8,4,256]{2,1,0:T(4,128)(2,1)S(1)}, bf16[8,4,256]{2,1,0:T(4,128)(2,1)S(1)}, u32[]{:S(2)}, u32[]{:S(2)}) collective-permute-start(bf16[8,4,256]{2,1,0:T(4,128)(2,1)S(1)} %get-tuple-element.34), channel_id=1, source_target_pairs={{1,2},{3,4},{5,6},{2,1},{4,3},{6,5},{9,10},{11,12},{13,14},{10,9},... | collective-permute-start | bytes 49160 | tf_op jit(solution)/shard_map/ppermute | solution.py:623
  5.6 0.0 slice-start
  5.6 0.0 slice-start.1
  5.6 0.0 copy-start
  5.6 0.1 collective-permute-start.1
  5.7 1.3 %collective-permute-done.refs_1_ = bf16[8,4,256]{2,1,0:T(4,128)(2,1)S(1)} collective-permute-done((bf16[8,4,256]{2,1,0:T(4,128)(2,1)S(1)}, bf16[8,4,256]{2,1,0:T(4,128)(2,1)S(1)}, u32[]{:S(2)}, u32[]{:S(2)}) %collective-permute-start) | collective-permute-done | bytes 16416 | tf_op jit(solution)/shard_map/ppermute | solution.py:623
  7.0 0.0 collective-permute-done.1.refs_2_
  7.0 0.1 shard_map.48
  7.1 1.3 %collective-permute-start.2 = (bf16[4,72,256]{2,1,0:T(8,128)(2,1)S(1)}, bf16[4,72,256]{2,1,0:T(8,128)(2,1)S(1)}, u32[]{:S(2)}, u32[]{:S(2)}) collective-permute-start(bf16[4,72,256]{2,1,0:T(8,128)(2,1)S(1)} %get-tuple-element.38), channel_id=1, source_target_pairs={{0,8},{16,24},{8,0},{24,16},{1,9},{17,25},{9,1},{25,17},{2,10},{18... | collective-permute-start | bytes 442376 | tf_op jit(solution)/shard_map/ppermute | solution.py:638
  8.3 0.7 %collective-permute-start.3 = (bf16[4,72,256]{2,1,0:T(8,128)(2,1)S(1)}, bf16[4,72,256]{2,1,0:T(8,128)(2,1)S(1)}, u32[]{:S(2)}, u32[]{:S(2)}) collective-permute-start(bf16[4,72,256]{2,1,0:T(8,128)(2,1)S(1)} %get-tuple-element.39), channel_id=1, source_target_pairs={{8,16},{16,8},{9,17},{17,9},{10,18},{18,10},{11,19},{19,11},{12,20... | collective-permute-start | bytes 442376 | tf_op jit(solution)/shard_map/ppermute | solution.py:639
  9.0 3.7 %shard_map.47 = (bf16[896,256]{1,0:T(8,128)(2,1)S(1)}, bf16[672,512]{1,0:T(8,128)(2,1)S(1)}, f32[480,512]{1,0:T(8,128)S(1)}, f32[480,512]{1,0:T(8,128)S(1)}, f32...) custom-call(f32[8,64,256]{2,1,0:T(8,128)S(1)} %copy-done.2, bf16[8,4,256]{2,1,0:T(4,128)(2,1)S(1)} %collective-permute-done.refs_1_, ...), custom_call_target="tpu_custom_call" | custom-call | flops 2642411520 | bytes 12058624 | tf_op jit(solution)/shard_map/pallas_call | solution.py:583
  12.7 0.0 collective-permute-done.2.refs_0_
  12.7 3.9 %shard_map.49 = (bf16[448,512]{1,0:T(8,128)(2,1)S(1)}, f32[320,512]{1,0:T(8,128)S(1)}, f32[320,512]{1,0:T(8,128)S(1)}, f32[320,512]{1,0:T(8,128)S(1)}, f32[320,5...) custom-call(bf16[4,72,256]{2,1,0:T(8,128)(2,1)S(1)} %collective-permute-done.2.refs_0_, ...), custom_call_target="tpu_custom_call" | custom-call | flops 2264924160 | bytes 13524992 | tf_op jit(solution)/shard_map/pallas_call | solution.py:583
  16.6 0.7 %collective-permute-start.4 = (bf16[1104,128]{1,0:T(8,128)(2,1)S(1)}, bf16[1104,128]{1,0:T(8,128)(2,1)S(1)}, u32[]{:S(2)}, u32[]{:S(2)}) collective-permute-start(bf16[1104,128]{1,0:T(8,128)(2,1)S(1)} %get-tuple-element.52), channel_id=1, source_target_pairs={{0,1},{1,0},{2,3},{3,2},{4,5},{5,4},{6,7},{7,6},{8,9},{9,8},{10,11... | collective-permute-start | bytes 847880 | tf_op jit(solution)/shard_map/ppermute | solution.py:727
  17.3 0.8 %shard_map.51.refs_0_ = f32[1088,128]{1,0:T(8,128)S(1)} custom-call(f32[320,512]{1,0:T(8,128)S(1)} %get-tuple-element.43.refs_0_.refs_2_, f32[480,512]{1,0:T(8,128)S(1)} %get-tuple-element.36.refs_4_.refs_1_.refs_0_, f32[320,512]{1,0:T(8,128)S(1)} %get-tuple-element.46.refs_2_.refs_6_, f32[320,512]{1,0:T(8,128)S(1)} %get-tuple-element.42.refs_5_.refs_3_.refs_4_, ...), custom_call_target="tpu_custom_call" | custom-call | flops 335544320 | bytes 3510272 | tf_op jit(solution)/shard_map/pallas_call | solution.py:583
  18.1 0.4 collective-permute-done.4.refs_2_
  18.5 0.4 shard_map.52
  18.9 5.4 %collective-permute-start.5 = (bf16[288,128]{1,0:T(8,128)(2,1)S(1)}, bf16[288,128]{1,0:T(8,128)(2,1)S(1)}, u32[]{:S(2)}, u32[]{:S(2)}) collective-permute-start(bf16[288,128]{1,0:T(8,128)(2,1)S(1)} %get-tuple-element.55), channel_id=1, source_target_pairs={{0,8},{8,0},{16,24},{24,16},{1,9},{9,1},{17,25},{25,17},{2,10},{10... | collective-permute-start | bytes 221192 | tf_op jit(solution)/shard_map/ppermute | solution.py:742
  24.3 0.0 collective-permute-start.6
  24.3 1.3 %collective-permute-start.7 = (bf16[288,128]{1,0:T(8,128)(2,1)S(1)}, bf16[288,128]{1,0:T(8,128)(2,1)S(1)}, u32[]{:S(2)}, u32[]{:S(2)}) collective-permute-start(bf16[288,128]{1,0:T(8,128)(2,1)S(1)} %get-tuple-element.57), channel_id=1, source_target_pairs={{0,24},{8,16},{16,8},{24,0},{1,25},{9,17},{17,9},{25,1},{2,26},{10... | collective-permute-start | bytes 221192 | tf_op jit(solution)/shard_map/ppermute | solution.py:742
  25.5 1.0 %collective-permute-done.5.refs_2_ = bf16[288,128]{1,0:T(8,128)(2,1)S(1)} collective-permute-done((bf16[288,128]{1,0:T(8,128)(2,1)S(1)}, bf16[288,128]{1,0:T(8,128)(2,1)S(1)}, u32[]{:S(2)}, u32[]{:S(2)}) %collective-permute-start.5) | collective-permute-done | bytes 73760 | tf_op jit(solution)/shard_map/ppermute | solution.py:742
  26.5 0.9 %collective-permute-done.6.refs_3_ = bf16[288,128]{1,0:T(8,128)(2,1)S(1)} collective-permute-done((bf16[288,128]{1,0:T(8,128)(2,1)S(1)}, bf16[288,128]{1,0:T(8,128)(2,1)S(1)}, u32[]{:S(2)}, u32[]{:S(2)}) %collective-permute-start.6) | collective-permute-done | bytes 73760 | tf_op jit(solution)/shard_map/ppermute | solution.py:742
  27.5 1.6 %collective-permute-done.7.refs_4_ = bf16[288,128]{1,0:T(8,128)(2,1)S(1)} collective-permute-done((bf16[288,128]{1,0:T(8,128)(2,1)S(1)}, bf16[288,128]{1,0:T(8,128)(2,1)S(1)}, u32[]{:S(2)}, u32[]{:S(2)}) %collective-permute-start.7) | collective-permute-done | bytes 73760 | tf_op jit(solution)/shard_map/ppermute | solution.py:742
  29.0 0.4 shard_map.53
  29.4 3.1 %collective-permute-start.10 = (bf16[288,128]{1,0:T(8,128)(2,1)S(1)}, bf16[288,128]{1,0:T(8,128)(2,1)S(1)}, u32[]{:S(2)}, u32[]{:S(2)}) collective-permute-start(bf16[288,128]{1,0:T(8,128)(2,1)S(1)} %get-tuple-element.60), channel_id=1, source_target_pairs={{0,6},{1,7},{2,4},{3,5},{4,2},{5,3},{6,0},{7,1},{8,14},{9,15},{10,... | collective-permute-start | bytes 221192 | tf_op jit(solution)/shard_map/ppermute | solution.py:752
  32.5 0.0 collective-permute-start.9
  32.5 0.5 collective-permute-start.8
  33.0 1.1 %shard_map.57.refs_19_ = bf16[4608,256]{1,0:T(8,128)(2,1)S(1)} custom-call(bf16[9,256,512]{2,1,0:T(8,128)(2,1)S(1)} %bitcast.12), custom_call_target="tpu_custom_call" | custom-call | flops 2000000000 | bytes 4718592 | tf_op jit(solution)/shard_map/pallas_call | solution.py:583
  34.1 0.5 copy-done.1
  34.6 0.3 shard_map.54.refs_5_
  34.9 4.7 %collective-permute-done.9.refs_3_ = bf16[288,128]{1,0:T(8,128)(2,1)S(1)} collective-permute-done((bf16[288,128]{1,0:T(8,128)(2,1)S(1)}, bf16[288,128]{1,0:T(8,128)(2,1)S(1)}, u32[]{:S(2)}, u32[]{:S(2)}) %collective-permute-start.9) | collective-permute-done | bytes 73760 | tf_op jit(solution)/shard_map/ppermute | solution.py:752
  39.6 0.0 collective-permute-done.8.refs_2_
  39.6 0.4 shard_map.55
  40.0 0.6 %collective-permute-start.13 = (bf16[272,128]{1,0:T(8,128)(2,1)S(1)}, bf16[272,128]{1,0:T(8,128)(2,1)S(1)}, u32[]{:S(2)}, u32[]{:S(2)}) collective-permute-start(bf16[272,128]{1,0:T(8,128)(2,1)S(1)} %get-tuple-element.62), channel_id=1, source_target_pairs={{0,24},{8,16},{16,8},{24,0},{1,25},{9,17},{17,9},{25,1},{2,26},{10... | collective-permute-start | bytes 208904 | tf_op jit(solution)/shard_map/ppermute | solution.py:762
  40.7 1.2 %collective-permute-start.12 = (bf16[272,128]{1,0:T(8,128)(2,1)S(1)}, bf16[272,128]{1,0:T(8,128)(2,1)S(1)}, u32[]{:S(2)}, u32[]{:S(2)}) collective-permute-start(bf16[272,128]{1,0:T(8,128)(2,1)S(1)} %get-tuple-element.62), channel_id=1, source_target_pairs={{0,16},{8,24},{16,0},{24,8},{1,17},{9,25},{17,1},{25,9},{2,18},{10... | collective-permute-start | bytes 208904 | tf_op jit(solution)/shard_map/ppermute | solution.py:762
  41.9 0.8 %collective-permute-start.11 = (bf16[272,128]{1,0:T(8,128)(2,1)S(1)}, bf16[272,128]{1,0:T(8,128)(2,1)S(1)}, u32[]{:S(2)}, u32[]{:S(2)}) collective-permute-start(bf16[272,128]{1,0:T(8,128)(2,1)S(1)} %get-tuple-element.62), channel_id=1, source_target_pairs={{0,8},{8,0},{16,24},{24,16},{1,9},{9,1},{17,25},{25,17},{2,10},{10... | collective-permute-start | bytes 208904 | tf_op jit(solution)/shard_map/ppermute | solution.py:762
  42.7 1.7 %shard_map.56.refs_18_ = bf16[4608,512]{1,0:T(8,128)(2,1)S(1)} custom-call(bf16[9,512,512]{2,1,0:T(8,128)(2,1)S(1)} %bitcast.8), custom_call_target="tpu_custom_call" | custom-call | flops 2000000000 | bytes 9437184 | tf_op jit(solution)/shard_map/pallas_call | solution.py:583
  44.4 2.0 %collective-permute-start.14 = (bf16[288,128]{1,0:T(8,128)(2,1)S(1)}, bf16[288,128]{1,0:T(8,128)(2,1)S(1)}, u32[]{:S(2)}, u32[]{:S(2)}) collective-permute-start(bf16[288,128]{1,0:T(8,128)(2,1)S(1)} %get-tuple-element.61.refs_10_), channel_id=1, source_target_pairs={{0,1},{1,0},{2,3},{3,2},{4,5},{5,4},{6,7},{7,6},{8,9},{9,8},{10,11... | collective-permute-start | bytes 221192 | tf_op jit(solution)/shard_map/ppermute | solution.py:766
  46.4 0.0 collective-permute-done.13.refs_13_
  46.4 0.1 collective-permute-start.17
  46.5 0.7 %collective-permute-start.16 = (bf16[272,128]{1,0:T(8,128)(2,1)S(1)}, bf16[272,128]{1,0:T(8,128)(2,1)S(1)}, u32[]{:S(2)}, u32[]{:S(2)}) collective-permute-start(bf16[272,128]{1,0:T(8,128)(2,1)S(1)} %collective-permute-done.12.refs_12_), channel_id=1, source_target_pairs={{0,1},{1,0},{2,3},{3,2},{4,5},{5,4},{6,7},{7,6},{8,9},{9,8},{10,11... | collective-permute-start | bytes 208904 | tf_op jit(solution)/shard_map/ppermute | solution.py:766
  47.2 0.8 %collective-permute-start.15 = (bf16[272,128]{1,0:T(8,128)(2,1)S(1)}, bf16[272,128]{1,0:T(8,128)(2,1)S(1)}, u32[]{:S(2)}, u32[]{:S(2)}) collective-permute-start(bf16[272,128]{1,0:T(8,128)(2,1)S(1)} %collective-permute-done.11.refs_11_), channel_id=1, source_target_pairs={{0,1},{1,0},{2,3},{3,2},{4,5},{5,4},{6,7},{7,6},{8,9},{9,8},{10,11... | collective-permute-start | bytes 208904 | tf_op jit(solution)/shard_map/ppermute | solution.py:766
  47.9 3.0 %shard_map.50 = (f32[320,512]{1,0:T(8,128)S(1)}, f32[320,512]{1,0:T(8,128)S(1)}) custom-call(bf16[4,72,256]{2,1,0:T(8,128)(2,1)S(1)} %collective-permute-done.2.refs_0_, bf16[4,72,256]{2,1,0:T(8,128)(2,1)S(1)} %collective-permute-done.3.refs_1_, bf16[448,512]{1,0:T(8,128)(2,1)S(1)} %get-tuple-element.48.refs_2_, bf16[2304,512]{1,0:T(8,128)(2,1)S(1)} %bitcast.13, ...), custom_call_target="tpu_custom_call" | custom-call | flops 2264924160 | bytes 9142272 | tf_op jit(solution)/shard_map/pallas_call | solution.py:583
  50.9 0.0 collective-permute-done.14.refs_14_
  50.9 0.0 collective-permute-done.17.refs_17_
  50.9 0.0 collective-permute-done.15.refs_15_
  50.9 7.6 %shard_map.58 = f32[8,64,256]{2,1,0:T(8,128)} custom-call(f32[480,512]{1,0:T(8,128)S(1)} %get-tuple-element.36.refs_4_.refs_1_.refs_0_, f32[480,512]{1,0:T(8,128)S(1)} %get-tuple-element.37.refs_1_, f32[320,512]{1,0:T(8,128)S(1)} %get-tuple-element.43.refs_0_.refs_2_, f32[320,512]{1,0:T(8,128)S(1)} %get-tuple-element.44.refs_3_, ...), custom_call_target="tpu_custom_call" | custom-call | flops 5284823040 | bytes 15376384 | tf_op jit(solution)/shard_map/pallas_call | solution.py:583
  (12 shorter events, 0.0 us)
Async XLA Ops:
  0.0 7.0 %copy-start.2 = (f32[8,64,256]{2,1,0:T(8,128)S(1)}, f32[8,64,256]{2,1,0:T(8,128)}, u32[]{:S(2)}) copy-start(f32[8,64,256]{2,1,0:T(8,128)} %refs_0_.6) | copy-start | bytes 1572868
  1.0 6.0 %collective-permute-start = (bf16[8,4,256]{2,1,0:T(4,128)(2,1)S(1)}, bf16[8,4,256]{2,1,0:T(4,128)(2,1)S(1)}, u32[]{:S(2)}, u32[]{:S(2)}) collective-permute-start(bf16[8,4,256]{2,1,0:T(4,128)(2,1)S(1)} %get-tuple-element.34), channel_id=1, source_target_pairs={{1,2},{3,4},{5,6},{2,1},{4,3},{6,5},{9,10},{11,12},{13,14},{10,9},... | collective-permute-start | bytes 49160 | tf_op jit(solution)/shard_map/ppermute | solution.py:623
  5.6 3.4 %slice-start = ((s8[4718592]{0:T(1024)(128)(4,1)}), s8[4194304]{0:T(1024)(128)(4,1)S(1)}, s32[]{:S(2)}) async-start(s8[4718592]{0:T(1024)(128)(4,1)} %bitcast.4), calls=%async_computation | async-start | bytes 8388608
  5.6 3.4 %slice-start.1 = ((s8[4718592]{0:T(1024)(128)(4,1)}), s8[524288]{0:T(1024)(128)(4,1)S(1)}, s32[]{:S(2)}) async-start(s8[4718592]{0:T(1024)(128)(4,1)} %bitcast.4), calls=%async_computation.1 | async-start | bytes 1048576
  5.6 3.4 %copy-start = (bf16[3,3,256,512]{3,2,1,0:T(8,128)(2,1)S(1)}, bf16[3,3,256,512]{3,2,1,0:T(8,128)(2,1)}, u32[]{:S(2)}) copy-start(bf16[3,3,256,512]{3,2,1,0:T(8,128)(2,1)} %param.5) | copy-start | bytes 7077892
  5.6 1.4 %collective-permute-start.1 = (bf16[8,4,256]{2,1,0:T(4,128)(2,1)S(1)}, bf16[8,4,256]{2,1,0:T(4,128)(2,1)S(1)}, u32[]{:S(2)}, u32[]{:S(2)}) collective-permute-start(bf16[8,4,256]{2,1,0:T(4,128)(2,1)S(1)} %get-tuple-element.35), channel_id=1, source_target_pairs={{0,1},{1,0},{2,3},{3,2},{4,5},{5,4},{6,7},{7,6},{8,9},{9,8},{10,11... | collective-permute-start | bytes 49160 | tf_op jit(solution)/shard_map/ppermute | solution.py:624
  7.1 5.7 %collective-permute-start.2 = (bf16[4,72,256]{2,1,0:T(8,128)(2,1)S(1)}, bf16[4,72,256]{2,1,0:T(8,128)(2,1)S(1)}, u32[]{:S(2)}, u32[]{:S(2)}) collective-permute-start(bf16[4,72,256]{2,1,0:T(8,128)(2,1)S(1)} %get-tuple-element.38), channel_id=1, source_target_pairs={{0,8},{16,24},{8,0},{24,16},{1,9},{17,25},{9,1},{25,17},{2,10},{18... | collective-permute-start | bytes 442376 | tf_op jit(solution)/shard_map/ppermute | solution.py:638
  8.3 4.4 %collective-permute-start.3 = (bf16[4,72,256]{2,1,0:T(8,128)(2,1)S(1)}, bf16[4,72,256]{2,1,0:T(8,128)(2,1)S(1)}, u32[]{:S(2)}, u32[]{:S(2)}) collective-permute-start(bf16[4,72,256]{2,1,0:T(8,128)(2,1)S(1)} %get-tuple-element.39), channel_id=1, source_target_pairs={{8,16},{16,8},{9,17},{17,9},{10,18},{18,10},{11,19},{19,11},{12,20... | collective-permute-start | bytes 442376 | tf_op jit(solution)/shard_map/ppermute | solution.py:639
  16.6 1.9 %collective-permute-start.4 = (bf16[1104,128]{1,0:T(8,128)(2,1)S(1)}, bf16[1104,128]{1,0:T(8,128)(2,1)S(1)}, u32[]{:S(2)}, u32[]{:S(2)}) collective-permute-start(bf16[1104,128]{1,0:T(8,128)(2,1)S(1)} %get-tuple-element.52), channel_id=1, source_target_pairs={{0,1},{1,0},{2,3},{3,2},{4,5},{5,4},{6,7},{7,6},{8,9},{9,8},{10,11... | collective-permute-start | bytes 847880 | tf_op jit(solution)/shard_map/ppermute | solution.py:727
  18.9 7.6 %collective-permute-start.5 = (bf16[288,128]{1,0:T(8,128)(2,1)S(1)}, bf16[288,128]{1,0:T(8,128)(2,1)S(1)}, u32[]{:S(2)}, u32[]{:S(2)}) collective-permute-start(bf16[288,128]{1,0:T(8,128)(2,1)S(1)} %get-tuple-element.55), channel_id=1, source_target_pairs={{0,8},{8,0},{16,24},{24,16},{1,9},{9,1},{17,25},{25,17},{2,10},{10... | collective-permute-start | bytes 221192 | tf_op jit(solution)/shard_map/ppermute | solution.py:742
  24.3 3.2 %collective-permute-start.6 = (bf16[288,128]{1,0:T(8,128)(2,1)S(1)}, bf16[288,128]{1,0:T(8,128)(2,1)S(1)}, u32[]{:S(2)}, u32[]{:S(2)}) collective-permute-start(bf16[288,128]{1,0:T(8,128)(2,1)S(1)} %get-tuple-element.56), channel_id=1, source_target_pairs={{0,16},{8,24},{16,0},{24,8},{1,17},{9,25},{17,1},{25,9},{2,18},{10... | collective-permute-start | bytes 221192 | tf_op jit(solution)/shard_map/ppermute | solution.py:742
  24.3 4.8 %collective-permute-start.7 = (bf16[288,128]{1,0:T(8,128)(2,1)S(1)}, bf16[288,128]{1,0:T(8,128)(2,1)S(1)}, u32[]{:S(2)}, u32[]{:S(2)}) collective-permute-start(bf16[288,128]{1,0:T(8,128)(2,1)S(1)} %get-tuple-element.57), channel_id=1, source_target_pairs={{0,24},{8,16},{16,8},{24,0},{1,25},{9,17},{17,9},{25,1},{2,26},{10... | collective-permute-start | bytes 221192 | tf_op jit(solution)/shard_map/ppermute | solution.py:742
  29.4 5.5 %collective-permute-start.10 = (bf16[288,128]{1,0:T(8,128)(2,1)S(1)}, bf16[288,128]{1,0:T(8,128)(2,1)S(1)}, u32[]{:S(2)}, u32[]{:S(2)}) collective-permute-start(bf16[288,128]{1,0:T(8,128)(2,1)S(1)} %get-tuple-element.60), channel_id=1, source_target_pairs={{0,6},{1,7},{2,4},{3,5},{4,2},{5,3},{6,0},{7,1},{8,14},{9,15},{10,... | collective-permute-start | bytes 221192 | tf_op jit(solution)/shard_map/ppermute | solution.py:752
  32.5 7.1 %collective-permute-start.9 = (bf16[288,128]{1,0:T(8,128)(2,1)S(1)}, bf16[288,128]{1,0:T(8,128)(2,1)S(1)}, u32[]{:S(2)}, u32[]{:S(2)}) collective-permute-start(bf16[288,128]{1,0:T(8,128)(2,1)S(1)} %get-tuple-element.60), channel_id=1, source_target_pairs={{0,4},{1,5},{2,6},{3,7},{4,0},{5,1},{6,2},{7,3},{8,12},{9,13},{10,... | collective-permute-start | bytes 221192 | tf_op jit(solution)/shard_map/ppermute | solution.py:752
  32.5 7.1 %collective-permute-start.8 = (bf16[288,128]{1,0:T(8,128)(2,1)S(1)}, bf16[288,128]{1,0:T(8,128)(2,1)S(1)}, u32[]{:S(2)}, u32[]{:S(2)}) collective-permute-start(bf16[288,128]{1,0:T(8,128)(2,1)S(1)} %get-tuple-element.60), channel_id=1, source_target_pairs={{0,2},{1,3},{2,0},{3,1},{4,6},{5,7},{6,4},{7,5},{8,10},{9,11},{10,... | collective-permute-start | bytes 221192 | tf_op jit(solution)/shard_map/ppermute | solution.py:752
  33.0 1.6 %copy-start.1 = (f32[2,512,512]{2,1,0:T(8,128)S(1)}, f32[2,512,512]{2,1,0:T(8,128)}, u32[]{:S(2)}) copy-start(f32[2,512,512]{2,1,0:T(8,128)} %refs_0_.7) | copy-start | bytes 6291460
  40.0 6.4 %collective-permute-start.13 = (bf16[272,128]{1,0:T(8,128)(2,1)S(1)}, bf16[272,128]{1,0:T(8,128)(2,1)S(1)}, u32[]{:S(2)}, u32[]{:S(2)}) collective-permute-start(bf16[272,128]{1,0:T(8,128)(2,1)S(1)} %get-tuple-element.62), channel_id=1, source_target_pairs={{0,24},{8,16},{16,8},{24,0},{1,25},{9,17},{17,9},{25,1},{2,26},{10... | collective-permute-start | bytes 208904 | tf_op jit(solution)/shard_map/ppermute | solution.py:762
  40.7 5.9 %collective-permute-start.12 = (bf16[272,128]{1,0:T(8,128)(2,1)S(1)}, bf16[272,128]{1,0:T(8,128)(2,1)S(1)}, u32[]{:S(2)}, u32[]{:S(2)}) collective-permute-start(bf16[272,128]{1,0:T(8,128)(2,1)S(1)} %get-tuple-element.62), channel_id=1, source_target_pairs={{0,16},{8,24},{16,0},{24,8},{1,17},{9,25},{17,1},{25,9},{2,18},{10... | collective-permute-start | bytes 208904 | tf_op jit(solution)/shard_map/ppermute | solution.py:762
  41.9 5.3 %collective-permute-start.11 = (bf16[272,128]{1,0:T(8,128)(2,1)S(1)}, bf16[272,128]{1,0:T(8,128)(2,1)S(1)}, u32[]{:S(2)}, u32[]{:S(2)}) collective-permute-start(bf16[272,128]{1,0:T(8,128)(2,1)S(1)} %get-tuple-element.62), channel_id=1, source_target_pairs={{0,8},{8,0},{16,24},{24,16},{1,9},{9,1},{17,25},{25,17},{2,10},{10... | collective-permute-start | bytes 208904 | tf_op jit(solution)/shard_map/ppermute | solution.py:762
  44.4 6.5 %collective-permute-start.14 = (bf16[288,128]{1,0:T(8,128)(2,1)S(1)}, bf16[288,128]{1,0:T(8,128)(2,1)S(1)}, u32[]{:S(2)}, u32[]{:S(2)}) collective-permute-start(bf16[288,128]{1,0:T(8,128)(2,1)S(1)} %get-tuple-element.61.refs_10_), channel_id=1, source_target_pairs={{0,1},{1,0},{2,3},{3,2},{4,5},{5,4},{6,7},{7,6},{8,9},{9,8},{10,11... | collective-permute-start | bytes 221192 | tf_op jit(solution)/shard_map/ppermute | solution.py:766
  46.4 4.5 %collective-permute-start.17 = (bf16[272,128]{1,0:T(8,128)(2,1)S(1)}, bf16[272,128]{1,0:T(8,128)(2,1)S(1)}, u32[]{:S(2)}, u32[]{:S(2)}) collective-permute-start(bf16[272,128]{1,0:T(8,128)(2,1)S(1)} %collective-permute-done.13.refs_13_), channel_id=1, source_target_pairs={{0,1},{1,0},{2,3},{3,2},{4,5},{5,4},{6,7},{7,6},{8,9},{9,8},{10,11... | collective-permute-start | bytes 208904 | tf_op jit(solution)/shard_map/ppermute | solution.py:766
  46.5 4.4 %collective-permute-start.16 = (bf16[272,128]{1,0:T(8,128)(2,1)S(1)}, bf16[272,128]{1,0:T(8,128)(2,1)S(1)}, u32[]{:S(2)}, u32[]{:S(2)}) collective-permute-start(bf16[272,128]{1,0:T(8,128)(2,1)S(1)} %collective-permute-done.12.refs_12_), channel_id=1, source_target_pairs={{0,1},{1,0},{2,3},{3,2},{4,5},{5,4},{6,7},{7,6},{8,9},{9,8},{10,11... | collective-permute-start | bytes 208904 | tf_op jit(solution)/shard_map/ppermute | solution.py:766
  47.2 3.8 %collective-permute-start.15 = (bf16[272,128]{1,0:T(8,128)(2,1)S(1)}, bf16[272,128]{1,0:T(8,128)(2,1)S(1)}, u32[]{:S(2)}, u32[]{:S(2)}) collective-permute-start(bf16[272,128]{1,0:T(8,128)(2,1)S(1)} %collective-permute-done.11.refs_11_), channel_id=1, source_target_pairs={{0,1},{1,0},{2,3},{3,2},{4,5},{5,4},{6,7},{7,6},{8,9},{9,8},{10,11... | collective-permute-start | bytes 208904 | tf_op jit(solution)/shard_map/ppermute | solution.py:766
